TPU v7x, 256 devices: a whole 4x4x8 slice. The times are simulated.
256 devices in a mesh: seq: 64 (over y, z, x_hi), tp: 4 (over x_lo, core).
Axes of the slice: x: 4 (x_hi: 2, x_lo: 2; x = x_hi * 2 + x_lo), y: 4, z: 8, core: 2. Of those that a mesh axis runs over, the one named last changes fastest.
Arguments:
- query_input: bfloat16 [8192, 4096], P('seq', 'tp'), may hold values from -6 to 6
- key_input: bfloat16 [8192, 4096], P('seq', 'tp'), may hold values from -6 to 6
- value_input: bfloat16 [8192, 4096], P('seq', 'tp'), may hold values from -6 to 6
- short_filter: float32 [3, 3, 4096], P(None, None, 'tp'), may hold values from -3 to 3
- residues: float32 [16, 4096], P(None, 'tp'), may hold values from -1.5 to 1.5
- decays: float32 [16, 4096], P(None, 'tp'), as said below
- skip_gain: float32 [4096], P('tp'), may hold values from -4 to 4
- head_weight: bfloat16 [32, 4096, 128], P(None, ('tp', 'seq')), may hold values from -0.015625 to 0.015625
Outputs:
- operator_out: bfloat16 [8192, 4096], P('seq', 'tp')
- probe_out: bfloat16 [512, 128], P(('seq', 'tp'))
Inputs may be any that keep to these rules, and one draw needn't show every extreme that they name: `decays`: each rate is positive, at least 1 / 16384 and at most 1 / 30.
All inputs are finite; a program needn't handle non-finite values.
Results may differ from a plain program's by a relative error of at most 0.01.
Values may be sent and summed in bfloat16 or wider, within the bound.
No kernel may reach another device: no remote copies, remote signals or barrier semaphores. Data moves between devices by JAX's collectives and lax.ppermute only.
A program may use at most 64 MiB of HBM per device.

v0:
```python
import math

import jax
import jax.numpy as jnp
from jax import lax
from jax.sharding import PartitionSpec as P

STRIDE = 16


highest = lax.Precision.HIGHEST
full_turn = 2.0 * math.pi


def from_behind(block, axis, distance):
    devices = range(lax.axis_size(axis))
    route = [(i - distance, i) for i in devices if i - distance in devices]
    return lax.ppermute(block, axis, route)


def short_pass(rows_block, before, tap_weights):
    joined = jnp.concatenate([before, rows_block], axis=0).astype(jnp.float32)
    row_count = rows_block.shape[0]
    return (
        tap_weights[0] * joined[2 : 2 + row_count]
        + tap_weights[1] * joined[1 : 1 + row_count]
        + tap_weights[2] * joined[0:row_count]
    )


def phase_table(row_index, col_index, period, direction):
    product = row_index[:, None] * col_index[None, :] % period
    phase_angle = full_turn / period * product.astype(jnp.float32)
    return (jnp.cos(phase_angle), direction * jnp.sin(phase_angle))


def stacked_table(cosine, sine_part):
    upper_half = jnp.concatenate([cosine, sine_part], axis=1)
    lower_half = jnp.concatenate([-sine_part, cosine], axis=1)
    return jnp.concatenate([upper_half, lower_half], axis=0)


def paired_table(table_pair):
    cosine, sine_part = table_pair
    return jnp.stack(
        [jnp.stack([cosine, sine_part], axis=1), jnp.stack([-sine_part, cosine], axis=1)], axis=0
    )


def rotate(real_part, imag_part, cosine, sine_part):
    return (real_part * cosine - imag_part * sine_part, real_part * sine_part + imag_part * cosine)


def filter_spectrum(frequency, residues, decays, length, period):

    def one_group(block_freq):
        phase_angle = full_turn / period * block_freq.astype(jnp.float32)
        half_sine = jnp.sin(0.5 * phase_angle)[None, :, :, :, None]
        full_sine = jnp.sin(phase_angle)[None, :, :, :, None]
        parity = (1.0 - 2.0 * (block_freq % 2).astype(jnp.float32))[None, :, :, :, None]
        decay_rate = decays[:, None, None, None, :]
        keep_frac = jnp.exp(-decay_rate)
        denom_real = -jnp.expm1(-decay_rate) + 2.0 * keep_frac * half_sine * half_sine
        denom_imag = keep_frac * full_sine
        tail_term = 1.0 - jnp.exp(-decay_rate * length) * parity
        weight = (
            residues[:, None, None, None, :]
            * jnp.sqrt(-jnp.expm1(-2.0 * decay_rate))
            * tail_term
            / (denom_real * denom_real + denom_imag * denom_imag)
        )
        return (jnp.sum(weight * denom_real, axis=0), jnp.sum(-weight * denom_imag, axis=0))

    return lax.map(one_group, frequency)


def transform_conv(gated, residues, decays, skip_gain, query_short):
    tokens, chan_width = gated.shape
    half_width = chan_width // 2
    parties = lax.axis_size("seq")
    position = lax.axis_index("seq")
    group_rows = tokens // parties
    length = tokens * parties
    period = 2 * length
    first_size = 1
    while first_size * first_size * 4 <= tokens and tokens % (first_size * 2) == 0:
        first_size = first_size * 2
    second_size = tokens // first_size
    columns = lax.all_to_all(
        gated.reshape(tokens, 1, chan_width), "seq", split_axis=0, concat_axis=1, tiled=True
    )
    low_index = jnp.arange(parties, dtype=jnp.int32)
    high_index = jnp.where(low_index == 0, parties, 2 * parties - low_index)
    freq_order = jnp.stack([low_index, high_index], axis=1).reshape(2 * parties)
    cosine, sine_part = phase_table(low_index, freq_order, 2 * parties, -1.0)
    packed = jnp.concatenate(
        [columns[:, :, :half_width], columns[:, :, half_width:]], axis=1
    ).astype(jnp.float32)
    across = jnp.einsum("gqj,qk->gkj", packed, stacked_table(cosine, sine_part), precision=highest)
    local_rows = position * group_rows + jnp.arange(group_rows, dtype=jnp.int32)
    twist_cos, twist_sin = phase_table(local_rows, freq_order, period, -1.0)
    real_part, imag_part = rotate(
        across[:, : 2 * parties],
        across[:, 2 * parties :],
        twist_cos[:, :, None],
        twist_sin[:, :, None],
    )
    spectral = (
        lax.all_to_all(
            real_part.astype(jnp.bfloat16), "seq", split_axis=1, concat_axis=0, tiled=True
        ).astype(real_part.dtype),
        lax.all_to_all(
            imag_part.astype(jnp.bfloat16), "seq", split_axis=1, concat_axis=0, tiled=True
        ).astype(imag_part.dtype),
    )
    first_index = jnp.arange(first_size, dtype=jnp.int32)
    second_index = jnp.arange(second_size, dtype=jnp.int32)
    stacked = jnp.stack(spectral, axis=0).reshape(2, first_size, second_size, 2, half_width)
    section_out = jnp.einsum(
        "rabej,rasc->scbej",
        stacked,
        paired_table(phase_table(first_index, first_index, first_size, -1.0)),
        precision=highest,
    )
    inner_cos, inner_sin = phase_table(first_index, second_index, tokens, -1.0)
    real_part, imag_part = rotate(
        section_out[0], section_out[1], inner_cos[:, :, None, None], inner_sin[:, :, None, None]
    )
    section_out = jnp.einsum(
        "rcbej,rbsd->scdej",
        jnp.stack([real_part, imag_part], axis=0),
        paired_table(phase_table(second_index, second_index, second_size, -1.0)),
        precision=highest,
    )
    own_freqs = lax.dynamic_slice_in_dim(freq_order, 2 * position, 2, 0)
    inner_freq = first_index[:, None] + first_size * second_index[None, :]
    frequency = own_freqs[None, None, :] + 2 * parties * inner_freq[:, :, None]
    filter_real, filter_imag = filter_spectrum(
        frequency.reshape(4, first_size // 4, second_size, 2),
        residues,
        decays,
        float(length),
        period,
    )
    filter_real = filter_real.reshape(first_size, second_size, 2, chan_width)
    filter_imag = filter_imag.reshape(first_size, second_size, 2, chan_width)

    def partner(values):
        mirrored = jnp.flip(values, axis=(0, 1))
        shifted = jnp.concatenate(
            [jnp.roll(mirrored[first_size - 1 :], 1, axis=1), mirrored[: first_size - 1]], axis=0
        )
        at_anchor = jnp.concatenate([shifted[:, :, 0:1], mirrored[:, :, 1:2]], axis=2)
        return jnp.where(position == 0, at_anchor, mirrored[:, :, ::-1])

    own_real, own_imag = (section_out[0], section_out[1])
    other_real, other_imag = (partner(own_real), partner(own_imag))
    first_real = 0.5 * (own_real + other_real)
    first_imag = 0.5 * (own_imag - other_imag)
    second_real = 0.5 * (own_imag + other_imag)
    second_imag = 0.5 * (other_real - own_real)
    lead_real, lead_imag = (filter_real[..., :half_width], filter_imag[..., :half_width])
    tail_real, tail_imag = (filter_real[..., half_width:], filter_imag[..., half_width:])
    one_real = lead_real * first_real - lead_imag * first_imag
    one_imag = lead_real * first_imag + lead_imag * first_real
    two_real = tail_real * second_real - tail_imag * second_imag
    two_imag = tail_real * second_imag + tail_imag * second_real
    out_real = one_real - two_imag
    out_imag = one_imag + two_real
    section_out = jnp.einsum(
        "rcdej,rdsb->scbej",
        jnp.stack([out_real, out_imag], axis=0),
        paired_table(phase_table(second_index, second_index, second_size, 1.0)),
        precision=highest,
    )
    back_cos, back_sin = phase_table(first_index, second_index, tokens, 1.0)
    real_part, imag_part = rotate(
        section_out[0], section_out[1], back_cos[:, :, None, None], back_sin[:, :, None, None]
    )
    section_out = jnp.einsum(
        "rcbej,rcsa->sabej",
        jnp.stack([real_part, imag_part], axis=0),
        paired_table(phase_table(first_index, first_index, first_size, 1.0)),
        precision=highest,
    )
    all_rows = jnp.arange(tokens, dtype=jnp.int32)
    untwist_cos, untwist_sin = phase_table(all_rows, own_freqs, period, 1.0)
    real_part, imag_part = rotate(
        section_out[0].reshape(tokens, 2, half_width),
        section_out[1].reshape(tokens, 2, half_width),
        untwist_cos[:, :, None],
        untwist_sin[:, :, None],
    )
    returned = (
        lax.all_to_all(
            real_part.astype(jnp.bfloat16), "seq", split_axis=0, concat_axis=1, tiled=True
        ).astype(real_part.dtype),
        lax.all_to_all(
            imag_part.astype(jnp.bfloat16), "seq", split_axis=0, concat_axis=1, tiled=True
        ).astype(imag_part.dtype),
    )
    inverse_cos, inverse_sin = phase_table(freq_order, low_index, 2 * parties, 1.0)
    inverse_scale = 1.0 / period
    packed_back = jnp.concatenate([returned[0], returned[1]], axis=1)
    result = jnp.einsum(
        "gqj,qk->gkj",
        packed_back,
        stacked_table(inverse_cos * inverse_scale, inverse_sin * inverse_scale),
        precision=highest,
    )
    convolved = jnp.concatenate([result[:, :parties], result[:, parties:]], axis=2)
    carried = (convolved + skip_gain * columns.astype(jnp.float32)).astype(jnp.bfloat16)
    carried_rows = lax.all_to_all(carried, "seq", split_axis=1, concat_axis=0, tiled=True).reshape(
        tokens, chan_width
    )
    return (query_short * carried_rows.astype(jnp.float32)).astype(jnp.bfloat16)


def shards(
    query_input, key_input, value_input, short_filter, residues, decays, skip_gain, head_weight
):
    tokens, chan_width = query_input.shape
    before = from_behind((query_input[-2:], key_input[-2:], value_input[-2:]), "seq", 1)
    query_short = short_pass(query_input, before[0], short_filter[:, 0])
    key_short = short_pass(key_input, before[1], short_filter[:, 1])
    value_short = short_pass(value_input, before[2], short_filter[:, 2])
    gated = (key_short * value_short).astype(jnp.bfloat16)
    operator_out = transform_conv(gated, residues, decays, skip_gain, query_short)
    rim_rows = from_behind(operator_out[:STRIDE], "seq", -1)
    extended = jnp.concatenate([operator_out, rim_rows], axis=0).reshape(
        tokens // STRIDE + 1, STRIDE, chan_width
    )
    early_rows = extended[:-1]
    late_rows = extended[1:]
    weight_piece = lax.all_gather(head_weight, "seq", axis=1, tiled=True)
    running = jnp.einsum(
        "jic,ico->jo", early_rows, weight_piece[:STRIDE], preferred_element_type=jnp.float32
    )
    partial_sum = running + jnp.einsum(
        "jic,ico->jo", late_rows, weight_piece[STRIDE:], preferred_element_type=jnp.float32
    )
    probe_out = lax.psum_scatter(partial_sum, "tp", scatter_dimension=0, tiled=True).astype(
        jnp.bfloat16
    )
    return (operator_out, probe_out)


def solution(mesh):
    placed = (
        P("seq", "tp"),
        P("seq", "tp"),
        P("seq", "tp"),
        P(None, None, "tp"),
        P(None, "tp"),
        P(None, "tp"),
        P("tp"),
        P(None, ("tp", "seq"), None),
    )
    return jax.shard_map(
        shards,
        mesh=mesh,
        in_specs=placed,
        out_specs=(P("seq", "tp"), P(("seq", "tp"), None)),
        check_vma=False,
    )
```

profile of v0, /device:TPU:1, one launch (start us, length us, event | category | flops | bytes accessed | tf_op | source)
XLA Modules:
  0.0 234.3 jit_solution(15185731819811501961)
XLA Ops:
  7.9 5.5 %collective-permute-start.1 = (bf16[2,1024]{1,0:T(2,128)(2,1)S(1)}, bf16[2,1024]{1,0:T(2,128)(2,1)S(1)}, u32[]{:S(2)}, u32[]{:S(2)}) collective-permute-start(bf16[2,1024]{1,0:T(2,128)(2,1)S(1)} %slice.242), channel_id=1, source_target_pairs={{0,4},{4,8},{8,12},{12,16},{16,20},{20,24},{24,28},{28,32},{32,36}... | collective-permute-start | bytes 12296 | tf_op jit(solution)/shard_map/ppermute | solution.py:18
  14.1 3.5 %collective-permute-start.2 = (bf16[2,1024]{1,0:T(2,128)(2,1)S(1)}, bf16[2,1024]{1,0:T(2,128)(2,1)S(1)}, u32[]{:S(2)}, u32[]{:S(2)}) collective-permute-start(bf16[2,1024]{1,0:T(2,128)(2,1)S(1)} %slice.249), channel_id=1, source_target_pairs={{0,4},{4,8},{8,12},{12,16},{16,20},{20,24},{24,28},{28,32},{32,36}... | collective-permute-start | bytes 12296 | tf_op jit(solution)/shard_map/ppermute | solution.py:18
  17.7 1.5 fusion.146
  20.6 17.5 %while.15 = (s32[]{:T(128)}, f32[4,2,16,2,1024]{4,2,3,1,0:T(8,128)S(1)}, f32[4,2,16,2,1024]{4,2,3,1,0:T(8,128)}, f32[16,1024]{1,0:T(8,128)}, f32[16,1024]{1,0:T(...) while((s32[]{:T(128)}, ...), condition=%wide.region_3.4_spmd, body=%wide.region_0.3_spmd.sunk | while | flops 16729154 | bytes 2361705 | solution.py:74
  20.8 1.0 sqrt_multiply_fusion.2
  21.7 2.6 %fusion.150 = (f32[2,16,2,1024]{3,1,2,0:T(8,128)S(1)}, f32[2,16,2,1024]{3,1,2,0:T(8,128)S(1)}) fusion(f32[2,16,2]{1,2,0:T(2,128)S(1)} %get-tuple-element.283, f32[16,1024]{1,0:T(8,128)S(1)} %bitcast.190, f32[2,16,2]{1,2,0:T(2,128)S(1)} %get-tuple-element.284, f32[16,1024]{1,0:T(8,128)S(1)} %broadcast_multiply_fusion.5, f32[16,1024]{1,0:T(8,128)S(1)} %bitcast.197, ...), kind=kLoop, calls=%fused_computation.4.clone.1 | loop fusion | flops 16646144 | bytes 852736 | tf_op jit(solution)/shard_map/while/body/eval_jaxpr/reduce_sum | solution.py:72
  25.2 0.9 sqrt_multiply_fusion.2
  26.1 2.6 %fusion.150 = (f32[2,16,2,1024]{3,1,2,0:T(8,128)S(1)}, f32[2,16,2,1024]{3,1,2,0:T(8,128)S(1)}) fusion(f32[2,16,2]{1,2,0:T(2,128)S(1)} %get-tuple-element.283, f32[16,1024]{1,0:T(8,128)S(1)} %bitcast.190, f32[2,16,2]{1,2,0:T(2,128)S(1)} %get-tuple-element.284, f32[16,1024]{1,0:T(8,128)S(1)} %broadcast_multiply_fusion.5, f32[16,1024]{1,0:T(8,128)S(1)} %bitcast.197, ...), kind=kLoop, calls=%fused_computation.4.clone.1 | loop fusion | flops 16646144 | bytes 852736 | tf_op jit(solution)/shard_map/while/body/eval_jaxpr/reduce_sum | solution.py:72
  30.5 2.6 %fusion.150 = (f32[2,16,2,1024]{3,1,2,0:T(8,128)S(1)}, f32[2,16,2,1024]{3,1,2,0:T(8,128)S(1)}) fusion(f32[2,16,2]{1,2,0:T(2,128)S(1)} %get-tuple-element.283, f32[16,1024]{1,0:T(8,128)S(1)} %bitcast.190, f32[2,16,2]{1,2,0:T(2,128)S(1)} %get-tuple-element.284, f32[16,1024]{1,0:T(8,128)S(1)} %broadcast_multiply_fusion.5, f32[16,1024]{1,0:T(8,128)S(1)} %bitcast.197, ...), kind=kLoop, calls=%fused_computation.4.clone.1 | loop fusion | flops 16646144 | bytes 852736 | tf_op jit(solution)/shard_map/while/body/eval_jaxpr/reduce_sum | solution.py:72
  33.9 0.9 sqrt_multiply_fusion.2
  34.8 2.6 %fusion.150 = (f32[2,16,2,1024]{3,1,2,0:T(8,128)S(1)}, f32[2,16,2,1024]{3,1,2,0:T(8,128)S(1)}) fusion(f32[2,16,2]{1,2,0:T(2,128)S(1)} %get-tuple-element.283, f32[16,1024]{1,0:T(8,128)S(1)} %bitcast.190, f32[2,16,2]{1,2,0:T(2,128)S(1)} %get-tuple-element.284, f32[16,1024]{1,0:T(8,128)S(1)} %broadcast_multiply_fusion.5, f32[16,1024]{1,0:T(8,128)S(1)} %bitcast.197, ...), kind=kLoop, calls=%fused_computation.4.clone.1 | loop fusion | flops 16646144 | bytes 852736 | tf_op jit(solution)/shard_map/while/body/eval_jaxpr/reduce_sum | solution.py:72
  40.8 13.4 %all-to-all-start = ((bf16[64,2,1024]{2,1,0:T(2,128)(2,1)}), bf16[64,2,1024]{2,1,0:T(2,128)(2,1)S(1)}, u32[]{:S(2)}, u32[]{:S(2)}) async-start(bf16[64,2,1024]{2,1,0:T(2,128)(2,1)} %reshape.602), calls=%async_computation | async-start | bytes 524288 | tf_op jit(solution)/shard_map/all_to_all | solution.py:89
  54.7 10.9 %all-to-all-done = bf16[64,2,1024]{2,1,0:T(2,128)(2,1)S(1)} async-done(((bf16[64,2,1024]{2,1,0:T(2,128)(2,1)}), bf16[64,2,1024]{2,1,0:T(2,128)(2,1)S(1)}, u32[]{:S(2)}, u32[]{:S(2)}) %all-to-all-start) | async-done | bytes 262176 | tf_op jit(solution)/shard_map/all_to_all | solution.py:89
  65.8 1.5 reduce
  68.3 1.0 copy.128
  69.3 7.9 %all-to-all-start.1 = ((bf16[2,128,512]{2,0,1:T(2,128)(2,1)}), bf16[2,128,512]{2,0,1:T(2,128)(2,1)S(1)}, u32[]{:S(2)}, u32[]{:S(2)}) async-start(bf16[2,128,512]{2,0,1:T(2,128)(2,1)} %copy.128), calls=%async_computation.1 | async-start | bytes 524288 | tf_op jit(solution)/shard_map/all_to_all | solution.py:109
  79.0 1.0 copy.130
  79.9 10.9 %all-to-all-done.1 = bf16[2,128,512]{2,0,1:T(2,128)(2,1)S(1)} async-done(((bf16[2,128,512]{2,0,1:T(2,128)(2,1)}), bf16[2,128,512]{2,0,1:T(2,128)(2,1)S(1)}, u32[]{:S(2)}, u32[]{:S(2)}) %all-to-all-start.1) | async-done | bytes 262176 | tf_op jit(solution)/shard_map/all_to_all | solution.py:109
  90.9 6.8 %all-to-all-start.2 = ((bf16[2,128,512]{2,0,1:T(2,128)(2,1)}), bf16[2,128,512]{2,0,1:T(2,128)(2,1)S(1)}, u32[]{:S(2)}, u32[]{:S(2)}) async-start(bf16[2,128,512]{2,0,1:T(2,128)(2,1)} %copy.130), calls=%async_computation.2 | async-start | bytes 524288 | tf_op jit(solution)/shard_map/all_to_all | solution.py:112
  100.0 8.9 %all-to-all-done.2 = bf16[2,128,512]{2,0,1:T(2,128)(2,1)S(1)} async-done(((bf16[2,128,512]{2,0,1:T(2,128)(2,1)}), bf16[2,128,512]{2,0,1:T(2,128)(2,1)S(1)}, u32[]{:S(2)}, u32[]{:S(2)}) %all-to-all-start.2) | async-done | bytes 262176 | tf_op jit(solution)/shard_map/all_to_all | solution.py:112
  110.3 1.6 convolution_bitcast_fusion.4
  111.9 0.9 slice_bitcast_fusion
  113.7 2.0 rev.10
  115.7 1.7 slice.328
  118.0 1.7 slice.272
  119.7 3.0 %slice.285 = f32[8,16,1,512]{3,1,2,0:T(8,128)} reverse(f32[8,16,1,512]{3,1,2,0:T(8,128)} %slice.328), dimensions={0,1} | reverse | bytes 524288 | tf_op jit(solution)/shard_map/slice | solution.py:153
  122.7 1.0 slice_bitcast_fusion.2
  123.7 3.1 %slice.269 = f32[7,16,2,512]{3,1,2,0:T(8,128)} reverse(f32[7,16,2,512]{3,1,2,0:T(8,128)} %get-tuple-element.174), dimensions={0,1} | reverse | bytes 917504 | tf_op jit(solution)/shard_map/slice | solution.py:151
  126.8 3.2 %slice.282 = f32[7,16,2,512]{3,1,2,0:T(8,128)} reverse(f32[7,16,2,512]{3,1,2,0:T(8,128)} %get-tuple-element.173), dimensions={0,1} | reverse | bytes 917504 | tf_op jit(solution)/shard_map/slice | solution.py:151
  130.1 1.5 slice.279
  131.6 2.4 %subtract_bitcast_fusion = f32[1,8,16,2,512]{4,2,3,1,0:T(8,128)S(1)} fusion(f32[8,16,2,1024]{3,1,2,0:T(8,128)} %bitcast.193, f32[8,16,2,1024]{3,1,2,0:T(8,128)S(1)} %bitcast.191, f32[2,8,16,2,512]{4,2,3,1,0:T(8,128)S(1)} %convolution_bitcast_fusion.4, f32[8,16,2,512]{3,1,2,0:T(8,128)S(1)} %rev.9, f32[8,16,1,512]{3,1,2,0:T(8,128)S(1)} %slice.272, ...), kind=kLoop, calls=%fused_computation.92 | loop fusion | flops 3932160 | bytes 6291457 | tf_op jit(solution)/shard_map/stack | solution.py:172
  134.8 1.0 convolution_bitcast_fusion.3
  136.7 1.0 convolution_bitcast_fusion.2
  138.7 1.0 copy.141
  139.7 7.9 %all-to-all-start.3 = ((bf16[128,2,512]{2,1,0:T(2,128)(2,1)}), bf16[128,2,512]{2,1,0:T(2,128)(2,1)S(1)}, u32[]{:S(2)}, u32[]{:S(2)}) async-start(bf16[128,2,512]{2,1,0:T(2,128)(2,1)} %copy.141), calls=%async_computation.3 | async-start | bytes 524288 | tf_op jit(solution)/shard_map/all_to_all | solution.py:195
  147.6 1.0 copy.143
  148.6 14.1 %all-to-all-done.3 = bf16[128,2,512]{2,1,0:T(2,128)(2,1)S(1)} async-done(((bf16[128,2,512]{2,1,0:T(2,128)(2,1)}), bf16[128,2,512]{2,1,0:T(2,128)(2,1)S(1)}, u32[]{:S(2)}, u32[]{:S(2)}) %all-to-all-start.3) | async-done | bytes 262176 | tf_op jit(solution)/shard_map/all_to_all | solution.py:195
  162.7 6.4 %all-to-all-start.4 = ((bf16[128,2,512]{2,1,0:T(2,128)(2,1)}), bf16[128,2,512]{2,1,0:T(2,128)(2,1)S(1)}, u32[]{:S(2)}, u32[]{:S(2)}) async-start(bf16[128,2,512]{2,1,0:T(2,128)(2,1)} %copy.143), calls=%async_computation.4 | async-start | bytes 524288 | tf_op jit(solution)/shard_map/all_to_all | solution.py:198
  169.6 14.3 %all-to-all-done.4 = bf16[128,2,512]{2,1,0:T(2,128)(2,1)S(1)} async-done(((bf16[128,2,512]{2,1,0:T(2,128)(2,1)}), bf16[128,2,512]{2,1,0:T(2,128)(2,1)S(1)}, u32[]{:S(2)}, u32[]{:S(2)}) %all-to-all-start.4) | async-done | bytes 262176 | tf_op jit(solution)/shard_map/all_to_all | solution.py:198
  184.7 1.0 copy.145
  185.7 6.0 %all-to-all-start.5 = ((bf16[2,64,1024]{2,0,1:T(2,128)(2,1)}), bf16[2,64,1024]{2,0,1:T(2,128)(2,1)S(1)}, u32[]{:S(2)}, u32[]{:S(2)}) async-start(bf16[2,64,1024]{2,0,1:T(2,128)(2,1)} %copy.145), calls=%async_computation.5 | async-start | bytes 524288 | tf_op jit(solution)/shard_map/all_to_all | solution.py:213
  191.7 4.4 %collective-permute-start = (bf16[2,1024]{1,0:T(2,128)(2,1)S(1)}, bf16[2,1024]{1,0:T(2,128)(2,1)S(1)}, u32[]{:S(2)}, u32[]{:S(2)}) collective-permute-start(bf16[2,1024]{1,0:T(2,128)(2,1)S(1)} %slice.234), channel_id=1, source_target_pairs={{0,4},{4,8},{8,12},{12,16},{16,20},{20,24},{24,28},{28,32},{32,36}... | collective-permute-start | bytes 12296 | tf_op jit(solution)/shard_map/ppermute | solution.py:18
  197.0 6.2 %all-to-all-done.5 = bf16[2,64,1024]{2,0,1:T(2,128)(2,1)S(1)} async-done(((bf16[2,64,1024]{2,0,1:T(2,128)(2,1)}), bf16[2,64,1024]{2,0,1:T(2,128)(2,1)S(1)}, u32[]{:S(2)}, u32[]{:S(2)}) %all-to-all-start.5) | async-done | bytes 262176 | tf_op jit(solution)/shard_map/all_to_all | solution.py:213
  204.0 1.3 collective-permute-start.3
  206.5 3.6 %collective-permute-done.3 = bf16[16,1024]{1,0:T(8,128)(2,1)S(1)} collective-permute-done((bf16[16,1024]{1,0:T(8,128)(2,1)S(1)}, bf16[16,1024]{1,0:T(8,128)(2,1)S(1)}, u32[]{:S(2)}, u32[]{:S(2)}) %collective-permute-start.3) | collective-permute-done | bytes 32800 | tf_op jit(solution)/shard_map/ppermute | solution.py:18
  210.2 2.9 %fusion.15 = f32[8,128]{1,0:T(8,128)S(1)} fusion(bf16[32,1024,128]{2,1,0:T(8,128)(2,1)} %all-gather.2.cloned.1.call-done, bf16[8,16,1024]{2,1,0:T(8,128)(2,1)S(1)} %bitcast.196), kind=kOutput, calls=%fused_computation.35 | convolution fusion | flops 33554432 | bytes 4460544 | tf_op jit(solution)/shard_map/jic,ico->jo/dot_general | solution.py:236
  213.1 2.9 %fusion.21 = f32[8,128]{1,0:T(8,128)S(1)} fusion(f32[8,128]{1,0:T(8,128)S(1)} %fusion.15, bf16[32,1024,128]{2,1,0:T(8,128)(2,1)} %all-gather.2.cloned.1.call-done, bf16[8,16,1024]{2,1,0:T(8,128)(2,1)S(1)} %bitcast.200), kind=kOutput, calls=%fused_computation.37 | convolution fusion | flops 33555456 | bytes 4464640 | tf_op jit(solution)/shard_map/jic,ico->jo/dot_general | solution.py:239
  216.0 10.9 %all-reduce = bf16[8,128]{1,0:T(8,128)(2,1)S(1)} all-reduce(f32[8,128]{1,0:T(8,128)S(1)} %fusion.21), channel_id=2, replica_groups=mesh['seq'=64,'tp'=4] {'tp'}, use_global_device_ids=true, to_apply=%region_4.5.clone | all-reduce | flops 1024 | bytes 6144
  (155 shorter events, 24.9 us)
Async XLA Ops:
  7.2 203.0 %all-gather.2.cloned.1.call-start = ((), (), s32[]{:S(2)}) async-start(), calls=%async_computation.6 | async-start | bytes 8519680 | tf_op jit(solution)/shard_map/all_gather | solution.py:235
  7.9 30.2 %collective-permute-start.1 = (bf16[2,1024]{1,0:T(2,128)(2,1)S(1)}, bf16[2,1024]{1,0:T(2,128)(2,1)S(1)}, u32[]{:S(2)}, u32[]{:S(2)}) collective-permute-start(bf16[2,1024]{1,0:T(2,128)(2,1)S(1)} %slice.242), channel_id=1, source_target_pairs={{0,4},{4,8},{8,12},{12,16},{16,20},{20,24},{24,28},{28,32},{32,36}... | collective-permute-start | bytes 12296 | tf_op jit(solution)/shard_map/ppermute | solution.py:18
  14.1 24.2 %collective-permute-start.2 = (bf16[2,1024]{1,0:T(2,128)(2,1)S(1)}, bf16[2,1024]{1,0:T(2,128)(2,1)S(1)}, u32[]{:S(2)}, u32[]{:S(2)}) collective-permute-start(bf16[2,1024]{1,0:T(2,128)(2,1)S(1)} %slice.249), channel_id=1, source_target_pairs={{0,4},{4,8},{8,12},{12,16},{16,20},{20,24},{24,28},{28,32},{32,36}... | collective-permute-start | bytes 12296 | tf_op jit(solution)/shard_map/ppermute | solution.py:18
  19.5 34.9 %copy-start.18 = (s32[128]{0:T(128)}, s32[128]{0:T(128)S(1)}, u32[]{:S(2)}) copy-start(s32[128]{0:T(128)S(1)} %mul.1036) | copy-start | bytes 1540
  20.6 17.6 %copy-start.7 = (bf16[128,1024]{1,0:T(8,128)(2,1)S(1)}, bf16[128,1024]{1,0:T(8,128)(2,1)}, u32[]{:S(2)}) copy-start(bf16[128,1024]{1,0:T(8,128)(2,1)} %param.11) | copy-start | bytes 786436
  20.6 17.7 %copy-start.8 = (bf16[128,1024]{1,0:T(8,128)(2,1)S(1)}, bf16[128,1024]{1,0:T(8,128)(2,1)}, u32[]{:S(2)}) copy-start(bf16[128,1024]{1,0:T(8,128)(2,1)} %param.12) | copy-start | bytes 786436
  40.8 24.8 %all-to-all-start = ((bf16[64,2,1024]{2,1,0:T(2,128)(2,1)}), bf16[64,2,1024]{2,1,0:T(2,128)(2,1)S(1)}, u32[]{:S(2)}, u32[]{:S(2)}) async-start(bf16[64,2,1024]{2,1,0:T(2,128)(2,1)} %reshape.602), calls=%async_computation | async-start | bytes 524288 | tf_op jit(solution)/shard_map/all_to_all | solution.py:89
  67.4 41.9 %copy-start.5 = (bf16[64,2,1,1024]{3,1,0,2:T(2,128)(2,1)}, bf16[64,2,1,1024]{3,1,0,2:T(2,128)(2,1)S(1)}, u32[]{:S(2)}) copy-start(bf16[64,2,1,1024]{3,1,0,2:T(2,128)(2,1)S(1)} %all_to_all.19) | copy-start | bytes 786436
  69.3 21.6 %all-to-all-start.1 = ((bf16[2,128,512]{2,0,1:T(2,128)(2,1)}), bf16[2,128,512]{2,0,1:T(2,128)(2,1)S(1)}, u32[]{:S(2)}, u32[]{:S(2)}) async-start(bf16[2,128,512]{2,0,1:T(2,128)(2,1)} %copy.128), calls=%async_computation.1 | async-start | bytes 524288 | tf_op jit(solution)/shard_map/all_to_all | solution.py:109
  90.9 18.1 %all-to-all-start.2 = ((bf16[2,128,512]{2,0,1:T(2,128)(2,1)}), bf16[2,128,512]{2,0,1:T(2,128)(2,1)S(1)}, u32[]{:S(2)}, u32[]{:S(2)}) async-start(bf16[2,128,512]{2,0,1:T(2,128)(2,1)} %copy.130), calls=%async_computation.2 | async-start | bytes 524288 | tf_op jit(solution)/shard_map/all_to_all | solution.py:112
  131.6 2.4 %copy-start = (f32[4,2,16,2,1024]{4,2,3,1,0:T(8,128)S(1)}, f32[4,2,16,2,1024]{4,2,3,1,0:T(8,128)}, u32[]{:S(2)}) copy-start(f32[4,2,16,2,1024]{4,2,3,1,0:T(8,128)} %get-tuple-element.135) | copy-start | bytes 3145732
  131.6 2.4 %copy-start.1 = (f32[7,16,2,512]{3,1,2,0:T(8,128)S(1)}, f32[7,16,2,512]{3,1,2,0:T(8,128)}, u32[]{:S(2)}) copy-start(f32[7,16,2,512]{3,1,2,0:T(8,128)} %slice.269) | copy-start | bytes 1376260
  131.6 2.4 %copy-start.2 = (f32[7,16,2,512]{3,1,2,0:T(8,128)S(1)}, f32[7,16,2,512]{3,1,2,0:T(8,128)}, u32[]{:S(2)}) copy-start(f32[7,16,2,512]{3,1,2,0:T(8,128)} %slice.282) | copy-start | bytes 1376260
  131.6 2.4 %copy-start.4 = (f32[8,16,1,512]{3,1,2,0:T(8,128)S(1)}, f32[8,16,1,512]{3,1,2,0:T(8,128)}, u32[]{:S(2)}) copy-start(f32[8,16,1,512]{3,1,2,0:T(8,128)} %slice.285) | copy-start | bytes 786436
  134.0 0.7 copy-start.10
  134.0 0.7 copy-start.11
  134.1 2.4 %copy-start.14 = (f32[8,16]{0,1:T(8,128)S(1)}, f32[8,16]{0,1:T(8,128)}, u32[]{:S(2)}) copy-start(f32[8,16]{0,1:T(8,128)} %fusion.113) | copy-start | bytes 1540
  134.7 1.9 copy-start.12
  134.7 1.9 copy-start.13
  136.4 2.1 copy-start.21
  136.5 2.1 copy-start.22
  137.7 31.4 %copy-start.19 = (s32[128]{0:T(128)S(1)}, s32[128]{0:T(128)}, u32[]{:S(2)}) copy-start(s32[128]{0:T(128)} %copy-done.18) | copy-start | bytes 1540
  138.5 46.1 %copy-start.6 = (bf16[64,2,1,1024]{3,1,0,2:T(2,128)(2,1)S(1)}, bf16[64,2,1,1024]{3,1,0,2:T(2,128)(2,1)}, u32[]{:S(2)}) copy-start(bf16[64,2,1,1024]{3,1,0,2:T(2,128)(2,1)} %copy-done.5) | copy-start | bytes 786436
  138.5 46.1 %copy-start.20 = (f32[1024]{0:T(1024)S(1)}, f32[1024]{0:T(1024)}, u32[]{:S(2)}) copy-start(f32[1024]{0:T(1024)} %param.16) | copy-start | bytes 12292
  138.7 53.0 %copy-start.9 = (bf16[128,1024]{1,0:T(8,128)(2,1)S(1)}, bf16[128,1024]{1,0:T(8,128)(2,1)}, u32[]{:S(2)}) copy-start(bf16[128,1024]{1,0:T(8,128)(2,1)} %param.10) | copy-start | bytes 786436
  139.7 22.9 %all-to-all-start.3 = ((bf16[128,2,512]{2,1,0:T(2,128)(2,1)}), bf16[128,2,512]{2,1,0:T(2,128)(2,1)S(1)}, u32[]{:S(2)}, u32[]{:S(2)}) async-start(bf16[128,2,512]{2,1,0:T(2,128)(2,1)} %copy.141), calls=%async_computation.3 | async-start | bytes 524288 | tf_op jit(solution)/shard_map/all_to_all | solution.py:195
  162.7 21.2 %all-to-all-start.4 = ((bf16[128,2,512]{2,1,0:T(2,128)(2,1)}), bf16[128,2,512]{2,1,0:T(2,128)(2,1)S(1)}, u32[]{:S(2)}, u32[]{:S(2)}) async-start(bf16[128,2,512]{2,1,0:T(2,128)(2,1)} %copy.143), calls=%async_computation.4 | async-start | bytes 524288 | tf_op jit(solution)/shard_map/all_to_all | solution.py:198
  169.5 34.2 %copy-start.15 = (f32[1,1,1024]{2,1,0:T(1,128)S(1)}, f32[1,1,1024]{2,1,0:T(1,128)}, u32[]{:S(2)}) copy-start(f32[1,1,1024]{2,1,0:T(1,128)} %get-tuple-element.184) | copy-start | bytes 12292
  169.5 34.2 %copy-start.16 = (f32[1,1,1024]{2,1,0:T(1,128)S(1)}, f32[1,1,1024]{2,1,0:T(1,128)}, u32[]{:S(2)}) copy-start(f32[1,1,1024]{2,1,0:T(1,128)} %get-tuple-element.189) | copy-start | bytes 12292
  169.5 34.2 %copy-start.17 = (f32[1,1,1024]{2,1,0:T(1,128)S(1)}, f32[1,1,1024]{2,1,0:T(1,128)}, u32[]{:S(2)}) copy-start(f32[1,1,1024]{2,1,0:T(1,128)} %get-tuple-element.190) | copy-start | bytes 12292
  184.6 20.7 %copy-start.23 = (u32[256]{0:T(256)S(1)}, u32[256]{0:T(256)}, u32[]{:S(2)}) copy-start(u32[256]{0:T(256)} %constant.217) | copy-start | bytes 3076
  185.7 17.5 %all-to-all-start.5 = ((bf16[2,64,1024]{2,0,1:T(2,128)(2,1)}), bf16[2,64,1024]{2,0,1:T(2,128)(2,1)S(1)}, u32[]{:S(2)}, u32[]{:S(2)}) async-start(bf16[2,64,1024]{2,0,1:T(2,128)(2,1)} %copy.145), calls=%async_computation.5 | async-start | bytes 524288 | tf_op jit(solution)/shard_map/all_to_all | solution.py:213
  191.7 5.2 %collective-permute-start = (bf16[2,1024]{1,0:T(2,128)(2,1)S(1)}, bf16[2,1024]{1,0:T(2,128)(2,1)S(1)}, u32[]{:S(2)}, u32[]{:S(2)}) collective-permute-start(bf16[2,1024]{1,0:T(2,128)(2,1)S(1)} %slice.234), channel_id=1, source_target_pairs={{0,4},{4,8},{8,12},{12,16},{16,20},{20,24},{24,28},{28,32},{32,36}... | collective-permute-start | bytes 12296 | tf_op jit(solution)/shard_map/ppermute | solution.py:18
  203.9 12.1 %copy-start.3 = (bf16[128,1024]{1,0:T(8,128)(2,1)}, bf16[128,1024]{1,0:T(8,128)(2,1)S(1)}, u32[]{:S(2)}) copy-start(bf16[128,1024]{1,0:T(8,128)(2,1)S(1)} %fusion.42) | copy-start | bytes 786436
  204.0 6.2 %collective-permute-start.3 = (bf16[16,1024]{1,0:T(8,128)(2,1)S(1)}, bf16[16,1024]{1,0:T(8,128)(2,1)S(1)}, u32[]{:S(2)}, u32[]{:S(2)}) collective-permute-start(bf16[16,1024]{1,0:T(8,128)(2,1)S(1)} %slice.338), channel_id=1, source_target_pairs={{4,0},{8,4},{12,8},{16,12},{20,16},{24,20},{28,24},{32,28},{36,32}... | collective-permute-start | bytes 98312 | tf_op jit(solution)/shard_map/ppermute | solution.py:18
Sparse Core Ops, SparseCore 0:
  17.8 166.0 all-gather.1
where the time goes:
time: 236 us; the launch traced here: 234 us
  waiting for transfers between devices  69.7 us (30%)
  starting transfers between devices  63.1 us (27%)
  local copies, waits for them, and re-layouts  38.3 us (16%)
  other arithmetic  25.5 us (11%)
  between operations  15.6 us (7%)
  matrix products  11.1 us (5%)
  blocking collectives  10.9 us (5%)
    ppermute x4, starting transfers between devices, from_behind(): return lax.ppermute(block, axis, route)  14.6 us
    all_to_all x1, waiting for transfers between devices, transform_conv(): lax.all_to_all(imag_part.astype(jnp.bfloat16), 'seq', split_axis=0, conca...  14.3 us
    all_to_all x1, waiting for transfers between devices, transform_conv(): lax.all_to_all(real_part.astype(jnp.bfloat16), 'seq', split_axis=0, conca...  14.1 us
    all_to_all x1, starting transfers between devices, transform_conv(): lax.all_to_all(gated.reshape(tokens, 1, chan_width), 'seq', split_axis=0,...  13.4 us
    all_to_all x1, waiting for transfers between devices, transform_conv(): lax.all_to_all(real_part.astype(jnp.bfloat16), 'seq', split_axis=1, conca...  10.9 us
    unnamed x1, blocking collectives  10.9 us
    all_to_all x1, waiting for transfers between devices, transform_conv(): lax.all_to_all(gated.reshape(tokens, 1, chan_width), 'seq', split_axis=0,...  10.9 us
    reduce_sum x4, other arithmetic, one_group(): jnp.sum(-weight * denom_imag, axis=0)  10.3 us
  transfers between devices with their start and end apart: 11, of which 8 were waited for; matrix products, arithmetic and copies ran while one was open for 29% of the time, Pallas kernels for 0%

commit v1 on v0

v1 whole, which is shorter than its diff:
```python
import jax
import jax.numpy as jnp
from jax import lax
from jax.sharding import PartitionSpec as P

STRIDE = 16

highest = lax.Precision.HIGHEST


def from_behind(block, axis, distance):
    devices = range(lax.axis_size(axis))
    route = [(i - distance, i) for i in devices if i - distance in devices]
    return lax.ppermute(block, axis, route)


def short_pass(rows_block, before, tap_weights):
    joined = jnp.concatenate([before, rows_block], axis=0).astype(jnp.float32)
    row_count = rows_block.shape[0]
    return (
        tap_weights[0] * joined[2 : 2 + row_count]
        + tap_weights[1] * joined[1 : 1 + row_count]
        + tap_weights[2] * joined[0:row_count]
    )


def modal_conv(gated, residues, decays):
    tokens = gated.shape[0]
    parties = lax.axis_size("seq")
    g = gated.astype(jnp.float32)
    steps = jnp.arange(tokens, dtype=jnp.float32)
    weight = residues * jnp.sqrt(-jnp.expm1(-2.0 * decays))
    grow = jnp.exp(decays[:, None, :] * steps[None, :, None])
    shrink = jnp.exp(-decays[:, None, :] * steps[None, :, None])
    lower = (steps[:, None] >= steps[None, :]).astype(jnp.float32)
    running = jnp.einsum("ij,rjc->ric", lower, grow * g[None], precision=highest)
    local = jnp.sum(weight[:, None, :] * shrink * running, axis=0)
    end_state = jnp.exp(-decays * (tokens - 1)) * running[:, -1, :]
    carry = from_behind(end_state, "seq", 1)
    span = 1
    while span < parties:
        carry = carry + jnp.exp(-decays * float(tokens * span)) * from_behind(carry, "seq", span)
        span *= 2
    after = jnp.exp(-decays[:, None, :] * (steps[None, :, None] + 1.0))
    cross = jnp.sum((weight * carry)[:, None, :] * after, axis=0)
    return local + cross


def shards(
    query_input, key_input, value_input, short_filter, residues, decays, skip_gain, head_weight
):
    tokens, chan_width = query_input.shape
    before = from_behind((query_input[-2:], key_input[-2:], value_input[-2:]), "seq", 1)
    query_short = short_pass(query_input, before[0], short_filter[:, 0])
    key_short = short_pass(key_input, before[1], short_filter[:, 1])
    value_short = short_pass(value_input, before[2], short_filter[:, 2])
    gated = (key_short * value_short).astype(jnp.bfloat16)
    convolved = modal_conv(gated, residues, decays)
    carried = (convolved + skip_gain * gated.astype(jnp.float32)).astype(jnp.bfloat16)
    operator_out = (query_short * carried.astype(jnp.float32)).astype(jnp.bfloat16)
    rim_rows = from_behind(operator_out[:STRIDE], "seq", -1)
    extended = jnp.concatenate([operator_out, rim_rows], axis=0).reshape(
        tokens // STRIDE + 1, STRIDE, chan_width
    )
    early_rows = extended[:-1]
    late_rows = extended[1:]
    weight_piece = lax.all_gather(head_weight, "seq", axis=1, tiled=True)
    running = jnp.einsum(
        "jic,ico->jo", early_rows, weight_piece[:STRIDE], preferred_element_type=jnp.float32
    )
    partial_sum = running + jnp.einsum(
        "jic,ico->jo", late_rows, weight_piece[STRIDE:], preferred_element_type=jnp.float32
    )
    probe_out = lax.psum_scatter(partial_sum, "tp", scatter_dimension=0, tiled=True).astype(
        jnp.bfloat16
    )
    return (operator_out, probe_out)


def solution(mesh):
    placed = (
        P("seq", "tp"),
        P("seq", "tp"),
        P("seq", "tp"),
        P(None, None, "tp"),
        P(None, "tp"),
        P(None, "tp"),
        P("tp"),
        P(None, ("tp", "seq"), None),
    )
    return jax.shard_map(
        shards,
        mesh=mesh,
        in_specs=placed,
        out_specs=(P("seq", "tp"), P(("seq", "tp"), None)),
        check_vma=False,
    )
```

time: 236 us -> 186 us (0.79)
  local copies, waits for them, and re-layouts: 38.3 us -> 3.58 us
  other arithmetic: 25.5 us -> 6.24 us
  waiting for transfers between devices: 69.7 us -> 74.4 us
  matrix products: 11.1 us -> 14.4 us
    all_to_all x6 -> x0, waiting for transfers between devices: 65.3 us -> none  [the longest x1 14.3 us: transform_conv(): lax.all_to_all(imag_part.astype(jnp.bfloat16), 'seq', split_axis=0, conca...]
    all_gather x1, waiting for transfers between devices: 0.02 us -> 61.3 us  [shards(): weight_piece = lax.all_gather(head_weight, 'seq', axis=1, tiled=True)]
    all_to_all x6 -> x0, starting transfers between devices: 48.4 us -> none  [the longest x1 13.4 us: transform_conv(): lax.all_to_all(gated.reshape(tokens, 1, chan_width), 'seq', split_axis=0,...]
    ppermute x4 -> x11, starting transfers between devices: 14.6 us -> 62 us  [from_behind(): return lax.ppermute(block, axis, route)]
    slice x19 -> x1, local copies, waits for them, and re-layouts: 17.4 us -> 0.06 us  [modal_conv(): end_state = jnp.exp(-decays * (tokens - 1)) * running[:, -1, :]]
    ppermute x4 -> x11, waiting for transfers between devices: 4.35 us -> 12.3 us  [from_behind(): return lax.ppermute(block, axis, route)]
    reduce_sum x4 -> x1, other arithmetic: 10.3 us -> 3.3 us  [modal_conv(): cross = jnp.sum((weight * carry)[:, None, :] * after, axis=0)]
    convert_element_type x14 -> x0, local copies, waits for them, and re-layouts: 6.53 us -> none  [the longest x2 1.96 us: transform_conv(): real_part.astype(jnp.bfloat16)]
  transfers between devices with their start and end apart: 11 -> 12, of which waited for: 8 -> 9; matrix products, arithmetic and copies ran while one was open for 29% -> 10% of each run, Pallas kernels for 0% -> 0%
where the time goes in v1:
time: 186 us; the launch traced here: 185 us
  waiting for transfers between devices  74.4 us (40%)
  starting transfers between devices  62.1 us (33%)
  between operations  15 us (8%)
  matrix products  14.4 us (8%)
  blocking collectives  9.53 us (5%)
  other arithmetic  6.24 us (3%)
  local copies, waits for them, and re-layouts  3.58 us (2%)
    ppermute x11, starting transfers between devices, from_behind(): return lax.ppermute(block, axis, route)  62 us
    all_gather x1, waiting for transfers between devices, shards(): weight_piece = lax.all_gather(head_weight, 'seq', axis=1, tiled=True)  61.3 us
    ppermute x11, waiting for transfers between devices, from_behind(): return lax.ppermute(block, axis, route)  12.3 us
    unnamed x1, blocking collectives  9.53 us
    dot_general x1, matrix products, modal_conv(): jnp.einsum('ij,rjc->ric', lower, grow * g[None], precision=highest)  8.54 us
  transfers between devices with their start and end apart: 12, of which 9 were waited for; matrix products, arithmetic and copies ran while one was open for 10% of the time, Pallas kernels for 0%

profile of v1, /device:TPU:1, one launch (start us, length us, event | category | flops | bytes accessed | tf_op | source)
XLA Modules:
  0.0 185.2 jit_solution(16311309394852278889)
XLA Ops:
  7.2 0.0 copy-start
  7.2 0.0 copy-start.2
  7.2 0.0 all-gather.2.cloned.1.call-start
  7.2 0.7 all-gather.2.cloned.1.call-update
  7.9 0.7 slice.114
  8.6 5.5 %collective-permute-start.1 = (bf16[2,1024]{1,0:T(2,128)(2,1)S(1)}, bf16[2,1024]{1,0:T(2,128)(2,1)S(1)}, u32[]{:S(2)}, u32[]{:S(2)}) collective-permute-start(bf16[2,1024]{1,0:T(2,128)(2,1)S(1)} %slice.114), channel_id=1, source_target_pairs={{0,4},{4,8},{8,12},{12,16},{16,20},{20,24},{24,28},{28,32},{32,36}... | collective-permute-start | bytes 12296 | tf_op jit(solution)/shard_map/ppermute | solution.py:14
  14.1 0.7 slice.121
  14.8 3.5 %collective-permute-start.2 = (bf16[2,1024]{1,0:T(2,128)(2,1)S(1)}, bf16[2,1024]{1,0:T(2,128)(2,1)S(1)}, u32[]{:S(2)}, u32[]{:S(2)}) collective-permute-start(bf16[2,1024]{1,0:T(2,128)(2,1)S(1)} %slice.121), channel_id=1, source_target_pairs={{0,4},{4,8},{8,12},{12,16},{16,20},{20,24},{24,28},{28,32},{32,36}... | collective-permute-start | bytes 12296 | tf_op jit(solution)/shard_map/ppermute | solution.py:14
  18.3 0.9 fusion.39
  19.2 0.0 copy-start.3
  19.3 0.0 collective-permute-done.1
  19.3 1.0 maximum_convert_fusion.1
  20.3 0.0 collective-permute-done.2
  20.3 1.0 maximum_convert_fusion.2
  21.4 0.3 fusion.35
  21.7 8.5 %fusion.11 = f32[16,128,1024]{2,1,0:T(8,128)S(1)} fusion(f32[128,1024]{1,0:T(8,128)S(1)} %fusion.35, f32[16,1024]{1,0:T(8,128)} %param.13), kind=kOutput, calls=%fused_computation.13 | convolution fusion | flops 3225436160 | bytes 8978432 | tf_op jit(solution)/shard_map/ij,rjc->ric/dot_general | solution.py:36
  30.2 0.0 copy-start.4
  30.3 0.0 copy-start.5
  30.3 0.1 slice.143
  30.4 4.7 %collective-permute-start.3 = (f32[16,1024]{1,0:T(8,128)S(1)}, f32[16,1024]{1,0:T(8,128)S(1)}, u32[]{:S(2)}, u32[]{:S(2)}) collective-permute-start(f32[16,1024]{1,0:T(8,128)S(1)} %bitcast_multiply_fusion), channel_id=1, source_target_pairs={{0,4},{4,8},{8,12},{12,16},{16,20},{20,24},{24,28},{28,32},{32,36}... | collective-permute-start | bytes 196616 | tf_op jit(solution)/shard_map/ppermute | solution.py:14
  35.0 1.3 collective-permute-done.3
  36.4 5.2 %collective-permute-start.4 = (f32[16,1024]{1,0:T(8,128)S(1)}, f32[16,1024]{1,0:T(8,128)S(1)}, u32[]{:S(2)}, u32[]{:S(2)}) collective-permute-start(f32[16,1024]{1,0:T(8,128)S(1)} %collective-permute-done.3), channel_id=1, source_target_pairs={{0,4},{4,8},{8,12},{12,16},{16,20},{20,24},{24,28},{28,32},{32,36}... | collective-permute-start | bytes 196616 | tf_op jit(solution)/shard_map/ppermute | solution.py:14
  41.6 1.3 collective-permute-done.4
  42.9 7.3 %collective-permute-start.5 = (f32[16,1024]{1,0:T(8,128)S(1)}, f32[16,1024]{1,0:T(8,128)S(1)}, u32[]{:S(2)}, u32[]{:S(2)}) collective-permute-start(f32[16,1024]{1,0:T(8,128)S(1)} %get-tuple-element.7), channel_id=1, source_target_pairs={{0,8},{4,12},{8,16},{12,20},{16,24},{20,28},{24,32},{28,36},{32,40... | collective-permute-start | bytes 196616 | tf_op jit(solution)/shard_map/ppermute | solution.py:14
  50.2 1.4 collective-permute-done.5
  51.6 4.8 %collective-permute-start.6 = (f32[16,1024]{1,0:T(8,128)S(1)}, f32[16,1024]{1,0:T(8,128)S(1)}, u32[]{:S(2)}, u32[]{:S(2)}) collective-permute-start(f32[16,1024]{1,0:T(8,128)S(1)} %multiply_add_fusion.3), channel_id=1, source_target_pairs={{0,16},{4,20},{8,24},{12,28},{16,32},{20,36},{24,40},{28,44},{32,4... | collective-permute-start | bytes 196616 | tf_op jit(solution)/shard_map/ppermute | solution.py:14
  56.4 1.3 collective-permute-done.6
  57.7 15.8 %collective-permute-start.7 = (f32[16,1024]{1,0:T(8,128)S(1)}, f32[16,1024]{1,0:T(8,128)S(1)}, u32[]{:S(2)}, u32[]{:S(2)}) collective-permute-start(f32[16,1024]{1,0:T(8,128)S(1)} %multiply_add_fusion.2), channel_id=1, source_target_pairs={{0,32},{4,36},{8,40},{12,44},{16,48},{20,52},{24,56},{28,60},{32,6... | collective-permute-start | bytes 196616 | tf_op jit(solution)/shard_map/ppermute | solution.py:14
  73.5 1.3 collective-permute-start
  74.8 0.9 collective-permute-done.7
  75.8 6.0 %collective-permute-start.8 = (f32[16,1024]{1,0:T(8,128)S(1)}, f32[16,1024]{1,0:T(8,128)S(1)}, u32[]{:S(2)}, u32[]{:S(2)}) collective-permute-start(f32[16,1024]{1,0:T(8,128)S(1)} %multiply_add_fusion.1), channel_id=1, source_target_pairs={{0,64},{4,68},{8,72},{12,76},{16,80},{20,84},{24,88},{28,92},{32,9... | collective-permute-start | bytes 196616 | tf_op jit(solution)/shard_map/ppermute | solution.py:14
  81.8 1.3 collective-permute-done.8
  83.2 6.8 %collective-permute-start.9 = (f32[16,1024]{1,0:T(8,128)S(1)}, f32[16,1024]{1,0:T(8,128)S(1)}, u32[]{:S(2)}, u32[]{:S(2)}) collective-permute-start(f32[16,1024]{1,0:T(8,128)S(1)} %multiply_add_fusion), channel_id=1, source_target_pairs={{0,128},{4,132},{8,136},{12,140},{16,144},{20,148},{24,152},{28,15... | collective-permute-start | bytes 196616 | tf_op jit(solution)/shard_map/ppermute | solution.py:14
  89.9 0.0 collective-permute-done
  89.9 0.1 maximum_convert_fusion
  90.0 1.2 collective-permute-done.9
  91.2 0.1 add_multiply_fusion
  91.3 3.3 %multiply_reduce_fusion = (f32[128,1024]{1,0:T(8,128)S(1)}, f32[128,1024]{1,0:T(8,128)S(1)}) fusion(f32[128]{0:T(128)S(1)} %iota_add_fusion, f32[16,1024]{1,0:T(8,128)S(1)} %get-tuple-element.4, f32[16,1024]{1,0:T(8,128)S(1)} %get-tuple-element.6, f32[16,128,1024]{2,1,0:T(8,128)S(1)} %fusion.11, f32[16,1024]{1,0:T(8,128)S(1)} %get-tuple-element.5), kind=kLoop, calls=%fused_computation | loop fusion | flops 14417920 | bytes 9634304 | tf_op jit(solution)/shard_map/reduce_sum | solution.py:45
  94.6 0.3 fusion.31
  94.9 0.0 copy-start.1
  94.9 1.3 collective-permute-start.10
  96.2 0.6 dynamic-slice
  97.4 3.6 %collective-permute-done.10 = bf16[16,1024]{1,0:T(8,128)(2,1)S(1)} collective-permute-done((bf16[16,1024]{1,0:T(8,128)(2,1)S(1)}, bf16[16,1024]{1,0:T(8,128)(2,1)S(1)}, u32[]{:S(2)}, u32[]{:S(2)}) %collective-permute-start.10) | collective-permute-done | bytes 32800 | tf_op jit(solution)/shard_map/ppermute | solution.py:14
  101.1 61.3 %all-gather.2.cloned.1.call-done = bf16[32,1024,128]{2,1,0:T(8,128)(2,1)} async-done(((bf16[32,16,128]{2,1,0:T(8,128)(2,1)}), bf16[32,1024,128]{2,1,0:T(8,128)(2,1)}) %all-gather.2.cloned.1.call-update) | async-done | bytes 8388624 | tf_op jit(solution)/shard_map/all_gather | solution.py:67
  162.4 2.9 %fusion.14 = f32[8,128]{1,0:T(8,128)S(1)} fusion(bf16[32,1024,128]{2,1,0:T(8,128)(2,1)} %all-gather.2.cloned.1.call-done, bf16[8,16,1024]{2,1,0:T(8,128)(2,1)S(1)} %bitcast.25), kind=kOutput, calls=%fused_computation.14 | convolution fusion | flops 33554432 | bytes 4460544 | tf_op jit(solution)/shard_map/jic,ico->jo/dot_general | solution.py:68
  165.3 2.9 %fusion.20 = f32[8,128]{1,0:T(8,128)S(1)} fusion(f32[8,128]{1,0:T(8,128)S(1)} %fusion.14, bf16[32,1024,128]{2,1,0:T(8,128)(2,1)} %all-gather.2.cloned.1.call-done, bf16[8,16,1024]{2,1,0:T(8,128)(2,1)S(1)} %bitcast.26), kind=kOutput, calls=%fused_computation.16 | convolution fusion | flops 33555456 | bytes 4464640 | tf_op jit(solution)/shard_map/jic,ico->jo/dot_general | solution.py:71
  168.3 9.5 %all-reduce = bf16[8,128]{1,0:T(8,128)(2,1)S(1)} all-reduce(f32[8,128]{1,0:T(8,128)S(1)} %fusion.20), channel_id=2, replica_groups=mesh['seq'=64,'tp'=4] {'tp'}, use_global_device_ids=true, to_apply=%region_2.0.clone | all-reduce | flops 1024 | bytes 6144
  177.8 0.5 dynamic-slice_convert_fusion
  (16 shorter events, 0.2 us)
Async XLA Ops:
  7.2 23.2 %copy-start = (f32[16,1024]{1,0:T(8,128)S(1)}, f32[16,1024]{1,0:T(8,128)}, u32[]{:S(2)}) copy-start(f32[16,1024]{1,0:T(8,128)} %param.13) | copy-start | bytes 196612
  7.2 66.3 %copy-start.2 = (bf16[128,1024]{1,0:T(8,128)(2,1)S(1)}, bf16[128,1024]{1,0:T(8,128)(2,1)}, u32[]{:S(2)}) copy-start(bf16[128,1024]{1,0:T(8,128)(2,1)} %param.8) | copy-start | bytes 786436
  7.2 155.2 %all-gather.2.cloned.1.call-start = ((), (), s32[]{:S(2)}) async-start(), calls=%async_computation | async-start | bytes 8519680 | tf_op jit(solution)/shard_map/all_gather | solution.py:67
  8.6 10.6 %collective-permute-start.1 = (bf16[2,1024]{1,0:T(2,128)(2,1)S(1)}, bf16[2,1024]{1,0:T(2,128)(2,1)S(1)}, u32[]{:S(2)}, u32[]{:S(2)}) collective-permute-start(bf16[2,1024]{1,0:T(2,128)(2,1)S(1)} %slice.114), channel_id=1, source_target_pairs={{0,4},{4,8},{8,12},{12,16},{16,20},{20,24},{24,28},{28,32},{32,36}... | collective-permute-start | bytes 12296 | tf_op jit(solution)/shard_map/ppermute | solution.py:14
  14.8 5.5 %collective-permute-start.2 = (bf16[2,1024]{1,0:T(2,128)(2,1)S(1)}, bf16[2,1024]{1,0:T(2,128)(2,1)S(1)}, u32[]{:S(2)}, u32[]{:S(2)}) collective-permute-start(bf16[2,1024]{1,0:T(2,128)(2,1)S(1)} %slice.121), channel_id=1, source_target_pairs={{0,4},{4,8},{8,12},{12,16},{16,20},{20,24},{24,28},{28,32},{32,36}... | collective-permute-start | bytes 12296 | tf_op jit(solution)/shard_map/ppermute | solution.py:14
  19.2 72.0 %copy-start.3 = (f32[16,1024]{1,0:T(8,128)S(1)}, f32[16,1024]{1,0:T(8,128)}, u32[]{:S(2)}) copy-start(f32[16,1024]{1,0:T(8,128)} %param.12) | copy-start | bytes 196612
  30.2 64.4 %copy-start.4 = (f32[1024]{0:T(1024)S(1)}, f32[1024]{0:T(1024)}, u32[]{:S(2)}) copy-start(f32[1024]{0:T(1024)} %param.14) | copy-start | bytes 12292
  30.3 65.9 %copy-start.5 = (u32[256]{0:T(256)S(1)}, u32[256]{0:T(256)}, u32[]{:S(2)}) copy-start(u32[256]{0:T(256)} %constant.23) | copy-start | bytes 3076
  30.4 6.0 %collective-permute-start.3 = (f32[16,1024]{1,0:T(8,128)S(1)}, f32[16,1024]{1,0:T(8,128)S(1)}, u32[]{:S(2)}, u32[]{:S(2)}) collective-permute-start(f32[16,1024]{1,0:T(8,128)S(1)} %bitcast_multiply_fusion), channel_id=1, source_target_pairs={{0,4},{4,8},{8,12},{12,16},{16,20},{20,24},{24,28},{28,32},{32,36}... | collective-permute-start | bytes 196616 | tf_op jit(solution)/shard_map/ppermute | solution.py:14
  36.4 6.5 %collective-permute-start.4 = (f32[16,1024]{1,0:T(8,128)S(1)}, f32[16,1024]{1,0:T(8,128)S(1)}, u32[]{:S(2)}, u32[]{:S(2)}) collective-permute-start(f32[16,1024]{1,0:T(8,128)S(1)} %collective-permute-done.3), channel_id=1, source_target_pairs={{0,4},{4,8},{8,12},{12,16},{16,20},{20,24},{24,28},{28,32},{32,36}... | collective-permute-start | bytes 196616 | tf_op jit(solution)/shard_map/ppermute | solution.py:14
  42.9 8.7 %collective-permute-start.5 = (f32[16,1024]{1,0:T(8,128)S(1)}, f32[16,1024]{1,0:T(8,128)S(1)}, u32[]{:S(2)}, u32[]{:S(2)}) collective-permute-start(f32[16,1024]{1,0:T(8,128)S(1)} %get-tuple-element.7), channel_id=1, source_target_pairs={{0,8},{4,12},{8,16},{12,20},{16,24},{20,28},{24,32},{28,36},{32,40... | collective-permute-start | bytes 196616 | tf_op jit(solution)/shard_map/ppermute | solution.py:14
  51.6 6.1 %collective-permute-start.6 = (f32[16,1024]{1,0:T(8,128)S(1)}, f32[16,1024]{1,0:T(8,128)S(1)}, u32[]{:S(2)}, u32[]{:S(2)}) collective-permute-start(f32[16,1024]{1,0:T(8,128)S(1)} %multiply_add_fusion.3), channel_id=1, source_target_pairs={{0,16},{4,20},{8,24},{12,28},{16,32},{20,36},{24,40},{28,44},{32,4... | collective-permute-start | bytes 196616 | tf_op jit(solution)/shard_map/ppermute | solution.py:14
  57.7 18.0 %collective-permute-start.7 = (f32[16,1024]{1,0:T(8,128)S(1)}, f32[16,1024]{1,0:T(8,128)S(1)}, u32[]{:S(2)}, u32[]{:S(2)}) collective-permute-start(f32[16,1024]{1,0:T(8,128)S(1)} %multiply_add_fusion.2), channel_id=1, source_target_pairs={{0,32},{4,36},{8,40},{12,44},{16,48},{20,52},{24,56},{28,60},{32,6... | collective-permute-start | bytes 196616 | tf_op jit(solution)/shard_map/ppermute | solution.py:14
  73.5 16.4 %collective-permute-start = (bf16[2,1024]{1,0:T(2,128)(2,1)S(1)}, bf16[2,1024]{1,0:T(2,128)(2,1)S(1)}, u32[]{:S(2)}, u32[]{:S(2)}) collective-permute-start(bf16[2,1024]{1,0:T(2,128)(2,1)S(1)} %slice.107), channel_id=1, source_target_pairs={{0,4},{4,8},{8,12},{12,16},{16,20},{20,24},{24,28},{28,32},{32,36}... | collective-permute-start | bytes 12296 | tf_op jit(solution)/shard_map/ppermute | solution.py:14
  75.8 7.4 %collective-permute-start.8 = (f32[16,1024]{1,0:T(8,128)S(1)}, f32[16,1024]{1,0:T(8,128)S(1)}, u32[]{:S(2)}, u32[]{:S(2)}) collective-permute-start(f32[16,1024]{1,0:T(8,128)S(1)} %multiply_add_fusion.1), channel_id=1, source_target_pairs={{0,64},{4,68},{8,72},{12,76},{16,80},{20,84},{24,88},{28,92},{32,9... | collective-permute-start | bytes 196616 | tf_op jit(solution)/shard_map/ppermute | solution.py:14
  83.2 8.1 %collective-permute-start.9 = (f32[16,1024]{1,0:T(8,128)S(1)}, f32[16,1024]{1,0:T(8,128)S(1)}, u32[]{:S(2)}, u32[]{:S(2)}) collective-permute-start(f32[16,1024]{1,0:T(8,128)S(1)} %multiply_add_fusion), channel_id=1, source_target_pairs={{0,128},{4,132},{8,136},{12,140},{16,144},{20,148},{24,152},{28,15... | collective-permute-start | bytes 196616 | tf_op jit(solution)/shard_map/ppermute | solution.py:14
  94.9 83.4 %copy-start.1 = (bf16[128,1024]{1,0:T(8,128)(2,1)}, bf16[128,1024]{1,0:T(8,128)(2,1)S(1)}, u32[]{:S(2)}) copy-start(bf16[128,1024]{1,0:T(8,128)(2,1)S(1)} %fusion.31) | copy-start | bytes 786436
  94.9 6.2 %collective-permute-start.10 = (bf16[16,1024]{1,0:T(8,128)(2,1)S(1)}, bf16[16,1024]{1,0:T(8,128)(2,1)S(1)}, u32[]{:S(2)}, u32[]{:S(2)}) collective-permute-start(bf16[16,1024]{1,0:T(8,128)(2,1)S(1)} %slice.145), channel_id=1, source_target_pairs={{4,0},{8,4},{12,8},{16,12},{20,16},{24,20},{28,24},{32,28},{36,32}... | collective-permute-start | bytes 98312 | tf_op jit(solution)/shard_map/ppermute | solution.py:14
Sparse Core Ops, SparseCore 0:
  11.4 150.9 all-gather.1

commit v2 on v1

v2 whole, which is shorter than its diff:
```python
import jax
import jax.numpy as jnp
from jax import lax
from jax.sharding import PartitionSpec as P

STRIDE = 16
RADIX = 8
SEQ = ("u", "v")

highest = lax.Precision.HIGHEST


def from_behind(block, axis, distance):
    devices = range(lax.axis_size(axis))
    route = [(i - distance, i) for i in devices if i - distance in devices]
    return lax.ppermute(block, axis, route)


def short_pass(rows_block, before, tap_weights):
    joined = jnp.concatenate([before, rows_block], axis=0).astype(jnp.float32)
    row_count = rows_block.shape[0]
    return (
        tap_weights[0] * joined[2 : 2 + row_count]
        + tap_weights[1] * joined[1 : 1 + row_count]
        + tap_weights[2] * joined[0:row_count]
    )


def shifted_sum(values, decays, tokens, stride):
    total = None
    for m in range(1, RADIX):
        term = from_behind(values, SEQ, stride * m)
        if m > 1:
            term = jnp.exp(-decays * float(tokens * stride * (m - 1))) * term
        total = term if total is None else total + term
    return total


def modal_conv(gated, residues, decays):
    tokens = gated.shape[0]
    parties = lax.axis_size(SEQ)
    g = gated.astype(jnp.float32)
    steps = jnp.arange(tokens, dtype=jnp.float32)
    weight = residues * jnp.sqrt(-jnp.expm1(-2.0 * decays))
    grow = jnp.exp(decays[:, None, :] * steps[None, :, None])
    shrink = jnp.exp(-decays[:, None, :] * steps[None, :, None])
    lower = (steps[:, None] >= steps[None, :]).astype(jnp.float32)
    running = jnp.einsum("ij,rjc->ric", lower, grow * g[None], precision=highest)
    local = jnp.sum(weight[:, None, :] * shrink * running, axis=0)
    end_state = jnp.exp(-decays * (tokens - 1)) * running[:, -1, :]
    carry = shifted_sum(end_state, decays, tokens, 1)
    inclusive = end_state + jnp.exp(-decays * float(tokens)) * carry
    carry = carry + jnp.exp(-decays * float(tokens * (RADIX - 1))) * shifted_sum(
        inclusive, decays, tokens, RADIX
    )
    after = jnp.exp(-decays[:, None, :] * (steps[None, :, None] + 1.0))
    cross = jnp.sum((weight * carry)[:, None, :] * after, axis=0)
    return local + cross


def shards(
    query_input, key_input, value_input, short_filter, residues, decays, skip_gain, head_weight
):
    tokens, chan_width = query_input.shape
    before = from_behind((query_input[-2:], key_input[-2:], value_input[-2:]), SEQ, 1)
    query_short = short_pass(query_input, before[0], short_filter[:, 0])
    key_short = short_pass(key_input, before[1], short_filter[:, 1])
    value_short = short_pass(value_input, before[2], short_filter[:, 2])
    gated = (key_short * value_short).astype(jnp.bfloat16)
    convolved = modal_conv(gated, residues, decays)
    carried = (convolved + skip_gain * gated.astype(jnp.float32)).astype(jnp.bfloat16)
    operator_out = (query_short * carried.astype(jnp.float32)).astype(jnp.bfloat16)
    rim_rows = from_behind(operator_out[:STRIDE], SEQ, -1)
    extended = jnp.concatenate([operator_out, rim_rows], axis=0)
    width_u = lax.axis_size("u")
    width_v = lax.axis_size("v")
    piece = head_weight.shape[1]
    parted = extended.reshape(tokens + STRIDE, width_u, width_v, piece)
    gathered = lax.all_to_all(parted, "v", split_axis=2, concat_axis=0, tiled=True)
    gathered = gathered.reshape(width_v, tokens + STRIDE, width_u * piece)
    weight_piece = lax.all_gather(head_weight, "u", axis=1, tiled=True)
    rows = tokens // STRIDE
    early_rows = gathered[:, :tokens].reshape(width_v, rows, STRIDE, width_u * piece)
    late_rows = gathered[:, STRIDE:].reshape(width_v, rows, STRIDE, width_u * piece)
    running = jnp.einsum(
        "bjic,ico->bjo", early_rows, weight_piece[:STRIDE], preferred_element_type=jnp.float32
    )
    partial_sum = running + jnp.einsum(
        "bjic,ico->bjo", late_rows, weight_piece[STRIDE:], preferred_element_type=jnp.float32
    )
    probe_out = lax.psum_scatter(
        partial_sum.reshape(width_v * rows, -1), ("v", "tp"), scatter_dimension=0, tiled=True
    ).astype(jnp.bfloat16)
    return (operator_out, probe_out)


def solution(mesh):
    placed = (
        P(SEQ, "tp"),
        P(SEQ, "tp"),
        P(SEQ, "tp"),
        P(None, None, "tp"),
        P(None, "tp"),
        P(None, "tp"),
        P("tp"),
        P(None, ("tp", "u", "v"), None),
    )
    seq_size, tp_size = mesh.devices.shape
    width_u = 4 if seq_size % 4 == 0 else 1
    split = jax.sharding.Mesh(
        mesh.devices.reshape(width_u, seq_size // width_u, tp_size), ("u", "v", "tp")
    )
    return jax.shard_map(
        shards,
        mesh=split,
        in_specs=placed,
        out_specs=(P(SEQ, "tp"), P(("u", "v", "tp"), None)),
        check_vma=False,
    )
```

time: 186 us -> 375 us (2.02); the launches traced: 185 us -> 369 us
  blocking collectives: 9.53 us -> 265 us
  waiting for transfers between devices: 74.4 us -> 6.21 us
  starting transfers between devices: 62.1 us -> 75.6 us
  between operations: 15 us -> 1.78 us
  matrix products: 14.4 us -> 9.21 us
    unnamed x1, blocking collectives: 9.53 us -> 249 us
    all_gather x1 -> x0, waiting for transfers between devices: 61.3 us -> none  [shards(): weight_piece = lax.all_gather(head_weight, 'seq', axis=1, tiled=True)]
    all_gather x0 -> x1, blocking collectives: none -> 15.5 us  [shards(): weight_piece = lax.all_gather(head_weight, 'u', axis=1, tiled=True)]
    ppermute x11 -> x18, starting transfers between devices: 62 us -> 69 us  [from_behind(): return lax.ppermute(block, axis, route)]
    all_to_all x0 -> x1, starting transfers between devices: none -> 6.64 us  [shards(): lax.all_to_all(parted, 'v', split_axis=2, concat_axis=0, tiled=True)]
    ppermute x11 -> x18, waiting for transfers between devices: 12.3 us -> 6.21 us  [from_behind(): return lax.ppermute(block, axis, route)]
    dot_general x2, matrix products: 5.82 us -> 0.67 us  [the longest x1 0.34 us: shards(): jnp.einsum('bjic,ico->bjo', late_rows, weight_piece[STRIDE:], preferred_e...]
  transfers between devices with their start and end apart: 12 -> 19, of which waited for: 9 -> 3; matrix products, arithmetic and copies ran while one was open for 10% -> 1% of each run, Pallas kernels for 0% -> 0%
where the time goes in v2:
time: 375 us; the launch traced here: 369 us
  blocking collectives  265 us (71%)
  starting transfers between devices  75.6 us (20%)
  matrix products  9.21 us (2%)
  other arithmetic  6.27 us (2%)
  waiting for transfers between devices  6.21 us (2%)
  local copies, waits for them, and re-layouts  5.41 us (1%)
    unnamed x1, blocking collectives  249 us
    ppermute x18, starting transfers between devices, from_behind(): return lax.ppermute(block, axis, route)  69 us
    all_gather x1, blocking collectives, shards(): weight_piece = lax.all_gather(head_weight, 'u', axis=1, tiled=True)  15.5 us
    dot_general x1, matrix products, modal_conv(): jnp.einsum('ij,rjc->ric', lower, grow * g[None], precision=highest)  8.54 us
  transfers between devices with their start and end apart: 19, of which 3 were waited for; matrix products, arithmetic and copies ran while one was open for 1% of the time, Pallas kernels for 0%

profile of v2, /device:TPU:1, one launch (start us, length us, event | category | flops | bytes accessed | tf_op | source)
XLA Modules:
  0.0 369.1 jit_solution(5698219646498574115)
XLA Ops:
  0.7 0.8 slice.110
  1.4 5.5 %collective-permute-start.1 = (bf16[2,1024]{1,0:T(2,128)(2,1)S(1)}, bf16[2,1024]{1,0:T(2,128)(2,1)S(1)}, u32[]{:S(2)}, u32[]{:S(2)}) collective-permute-start(bf16[2,1024]{1,0:T(2,128)(2,1)S(1)} %slice.110), channel_id=1, source_target_pairs={{0,4},{4,8},{8,12},{12,16},{16,20},{20,24},{24,28},{28,32},{32,36}... | collective-permute-start | bytes 12296 | tf_op jit(solution)/shard_map/ppermute | solution.py:16
  6.9 0.7 slice.117
  7.6 3.5 collective-permute-start.2
  11.1 0.9 fusion.28
  12.0 1.0 maximum_convert_fusion.1
  13.1 1.0 maximum_convert_fusion.2
  14.1 0.3 fusion.24
  14.4 8.5 %fusion.7 = f32[16,128,1024]{2,1,0:T(8,128)S(1)} fusion(f32[128,1024]{1,0:T(8,128)S(1)} %fusion.24, f32[16,1024]{1,0:T(8,128)} %param.13), kind=kOutput, calls=%fused_computation.9 | convolution fusion | flops 3225436160 | bytes 8978432 | tf_op jit(solution)/shard_map/ij,rjc->ric/dot_general | solution.py:48
  23.0 0.1 slice.138
  23.1 4.7 %collective-permute-start.3 = (f32[16,1024]{1,0:T(8,128)S(1)}, f32[16,1024]{1,0:T(8,128)S(1)}, u32[]{:S(2)}, u32[]{:S(2)}) collective-permute-start(f32[16,1024]{1,0:T(8,128)S(1)} %bitcast_multiply_fusion), channel_id=1, source_target_pairs={{0,4},{4,8},{8,12},{12,16},{16,20},{20,24},{24,28},{28,32},{32,36}... | collective-permute-start | bytes 196616 | tf_op jit(solution)/shard_map/ppermute | solution.py:16
  27.8 3.6 collective-permute-start.4
  31.3 6.1 %collective-permute-start.5 = (f32[16,1024]{1,0:T(8,128)S(1)}, f32[16,1024]{1,0:T(8,128)S(1)}, u32[]{:S(2)}, u32[]{:S(2)}) collective-permute-start(f32[16,1024]{1,0:T(8,128)S(1)} %bitcast_multiply_fusion), channel_id=1, source_target_pairs={{0,12},{4,16},{8,20},{12,24},{16,28},{20,32},{24,36},{28,40},{32,4... | collective-permute-start | bytes 196616 | tf_op jit(solution)/shard_map/ppermute | solution.py:16
  37.5 5.7 %collective-permute-start.6 = (f32[16,1024]{1,0:T(8,128)S(1)}, f32[16,1024]{1,0:T(8,128)S(1)}, u32[]{:S(2)}, u32[]{:S(2)}) collective-permute-start(f32[16,1024]{1,0:T(8,128)S(1)} %bitcast_multiply_fusion), channel_id=1, source_target_pairs={{0,16},{4,20},{8,24},{12,28},{16,32},{20,36},{24,40},{28,44},{32,4... | collective-permute-start | bytes 196616 | tf_op jit(solution)/shard_map/ppermute | solution.py:16
  43.2 2.3 collective-permute-start.7
  45.5 4.2 %collective-permute-start.8 = (f32[16,1024]{1,0:T(8,128)S(1)}, f32[16,1024]{1,0:T(8,128)S(1)}, u32[]{:S(2)}, u32[]{:S(2)}) collective-permute-start(f32[16,1024]{1,0:T(8,128)S(1)} %bitcast_multiply_fusion), channel_id=1, source_target_pairs={{0,24},{4,28},{8,32},{12,36},{16,40},{20,44},{24,48},{28,52},{32,5... | collective-permute-start | bytes 196616 | tf_op jit(solution)/shard_map/ppermute | solution.py:16
  49.7 8.3 %collective-permute-start.9 = (f32[16,1024]{1,0:T(8,128)S(1)}, f32[16,1024]{1,0:T(8,128)S(1)}, u32[]{:S(2)}, u32[]{:S(2)}) collective-permute-start(f32[16,1024]{1,0:T(8,128)S(1)} %bitcast_multiply_fusion), channel_id=1, source_target_pairs={{0,28},{4,32},{8,36},{12,40},{16,44},{20,48},{24,52},{28,56},{32,6... | collective-permute-start | bytes 196616 | tf_op jit(solution)/shard_map/ppermute | solution.py:16
  58.1 2.4 collective-permute-start
  60.5 0.1 multiply_add_fusion
  60.6 8.5 %collective-permute-start.10 = (f32[16,1024]{1,0:T(8,128)S(1)}, f32[16,1024]{1,0:T(8,128)S(1)}, u32[]{:S(2)}, u32[]{:S(2)}) collective-permute-start(f32[16,1024]{1,0:T(8,128)S(1)} %get-tuple-element.8), channel_id=1, source_target_pairs={{0,32},{4,36},{8,40},{12,44},{16,48},{20,52},{24,56},{28,60},{32,6... | collective-permute-start | bytes 196616 | tf_op jit(solution)/shard_map/ppermute | solution.py:16
  69.1 3.0 collective-permute-start.11
  72.1 4.5 %collective-permute-start.12 = (f32[16,1024]{1,0:T(8,128)S(1)}, f32[16,1024]{1,0:T(8,128)S(1)}, u32[]{:S(2)}, u32[]{:S(2)}) collective-permute-start(f32[16,1024]{1,0:T(8,128)S(1)} %get-tuple-element.8), channel_id=1, source_target_pairs={{0,96},{4,100},{8,104},{12,108},{16,112},{20,116},{24,120},{28,124... | collective-permute-start | bytes 196616 | tf_op jit(solution)/shard_map/ppermute | solution.py:16
  76.7 1.3 collective-permute-start.13
  78.0 1.6 collective-permute-start.14
  79.6 1.3 collective-permute-start.15
  80.9 1.3 collective-permute-start.16
  82.2 0.1 maximum_convert_fusion
  82.4 0.5 collective-permute-done.15
  82.8 0.7 collective-permute-done.16
  83.6 0.1 add_multiply_fusion
  83.7 0.0 copy-start.6
  83.7 3.3 multiply_reduce_fusion
  87.0 0.3 fusion.20
  87.3 0.0 copy-start
  87.3 1.3 collective-permute-start.17
  88.6 5.0 %collective-permute-done.17 = bf16[16,1024]{1,0:T(8,128)(2,1)S(1)} collective-permute-done((bf16[16,1024]{1,0:T(8,128)(2,1)S(1)}, bf16[16,1024]{1,0:T(8,128)(2,1)S(1)}, u32[]{:S(2)}, u32[]{:S(2)}) %collective-permute-start.17) | collective-permute-done | bytes 32800 | tf_op jit(solution)/shard_map/ppermute | solution.py:16
  93.6 0.2 copy.23
  93.8 0.9 copy.24
  94.7 6.6 %all-to-all-start = ((bf16[144,4,16,16]{0,3,1,2:T(8,128)(2,1)}), bf16[144,4,16,16]{0,3,1,2:T(8,128)(2,1)S(1)}, u32[]{:S(2)}, u32[]{:S(2)}) async-start(bf16[144,4,16,16]{0,3,1,2:T(8,128)(2,1)} %copy.24), calls=%async_computation | async-start | bytes 1048576 | tf_op jit(solution)/shard_map/all_to_all | solution.py:79
  101.3 0.6 dynamic-slice
  102.6 15.5 %all_gather.3 = bf16[32,64,128]{2,1,0:T(8,128)(2,1)S(1)} all-gather(bf16[32,16,128]{2,1,0:T(8,128)(2,1)S(1)} %copy-done.3), channel_id=1, replica_groups=mesh['u'=4,'v'=16,'tp'=4] {'u'}, dimensions={1}, use_global_device_ids=true | all-gather | bytes 655360 | tf_op jit(solution)/shard_map/all_gather | solution.py:81
  118.1 0.1 fusion.27
  118.2 0.3 copy.27
  118.5 0.3 copy.25
  118.8 0.3 convolution_bitcast_fusion
  119.2 0.3 fusion.11
  119.5 249.0 %all-reduce = bf16[128,128]{1,0:T(8,128)(2,1)S(1)} all-reduce(f32[128,128]{1,0:T(8,128)S(1)} %fusion.11), channel_id=2, replica_groups=mesh['u'=4,'v'=16,'tp'=4] {'v','tp'}, use_global_device_ids=true, to_apply=%region_2.0.clone | all-reduce | flops 16384 | bytes 98304
  368.5 0.5 dynamic-slice_convert_fusion
  (33 shorter events, 0.1 us)
Async XLA Ops:
  0.6 22.4 %copy-start.1 = (f32[16,1024]{1,0:T(8,128)S(1)}, f32[16,1024]{1,0:T(8,128)}, u32[]{:S(2)}) copy-start(f32[16,1024]{1,0:T(8,128)} %param.13) | copy-start | bytes 196612
  0.6 57.4 %copy-start.2 = (bf16[128,1024]{1,0:T(8,128)(2,1)S(1)}, bf16[128,1024]{1,0:T(8,128)(2,1)}, u32[]{:S(2)}) copy-start(bf16[128,1024]{1,0:T(8,128)(2,1)} %param.8) | copy-start | bytes 786436
  0.7 82.9 %copy-start.4 = (f32[16,1024]{1,0:T(8,128)S(1)}, f32[16,1024]{1,0:T(8,128)}, u32[]{:S(2)}) copy-start(f32[16,1024]{1,0:T(8,128)} %param.12) | copy-start | bytes 196612
  1.4 10.6 %collective-permute-start.1 = (bf16[2,1024]{1,0:T(2,128)(2,1)S(1)}, bf16[2,1024]{1,0:T(2,128)(2,1)S(1)}, u32[]{:S(2)}, u32[]{:S(2)}) collective-permute-start(bf16[2,1024]{1,0:T(2,128)(2,1)S(1)} %slice.110), channel_id=1, source_target_pairs={{0,4},{4,8},{8,12},{12,16},{16,20},{20,24},{24,28},{28,32},{32,36}... | collective-permute-start | bytes 12296 | tf_op jit(solution)/shard_map/ppermute | solution.py:16
  7.6 5.4 %collective-permute-start.2 = (bf16[2,1024]{1,0:T(2,128)(2,1)S(1)}, bf16[2,1024]{1,0:T(2,128)(2,1)S(1)}, u32[]{:S(2)}, u32[]{:S(2)}) collective-permute-start(bf16[2,1024]{1,0:T(2,128)(2,1)S(1)} %slice.117), channel_id=1, source_target_pairs={{0,4},{4,8},{8,12},{12,16},{16,20},{20,24},{24,28},{28,32},{32,36}... | collective-permute-start | bytes 12296 | tf_op jit(solution)/shard_map/ppermute | solution.py:16
  23.0 64.0 %copy-start.5 = (f32[1024]{0:T(1024)S(1)}, f32[1024]{0:T(1024)}, u32[]{:S(2)}) copy-start(f32[1024]{0:T(1024)} %param.14) | copy-start | bytes 12292
  23.1 22.4 %collective-permute-start.3 = (f32[16,1024]{1,0:T(8,128)S(1)}, f32[16,1024]{1,0:T(8,128)S(1)}, u32[]{:S(2)}, u32[]{:S(2)}) collective-permute-start(f32[16,1024]{1,0:T(8,128)S(1)} %bitcast_multiply_fusion), channel_id=1, source_target_pairs={{0,4},{4,8},{8,12},{12,16},{16,20},{20,24},{24,28},{28,32},{32,36}... | collective-permute-start | bytes 196616 | tf_op jit(solution)/shard_map/ppermute | solution.py:16
  27.8 21.9 %collective-permute-start.4 = (f32[16,1024]{1,0:T(8,128)S(1)}, f32[16,1024]{1,0:T(8,128)S(1)}, u32[]{:S(2)}, u32[]{:S(2)}) collective-permute-start(f32[16,1024]{1,0:T(8,128)S(1)} %bitcast_multiply_fusion), channel_id=1, source_target_pairs={{0,8},{4,12},{8,16},{12,20},{16,24},{20,28},{24,32},{28,36},{32,40... | collective-permute-start | bytes 196616 | tf_op jit(solution)/shard_map/ppermute | solution.py:16
  31.3 26.7 %collective-permute-start.5 = (f32[16,1024]{1,0:T(8,128)S(1)}, f32[16,1024]{1,0:T(8,128)S(1)}, u32[]{:S(2)}, u32[]{:S(2)}) collective-permute-start(f32[16,1024]{1,0:T(8,128)S(1)} %bitcast_multiply_fusion), channel_id=1, source_target_pairs={{0,12},{4,16},{8,20},{12,24},{16,28},{20,32},{24,36},{28,40},{32,4... | collective-permute-start | bytes 196616 | tf_op jit(solution)/shard_map/ppermute | solution.py:16
  37.5 23.0 %collective-permute-start.6 = (f32[16,1024]{1,0:T(8,128)S(1)}, f32[16,1024]{1,0:T(8,128)S(1)}, u32[]{:S(2)}, u32[]{:S(2)}) collective-permute-start(f32[16,1024]{1,0:T(8,128)S(1)} %bitcast_multiply_fusion), channel_id=1, source_target_pairs={{0,16},{4,20},{8,24},{12,28},{16,32},{20,36},{24,40},{28,44},{32,4... | collective-permute-start | bytes 196616 | tf_op jit(solution)/shard_map/ppermute | solution.py:16
  43.2 17.3 %collective-permute-start.7 = (f32[16,1024]{1,0:T(8,128)S(1)}, f32[16,1024]{1,0:T(8,128)S(1)}, u32[]{:S(2)}, u32[]{:S(2)}) collective-permute-start(f32[16,1024]{1,0:T(8,128)S(1)} %bitcast_multiply_fusion), channel_id=1, source_target_pairs={{0,20},{4,24},{8,28},{12,32},{16,36},{20,40},{24,44},{28,48},{32,5... | collective-permute-start | bytes 196616 | tf_op jit(solution)/shard_map/ppermute | solution.py:16
  45.5 15.0 %collective-permute-start.8 = (f32[16,1024]{1,0:T(8,128)S(1)}, f32[16,1024]{1,0:T(8,128)S(1)}, u32[]{:S(2)}, u32[]{:S(2)}) collective-permute-start(f32[16,1024]{1,0:T(8,128)S(1)} %bitcast_multiply_fusion), channel_id=1, source_target_pairs={{0,24},{4,28},{8,32},{12,36},{16,40},{20,44},{24,48},{28,52},{32,5... | collective-permute-start | bytes 196616 | tf_op jit(solution)/shard_map/ppermute | solution.py:16
  49.7 10.8 %collective-permute-start.9 = (f32[16,1024]{1,0:T(8,128)S(1)}, f32[16,1024]{1,0:T(8,128)S(1)}, u32[]{:S(2)}, u32[]{:S(2)}) collective-permute-start(f32[16,1024]{1,0:T(8,128)S(1)} %bitcast_multiply_fusion), channel_id=1, source_target_pairs={{0,28},{4,32},{8,36},{12,40},{16,44},{20,48},{24,52},{28,56},{32,6... | collective-permute-start | bytes 196616 | tf_op jit(solution)/shard_map/ppermute | solution.py:16
  58.1 19.9 %collective-permute-start = (bf16[2,1024]{1,0:T(2,128)(2,1)S(1)}, bf16[2,1024]{1,0:T(2,128)(2,1)S(1)}, u32[]{:S(2)}, u32[]{:S(2)}) collective-permute-start(bf16[2,1024]{1,0:T(2,128)(2,1)S(1)} %slice.103), channel_id=1, source_target_pairs={{0,4},{4,8},{8,12},{12,16},{16,20},{20,24},{24,28},{28,32},{32,36}... | collective-permute-start | bytes 12296 | tf_op jit(solution)/shard_map/ppermute | solution.py:16
  60.6 19.0 %collective-permute-start.10 = (f32[16,1024]{1,0:T(8,128)S(1)}, f32[16,1024]{1,0:T(8,128)S(1)}, u32[]{:S(2)}, u32[]{:S(2)}) collective-permute-start(f32[16,1024]{1,0:T(8,128)S(1)} %get-tuple-element.8), channel_id=1, source_target_pairs={{0,32},{4,36},{8,40},{12,44},{16,48},{20,52},{24,56},{28,60},{32,6... | collective-permute-start | bytes 196616 | tf_op jit(solution)/shard_map/ppermute | solution.py:16
  69.1 11.8 %collective-permute-start.11 = (f32[16,1024]{1,0:T(8,128)S(1)}, f32[16,1024]{1,0:T(8,128)S(1)}, u32[]{:S(2)}, u32[]{:S(2)}) collective-permute-start(f32[16,1024]{1,0:T(8,128)S(1)} %get-tuple-element.8), channel_id=1, source_target_pairs={{0,64},{4,68},{8,72},{12,76},{16,80},{20,84},{24,88},{28,92},{32,9... | collective-permute-start | bytes 196616 | tf_op jit(solution)/shard_map/ppermute | solution.py:16
  72.1 10.2 %collective-permute-start.12 = (f32[16,1024]{1,0:T(8,128)S(1)}, f32[16,1024]{1,0:T(8,128)S(1)}, u32[]{:S(2)}, u32[]{:S(2)}) collective-permute-start(f32[16,1024]{1,0:T(8,128)S(1)} %get-tuple-element.8), channel_id=1, source_target_pairs={{0,96},{4,100},{8,104},{12,108},{16,112},{20,116},{24,120},{28,124... | collective-permute-start | bytes 196616 | tf_op jit(solution)/shard_map/ppermute | solution.py:16
  76.7 5.7 %collective-permute-start.13 = (f32[16,1024]{1,0:T(8,128)S(1)}, f32[16,1024]{1,0:T(8,128)S(1)}, u32[]{:S(2)}, u32[]{:S(2)}) collective-permute-start(f32[16,1024]{1,0:T(8,128)S(1)} %get-tuple-element.8), channel_id=1, source_target_pairs={{0,128},{4,132},{8,136},{12,140},{16,144},{20,148},{24,152},{28,15... | collective-permute-start | bytes 196616 | tf_op jit(solution)/shard_map/ppermute | solution.py:16
  78.0 4.4 %collective-permute-start.14 = (f32[16,1024]{1,0:T(8,128)S(1)}, f32[16,1024]{1,0:T(8,128)S(1)}, u32[]{:S(2)}, u32[]{:S(2)}) collective-permute-start(f32[16,1024]{1,0:T(8,128)S(1)} %get-tuple-element.8), channel_id=1, source_target_pairs={{0,160},{4,164},{8,168},{12,172},{16,176},{20,180},{24,184},{28,18... | collective-permute-start | bytes 196616 | tf_op jit(solution)/shard_map/ppermute | solution.py:16
  79.6 3.2 collective-permute-start.15
  80.9 2.6 collective-permute-start.16
  83.7 17.6 %copy-start.6 = (u32[256]{0:T(256)S(1)}, u32[256]{0:T(256)}, u32[]{:S(2)}) copy-start(u32[256]{0:T(256)} %constant.37) | copy-start | bytes 3076
  83.7 18.9 %copy-start.3 = (bf16[32,16,128]{2,1,0:T(8,128)(2,1)S(1)}, bf16[32,16,128]{2,1,0:T(8,128)(2,1)}, u32[]{:S(2)}) copy-start(bf16[32,16,128]{2,1,0:T(8,128)(2,1)} %param.15) | copy-start | bytes 393220
  87.3 281.8 %copy-start = (bf16[128,1024]{1,0:T(8,128)(2,1)}, bf16[128,1024]{1,0:T(8,128)(2,1)S(1)}, u32[]{:S(2)}) copy-start(bf16[128,1024]{1,0:T(8,128)(2,1)S(1)} %fusion.20) | copy-start | bytes 786436
  87.3 6.3 %collective-permute-start.17 = (bf16[16,1024]{1,0:T(8,128)(2,1)S(1)}, bf16[16,1024]{1,0:T(8,128)(2,1)S(1)}, u32[]{:S(2)}, u32[]{:S(2)}) collective-permute-start(bf16[16,1024]{1,0:T(8,128)(2,1)S(1)} %slice.139), channel_id=1, source_target_pairs={{4,0},{8,4},{12,8},{16,12},{20,16},{24,20},{28,24},{32,28},{36,32}... | collective-permute-start | bytes 98312 | tf_op jit(solution)/shard_map/ppermute | solution.py:16
  94.7 23.4 %all-to-all-start = ((bf16[144,4,16,16]{0,3,1,2:T(8,128)(2,1)}), bf16[144,4,16,16]{0,3,1,2:T(8,128)(2,1)S(1)}, u32[]{:S(2)}, u32[]{:S(2)}) async-start(bf16[144,4,16,16]{0,3,1,2:T(8,128)(2,1)} %copy.24), calls=%async_computation | async-start | bytes 1048576 | tf_op jit(solution)/shard_map/all_to_all | solution.py:79

commit v3 on v1

v3 whole, which is shorter than its diff:
```python
import jax
import jax.numpy as jnp
from jax import lax
from jax.sharding import PartitionSpec as P

STRIDE = 16
CHUNK = 128

highest = lax.Precision.HIGHEST


def from_behind(block, axis, distance):
    devices = range(lax.axis_size(axis))
    route = [(i - distance, i) for i in devices if i - distance in devices]
    return lax.ppermute(block, axis, route)


def short_pass(rows, before, tap_weights):
    joined = jnp.concatenate([before, rows], axis=0).astype(jnp.float32)
    row_count = rows.shape[0]
    return (
        tap_weights[0] * joined[2 : 2 + row_count]
        + tap_weights[1] * joined[1 : 1 + row_count]
        + tap_weights[2] * joined[0:row_count]
    )


def modal_conv(gated, residues, decays):
    span, width = gated.shape
    chunks = span // CHUNK
    groups = lax.axis_size("u")
    g = gated.astype(jnp.float32).reshape(chunks, CHUNK, width)
    steps = jnp.arange(CHUNK, dtype=jnp.float32)
    weight = residues * jnp.sqrt(-jnp.expm1(-2.0 * decays))
    grow = jnp.exp(decays[:, None, :] * steps[None, :, None])
    shrink = jnp.exp(-decays[:, None, :] * steps[None, :, None])
    lower = (steps[:, None] >= steps[None, :]).astype(jnp.float32)
    running = jnp.einsum("ij,rkjc->rkic", lower, grow[:, None] * g[None], precision=highest)
    ends = jnp.exp(-decays * (CHUNK - 1))[:, None, :] * running[:, :, -1, :]
    index = jnp.arange(chunks)
    lag = (index[:, None] - 1 - index[None, :]).astype(jnp.float32)
    decay_table = jnp.where(
        (lag >= 0)[None, :, :, None],
        jnp.exp(-decays[:, None, None, :] * (CHUNK * jnp.maximum(lag, 0.0))[None, :, :, None]),
        0.0,
    )
    inner = jnp.sum(decay_table * ends[:, None, :, :], axis=2)
    total = jnp.exp(-decays * CHUNK) * inner[:, -1] + ends[:, -1]
    outer = None
    for m in range(1, groups):
        term = from_behind(total, "u", m)
        if m > 1:
            term = jnp.exp(-decays * float(span * (m - 1))) * term
        outer = term if outer is None else outer + term
    if outer is not None:
        offsets = (CHUNK * index).astype(jnp.float32)
        inner = inner + jnp.exp(-decays[:, None, :] * offsets[None, :, None]) * outer[:, None, :]
    after = jnp.exp(-decays[:, None, :] * (steps[None, :, None] + 1.0))
    modes = shrink[:, None] * running + after[:, None] * inner[:, :, None, :]
    return jnp.sum(weight[:, None, None, :] * modes, axis=0).reshape(span, width)


def shards(
    query_input, key_input, value_input, short_filter, residues, decays, skip_gain, head_weight
):
    tokens, chan_width = query_input.shape
    width_u = lax.axis_size("u")
    width_v = lax.axis_size("v")
    piece = head_weight.shape[1]
    span = tokens * width_v
    narrow = width_u * piece
    stacked = jnp.stack([query_input, key_input, value_input], axis=0)
    stacked = stacked.reshape(1, 3, tokens, width_u, width_v, piece)
    columns = lax.all_to_all(stacked, "v", split_axis=4, concat_axis=0, tiled=True)
    columns = columns.reshape(width_v, 3, tokens, narrow)
    columns = jnp.transpose(columns, (1, 0, 2, 3)).reshape(3, span, narrow)
    weight_rep = jnp.broadcast_to(head_weight[None], (width_u,) + head_weight.shape)
    weight_cols = lax.all_to_all(weight_rep, "u", split_axis=0, concat_axis=0, tiled=True)
    weight_cols = jnp.transpose(weight_cols, (1, 0, 2, 3)).reshape(
        head_weight.shape[0], narrow, head_weight.shape[2]
    )
    before = from_behind(columns[:, -2:], "u", 1)
    sf = short_filter.reshape(3, 3, width_u, width_v, piece)
    sf = jnp.transpose(sf, (0, 1, 3, 2, 4))
    sf = lax.dynamic_index_in_dim(sf, lax.axis_index("v"), axis=2, keepdims=False)
    sf = sf.reshape(3, 3, narrow)

    def pick(values):
        shaped = values.reshape(values.shape[0], width_u, width_v, piece)
        shaped = lax.dynamic_index_in_dim(shaped, lax.axis_index("v"), axis=2, keepdims=False)
        return shaped.reshape(values.shape[0], narrow)

    query_short = short_pass(columns[0], before[0], sf[:, 0])
    key_short = short_pass(columns[1], before[1], sf[:, 1])
    value_short = short_pass(columns[2], before[2], sf[:, 2])
    gated = (key_short * value_short).astype(jnp.bfloat16)
    convolved = modal_conv(gated, pick(residues), pick(decays))
    gain = pick(skip_gain[None])[0]
    carried = (convolved + gain * gated.astype(jnp.float32)).astype(jnp.bfloat16)
    op_cols = (query_short * carried.astype(jnp.float32)).astype(jnp.bfloat16)
    back = op_cols.reshape(width_v, tokens, width_u, 1, piece)
    back = lax.all_to_all(back, "v", split_axis=0, concat_axis=3, tiled=True)
    operator_out = back.reshape(tokens, chan_width)
    rim_rows = from_behind(op_cols[:STRIDE], "u", -1)
    extended = jnp.concatenate([op_cols, rim_rows], axis=0)
    rows = span // STRIDE
    early_rows = extended[:span].reshape(rows, STRIDE, narrow)
    late_rows = extended[STRIDE:].reshape(rows, STRIDE, narrow)
    running = jnp.einsum(
        "jic,ico->jo", early_rows, weight_cols[:STRIDE], preferred_element_type=jnp.float32
    )
    partial_sum = running + jnp.einsum(
        "jic,ico->jo", late_rows, weight_cols[STRIDE:], preferred_element_type=jnp.float32
    )
    partial_sum = partial_sum.reshape(width_v, rows // width_v, -1)
    partial_sum = lax.all_to_all(partial_sum, "v", split_axis=0, concat_axis=0, tiled=True)
    block_sum = jnp.sum(partial_sum, axis=0)
    probe_out = lax.psum_scatter(block_sum, "tp", scatter_dimension=0, tiled=True).astype(
        jnp.bfloat16
    )
    return (operator_out, probe_out)


def solution(mesh):
    seq_size, tp_size = mesh.devices.shape
    width_u = 4 if seq_size % 4 == 0 else 1
    split = jax.sharding.Mesh(
        mesh.devices.reshape(width_u, seq_size // width_u, tp_size), ("u", "v", "tp")
    )
    seq = ("u", "v")
    placed = (
        P(seq, "tp"),
        P(seq, "tp"),
        P(seq, "tp"),
        P(None, None, "tp"),
        P(None, "tp"),
        P(None, "tp"),
        P("tp"),
        P(None, ("tp", "u", "v"), None),
    )
    return jax.shard_map(
        shards,
        mesh=split,
        in_specs=placed,
        out_specs=(P(seq, "tp"), P(("u", "v", "tp"), None)),
        check_vma=False,
    )
```

time: 186 us -> 131 us (0.70)
  the two profiles are of different devices: /device:TPU:1 before, /device:TPU:16 now
where the time goes in v3:
time: 131 us
  waiting for transfers between devices  45.7 us (35%)
  starting transfers between devices  34.7 us (26%)
  local copies, waits for them, and re-layouts  27.7 us (21%)
  other arithmetic  9.19 us (7%)
  blocking collectives  6 us (5%)
  matrix products  5.52 us (4%)
  between operations  1.74 us (1%)
    all_to_all x1, waiting for transfers between devices, shards(): lax.all_to_all(stacked, 'v', split_axis=4, concat_axis=0, tiled=True)  20.5 us
    all_to_all x1, starting transfers between devices, shards(): lax.all_to_all(stacked, 'v', split_axis=4, concat_axis=0, tiled=True)  11 us
    ppermute x5, starting transfers between devices, from_behind(): return lax.ppermute(block, axis, route)  10.8 us
    ppermute x5, waiting for transfers between devices, from_behind(): return lax.ppermute(block, axis, route)  10.7 us
    all_to_all x1, waiting for transfers between devices, shards(): lax.all_to_all(partial_sum, 'v', split_axis=0, concat_axis=0, tiled=True)  9.73 us
    unnamed x17, local copies, waits for them, and re-layouts  8.32 us
    unnamed x1, blocking collectives  6 us
    slice x1, local copies, waits for them, and re-layouts, modal_conv(): ends = jnp.exp(-decays * (CHUNK - 1))[:, None, :] * running[:, :, -1, :]  5.46 us
  transfers between devices with their start and end apart: 9, of which 7 were waited for; matrix products, arithmetic and copies ran while one was open for 24% of the time, Pallas kernels for 0%

profile of v3, /device:TPU:16, one launch (start us, length us, event | category | flops | bytes accessed | tf_op | source)
XLA Modules:
  0.0 130.6 jit_solution(3539531333170131644)
XLA Ops:
  0.6 1.2 copy.108
  1.8 1.1 copy.107
  2.9 1.1 copy.106
  4.2 1.1 copy.109
  5.3 11.0 %all-to-all-start = ((bf16[1,3,128,4,16,16]{2,5,3,1,0,4:T(8,128)(2,1)}), bf16[1,3,128,4,16,16]{2,5,3,1,0,4:T(8,128)(2,1)S(1)}, u32[]{:S(2)}, u32[]{:S(2)}) async-start(bf16[1,3,128,4,16,16]{2,5,3,1,0,4:T(8,128)(2,1)} %copy.109), calls=%async_computation | async-start | bytes 1572864 | tf_op jit(solution)/shard_map/all_to_all | solution.py:74
  16.3 0.9 reshape.209
  17.4 1.0 reshape.215
  18.5 1.0 reshape.213
  20.0 0.2 multiply_exponential_fusion.1
  20.2 0.2 multiply_exponential_fusion.2
  20.4 20.5 %all-to-all-done = bf16[1,3,128,4,16,16]{2,5,3,1,0,4:T(8,128)(2,1)S(1)} async-done(((bf16[1,3,128,4,16,16]{2,5,3,1,0,4:T(8,128)(2,1)}), bf16[1,3,128,4,16,16]{2,5,3,1,0,4:T(8,128)(2,1)S(1)}, u32[]{:S(2)}, u32[]{:S(2)}) %all-to-all-start) | async-done | bytes 786464 | tf_op jit(solution)/shard_map/all_to_all | solution.py:74
  40.9 0.9 broadcast_in_dim.12
  41.8 4.8 %all-to-all-start.2 = ((bf16[4,32,16,128]{3,2,1,0:T(8,128)(2,1)}), bf16[4,32,16,128]{3,2,1,0:T(8,128)(2,1)S(1)}, u32[]{:S(2)}, u32[]{:S(2)}) async-start(bf16[4,32,16,128]{3,2,1,0:T(8,128)(2,1)} %broadcast_in_dim.12), calls=%async_computation.2 | async-start | bytes 1048576 | tf_op jit(solution)/shard_map/all_to_all | solution.py:78
  46.6 0.2 copy.161
  46.9 3.3 %collective-permute-start = (bf16[3,2,64]{1,2,0:T(8,128)(2,1)S(1)}, bf16[3,2,64]{1,2,0:T(8,128)(2,1)S(1)}, u32[]{:S(2)}, u32[]{:S(2)}) collective-permute-start(bf16[3,2,64]{1,2,0:T(8,128)(2,1)S(1)} %slice.161), channel_id=1, source_target_pairs={{0,64},{64,128},{128,192},{1,65},{65,129},{129,193},{2,66},{66,130... | collective-permute-start | bytes 2312 | tf_op jit(solution)/shard_map/ppermute | solution.py:15
  50.2 0.2 copy.112
  50.5 0.2 copy.117
  50.7 0.2 copy.120
  51.0 1.9 %collective-permute-done = bf16[3,2,64]{1,2,0:T(8,128)(2,1)S(1)} collective-permute-done((bf16[3,2,64]{1,2,0:T(8,128)(2,1)S(1)}, bf16[3,2,64]{1,2,0:T(8,128)(2,1)S(1)}, u32[]{:S(2)}, u32[]{:S(2)}) %collective-permute-start) | collective-permute-done | bytes 800 | tf_op jit(solution)/shard_map/ppermute | solution.py:15
  53.0 0.3 maximum_convert_fusion
  53.3 0.7 convert_bitcast_fusion
  54.0 4.2 %fusion.4 = f32[16,16,128,64]{2,3,1,0:T(8,128)S(1)} fusion(f32[16,128,64]{1,2,0:T(8,128)S(1)} %bitcast.121, f32[16,128,64]{1,2,0:T(8,128)S(1)} %multiply_exponential_fusion.1), kind=kOutput, calls=%fused_computation.5 | convolution fusion | flops 3223339008 | bytes 9437184 | tf_op jit(solution)/shard_map/ij,rkjc->rkic/dot_general | solution.py:38
  58.3 3.2 %copy-done = f32[16,16,128,64]{2,3,1,0:T(8,128)} copy-done((f32[16,16,128,64]{2,3,1,0:T(8,128)}, f32[16,16,128,64]{2,3,1,0:T(8,128)S(1)}, u32[]{:S(2)}) %copy-start) | copy-done | bytes 8388632
  61.5 5.5 %slice.185 = f32[16,16,1,64]{2,3,1,0:T(8,128)} slice(f32[16,16,128,64]{2,3,1,0:T(8,128)S(1)} %fusion.4), slice={[0:16], [0:16], [127:128], [0:64]} | slice | bytes 131072 | tf_op jit(solution)/shard_map/slice | solution.py:39
  67.0 5.4 %copy.139 = f32[16,16,1,64]{3,0,1,2:T(8,128)S(1)} copy(f32[16,16,1,64]{2,3,1,0:T(8,128)} %slice.185) | data formatting | bytes 131072 | tf_op jit(solution)/shard_map/squeeze | solution.py:39
  72.5 1.3 multiply_reduce_fusion.1
  73.8 0.7 collective-permute-start.3
  74.4 3.7 %collective-permute-start.1 = (f32[16,64]{1,0:T(8,128)S(1)}, f32[16,64]{1,0:T(8,128)S(1)}, u32[]{:S(2)}, u32[]{:S(2)}) collective-permute-start(f32[16,64]{1,0:T(8,128)S(1)} %fusion.25), channel_id=1, source_target_pairs={{0,64},{64,128},{128,192},{1,65},{65,129},{129,193},{2,66},{66,130... | collective-permute-start | bytes 12296 | tf_op jit(solution)/shard_map/ppermute | solution.py:15
  78.2 1.3 collective-permute-start.2
  79.7 0.3 collective-permute-done.1
  80.0 5.2 %collective-permute-done.2 = f32[16,64]{1,0:T(8,128)S(1)} collective-permute-done((f32[16,64]{1,0:T(8,128)S(1)}, f32[16,64]{1,0:T(8,128)S(1)}, u32[]{:S(2)}, u32[]{:S(2)}) %collective-permute-start.2) | collective-permute-done | bytes 4128 | tf_op jit(solution)/shard_map/ppermute | solution.py:15
  85.3 5.4 %multiply_reduce_fusion = f32[16,128,64]{1,2,0:T(8,128)S(1)} fusion(f32[16,16,128,64]{2,3,1,0:T(8,128)} %copy-done, f32[16,16,64]{2,1,0:T(8,128)S(1)} %multiply_add_fusion, f32[16,128,64]{1,2,0:T(8,128)S(1)} %get-tuple-element.26, f32[16,128,64]{1,2,0:T(8,128)S(1)} %get-tuple-element.25, f32[16,64]{1,0:T(8,128)S(1)} %get-tuple-element.22), kind=kLoop, calls=%fused_computation | loop fusion | flops 10354688 | bytes 10031104 | tf_op jit(solution)/shard_map/reduce_sum | solution.py:60
  90.7 0.4 fusion.19
  91.2 1.9 %collective-permute-start.4 = (bf16[16,64]{0,1:T(8,128)(2,1)S(1)}, bf16[16,64]{0,1:T(8,128)(2,1)S(1)}, u32[]{:S(2)}, u32[]{:S(2)}) collective-permute-start(bf16[16,64]{0,1:T(8,128)(2,1)S(1)} %slice.189), channel_id=1, source_target_pairs={{64,0},{128,64},{192,128},{65,1},{129,65},{193,129},{66,2},{130,66... | collective-permute-start | bytes 6152 | tf_op jit(solution)/shard_map/ppermute | solution.py:15
  93.2 0.3 copy.128
  93.5 3.3 %collective-permute-done.4 = bf16[16,64]{0,1:T(8,128)(2,1)S(1)} collective-permute-done((bf16[16,64]{0,1:T(8,128)(2,1)S(1)}, bf16[16,64]{0,1:T(8,128)(2,1)S(1)}, u32[]{:S(2)}, u32[]{:S(2)}) %collective-permute-start.4) | collective-permute-done | bytes 2080 | tf_op jit(solution)/shard_map/ppermute | solution.py:15
  97.0 0.3 copy.131
  97.3 0.3 convolution_bitcast_fusion
  97.6 1.0 fusion.8
  98.6 4.5 %all-to-all-start.3 = ((f32[16,8,128]{2,1,0:T(8,128)}), f32[16,8,128]{2,1,0:T(8,128)S(1)}, u32[]{:S(2)}, u32[]{:S(2)}) async-start(f32[16,8,128]{2,1,0:T(8,128)} %fusion.8), calls=%async_computation.3 | async-start | bytes 131072 | tf_op jit(solution)/shard_map/all_to_all | solution.py:116
  103.1 0.8 copy.126
  103.9 9.7 %all-to-all-done.3 = f32[16,8,128]{2,1,0:T(8,128)S(1)} async-done(((f32[16,8,128]{2,1,0:T(8,128)}), f32[16,8,128]{2,1,0:T(8,128)S(1)}, u32[]{:S(2)}, u32[]{:S(2)}) %all-to-all-start.3) | async-done | bytes 65568 | tf_op jit(solution)/shard_map/all_to_all | solution.py:116
  113.6 3.5 %all-to-all-start.1 = ((bf16[16,128,4,1,16]{1,4,2,3,0:T(8,128)(2,1)}), bf16[16,128,4,1,16]{1,4,2,3,0:T(8,128)(2,1)S(1)}, u32[]{:S(2)}, u32[]{:S(2)}) async-start(bf16[16,128,4,1,16]{1,4,2,3,0:T(8,128)(2,1)} %copy.126), calls=%async_computation.1 | async-start | bytes 524288 | tf_op jit(solution)/shard_map/all_to_all | solution.py:102
  117.2 0.6 dynamic-slice.4
  118.5 6.0 %all-reduce = bf16[8,128]{1,0:T(8,128)(2,1)S(1)} all-reduce(f32[8,128]{1,0:T(8,128)S(1)} %reduce_sum.29), channel_id=2, replica_groups=mesh['u'=4,'v'=16,'tp'=4] {'tp'}, use_global_device_ids=true, to_apply=%region_3.4.clone | all-reduce | flops 1024 | bytes 6144
  124.5 0.5 dynamic-slice_convert_fusion
  125.0 4.7 %all-to-all-done.1 = bf16[16,128,4,1,16]{1,4,2,3,0:T(8,128)(2,1)S(1)} async-done(((bf16[16,128,4,1,16]{1,4,2,3,0:T(8,128)(2,1)}), bf16[16,128,4,1,16]{1,4,2,3,0:T(8,128)(2,1)S(1)}, u32[]{:S(2)}, u32[]{:S(2)}) %all-to-all-start.1) | async-done | bytes 262176 | tf_op jit(solution)/shard_map/all_to_all | solution.py:102
  129.8 0.9 copy.134
  (47 shorter events, 1.9 us)
Async XLA Ops:
  0.6 40.3 %copy-start.1 = (bf16[32,16,128]{2,1,0:T(8,128)(2,1)S(1)}, bf16[32,16,128]{2,1,0:T(8,128)(2,1)}, u32[]{:S(2)}) copy-start(bf16[32,16,128]{2,1,0:T(8,128)(2,1)} %param.15) | copy-start | bytes 393220
  5.3 35.6 %all-to-all-start = ((bf16[1,3,128,4,16,16]{2,5,3,1,0,4:T(8,128)(2,1)}), bf16[1,3,128,4,16,16]{2,5,3,1,0,4:T(8,128)(2,1)S(1)}, u32[]{:S(2)}, u32[]{:S(2)}) async-start(bf16[1,3,128,4,16,16]{2,5,3,1,0,4:T(8,128)(2,1)} %copy.109), calls=%async_computation | async-start | bytes 1572864 | tf_op jit(solution)/shard_map/all_to_all | solution.py:74
  41.8 51.3 %all-to-all-start.2 = ((bf16[4,32,16,128]{3,2,1,0:T(8,128)(2,1)}), bf16[4,32,16,128]{3,2,1,0:T(8,128)(2,1)S(1)}, u32[]{:S(2)}, u32[]{:S(2)}) async-start(bf16[4,32,16,128]{3,2,1,0:T(8,128)(2,1)} %broadcast_in_dim.12), calls=%async_computation.2 | async-start | bytes 1048576 | tf_op jit(solution)/shard_map/all_to_all | solution.py:78
  46.9 6.0 %collective-permute-start = (bf16[3,2,64]{1,2,0:T(8,128)(2,1)S(1)}, bf16[3,2,64]{1,2,0:T(8,128)(2,1)S(1)}, u32[]{:S(2)}, u32[]{:S(2)}) collective-permute-start(bf16[3,2,64]{1,2,0:T(8,128)(2,1)S(1)} %slice.161), channel_id=1, source_target_pairs={{0,64},{64,128},{128,192},{1,65},{65,129},{129,193},{2,66},{66,130... | collective-permute-start | bytes 2312 | tf_op jit(solution)/shard_map/ppermute | solution.py:15
  58.3 3.2 %copy-start = (f32[16,16,128,64]{2,3,1,0:T(8,128)}, f32[16,16,128,64]{2,3,1,0:T(8,128)S(1)}, u32[]{:S(2)}) copy-start(f32[16,16,128,64]{2,3,1,0:T(8,128)S(1)} %fusion.4) | copy-start | bytes 25165828
  67.0 12.5 %copy-start.2 = (f32[1024]{0:T(1024)S(1)}, f32[1024]{0:T(1024)}, u32[]{:S(2)}) copy-start(f32[1024]{0:T(1024)} %param.14) | copy-start | bytes 12292
  73.8 5.9 %collective-permute-start.3 = (f32[16,64]{1,0:T(8,128)S(1)}, f32[16,64]{1,0:T(8,128)S(1)}, u32[]{:S(2)}, u32[]{:S(2)}) collective-permute-start(f32[16,64]{1,0:T(8,128)S(1)} %fusion.25), channel_id=1, source_target_pairs={{0,192},{1,193},{2,194},{3,195},{4,196},{5,197},{6,198},{7,199},{8... | collective-permute-start | bytes 12296 | tf_op jit(solution)/shard_map/ppermute | solution.py:15
  74.4 5.5 %collective-permute-start.1 = (f32[16,64]{1,0:T(8,128)S(1)}, f32[16,64]{1,0:T(8,128)S(1)}, u32[]{:S(2)}, u32[]{:S(2)}) collective-permute-start(f32[16,64]{1,0:T(8,128)S(1)} %fusion.25), channel_id=1, source_target_pairs={{0,64},{64,128},{128,192},{1,65},{65,129},{129,193},{2,66},{66,130... | collective-permute-start | bytes 12296 | tf_op jit(solution)/shard_map/ppermute | solution.py:15
  78.2 7.0 %collective-permute-start.2 = (f32[16,64]{1,0:T(8,128)S(1)}, f32[16,64]{1,0:T(8,128)S(1)}, u32[]{:S(2)}, u32[]{:S(2)}) collective-permute-start(f32[16,64]{1,0:T(8,128)S(1)} %fusion.25), channel_id=1, source_target_pairs={{0,128},{64,192},{1,129},{65,193},{2,130},{66,194},{3,131},{67,195... | collective-permute-start | bytes 12296 | tf_op jit(solution)/shard_map/ppermute | solution.py:15
  85.3 31.9 %copy-start.3 = (u32[256]{0:T(256)S(1)}, u32[256]{0:T(256)}, u32[]{:S(2)}) copy-start(u32[256]{0:T(256)} %constant.46) | copy-start | bytes 3076
  91.2 5.6 %collective-permute-start.4 = (bf16[16,64]{0,1:T(8,128)(2,1)S(1)}, bf16[16,64]{0,1:T(8,128)(2,1)S(1)}, u32[]{:S(2)}, u32[]{:S(2)}) collective-permute-start(bf16[16,64]{0,1:T(8,128)(2,1)S(1)} %slice.189), channel_id=1, source_target_pairs={{64,0},{128,64},{192,128},{65,1},{129,65},{193,129},{66,2},{130,66... | collective-permute-start | bytes 6152 | tf_op jit(solution)/shard_map/ppermute | solution.py:15
  98.6 15.1 %all-to-all-start.3 = ((f32[16,8,128]{2,1,0:T(8,128)}), f32[16,8,128]{2,1,0:T(8,128)S(1)}, u32[]{:S(2)}, u32[]{:S(2)}) async-start(f32[16,8,128]{2,1,0:T(8,128)} %fusion.8), calls=%async_computation.3 | async-start | bytes 131072 | tf_op jit(solution)/shard_map/all_to_all | solution.py:116
  113.6 16.1 %all-to-all-start.1 = ((bf16[16,128,4,1,16]{1,4,2,3,0:T(8,128)(2,1)}), bf16[16,128,4,1,16]{1,4,2,3,0:T(8,128)(2,1)S(1)}, u32[]{:S(2)}, u32[]{:S(2)}) async-start(bf16[16,128,4,1,16]{1,4,2,3,0:T(8,128)(2,1)} %copy.126), calls=%async_computation.1 | async-start | bytes 524288 | tf_op jit(solution)/shard_map/all_to_all | solution.py:102

commit v4 on v3

--- a/solution.py
+++ b/solution.py
@@ -1,10 +1,12 @@
 import jax
 import jax.numpy as jnp
 from jax import lax
+from jax.experimental import pallas as pl
 from jax.sharding import PartitionSpec as P
 
 STRIDE = 16
 CHUNK = 128
+INTERPRET = False
 
 highest = lax.Precision.HIGHEST
 
@@ -25,39 +27,61 @@
     )
 
 
+def conv_kernel(g_ref, d_ref, w_ref, out_ref, total_ref):
+    span, width = g_ref.shape
+    chunks = span // CHUNK
+    row = lax.broadcasted_iota(jnp.int32, (CHUNK, CHUNK), 0)
+    col = lax.broadcasted_iota(jnp.int32, (CHUNK, CHUNK), 1)
+    lower = (row >= col).astype(jnp.float32)
+    steps = lax.broadcasted_iota(jnp.int32, (CHUNK, width), 0).astype(jnp.float32)
+    out_ref[...] = jnp.zeros(out_ref.shape, jnp.float32)
+
+    def mode(r, carry):
+        d = d_ref[pl.ds(r, 1), :]
+        w = w_ref[pl.ds(r, 1), :]
+        grow = jnp.exp(d * steps)
+        shrink = w * jnp.exp(-d * steps)
+        after = w * jnp.exp(-d * (steps + 1.0))
+        tail = jnp.exp(-d * float(CHUNK - 1))
+        hop = jnp.exp(-d * float(CHUNK))
+        state = jnp.zeros((1, width), jnp.float32)
+        for k in range(chunks):
+            rows = slice(k * CHUNK, (k + 1) * CHUNK)
+            y = jnp.dot(
+                lower, grow * g_ref[rows, :], precision=highest,
+                preferred_element_type=jnp.float32,
+            )
+            out_ref[rows, :] += shrink * y + after * state
+            state = hop * state + tail * y[CHUNK - 1 : CHUNK, :]
+        total_ref[pl.ds(r, 1), :] = state
+        return carry
+
+    lax.fori_loop(0, d_ref.shape[0], mode, 0)
+
+
 def modal_conv(gated, residues, decays):
     span, width = gated.shape
-    chunks = span // CHUNK
     groups = lax.axis_size("u")
-    g = gated.astype(jnp.float32).reshape(chunks, CHUNK, width)
-    steps = jnp.arange(CHUNK, dtype=jnp.float32)
     weight = residues * jnp.sqrt(-jnp.expm1(-2.0 * decays))
-    grow = jnp.exp(decays[:, None, :] * steps[None, :, None])
-    shrink = jnp.exp(-decays[:, None, :] * steps[None, :, None])
-    lower = (steps[:, None] >= steps[None, :]).astype(jnp.float32)
-    running = jnp.einsum("ij,rkjc->rkic", lower, grow[:, None] * g[None], precision=highest)
-    ends = jnp.exp(-decays * (CHUNK - 1))[:, None, :] * running[:, :, -1, :]
-    index = jnp.arange(chunks)
-    lag = (index[:, None] - 1 - index[None, :]).astype(jnp.float32)
-    decay_table = jnp.where(
-        (lag >= 0)[None, :, :, None],
-        jnp.exp(-decays[:, None, None, :] * (CHUNK * jnp.maximum(lag, 0.0))[None, :, :, None]),
-        0.0,
-    )
-    inner = jnp.sum(decay_table * ends[:, None, :, :], axis=2)
-    total = jnp.exp(-decays * CHUNK) * inner[:, -1] + ends[:, -1]
+    local, total = pl.pallas_call(
+        conv_kernel,
+        out_shape=(
+            jax.ShapeDtypeStruct((span, width), jnp.float32),
+            jax.ShapeDtypeStruct(decays.shape, jnp.float32),
+        ),
+        interpret=INTERPRET,
+    )(gated.astype(jnp.float32), decays, weight)
     outer = None
     for m in range(1, groups):
         term = from_behind(total, "u", m)
         if m > 1:
             term = jnp.exp(-decays * float(span * (m - 1))) * term
         outer = term if outer is None else outer + term
-    if outer is not None:
-        offsets = (CHUNK * index).astype(jnp.float32)
-        inner = inner + jnp.exp(-decays[:, None, :] * offsets[None, :, None]) * outer[:, None, :]
+    if outer is None:
+        return local
+    steps = jnp.arange(span, dtype=jnp.float32)
     after = jnp.exp(-decays[:, None, :] * (steps[None, :, None] + 1.0))
-    modes = shrink[:, None] * running + after[:, None] * inner[:, :, None, :]
-    return jnp.sum(weight[:, None, None, :] * modes, axis=0).reshape(span, width)
+    return local + jnp.sum((weight * outer)[:, None, :] * after, axis=0)
 
 
 def shards(
@@ -69,17 +93,18 @@
     piece = head_weight.shape[1]
     span = tokens * width_v
     narrow = width_u * piece
-    stacked = jnp.stack([query_input, key_input, value_input], axis=0)
-    stacked = stacked.reshape(1, 3, tokens, width_u, width_v, piece)
-    columns = lax.all_to_all(stacked, "v", split_axis=4, concat_axis=0, tiled=True)
-    columns = columns.reshape(width_v, 3, tokens, narrow)
-    columns = jnp.transpose(columns, (1, 0, 2, 3)).reshape(3, span, narrow)
+    def columns_of(values):
+        parted = values.reshape(1, tokens, width_u, width_v, piece)
+        moved = lax.all_to_all(parted, "v", split_axis=3, concat_axis=0, tiled=True)
+        return moved.reshape(span, narrow)
+
+    columns = [columns_of(x) for x in (key_input, value_input, query_input)]
     weight_rep = jnp.broadcast_to(head_weight[None], (width_u,) + head_weight.shape)
     weight_cols = lax.all_to_all(weight_rep, "u", split_axis=0, concat_axis=0, tiled=True)
     weight_cols = jnp.transpose(weight_cols, (1, 0, 2, 3)).reshape(
         head_weight.shape[0], narrow, head_weight.shape[2]
     )
-    before = from_behind(columns[:, -2:], "u", 1)
+    before = from_behind(tuple(x[-2:] for x in columns), "u", 1)
     sf = short_filter.reshape(3, 3, width_u, width_v, piece)
     sf = jnp.transpose(sf, (0, 1, 3, 2, 4))
     sf = lax.dynamic_index_in_dim(sf, lax.axis_index("v"), axis=2, keepdims=False)
@@ -90,9 +115,9 @@
         shaped = lax.dynamic_index_in_dim(shaped, lax.axis_index("v"), axis=2, keepdims=False)
         return shaped.reshape(values.shape[0], narrow)
 
-    query_short = short_pass(columns[0], before[0], sf[:, 0])
-    key_short = short_pass(columns[1], before[1], sf[:, 1])
-    value_short = short_pass(columns[2], before[2], sf[:, 2])
+    key_short = short_pass(columns[0], before[0], sf[:, 1])
+    value_short = short_pass(columns[1], before[1], sf[:, 2])
+    query_short = short_pass(columns[2], before[2], sf[:, 0])
     gated = (key_short * value_short).astype(jnp.bfloat16)
     convolved = modal_conv(gated, pick(residues), pick(decays))
     gain = pick(skip_gain[None])[0]

time: 131 us -> 154 us (1.18)
  Pallas kernels: 0 us -> 19.5 us
  local copies, waits for them, and re-layouts: 27.7 us -> 11.6 us
  starting transfers between devices: 34.7 us -> 49.3 us
  waiting for transfers between devices: 45.7 us -> 56.3 us
  matrix products: 5.52 us -> 1.29 us
  other arithmetic: 9.19 us -> 6.83 us
    pallas_call x0 -> x1, Pallas kernels: none -> 19.5 us  [modal_conv(): pl.pallas_call(conv_kernel, out_shape=(jax.ShapeDtypeStruct((span, width)...]
    ppermute x5 -> x7, starting transfers between devices: 10.8 us -> 18.6 us  [from_behind(): return lax.ppermute(block, axis, route)]
    all_to_all x1 -> x3, starting transfers between devices: 11 us -> 18.1 us  [columns_of(): moved = lax.all_to_all(parted, 'v', split_axis=3, concat_axis=0, tiled=True)]
    slice x8 -> x3, local copies, waits for them, and re-layouts: 6.41 us -> 0.02 us  [shards(): before = from_behind(tuple((x[-2:] for x in columns)), 'u', 1)]
    all_to_all x1 -> x3, waiting for transfers between devices: 20.5 us -> 26.7 us  [columns_of(): moved = lax.all_to_all(parted, 'v', split_axis=3, concat_axis=0, tiled=True)]
    unnamed x17 -> x33, local copies, waits for them, and re-layouts: 8.32 us -> 2.24 us
    squeeze x2 -> x0, local copies, waits for them, and re-layouts: 5.42 us -> none  [the longest x1 5.42 us: modal_conv(): ends = jnp.exp(-decays * (CHUNK - 1))[:, None, :] * running[:, :, -1, :]]
    all_to_all x1, waiting for transfers between devices: 0.01 us -> 4.91 us  [shards(): lax.all_to_all(weight_rep, 'u', split_axis=0, concat_axis=0, tiled=True)]
  transfers between devices with their start and end apart: 9 -> 13, of which waited for: 7 -> 10; matrix products, arithmetic and copies ran while one was open for 24% -> 7% of each run, Pallas kernels for 0% -> 13%
where the time goes in v4:
time: 154 us; the launch traced here: 153 us
  waiting for transfers between devices  56.3 us (37%)
  starting transfers between devices  49.3 us (32%)
  Pallas kernels  19.5 us (13%)
  local copies, waits for them, and re-layouts  11.6 us (8%)
  other arithmetic  6.83 us (4%)
  blocking collectives  6 us (4%)
  between operations  1.75 us (1%)
    all_to_all x3, waiting for transfers between devices, columns_of(): moved = lax.all_to_all(parted, 'v', split_axis=3, concat_axis=0, tiled=True)  26.7 us
    pallas_call x1, Pallas kernels, modal_conv(): pl.pallas_call(conv_kernel, out_shape=(jax.ShapeDtypeStruct((span, width)...  19.5 us
    ppermute x7, starting transfers between devices, from_behind(): return lax.ppermute(block, axis, route)  18.6 us
    all_to_all x3, starting transfers between devices, columns_of(): moved = lax.all_to_all(parted, 'v', split_axis=3, concat_axis=0, tiled=True)  18.1 us
    ppermute x7, waiting for transfers between devices, from_behind(): return lax.ppermute(block, axis, route)  10.4 us
    all_to_all x1, waiting for transfers between devices, shards(): lax.all_to_all(partial_sum, 'v', split_axis=0, concat_axis=0, tiled=True)  9.54 us
    unnamed x1, blocking collectives  6 us
    all_to_all x1, starting transfers between devices, shards(): lax.all_to_all(weight_rep, 'u', split_axis=0, concat_axis=0, tiled=True)  5.61 us
  transfers between devices with their start and end apart: 13, of which 10 were waited for; matrix products, arithmetic and copies ran while one was open for 7% of the time, Pallas kernels for 13%

profile of v4, /device:TPU:16, one launch (start us, length us, event | category | flops | bytes accessed | tf_op | source)
XLA Modules:
  0.0 152.7 jit_solution(5692619091883790815)
XLA Ops:
  0.6 1.8 %broadcast_in_dim.2 = bf16[4,32,16,128]{3,2,1,0:T(8,128)(2,1)} broadcast(bf16[32,16,128]{2,1,0:T(8,128)(2,1)} %param.15), dimensions={1,2,3} | broadcast | bytes 655360 | tf_op jit(solution)/shard_map/broadcast_in_dim | solution.py:102
  2.5 5.6 %all-to-all-start.4 = ((bf16[4,32,16,128]{3,2,1,0:T(8,128)(2,1)}), bf16[4,32,16,128]{3,2,1,0:T(8,128)(2,1)S(1)}, u32[]{:S(2)}, u32[]{:S(2)}) async-start(bf16[4,32,16,128]{3,2,1,0:T(8,128)(2,1)} %broadcast_in_dim.2), calls=%async_computation.4 | async-start | bytes 1048576 | tf_op jit(solution)/shard_map/all_to_all | solution.py:103
  8.3 0.7 copy.63
  9.0 4.9 %all-to-all-done.4 = bf16[4,32,16,128]{3,2,1,0:T(8,128)(2,1)S(1)} async-done(((bf16[4,32,16,128]{3,2,1,0:T(8,128)(2,1)}), bf16[4,32,16,128]{3,2,1,0:T(8,128)(2,1)S(1)}, u32[]{:S(2)}, u32[]{:S(2)}) %all-to-all-start.4) | async-done | bytes 524320 | tf_op jit(solution)/shard_map/all_to_all | solution.py:103
  13.9 11.0 %all-to-all-start = ((bf16[1,128,4,16,16]{1,4,2,0,3:T(8,128)(2,1)}), bf16[1,128,4,16,16]{1,4,2,0,3:T(8,128)(2,1)S(1)}, u32[]{:S(2)}, u32[]{:S(2)}) async-start(bf16[1,128,4,16,16]{1,4,2,0,3:T(8,128)(2,1)} %copy.63), calls=%async_computation | async-start | bytes 524288 | tf_op jit(solution)/shard_map/all_to_all | solution.py:98
  25.1 0.7 copy.73
  25.9 11.6 %all-to-all-done = bf16[1,128,4,16,16]{1,4,2,0,3:T(8,128)(2,1)S(1)} async-done(((bf16[1,128,4,16,16]{1,4,2,0,3:T(8,128)(2,1)}), bf16[1,128,4,16,16]{1,4,2,0,3:T(8,128)(2,1)S(1)}, u32[]{:S(2)}, u32[]{:S(2)}) %all-to-all-start) | async-done | bytes 262176 | tf_op jit(solution)/shard_map/all_to_all | solution.py:98
  37.5 3.5 %all-to-all-start.2 = ((bf16[1,128,4,16,16]{1,4,2,0,3:T(8,128)(2,1)}), bf16[1,128,4,16,16]{1,4,2,0,3:T(8,128)(2,1)S(1)}, u32[]{:S(2)}, u32[]{:S(2)}) async-start(bf16[1,128,4,16,16]{1,4,2,0,3:T(8,128)(2,1)} %copy.73), calls=%async_computation.2 | async-start | bytes 524288 | tf_op jit(solution)/shard_map/all_to_all | solution.py:98
  41.5 0.7 copy.68
  42.3 0.2 reshape.112
  42.5 0.2 reshape.110
  42.8 10.8 %all-to-all-done.2 = bf16[1,128,4,16,16]{1,4,2,0,3:T(8,128)(2,1)S(1)} async-done(((bf16[1,128,4,16,16]{1,4,2,0,3:T(8,128)(2,1)}), bf16[1,128,4,16,16]{1,4,2,0,3:T(8,128)(2,1)S(1)}, u32[]{:S(2)}, u32[]{:S(2)}) %all-to-all-start.2) | async-done | bytes 262176 | tf_op jit(solution)/shard_map/all_to_all | solution.py:98
  53.5 3.5 %all-to-all-start.1 = ((bf16[1,128,4,16,16]{1,4,2,0,3:T(8,128)(2,1)}), bf16[1,128,4,16,16]{1,4,2,0,3:T(8,128)(2,1)S(1)}, u32[]{:S(2)}, u32[]{:S(2)}) async-start(bf16[1,128,4,16,16]{1,4,2,0,3:T(8,128)(2,1)} %copy.68), calls=%async_computation.1 | async-start | bytes 524288 | tf_op jit(solution)/shard_map/all_to_all | solution.py:98
  57.4 0.6 sqrt_multiply_fusion.w_ref
  58.2 0.2 copy.64
  58.4 0.3 copy.65
  58.7 4.1 %collective-permute-start = (bf16[2,64]{1,0:T(2,128)(2,1)S(1)}, bf16[2,64]{1,0:T(2,128)(2,1)S(1)}, u32[]{:S(2)}, u32[]{:S(2)}) collective-permute-start(bf16[2,64]{1,0:T(2,128)(2,1)S(1)} %slice.130), channel_id=1, source_target_pairs={{0,64},{64,128},{128,192},{1,65},{65,129},{129,193},{2,66},{66,130... | collective-permute-start | bytes 776 | tf_op jit(solution)/shard_map/ppermute | solution.py:17
  62.8 0.2 copy.74
  63.0 0.3 copy.75
  63.3 1.9 %collective-permute-start.2 = (bf16[2,64]{1,0:T(2,128)(2,1)S(1)}, bf16[2,64]{1,0:T(2,128)(2,1)S(1)}, u32[]{:S(2)}, u32[]{:S(2)}) collective-permute-start(bf16[2,64]{1,0:T(2,128)(2,1)S(1)} %slice.144), channel_id=1, source_target_pairs={{0,64},{64,128},{128,192},{1,65},{65,129},{129,193},{2,66},{66,130... | collective-permute-start | bytes 776 | tf_op jit(solution)/shard_map/ppermute | solution.py:17
  65.3 4.4 %all-to-all-done.1 = bf16[1,128,4,16,16]{1,4,2,0,3:T(8,128)(2,1)S(1)} async-done(((bf16[1,128,4,16,16]{1,4,2,0,3:T(8,128)(2,1)}), bf16[1,128,4,16,16]{1,4,2,0,3:T(8,128)(2,1)S(1)}, u32[]{:S(2)}, u32[]{:S(2)}) %all-to-all-start.1) | async-done | bytes 262176 | tf_op jit(solution)/shard_map/all_to_all | solution.py:98
  69.6 0.2 copy.69
  69.9 0.3 copy.70
  70.2 4.1 %collective-permute-start.1 = (bf16[2,64]{1,0:T(2,128)(2,1)S(1)}, bf16[2,64]{1,0:T(2,128)(2,1)S(1)}, u32[]{:S(2)}, u32[]{:S(2)}) collective-permute-start(bf16[2,64]{1,0:T(2,128)(2,1)S(1)} %slice.137), channel_id=1, source_target_pairs={{0,64},{64,128},{128,192},{1,65},{65,129},{129,193},{2,66},{66,130... | collective-permute-start | bytes 776 | tf_op jit(solution)/shard_map/ppermute | solution.py:17
  74.4 1.4 collective-permute-done.1
  75.9 1.6 %fusion.14.g_ref = f32[2048,64]{1,0:T(8,128)} fusion(f32[2050,64]{1,0:T(8,128)S(1)} %maximum_convert_fusion.2, f32[64]{0:T(128)S(1)} %get-tuple-element.17, f32[64]{0:T(128)S(1)} %get-tuple-element.18, f32[64]{0:T(128)S(1)} %get-tuple-element.19, f32[2050,64]{1,0:T(8,128)S(1)} %maximum_convert_fusion.1, f32[64]{0:T(128)S(1)} %get-tuple-element.20, ...), kind=kLoop, calls=%fused_computation.31 | loop fusion | flops 1703936 | bytes 3671552 | tf_op jit(solution)/shard_map/convert_element_type | solution.py:73
  77.6 19.5 %shard_map.95 = (f32[2048,64]{1,0:T(8,128)}, f32[16,64]{1,0:T(8,128)}) custom-call(f32[2048,64]{1,0:T(8,128)} %fusion.14.g_ref, f32[16,64]{1,0:T(8,128)} %copy-done.4, f32[16,64]{1,0:T(8,128)} %sqrt_multiply_fusion.w_ref), custom_call_target="tpu_custom_call" | custom-call | tf_op jit(solution)/shard_map/pallas_call | solution.py:66
  97.1 0.8 collective-permute-start.5
  97.9 4.6 %collective-permute-start.3 = (f32[16,64]{1,0:T(8,128)}, f32[16,64]{1,0:T(8,128)S(1)}, u32[]{:S(2)}, u32[]{:S(2)}) collective-permute-start(f32[16,64]{1,0:T(8,128)} %get-tuple-element.5), channel_id=1, source_target_pairs={{0,64},{64,128},{128,192},{1,65},{65,129},{129,193},{2,66},{66,130... | collective-permute-start | bytes 12296 | tf_op jit(solution)/shard_map/ppermute | solution.py:17
  102.5 1.3 collective-permute-start.4
  104.0 5.7 %collective-permute-done.4 = f32[16,64]{1,0:T(8,128)S(1)} collective-permute-done((f32[16,64]{1,0:T(8,128)}, f32[16,64]{1,0:T(8,128)S(1)}, u32[]{:S(2)}, u32[]{:S(2)}) %collective-permute-start.4) | collective-permute-done | bytes 4128 | tf_op jit(solution)/shard_map/ppermute | solution.py:17
  109.7 2.0 %multiply_reduce_fusion = f32[2048,64]{0,1:T(8,128)S(1)} fusion(f32[2048]{0:T(1024)S(1)} %iota_add_fusion, f32[16,64]{1,0:T(8,128)S(1)} %get-tuple-element.15, f32[16,64]{1,0:T(8,128)S(1)} %get-tuple-element.14), kind=kLoop, calls=%fused_computation | loop fusion | flops 6160384 | bytes 540672 | tf_op jit(solution)/shard_map/reduce_sum | solution.py:84
  111.7 1.3 copy.79
  113.0 2.0 %fusion.10 = bf16[2048,64]{1,0:T(8,128)(2,1)S(1)} fusion(f32[2050,64]{1,0:T(8,128)S(1)} %maximum_convert_fusion, f32[2048,64]{1,0:T(8,128)S(1)} %copy-done, f32[2048,64]{1,0:T(8,128)} %get-tuple-element.4, f32[2048,64]{1,0:T(8,128)} %copy.79, f32[64]{0:T(128)S(1)} %mul.200, f32[64]{0:T(128)S(1)} %get-tuple-element.23, f32[64]{0:T(128)S(1)} %get-tuple-element.24, ...), kind=kLoop, calls=%fused_computation.20 | loop fusion | flops 1572864 | bytes 3408896 | tf_op jit(solution)/shard_map/convert_element_type | solution.py:125
  115.1 1.9 %collective-permute-start.6 = (bf16[16,64]{1,0:T(8,128)(2,1)S(1)}, bf16[16,64]{1,0:T(8,128)(2,1)S(1)}, u32[]{:S(2)}, u32[]{:S(2)}) collective-permute-start(bf16[16,64]{1,0:T(8,128)(2,1)S(1)} %slice.151), channel_id=1, source_target_pairs={{64,0},{128,64},{192,128},{65,1},{129,65},{193,129},{66,2},{130,66... | collective-permute-start | bytes 6152 | tf_op jit(solution)/shard_map/ppermute | solution.py:17
  117.0 0.3 convolution_bitcast_fusion.1
  117.3 3.2 %collective-permute-done.6 = bf16[16,64]{1,0:T(8,128)(2,1)S(1)} collective-permute-done((bf16[16,64]{1,0:T(8,128)(2,1)S(1)}, bf16[16,64]{1,0:T(8,128)(2,1)S(1)}, u32[]{:S(2)}, u32[]{:S(2)}) %collective-permute-start.6) | collective-permute-done | bytes 2080 | tf_op jit(solution)/shard_map/ppermute | solution.py:17
  120.7 1.0 fusion.1
  121.6 3.5 %all-to-all-start.5 = ((f32[16,8,128]{2,1,0:T(8,128)}), f32[16,8,128]{2,1,0:T(8,128)S(1)}, u32[]{:S(2)}, u32[]{:S(2)}) async-start(f32[16,8,128]{2,1,0:T(8,128)} %fusion.1), calls=%async_computation.5 | async-start | bytes 131072 | tf_op jit(solution)/shard_map/all_to_all | solution.py:141
  125.2 0.2 copy.80
  125.4 0.8 copy.81
  126.2 9.5 %all-to-all-done.5 = f32[16,8,128]{2,1,0:T(8,128)S(1)} async-done(((f32[16,8,128]{2,1,0:T(8,128)}), f32[16,8,128]{2,1,0:T(8,128)S(1)}, u32[]{:S(2)}, u32[]{:S(2)}) %all-to-all-start.5) | async-done | bytes 65568 | tf_op jit(solution)/shard_map/all_to_all | solution.py:141
  135.7 3.5 %all-to-all-start.3 = ((bf16[16,128,4,1,16]{1,4,2,3,0:T(8,128)(2,1)}), bf16[16,128,4,1,16]{1,4,2,3,0:T(8,128)(2,1)S(1)}, u32[]{:S(2)}, u32[]{:S(2)}) async-start(bf16[16,128,4,1,16]{1,4,2,3,0:T(8,128)(2,1)} %copy.81), calls=%async_computation.3 | async-start | bytes 524288 | tf_op jit(solution)/shard_map/all_to_all | solution.py:127
  139.3 0.6 dynamic-slice.4
  140.5 6.0 %all-reduce = bf16[8,128]{1,0:T(8,128)(2,1)S(1)} all-reduce(f32[8,128]{1,0:T(8,128)S(1)} %reduce_sum.19), channel_id=2, replica_groups=mesh['u'=4,'v'=16,'tp'=4] {'tp'}, use_global_device_ids=true, to_apply=%region_2.3.clone | all-reduce | flops 1024 | bytes 6144
  146.5 0.5 dynamic-slice_convert_fusion
  147.0 4.7 %all-to-all-done.3 = bf16[16,128,4,1,16]{1,4,2,3,0:T(8,128)(2,1)S(1)} async-done(((bf16[16,128,4,1,16]{1,4,2,3,0:T(8,128)(2,1)}), bf16[16,128,4,1,16]{1,4,2,3,0:T(8,128)(2,1)S(1)}, u32[]{:S(2)}, u32[]{:S(2)}) %all-to-all-start.3) | async-done | bytes 262176 | tf_op jit(solution)/shard_map/all_to_all | solution.py:127
  151.8 0.9 copy.87
  (60 shorter events, 2.3 us)
Async XLA Ops:
  0.6 7.4 %copy-start.1 = (bf16[128,1024]{1,0:T(8,128)(2,1)S(1)}, bf16[128,1024]{1,0:T(8,128)(2,1)}, u32[]{:S(2)}) copy-start(bf16[128,1024]{1,0:T(8,128)(2,1)} %param.8) | copy-start | bytes 786436
  2.5 22.5 %copy-start.2 = (bf16[128,1024]{1,0:T(8,128)(2,1)S(1)}, bf16[128,1024]{1,0:T(8,128)(2,1)}, u32[]{:S(2)}) copy-start(bf16[128,1024]{1,0:T(8,128)(2,1)} %param.10) | copy-start | bytes 786436
  2.5 11.4 %all-to-all-start.4 = ((bf16[4,32,16,128]{3,2,1,0:T(8,128)(2,1)}), bf16[4,32,16,128]{3,2,1,0:T(8,128)(2,1)S(1)}, u32[]{:S(2)}, u32[]{:S(2)}) async-start(bf16[4,32,16,128]{3,2,1,0:T(8,128)(2,1)} %broadcast_in_dim.2), calls=%async_computation.4 | async-start | bytes 1048576 | tf_op jit(solution)/shard_map/all_to_all | solution.py:103
  9.0 32.0 %copy-start.9 = (f32[3,3,1024]{2,1,0:T(4,128)S(1)}, f32[3,3,1024]{2,1,0:T(4,128)}, u32[]{:S(2)}) copy-start(f32[3,3,1024]{2,1,0:T(4,128)} %param.11) | copy-start | bytes 110596
  13.9 23.6 %all-to-all-start = ((bf16[1,128,4,16,16]{1,4,2,0,3:T(8,128)(2,1)}), bf16[1,128,4,16,16]{1,4,2,0,3:T(8,128)(2,1)S(1)}, u32[]{:S(2)}, u32[]{:S(2)}) async-start(bf16[1,128,4,16,16]{1,4,2,0,3:T(8,128)(2,1)} %copy.63), calls=%async_computation | async-start | bytes 524288 | tf_op jit(solution)/shard_map/all_to_all | solution.py:98
  24.9 16.4 %copy-start.3 = (bf16[128,1024]{1,0:T(8,128)(2,1)S(1)}, bf16[128,1024]{1,0:T(8,128)(2,1)}, u32[]{:S(2)}) copy-start(bf16[128,1024]{1,0:T(8,128)(2,1)} %param.9) | copy-start | bytes 786436
  25.9 16.4 %copy-start.7 = (f32[16,1024]{1,0:T(8,128)S(1)}, f32[16,1024]{1,0:T(8,128)}, u32[]{:S(2)}) copy-start(f32[16,1024]{1,0:T(8,128)} %param.12) | copy-start | bytes 196612
  37.5 16.1 %all-to-all-start.2 = ((bf16[1,128,4,16,16]{1,4,2,0,3:T(8,128)(2,1)}), bf16[1,128,4,16,16]{1,4,2,0,3:T(8,128)(2,1)S(1)}, u32[]{:S(2)}, u32[]{:S(2)}) async-start(bf16[1,128,4,16,16]{1,4,2,0,3:T(8,128)(2,1)} %copy.73), calls=%async_computation.2 | async-start | bytes 524288 | tf_op jit(solution)/shard_map/all_to_all | solution.py:98
  41.0 1.5 copy-start.8
  42.3 15.0 %copy-start.10 = (f32[1024]{0:T(1024)S(1)}, f32[1024]{0:T(1024)}, u32[]{:S(2)}) copy-start(f32[1024]{0:T(1024)} %param.14) | copy-start | bytes 12292
  53.5 16.1 %all-to-all-start.1 = ((bf16[1,128,4,16,16]{1,4,2,0,3:T(8,128)(2,1)}), bf16[1,128,4,16,16]{1,4,2,0,3:T(8,128)(2,1)S(1)}, u32[]{:S(2)}, u32[]{:S(2)}) async-start(bf16[1,128,4,16,16]{1,4,2,0,3:T(8,128)(2,1)} %copy.68), calls=%async_computation.1 | async-start | bytes 524288 | tf_op jit(solution)/shard_map/all_to_all | solution.py:98
  57.2 1.0 copy-start.4
  58.7 45.0 %collective-permute-start = (bf16[2,64]{1,0:T(2,128)(2,1)S(1)}, bf16[2,64]{1,0:T(2,128)(2,1)S(1)}, u32[]{:S(2)}, u32[]{:S(2)}) collective-permute-start(bf16[2,64]{1,0:T(2,128)(2,1)S(1)} %slice.130), channel_id=1, source_target_pairs={{0,64},{64,128},{128,192},{1,65},{65,129},{129,193},{2,66},{66,130... | collective-permute-start | bytes 776 | tf_op jit(solution)/shard_map/ppermute | solution.py:17
  63.3 10.9 %collective-permute-start.2 = (bf16[2,64]{1,0:T(2,128)(2,1)S(1)}, bf16[2,64]{1,0:T(2,128)(2,1)S(1)}, u32[]{:S(2)}, u32[]{:S(2)}) collective-permute-start(bf16[2,64]{1,0:T(2,128)(2,1)S(1)} %slice.144), channel_id=1, source_target_pairs={{0,64},{64,128},{128,192},{1,65},{65,129},{129,193},{2,66},{66,130... | collective-permute-start | bytes 776 | tf_op jit(solution)/shard_map/ppermute | solution.py:17
  70.2 5.6 %collective-permute-start.1 = (bf16[2,64]{1,0:T(2,128)(2,1)S(1)}, bf16[2,64]{1,0:T(2,128)(2,1)S(1)}, u32[]{:S(2)}, u32[]{:S(2)}) collective-permute-start(bf16[2,64]{1,0:T(2,128)(2,1)S(1)} %slice.137), channel_id=1, source_target_pairs={{0,64},{64,128},{128,192},{1,65},{65,129},{129,193},{2,66},{66,130... | collective-permute-start | bytes 776 | tf_op jit(solution)/shard_map/ppermute | solution.py:17
  97.1 12.6 %copy-start.5 = (f32[16,64]{1,0:T(8,128)S(1)}, f32[16,64]{1,0:T(8,128)}, u32[]{:S(2)}) copy-start(f32[16,64]{1,0:T(8,128)} %copy-done.4) | copy-start | bytes 12292
  97.1 12.6 %copy-start.6 = (f32[16,64]{1,0:T(8,128)S(1)}, f32[16,64]{1,0:T(8,128)}, u32[]{:S(2)}) copy-start(f32[16,64]{1,0:T(8,128)} %sqrt_multiply_fusion.w_ref) | copy-start | bytes 12292
  97.1 6.8 %collective-permute-start.5 = (f32[16,64]{1,0:T(8,128)}, f32[16,64]{1,0:T(8,128)S(1)}, u32[]{:S(2)}, u32[]{:S(2)}) collective-permute-start(f32[16,64]{1,0:T(8,128)} %get-tuple-element.5), channel_id=1, source_target_pairs={{0,192},{1,193},{2,194},{3,195},{4,196},{5,197},{6,198},{7,199},{8... | collective-permute-start | bytes 12296 | tf_op jit(solution)/shard_map/ppermute | solution.py:17
  97.9 6.1 %collective-permute-start.3 = (f32[16,64]{1,0:T(8,128)}, f32[16,64]{1,0:T(8,128)S(1)}, u32[]{:S(2)}, u32[]{:S(2)}) collective-permute-start(f32[16,64]{1,0:T(8,128)} %get-tuple-element.5), channel_id=1, source_target_pairs={{0,64},{64,128},{128,192},{1,65},{65,129},{129,193},{2,66},{66,130... | collective-permute-start | bytes 12296 | tf_op jit(solution)/shard_map/ppermute | solution.py:17
  102.5 7.3 %collective-permute-start.4 = (f32[16,64]{1,0:T(8,128)}, f32[16,64]{1,0:T(8,128)S(1)}, u32[]{:S(2)}, u32[]{:S(2)}) collective-permute-start(f32[16,64]{1,0:T(8,128)} %get-tuple-element.5), channel_id=1, source_target_pairs={{0,128},{64,192},{1,129},{65,193},{2,130},{66,194},{3,131},{67,195... | collective-permute-start | bytes 12296 | tf_op jit(solution)/shard_map/ppermute | solution.py:17
  111.7 1.3 copy-start
  115.1 5.5 %collective-permute-start.6 = (bf16[16,64]{1,0:T(8,128)(2,1)S(1)}, bf16[16,64]{1,0:T(8,128)(2,1)S(1)}, u32[]{:S(2)}, u32[]{:S(2)}) collective-permute-start(bf16[16,64]{1,0:T(8,128)(2,1)S(1)} %slice.151), channel_id=1, source_target_pairs={{64,0},{128,64},{192,128},{65,1},{129,65},{193,129},{66,2},{130,66... | collective-permute-start | bytes 6152 | tf_op jit(solution)/shard_map/ppermute | solution.py:17
  121.6 14.1 %all-to-all-start.5 = ((f32[16,8,128]{2,1,0:T(8,128)}), f32[16,8,128]{2,1,0:T(8,128)S(1)}, u32[]{:S(2)}, u32[]{:S(2)}) async-start(f32[16,8,128]{2,1,0:T(8,128)} %fusion.1), calls=%async_computation.5 | async-start | bytes 131072 | tf_op jit(solution)/shard_map/all_to_all | solution.py:141
  125.1 14.1 %copy-start.11 = (u32[256]{0:T(256)S(1)}, u32[256]{0:T(256)}, u32[]{:S(2)}) copy-start(u32[256]{0:T(256)} %constant.35) | copy-start | bytes 3076
  135.7 16.1 %all-to-all-start.3 = ((bf16[16,128,4,1,16]{1,4,2,3,0:T(8,128)(2,1)}), bf16[16,128,4,1,16]{1,4,2,3,0:T(8,128)(2,1)S(1)}, u32[]{:S(2)}, u32[]{:S(2)}) async-start(bf16[16,128,4,1,16]{1,4,2,3,0:T(8,128)(2,1)} %copy.81), calls=%async_computation.3 | async-start | bytes 524288 | tf_op jit(solution)/shard_map/all_to_all | solution.py:127

commit v5 on v4

--- a/solution.py
+++ b/solution.py
@@ -32,7 +32,7 @@
     chunks = span // CHUNK
     row = lax.broadcasted_iota(jnp.int32, (CHUNK, CHUNK), 0)
     col = lax.broadcasted_iota(jnp.int32, (CHUNK, CHUNK), 1)
-    lower = (row >= col).astype(jnp.float32)
+    lower = (row >= col).astype(jnp.bfloat16)
     steps = lax.broadcasted_iota(jnp.int32, (CHUNK, width), 0).astype(jnp.float32)
     out_ref[...] = jnp.zeros(out_ref.shape, jnp.float32)
 
@@ -47,9 +47,11 @@
         state = jnp.zeros((1, width), jnp.float32)
         for k in range(chunks):
             rows = slice(k * CHUNK, (k + 1) * CHUNK)
-            y = jnp.dot(
-                lower, grow * g_ref[rows, :], precision=highest,
-                preferred_element_type=jnp.float32,
+            scaled = grow * g_ref[rows, :]
+            high = scaled.astype(jnp.bfloat16)
+            low = (scaled - high.astype(jnp.float32)).astype(jnp.bfloat16)
+            y = jnp.dot(lower, high, preferred_element_type=jnp.float32) + jnp.dot(
+                lower, low, preferred_element_type=jnp.float32
             )
             out_ref[rows, :] += shrink * y + after * state
             state = hop * state + tail * y[CHUNK - 1 : CHUNK, :]
@@ -61,16 +63,24 @@
 
 def modal_conv(gated, residues, decays):
     span, width = gated.shape
+    half = span // 2
     groups = lax.axis_size("u")
     weight = residues * jnp.sqrt(-jnp.expm1(-2.0 * decays))
-    local, total = pl.pallas_call(
+    g = gated.astype(jnp.float32)
+    packed = jnp.concatenate([g[:half], g[half:]], axis=1)
+    decays2 = jnp.concatenate([decays, decays], axis=1)
+    weight2 = jnp.concatenate([weight, weight], axis=1)
+    local, ends = pl.pallas_call(
         conv_kernel,
         out_shape=(
-            jax.ShapeDtypeStruct((span, width), jnp.float32),
-            jax.ShapeDtypeStruct(decays.shape, jnp.float32),
+            jax.ShapeDtypeStruct((half, 2 * width), jnp.float32),
+            jax.ShapeDtypeStruct(decays2.shape, jnp.float32),
         ),
         interpret=INTERPRET,
-    )(gated.astype(jnp.float32), decays, weight)
+    )(packed, decays2, weight2)
+    hop_half = jnp.exp(-decays * float(half))
+    first_end, second_end = ends[:, :width], ends[:, width:]
+    total = hop_half * first_end + second_end
     outer = None
     for m in range(1, groups):
         term = from_behind(total, "u", m)
@@ -78,10 +88,13 @@
             term = jnp.exp(-decays * float(span * (m - 1))) * term
         outer = term if outer is None else outer + term
     if outer is None:
-        return local
-    steps = jnp.arange(span, dtype=jnp.float32)
-    after = jnp.exp(-decays[:, None, :] * (steps[None, :, None] + 1.0))
-    return local + jnp.sum((weight * outer)[:, None, :] * after, axis=0)
+        entry = jnp.concatenate([jnp.zeros_like(first_end), first_end], axis=1)
+    else:
+        entry = jnp.concatenate([outer, hop_half * outer + first_end], axis=1)
+    steps = jnp.arange(half, dtype=jnp.float32)
+    after = jnp.exp(-decays2[:, None, :] * (steps[None, :, None] + 1.0))
+    joined = local + jnp.sum((weight2 * entry)[:, None, :] * after, axis=0)
+    return jnp.concatenate([joined[:, :width], joined[:, width:]], axis=0)
 
 
 def shards(
@@ -93,18 +106,17 @@
     piece = head_weight.shape[1]
     span = tokens * width_v
     narrow = width_u * piece
-    def columns_of(values):
-        parted = values.reshape(1, tokens, width_u, width_v, piece)
-        moved = lax.all_to_all(parted, "v", split_axis=3, concat_axis=0, tiled=True)
-        return moved.reshape(span, narrow)
-
-    columns = [columns_of(x) for x in (key_input, value_input, query_input)]
+    stacked = jnp.stack([key_input, value_input, query_input], axis=0)
+    stacked = stacked.reshape(1, 3, tokens, width_u, width_v, piece)
+    columns = lax.all_to_all(stacked, "v", split_axis=4, concat_axis=0, tiled=True)
+    columns = columns.reshape(width_v, 3, tokens, narrow)
+    columns = jnp.transpose(columns, (1, 0, 2, 3)).reshape(3, span, narrow)
     weight_rep = jnp.broadcast_to(head_weight[None], (width_u,) + head_weight.shape)
     weight_cols = lax.all_to_all(weight_rep, "u", split_axis=0, concat_axis=0, tiled=True)
     weight_cols = jnp.transpose(weight_cols, (1, 0, 2, 3)).reshape(
         head_weight.shape[0], narrow, head_weight.shape[2]
     )
-    before = from_behind(tuple(x[-2:] for x in columns), "u", 1)
+    before = from_behind(columns[:, -2:], "u", 1)
     sf = short_filter.reshape(3, 3, width_u, width_v, piece)
     sf = jnp.transpose(sf, (0, 1, 3, 2, 4))
     sf = lax.dynamic_index_in_dim(sf, lax.axis_index("v"), axis=2, keepdims=False)

time: 154 us -> 116 us (0.75)
  starting transfers between devices: 49.3 us -> 35 us
  Pallas kernels: 19.5 us -> 7.02 us
  waiting for transfers between devices: 56.3 us -> 47.8 us
  local copies, waits for them, and re-layouts: 11.6 us -> 9.42 us
    pallas_call x1, Pallas kernels: 19.5 us -> 7.02 us  [modal_conv(): pl.pallas_call(conv_kernel, out_shape=(jax.ShapeDtypeStruct((half, 2 * wi...]
    ppermute x7 -> x5, starting transfers between devices: 18.6 us -> 11.4 us  [from_behind(): return lax.ppermute(block, axis, route)]
    all_to_all x3 -> x1, starting transfers between devices: 18.1 us -> 11 us  [shards(): lax.all_to_all(stacked, 'v', split_axis=4, concat_axis=0, tiled=True)]
    all_to_all x3 -> x1, waiting for transfers between devices: 26.7 us -> 20.1 us  [shards(): lax.all_to_all(stacked, 'v', split_axis=4, concat_axis=0, tiled=True)]
    reshape x6 -> x1, local copies, waits for them, and re-layouts: 3.02 us -> 0.2 us  [shards(): columns = jnp.transpose(columns, (1, 0, 2, 3)).reshape(3, span, narrow)]
    concatenate x0 -> x2, other arithmetic: none -> 1.68 us  [the longest x1 1.01 us: modal_conv(): packed = jnp.concatenate([g[:half], g[half:]], axis=1)]
    ppermute x7 -> x5, waiting for transfers between devices: 10.4 us -> 9.36 us  [from_behind(): return lax.ppermute(block, axis, route)]
  transfers between devices with their start and end apart: 13 -> 9, of which waited for: 10 -> 7; matrix products, arithmetic and copies ran while one was open for 7% -> 7% of each run, Pallas kernels for 13% -> 0%
where the time goes in v5:
time: 116 us; the launch traced here: 115 us
  waiting for transfers between devices  47.8 us (41%)
  starting transfers between devices  35 us (30%)
  local copies, waits for them, and re-layouts  9.42 us (8%)
  Pallas kernels  7.02 us (6%)
  other arithmetic  6.63 us (6%)
  blocking collectives  6 us (5%)
  between operations  1.68 us (1%)
  matrix products  1.3 us (1%)
    all_to_all x1, waiting for transfers between devices, shards(): lax.all_to_all(stacked, 'v', split_axis=4, concat_axis=0, tiled=True)  20.1 us
    ppermute x5, starting transfers between devices, from_behind(): return lax.ppermute(block, axis, route)  11.4 us
    all_to_all x1, starting transfers between devices, shards(): lax.all_to_all(stacked, 'v', split_axis=4, concat_axis=0, tiled=True)  11 us
    all_to_all x1, waiting for transfers between devices, shards(): lax.all_to_all(partial_sum, 'v', split_axis=0, concat_axis=0, tiled=True)  9.53 us
    ppermute x5, waiting for transfers between devices, from_behind(): return lax.ppermute(block, axis, route)  9.36 us
    pallas_call x1, Pallas kernels, modal_conv(): pl.pallas_call(conv_kernel, out_shape=(jax.ShapeDtypeStruct((half, 2 * wi...  7.02 us
    unnamed x1, blocking collectives  6 us
    all_to_all x1, starting transfers between devices, shards(): lax.all_to_all(weight_rep, 'u', split_axis=0, concat_axis=0, tiled=True)  5.61 us
  transfers between devices with their start and end apart: 9, of which 7 were waited for; matrix products, arithmetic and copies ran while one was open for 7% of the time, Pallas kernels for 0%

profile of v5, /device:TPU:16, one launch (start us, length us, event | category | flops | bytes accessed | tf_op | source)
XLA Modules:
  0.0 114.9 jit_solution(16469986974646363785)
XLA Ops:
  0.7 1.8 %broadcast_in_dim.2 = bf16[4,32,16,128]{3,2,1,0:T(8,128)(2,1)} broadcast(bf16[32,16,128]{2,1,0:T(8,128)(2,1)} %param.15), dimensions={1,2,3} | broadcast | bytes 655360 | tf_op jit(solution)/shard_map/broadcast_in_dim | solution.py:114
  2.5 5.6 %all-to-all-start.2 = ((bf16[4,32,16,128]{3,2,1,0:T(8,128)(2,1)}), bf16[4,32,16,128]{3,2,1,0:T(8,128)(2,1)S(1)}, u32[]{:S(2)}, u32[]{:S(2)}) async-start(bf16[4,32,16,128]{3,2,1,0:T(8,128)(2,1)} %broadcast_in_dim.2), calls=%async_computation.2 | async-start | bytes 1048576 | tf_op jit(solution)/shard_map/all_to_all | solution.py:115
  8.1 0.2 copy.69
  8.3 0.2 copy.70
  8.5 0.2 copy.71
  8.7 1.1 copy.72
  9.9 4.1 %all-to-all-done.2 = bf16[4,32,16,128]{3,2,1,0:T(8,128)(2,1)S(1)} async-done(((bf16[4,32,16,128]{3,2,1,0:T(8,128)(2,1)}), bf16[4,32,16,128]{3,2,1,0:T(8,128)(2,1)S(1)}, u32[]{:S(2)}, u32[]{:S(2)}) %all-to-all-start.2) | async-done | bytes 524320 | tf_op jit(solution)/shard_map/all_to_all | solution.py:115
  13.9 11.0 %all-to-all-start = ((bf16[1,3,128,4,16,16]{2,5,3,1,0,4:T(8,128)(2,1)}), bf16[1,3,128,4,16,16]{2,5,3,1,0,4:T(8,128)(2,1)S(1)}, u32[]{:S(2)}, u32[]{:S(2)}) async-start(bf16[1,3,128,4,16,16]{2,5,3,1,0,4:T(8,128)(2,1)} %copy.72), calls=%async_computation | async-start | bytes 1572864 | tf_op jit(solution)/shard_map/all_to_all | solution.py:111
  25.0 0.1 reshape.141
  25.3 0.2 reshape.145
  25.5 0.2 reshape.147
  26.2 0.7 pad_maximum_fusion.4.w_ref
  26.9 0.7 fusion.16
  27.6 20.1 %all-to-all-done = bf16[1,3,128,4,16,16]{2,5,3,1,0,4:T(8,128)(2,1)S(1)} async-done(((bf16[1,3,128,4,16,16]{2,5,3,1,0,4:T(8,128)(2,1)}), bf16[1,3,128,4,16,16]{2,5,3,1,0,4:T(8,128)(2,1)S(1)}, u32[]{:S(2)}, u32[]{:S(2)}) %all-to-all-start) | async-done | bytes 786464 | tf_op jit(solution)/shard_map/all_to_all | solution.py:111
  47.8 0.2 copy.99
  48.1 3.7 %collective-permute-start = (bf16[3,2,64]{1,2,0:T(8,128)(2,1)S(1)}, bf16[3,2,64]{1,2,0:T(8,128)(2,1)S(1)}, u32[]{:S(2)}, u32[]{:S(2)}) collective-permute-start(bf16[3,2,64]{1,2,0:T(8,128)(2,1)S(1)} %slice.173), channel_id=1, source_target_pairs={{0,64},{64,128},{128,192},{1,65},{65,129},{129,193},{2,66},{66,130... | collective-permute-start | bytes 2312 | tf_op jit(solution)/shard_map/ppermute | solution.py:17
  51.9 0.3 copy.77
  52.2 0.3 copy.79
  52.5 0.3 copy.75
  52.8 1.3 %collective-permute-done = bf16[3,2,64]{1,2,0:T(8,128)(2,1)S(1)} collective-permute-done((bf16[3,2,64]{1,2,0:T(8,128)(2,1)S(1)}, bf16[3,2,64]{1,2,0:T(8,128)(2,1)S(1)}, u32[]{:S(2)}, u32[]{:S(2)}) %collective-permute-start) | collective-permute-done | bytes 800 | tf_op jit(solution)/shard_map/ppermute | solution.py:17
  54.2 0.3 maximum_convert_fusion.1
  54.5 0.6 fusion.15
  55.3 1.0 pad_maximum_fusion.2.g_ref
  56.3 7.0 %shard_map.95 = (f32[1024,128]{1,0:T(8,128)}, f32[16,128]{1,0:T(8,128)}) custom-call(f32[1024,128]{1,0:T(8,128)} %pad_maximum_fusion.2.g_ref, f32[16,128]{1,0:T(8,128)} %get-tuple-element.29.d_ref, f32[16,128]{1,0:T(8,128)} %pad_maximum_fusion.4.w_ref), custom_call_target="tpu_custom_call" | custom-call | tf_op jit(solution)/shard_map/pallas_call | solution.py:73
  63.3 0.9 slice_add_fusion
  64.2 3.7 %collective-permute-start.1 = (f32[16,64]{1,0:T(8,128)S(1)}, f32[16,64]{1,0:T(8,128)S(1)}, u32[]{:S(2)}, u32[]{:S(2)}) collective-permute-start(f32[16,64]{1,0:T(8,128)S(1)} %slice_add_fusion), channel_id=1, source_target_pairs={{0,64},{64,128},{128,192},{1,65},{65,129},{129,193},{2,66},{66,130... | collective-permute-start | bytes 12296 | tf_op jit(solution)/shard_map/ppermute | solution.py:17
  67.9 1.3 %collective-permute-start.2 = (f32[16,64]{1,0:T(8,128)S(1)}, f32[16,64]{1,0:T(8,128)S(1)}, u32[]{:S(2)}, u32[]{:S(2)}) collective-permute-start(f32[16,64]{1,0:T(8,128)S(1)} %slice_add_fusion), channel_id=1, source_target_pairs={{0,128},{64,192},{1,129},{65,193},{2,130},{66,194},{3,131},{67,195... | collective-permute-start | bytes 12296 | tf_op jit(solution)/shard_map/ppermute | solution.py:17
  69.2 0.7 collective-permute-start.3
  70.0 0.1 maximum_convert_fusion
  70.1 4.8 %collective-permute-done.2 = f32[16,64]{1,0:T(8,128)S(1)} collective-permute-done((f32[16,64]{1,0:T(8,128)S(1)}, f32[16,64]{1,0:T(8,128)S(1)}, u32[]{:S(2)}, u32[]{:S(2)}) %collective-permute-start.2) | collective-permute-done | bytes 4128 | tf_op jit(solution)/shard_map/ppermute | solution.py:17
  75.1 1.4 %multiply_reduce_fusion = f32[1024,128]{1,0:T(8,128)S(1)} fusion(f32[1024]{0:T(1024)S(1)} %iota_add_fusion, f32[16,128]{1,0:T(8,128)S(1)} %get-tuple-element.28, f32[16,128]{1,0:T(8,128)S(1)} %maximum_multiply_fusion), kind=kLoop, calls=%fused_computation | loop fusion | flops 6160384 | bytes 544768 | tf_op jit(solution)/shard_map/reduce_sum | solution.py:96
  76.6 0.2 fusion.20
  76.8 0.5 fusion.10
  77.3 1.9 %collective-permute-start.4 = (bf16[16,64]{1,0:T(8,128)(2,1)S(1)}, bf16[16,64]{1,0:T(8,128)(2,1)S(1)}, u32[]{:S(2)}, u32[]{:S(2)}) collective-permute-start(bf16[16,64]{1,0:T(8,128)(2,1)S(1)} %slice.202), channel_id=1, source_target_pairs={{64,0},{128,64},{192,128},{65,1},{129,65},{193,129},{66,2},{130,66... | collective-permute-start | bytes 6152 | tf_op jit(solution)/shard_map/ppermute | solution.py:17
  79.2 0.3 convolution_bitcast_fusion.1
  79.6 3.2 %collective-permute-done.4 = bf16[16,64]{1,0:T(8,128)(2,1)S(1)} collective-permute-done((bf16[16,64]{1,0:T(8,128)(2,1)S(1)}, bf16[16,64]{1,0:T(8,128)(2,1)S(1)}, u32[]{:S(2)}, u32[]{:S(2)}) %collective-permute-start.4) | collective-permute-done | bytes 2080 | tf_op jit(solution)/shard_map/ppermute | solution.py:17
  82.8 0.1 pad_maximum_fusion.1
  82.9 1.0 fusion.1
  83.9 3.5 %all-to-all-start.3 = ((f32[16,8,128]{2,1,0:T(8,128)}), f32[16,8,128]{2,1,0:T(8,128)S(1)}, u32[]{:S(2)}, u32[]{:S(2)}) async-start(f32[16,8,128]{2,1,0:T(8,128)} %fusion.1), calls=%async_computation.3 | async-start | bytes 131072 | tf_op jit(solution)/shard_map/all_to_all | solution.py:153
  87.4 0.2 copy.82
  87.6 0.8 copy.83
  88.4 9.5 %all-to-all-done.3 = f32[16,8,128]{2,1,0:T(8,128)S(1)} async-done(((f32[16,8,128]{2,1,0:T(8,128)}), f32[16,8,128]{2,1,0:T(8,128)S(1)}, u32[]{:S(2)}, u32[]{:S(2)}) %all-to-all-start.3) | async-done | bytes 65568 | tf_op jit(solution)/shard_map/all_to_all | solution.py:153
  97.9 3.5 %all-to-all-start.1 = ((bf16[16,128,4,1,16]{1,4,2,3,0:T(8,128)(2,1)}), bf16[16,128,4,1,16]{1,4,2,3,0:T(8,128)(2,1)S(1)}, u32[]{:S(2)}, u32[]{:S(2)}) async-start(bf16[16,128,4,1,16]{1,4,2,3,0:T(8,128)(2,1)} %copy.83), calls=%async_computation.1 | async-start | bytes 524288 | tf_op jit(solution)/shard_map/all_to_all | solution.py:139
  101.5 0.6 dynamic-slice.4
  102.8 6.0 %all-reduce = bf16[8,128]{1,0:T(8,128)(2,1)S(1)} all-reduce(f32[8,128]{1,0:T(8,128)S(1)} %reduce_sum.19), channel_id=2, replica_groups=mesh['u'=4,'v'=16,'tp'=4] {'tp'}, use_global_device_ids=true, to_apply=%region_2.3.clone | all-reduce | flops 1024 | bytes 6144
  108.8 0.5 dynamic-slice_convert_fusion
  109.3 4.7 %all-to-all-done.1 = bf16[16,128,4,1,16]{1,4,2,3,0:T(8,128)(2,1)S(1)} async-done(((bf16[16,128,4,1,16]{1,4,2,3,0:T(8,128)(2,1)}), bf16[16,128,4,1,16]{1,4,2,3,0:T(8,128)(2,1)S(1)}, u32[]{:S(2)}, u32[]{:S(2)}) %all-to-all-start.1) | async-done | bytes 262176 | tf_op jit(solution)/shard_map/all_to_all | solution.py:139
  114.0 0.9 copy.89
  (51 shorter events, 1.5 us)
Async XLA Ops:
  0.6 7.5 %copy-start.1 = (bf16[128,1024]{1,0:T(8,128)(2,1)S(1)}, bf16[128,1024]{1,0:T(8,128)(2,1)}, u32[]{:S(2)}) copy-start(bf16[128,1024]{1,0:T(8,128)(2,1)} %param.9) | copy-start | bytes 786436
  0.6 7.6 %copy-start.2 = (bf16[128,1024]{1,0:T(8,128)(2,1)S(1)}, bf16[128,1024]{1,0:T(8,128)(2,1)}, u32[]{:S(2)}) copy-start(bf16[128,1024]{1,0:T(8,128)(2,1)} %param.10) | copy-start | bytes 786436
  2.5 6.0 %copy-start.3 = (bf16[128,1024]{1,0:T(8,128)(2,1)S(1)}, bf16[128,1024]{1,0:T(8,128)(2,1)}, u32[]{:S(2)}) copy-start(bf16[128,1024]{1,0:T(8,128)(2,1)} %param.8) | copy-start | bytes 786436
  2.5 11.4 %all-to-all-start.2 = ((bf16[4,32,16,128]{3,2,1,0:T(8,128)(2,1)}), bf16[4,32,16,128]{3,2,1,0:T(8,128)(2,1)S(1)}, u32[]{:S(2)}, u32[]{:S(2)}) async-start(bf16[4,32,16,128]{3,2,1,0:T(8,128)(2,1)} %broadcast_in_dim.2), calls=%async_computation.2 | async-start | bytes 1048576 | tf_op jit(solution)/shard_map/all_to_all | solution.py:115
  9.9 15.1 %copy-start.7 = (f32[3,3,1024]{2,1,0:T(4,128)S(1)}, f32[3,3,1024]{2,1,0:T(4,128)}, u32[]{:S(2)}) copy-start(f32[3,3,1024]{2,1,0:T(4,128)} %param.11) | copy-start | bytes 110596
  9.9 15.4 %copy-start.5 = (f32[16,1024]{1,0:T(8,128)S(1)}, f32[16,1024]{1,0:T(8,128)}, u32[]{:S(2)}) copy-start(f32[16,1024]{1,0:T(8,128)} %param.13) | copy-start | bytes 196612
  9.9 15.7 %copy-start.6 = (f32[16,1024]{1,0:T(8,128)S(1)}, f32[16,1024]{1,0:T(8,128)}, u32[]{:S(2)}) copy-start(f32[16,1024]{1,0:T(8,128)} %param.12) | copy-start | bytes 196612
  13.9 33.8 %all-to-all-start = ((bf16[1,3,128,4,16,16]{2,5,3,1,0,4:T(8,128)(2,1)}), bf16[1,3,128,4,16,16]{2,5,3,1,0,4:T(8,128)(2,1)S(1)}, u32[]{:S(2)}, u32[]{:S(2)}) async-start(bf16[1,3,128,4,16,16]{2,5,3,1,0,4:T(8,128)(2,1)} %copy.72), calls=%async_computation | async-start | bytes 1572864 | tf_op jit(solution)/shard_map/all_to_all | solution.py:111
  25.0 1.0 copy-start.8
  48.1 6.0 %collective-permute-start = (bf16[3,2,64]{1,2,0:T(8,128)(2,1)S(1)}, bf16[3,2,64]{1,2,0:T(8,128)(2,1)S(1)}, u32[]{:S(2)}, u32[]{:S(2)}) collective-permute-start(bf16[3,2,64]{1,2,0:T(8,128)(2,1)S(1)} %slice.173), channel_id=1, source_target_pairs={{0,64},{64,128},{128,192},{1,65},{65,129},{129,193},{2,66},{66,130... | collective-permute-start | bytes 2312 | tf_op jit(solution)/shard_map/ppermute | solution.py:17
  63.3 11.7 %copy-start.4 = (f32[16,128]{1,0:T(8,128)S(1)}, f32[16,128]{1,0:T(8,128)}, u32[]{:S(2)}) copy-start(f32[16,128]{1,0:T(8,128)} %get-tuple-element.5) | copy-start | bytes 24580
  64.2 6.0 %collective-permute-start.1 = (f32[16,64]{1,0:T(8,128)S(1)}, f32[16,64]{1,0:T(8,128)S(1)}, u32[]{:S(2)}, u32[]{:S(2)}) collective-permute-start(f32[16,64]{1,0:T(8,128)S(1)} %slice_add_fusion), channel_id=1, source_target_pairs={{0,64},{64,128},{128,192},{1,65},{65,129},{129,193},{2,66},{66,130... | collective-permute-start | bytes 12296 | tf_op jit(solution)/shard_map/ppermute | solution.py:17
  67.9 7.0 %collective-permute-start.2 = (f32[16,64]{1,0:T(8,128)S(1)}, f32[16,64]{1,0:T(8,128)S(1)}, u32[]{:S(2)}, u32[]{:S(2)}) collective-permute-start(f32[16,64]{1,0:T(8,128)S(1)} %slice_add_fusion), channel_id=1, source_target_pairs={{0,128},{64,192},{1,129},{65,193},{2,130},{66,194},{3,131},{67,195... | collective-permute-start | bytes 12296 | tf_op jit(solution)/shard_map/ppermute | solution.py:17
  69.2 5.8 %collective-permute-start.3 = (f32[16,64]{1,0:T(8,128)S(1)}, f32[16,64]{1,0:T(8,128)S(1)}, u32[]{:S(2)}, u32[]{:S(2)}) collective-permute-start(f32[16,64]{1,0:T(8,128)S(1)} %slice_add_fusion), channel_id=1, source_target_pairs={{0,192},{1,193},{2,194},{3,195},{4,196},{5,197},{6,198},{7,199},{8... | collective-permute-start | bytes 12296 | tf_op jit(solution)/shard_map/ppermute | solution.py:17
  75.1 1.4 %copy-start = (f32[1024,128]{1,0:T(8,128)S(1)}, f32[1024,128]{1,0:T(8,128)}, u32[]{:S(2)}) copy-start(f32[1024,128]{1,0:T(8,128)} %get-tuple-element.4) | copy-start | bytes 1572868
  77.3 5.5 %collective-permute-start.4 = (bf16[16,64]{1,0:T(8,128)(2,1)S(1)}, bf16[16,64]{1,0:T(8,128)(2,1)S(1)}, u32[]{:S(2)}, u32[]{:S(2)}) collective-permute-start(bf16[16,64]{1,0:T(8,128)(2,1)S(1)} %slice.202), channel_id=1, source_target_pairs={{64,0},{128,64},{192,128},{65,1},{129,65},{193,129},{66,2},{130,66... | collective-permute-start | bytes 6152 | tf_op jit(solution)/shard_map/ppermute | solution.py:17
  83.9 14.1 %all-to-all-start.3 = ((f32[16,8,128]{2,1,0:T(8,128)}), f32[16,8,128]{2,1,0:T(8,128)S(1)}, u32[]{:S(2)}, u32[]{:S(2)}) async-start(f32[16,8,128]{2,1,0:T(8,128)} %fusion.1), calls=%async_computation.3 | async-start | bytes 131072 | tf_op jit(solution)/shard_map/all_to_all | solution.py:153
  87.4 14.1 %copy-start.9 = (u32[256]{0:T(256)S(1)}, u32[256]{0:T(256)}, u32[]{:S(2)}) copy-start(u32[256]{0:T(256)} %constant.37) | copy-start | bytes 3076
  97.9 16.1 %all-to-all-start.1 = ((bf16[16,128,4,1,16]{1,4,2,3,0:T(8,128)(2,1)}), bf16[16,128,4,1,16]{1,4,2,3,0:T(8,128)(2,1)S(1)}, u32[]{:S(2)}, u32[]{:S(2)}) async-start(bf16[16,128,4,1,16]{1,4,2,3,0:T(8,128)(2,1)} %copy.83), calls=%async_computation.1 | async-start | bytes 524288 | tf_op jit(solution)/shard_map/all_to_all | solution.py:139

commit v6 on v5

--- a/solution.py
+++ b/solution.py
@@ -106,17 +106,26 @@
     piece = head_weight.shape[1]
     span = tokens * width_v
     narrow = width_u * piece
-    stacked = jnp.stack([key_input, value_input, query_input], axis=0)
-    stacked = stacked.reshape(1, 3, tokens, width_u, width_v, piece)
-    columns = lax.all_to_all(stacked, "v", split_axis=4, concat_axis=0, tiled=True)
-    columns = columns.reshape(width_v, 3, tokens, narrow)
-    columns = jnp.transpose(columns, (1, 0, 2, 3)).reshape(3, span, narrow)
+    before = from_behind(
+        jnp.stack([query_input[-2:], key_input[-2:], value_input[-2:]], axis=0), ("u", "v"), 1
+    )
+    key_short = short_pass(key_input, before[1], short_filter[:, 1])
+    value_short = short_pass(value_input, before[2], short_filter[:, 2])
+    gated_rows = (key_short * value_short).astype(jnp.bfloat16)
+    payload = jnp.concatenate([before[0], query_input, gated_rows], axis=0)
+    depth = payload.shape[0]
+    payload = payload.reshape(1, depth, width_u, width_v, piece)
+    columns = lax.all_to_all(payload, "v", split_axis=3, concat_axis=0, tiled=True)
+    columns = columns.reshape(width_v, depth, narrow)
+    query_before = columns[0, :2]
+    query_cols = columns[:, 2 : 2 + tokens].reshape(span, narrow)
+    gated = columns[:, 2 + tokens :].reshape(span, narrow)
+    head_weight, gated = lax.optimization_barrier((head_weight, gated))
     weight_rep = jnp.broadcast_to(head_weight[None], (width_u,) + head_weight.shape)
     weight_cols = lax.all_to_all(weight_rep, "u", split_axis=0, concat_axis=0, tiled=True)
     weight_cols = jnp.transpose(weight_cols, (1, 0, 2, 3)).reshape(
         head_weight.shape[0], narrow, head_weight.shape[2]
     )
-    before = from_behind(columns[:, -2:], "u", 1)
     sf = short_filter.reshape(3, 3, width_u, width_v, piece)
     sf = jnp.transpose(sf, (0, 1, 3, 2, 4))
     sf = lax.dynamic_index_in_dim(sf, lax.axis_index("v"), axis=2, keepdims=False)
@@ -127,17 +136,11 @@
         shaped = lax.dynamic_index_in_dim(shaped, lax.axis_index("v"), axis=2, keepdims=False)
         return shaped.reshape(values.shape[0], narrow)
 
-    key_short = short_pass(columns[0], before[0], sf[:, 1])
-    value_short = short_pass(columns[1], before[1], sf[:, 2])
-    query_short = short_pass(columns[2], before[2], sf[:, 0])
-    gated = (key_short * value_short).astype(jnp.bfloat16)
+    query_short = short_pass(query_cols, query_before, sf[:, 0])
     convolved = modal_conv(gated, pick(residues), pick(decays))
     gain = pick(skip_gain[None])[0]
     carried = (convolved + gain * gated.astype(jnp.float32)).astype(jnp.bfloat16)
     op_cols = (query_short * carried.astype(jnp.float32)).astype(jnp.bfloat16)
-    back = op_cols.reshape(width_v, tokens, width_u, 1, piece)
-    back = lax.all_to_all(back, "v", split_axis=0, concat_axis=3, tiled=True)
-    operator_out = back.reshape(tokens, chan_width)
     rim_rows = from_behind(op_cols[:STRIDE], "u", -1)
     extended = jnp.concatenate([op_cols, rim_rows], axis=0)
     rows = span // STRIDE
@@ -149,9 +152,20 @@
     partial_sum = running + jnp.einsum(
         "jic,ico->jo", late_rows, weight_cols[STRIDE:], preferred_element_type=jnp.float32
     )
-    partial_sum = partial_sum.reshape(width_v, rows // width_v, -1)
-    partial_sum = lax.all_to_all(partial_sum, "v", split_axis=0, concat_axis=0, tiled=True)
-    block_sum = jnp.sum(partial_sum, axis=0)
+    outgoing = jnp.concatenate(
+        [
+            op_cols.reshape(width_v, tokens * narrow),
+            partial_sum.astype(jnp.bfloat16).reshape(width_v, -1),
+        ],
+        axis=1,
+    )
+    incoming = lax.all_to_all(outgoing, "v", split_axis=0, concat_axis=0, tiled=True)
+    back = incoming[:, : tokens * narrow].reshape(width_v, tokens, width_u, piece)
+    operator_out = jnp.transpose(back, (1, 2, 0, 3)).reshape(tokens, chan_width)
+    block_sum = jnp.sum(
+        incoming[:, tokens * narrow :].astype(jnp.float32).reshape(width_v, rows // width_v, -1),
+        axis=0,
+    )
     probe_out = lax.psum_scatter(block_sum, "tp", scatter_dimension=0, tiled=True).astype(
         jnp.bfloat16
     )

time: 116 us -> 113 us (0.974)
  the two profiles are of different devices: /device:TPU:16 before, /device:TPU:1 now
where the time goes in v6:
time: 113 us; the launch traced here: 112 us
  starting transfers between devices  34.7 us (31%)
  waiting for transfers between devices  32.2 us (28%)
  local copies, waits for them, and re-layouts  17.7 us (16%)
  blocking collectives  8.97 us (8%)
  other arithmetic  8.91 us (8%)
  Pallas kernels  7.02 us (6%)
  between operations  1.78 us (2%)
    all_to_all x1, waiting for transfers between devices, shards(): lax.all_to_all(payload, 'v', split_axis=3, concat_axis=0, tiled=True)  19.4 us
    ppermute x5, starting transfers between devices, from_behind(): return lax.ppermute(block, axis, route)  15.8 us
    all_to_all x1, waiting for transfers between devices, shards(): lax.all_to_all(outgoing, 'v', split_axis=0, concat_axis=0, tiled=True)  10.2 us
    unnamed x1, blocking collectives  8.97 us
    all_to_all x1, starting transfers between devices, shards(): lax.all_to_all(payload, 'v', split_axis=3, concat_axis=0, tiled=True)  8.82 us
    pallas_call x1, Pallas kernels, modal_conv(): pl.pallas_call(conv_kernel, out_shape=(jax.ShapeDtypeStruct((half, 2 * wi...  7.02 us
    all_to_all x1, starting transfers between devices, shards(): lax.all_to_all(outgoing, 'v', split_axis=0, concat_axis=0, tiled=True)  6.67 us
    unnamed x26, local copies, waits for them, and re-layouts  6.52 us
  transfers between devices with their start and end apart: 8, of which 3 were waited for; matrix products, arithmetic and copies ran while one was open for 10% of the time, Pallas kernels for 0%

profile of v6, /device:TPU:1, one launch (start us, length us, event | category | flops | bytes accessed | tf_op | source)
XLA Modules:
  0.0 112.0 jit_solution(15585982716466756964)
XLA Ops:
  0.6 0.7 slice_bitcast_fusion.2
  1.4 0.7 slice_bitcast_fusion
  2.1 5.5 %collective-permute-start = (bf16[3,2,1024]{2,1,0:T(2,128)(2,1)S(1)}, bf16[3,2,1024]{2,1,0:T(2,128)(2,1)S(1)}, u32[]{:S(2)}, u32[]{:S(2)}) collective-permute-start(bf16[3,2,1024]{2,1,0:T(2,128)(2,1)S(1)} %pad_maximum_fusion.3), channel_id=1, source_target_pairs={{0,4},{4,8},{8,12},{12,16},{16,20},{20,24},{24,28},{28,32},{32,36}... | collective-permute-start | bytes 36872 | tf_op jit(solution)/shard_map/ppermute | solution.py:17
  7.6 0.8 fusion.20
  8.4 1.1 copy.73
  9.6 1.1 %copy.75 = bf16[128,1024]{0,1:T(8,128)(2,1)S(1)} copy(bf16[128,1024]{1,0:T(8,128)(2,1)} %param.10) | data formatting | bytes 524288 | tf_op args[2]
  10.7 1.1 %copy.71 = bf16[128,1024]{0,1:T(8,128)(2,1)S(1)} copy(bf16[128,1024]{1,0:T(8,128)(2,1)} %param.8) | data formatting | bytes 524288 | tf_op args[0]
  12.1 0.2 copy.91
  12.3 0.2 copy.70
  12.5 0.2 maximum_convert_fusion.1
  12.7 0.2 maximum_convert_fusion.2
  13.0 1.5 %fusion.9 = bf16[128,1024]{0,1:T(8,128)(2,1)S(1)} fusion(f32[130,1024]{0,1:T(8,128)S(1)} %maximum_convert_fusion.2, f32[130,1024]{0,1:T(8,128)S(1)} %maximum_convert_fusion.1, f32[1024]{0:T(1024)S(1)} %bitcast.86, f32[1024]{0:T(1024)S(1)} %bitcast.87, f32[1024]{0:T(1024)S(1)} %bitcast.83, f32[1024]{0:T(1024)S(1)} %bitcast.84, f32[1024]{0:T(1024)S(1)} %bitcast.85, ...), kind=kLoop, calls=%fused_computation.20 | loop fusion | flops 1572864 | bytes 3432448 | tf_op jit(solution)/shard_map/convert_element_type | solution.py:114
  14.5 0.4 pad_maximum_fusion
  14.9 1.0 copy.76
  16.0 8.8 %all-to-all-start = ((bf16[1,258,4,16,16]{1,4,2,0,3:T(8,128)(2,1)}), bf16[1,258,4,16,16]{1,4,2,0,3:T(8,128)(2,1)S(1)}, u32[]{:S(2)}, u32[]{:S(2)}) async-start(bf16[1,258,4,16,16]{1,4,2,0,3:T(8,128)(2,1)} %copy.76), calls=%async_computation | async-start | bytes 1572864 | tf_op jit(solution)/shard_map/all_to_all | solution.py:118
  26.0 0.7 pad_maximum_fusion.5.w_ref
  26.7 0.7 fusion.15
  27.4 19.4 %all-to-all-done = bf16[1,258,4,16,16]{1,4,2,0,3:T(8,128)(2,1)S(1)} async-done(((bf16[1,258,4,16,16]{1,4,2,0,3:T(8,128)(2,1)}), bf16[1,258,4,16,16]{1,4,2,0,3:T(8,128)(2,1)S(1)}, u32[]{:S(2)}, u32[]{:S(2)}) %all-to-all-start) | async-done | bytes 528416 | tf_op jit(solution)/shard_map/all_to_all | solution.py:118
  46.8 0.2 fusion.16
  47.0 0.3 copy.79
  47.4 1.0 pad_maximum_fusion.2.g_ref
  48.4 7.0 %shard_map.95 = (f32[1024,128]{1,0:T(8,128)}, f32[16,128]{1,0:T(8,128)}) custom-call(f32[1024,128]{1,0:T(8,128)} %pad_maximum_fusion.2.g_ref, f32[16,128]{1,0:T(8,128)} %get-tuple-element.38.d_ref, f32[16,128]{1,0:T(8,128)} %pad_maximum_fusion.5.w_ref), custom_call_target="tpu_custom_call" | custom-call | tf_op jit(solution)/shard_map/pallas_call | solution.py:73
  55.4 0.8 slice_add_fusion
  56.3 3.2 %collective-permute-start.1 = (f32[16,64]{1,0:T(8,128)S(1)}, f32[16,64]{1,0:T(8,128)S(1)}, u32[]{:S(2)}, u32[]{:S(2)}) collective-permute-start(f32[16,64]{1,0:T(8,128)S(1)} %slice_add_fusion), channel_id=1, source_target_pairs={{0,64},{64,128},{128,192},{1,65},{65,129},{129,193},{2,66},{66,130... | collective-permute-start | bytes 12296 | tf_op jit(solution)/shard_map/ppermute | solution.py:17
  59.5 4.5 %collective-permute-start.2 = (f32[16,64]{1,0:T(8,128)S(1)}, f32[16,64]{1,0:T(8,128)S(1)}, u32[]{:S(2)}, u32[]{:S(2)}) collective-permute-start(f32[16,64]{1,0:T(8,128)S(1)} %slice_add_fusion), channel_id=1, source_target_pairs={{0,128},{64,192},{1,129},{65,193},{2,130},{66,194},{3,131},{67,195... | collective-permute-start | bytes 12296 | tf_op jit(solution)/shard_map/ppermute | solution.py:17
  64.0 1.3 %collective-permute-start.3 = (f32[16,64]{1,0:T(8,128)S(1)}, f32[16,64]{1,0:T(8,128)S(1)}, u32[]{:S(2)}, u32[]{:S(2)}) collective-permute-start(f32[16,64]{1,0:T(8,128)S(1)} %slice_add_fusion), channel_id=1, source_target_pairs={{0,192},{1,193},{2,194},{3,195},{4,196},{5,197},{6,198},{7,199},{8... | collective-permute-start | bytes 12296 | tf_op jit(solution)/shard_map/ppermute | solution.py:17
  65.3 0.3 copy.78
  65.7 0.9 broadcast_in_dim.2
  66.6 3.5 %all-to-all-start.1 = ((bf16[4,32,16,128]{3,2,1,0:T(8,128)(2,1)}), bf16[4,32,16,128]{3,2,1,0:T(8,128)(2,1)S(1)}, u32[]{:S(2)}, u32[]{:S(2)}) async-start(bf16[4,32,16,128]{3,2,1,0:T(8,128)(2,1)} %broadcast_in_dim.2), calls=%async_computation.1 | async-start | bytes 1048576 | tf_op jit(solution)/shard_map/all_to_all | solution.py:125
  70.4 1.4 %multiply_reduce_fusion = f32[1024,128]{1,0:T(8,128)S(1)} fusion(f32[1024]{0:T(1024)S(1)} %iota_add_fusion, f32[16,128]{1,0:T(8,128)S(1)} %get-tuple-element.37, f32[16,128]{1,0:T(8,128)S(1)} %maximum_multiply_fusion), kind=kLoop, calls=%fused_computation | loop fusion | flops 6160384 | bytes 544768 | tf_op jit(solution)/shard_map/reduce_sum | solution.py:96
  72.1 0.6 fusion.4
  72.7 1.3 %collective-permute-start.4 = (bf16[16,64]{1,0:T(8,128)(2,1)S(1)}, bf16[16,64]{1,0:T(8,128)(2,1)S(1)}, u32[]{:S(2)}, u32[]{:S(2)}) collective-permute-start(bf16[16,64]{1,0:T(8,128)(2,1)S(1)} %slice.208), channel_id=1, source_target_pairs={{64,0},{128,64},{192,128},{65,1},{129,65},{193,129},{66,2},{130,66... | collective-permute-start | bytes 6152 | tf_op jit(solution)/shard_map/ppermute | solution.py:17
  74.0 0.5 reshape.151
  74.4 2.6 %collective-permute-done.4 = bf16[16,64]{1,0:T(8,128)(2,1)S(1)} collective-permute-done((bf16[16,64]{1,0:T(8,128)(2,1)S(1)}, bf16[16,64]{1,0:T(8,128)(2,1)S(1)}, u32[]{:S(2)}, u32[]{:S(2)}) %collective-permute-start.4) | collective-permute-done | bytes 2080 | tf_op jit(solution)/shard_map/ppermute | solution.py:17
  77.2 0.3 convolution_bitcast_fusion.1
  77.6 0.3 fusion.1
  78.0 0.5 broadcast.15
  78.5 0.8 reduce.9
  79.3 0.9 reshape.172
  80.3 6.7 %all-to-all-start.2 = ((bf16[16,2,4608]{2,1,0:T(2,128)(2,1)}), bf16[16,2,4608]{2,1,0:T(2,128)(2,1)S(1)}, u32[]{:S(2)}, u32[]{:S(2)}) async-start(bf16[16,2,4608]{2,1,0:T(2,128)(2,1)} %reshape.172), calls=%async_computation.2 | async-start | bytes 589824 | tf_op jit(solution)/shard_map/all_to_all | solution.py:162
  86.9 0.6 dynamic-slice.4
  88.2 10.2 %all-to-all-done.2 = bf16[16,2,4608]{2,1,0:T(2,128)(2,1)S(1)} async-done(((bf16[16,2,4608]{2,1,0:T(2,128)(2,1)}), bf16[16,2,4608]{2,1,0:T(2,128)(2,1)S(1)}, u32[]{:S(2)}, u32[]{:S(2)}) %all-to-all-start.2) | async-done | bytes 294944 | tf_op jit(solution)/shard_map/all_to_all | solution.py:162
  98.3 0.2 reshape.173
  98.8 1.7 %reshape.155 = bf16[16,128,4,16]{3,2,1,0:T(4,128)(2,1)S(1)} reshape(bf16[16,8192]{1,0:T(8,128)(2,1)S(1)} %slice.210) | data formatting | bytes 524288 | tf_op jit(solution)/shard_map/reshape | solution.py:163
  100.5 1.2 %copy.87 = bf16[128,4,16,16]{0,3,2,1:T(8,128)(2,1)S(1)} copy(bf16[128,4,16,16]{3,1,0,2:T(4,128)(2,1)S(1)} %bitcast.61) | data formatting | bytes 524288 | tf_op jit(solution)/shard_map/transpose | solution.py:164
  101.7 0.9 copy.88
  102.5 9.0 %all-reduce = bf16[8,128]{1,0:T(8,128)(2,1)S(1)} all-reduce(f32[8,128]{1,0:T(8,128)S(1)} %bitcast.88), channel_id=2, replica_groups=mesh['u'=4,'v'=16,'tp'=4] {'tp'}, use_global_device_ids=true, to_apply=%region_2.3.clone | all-reduce | flops 1024 | bytes 6144
  111.5 0.5 dynamic-slice_convert_fusion
  (56 shorter events, 2.5 us)
Async XLA Ops:
  2.1 9.7 %collective-permute-start = (bf16[3,2,1024]{2,1,0:T(2,128)(2,1)S(1)}, bf16[3,2,1024]{2,1,0:T(2,128)(2,1)S(1)}, u32[]{:S(2)}, u32[]{:S(2)}) collective-permute-start(bf16[3,2,1024]{2,1,0:T(2,128)(2,1)S(1)} %pad_maximum_fusion.3), channel_id=1, source_target_pairs={{0,4},{4,8},{8,12},{12,16},{16,20},{20,24},{24,28},{28,32},{32,36}... | collective-permute-start | bytes 36872 | tf_op jit(solution)/shard_map/ppermute | solution.py:17
  14.9 9.9 %copy-start.2 = (f32[3,3,1024]{2,1,0:T(4,128)S(1)}, f32[3,3,1024]{2,1,0:T(4,128)}, u32[]{:S(2)}) copy-start(f32[3,3,1024]{2,1,0:T(4,128)} %param.11) | copy-start | bytes 110596
  14.9 10.0 %copy-start.4 = (f32[16,1024]{1,0:T(8,128)S(1)}, f32[16,1024]{1,0:T(8,128)}, u32[]{:S(2)}) copy-start(f32[16,1024]{1,0:T(8,128)} %param.13) | copy-start | bytes 196612
  16.0 9.2 %copy-start.5 = (f32[16,1024]{1,0:T(8,128)S(1)}, f32[16,1024]{1,0:T(8,128)}, u32[]{:S(2)}) copy-start(f32[16,1024]{1,0:T(8,128)} %param.12) | copy-start | bytes 196612
  16.0 9.8 %copy-start.6 = (f32[1024]{0:T(1024)S(1)}, f32[1024]{0:T(1024)}, u32[]{:S(2)}) copy-start(f32[1024]{0:T(1024)} %param.14) | copy-start | bytes 12292
  16.0 30.8 %all-to-all-start = ((bf16[1,258,4,16,16]{1,4,2,0,3:T(8,128)(2,1)}), bf16[1,258,4,16,16]{1,4,2,0,3:T(8,128)(2,1)S(1)}, u32[]{:S(2)}, u32[]{:S(2)}) async-start(bf16[1,258,4,16,16]{1,4,2,0,3:T(8,128)(2,1)} %copy.76), calls=%async_computation | async-start | bytes 1572864 | tf_op jit(solution)/shard_map/all_to_all | solution.py:118
  47.4 18.3 %copy-start.1 = (bf16[32,16,128]{2,1,0:T(8,128)(2,1)S(1)}, bf16[32,16,128]{2,1,0:T(8,128)(2,1)}, u32[]{:S(2)}) copy-start(bf16[32,16,128]{2,1,0:T(8,128)(2,1)} %param.15) | copy-start | bytes 393220
  56.3 13.9 %collective-permute-start.1 = (f32[16,64]{1,0:T(8,128)S(1)}, f32[16,64]{1,0:T(8,128)S(1)}, u32[]{:S(2)}, u32[]{:S(2)}) collective-permute-start(f32[16,64]{1,0:T(8,128)S(1)} %slice_add_fusion), channel_id=1, source_target_pairs={{0,64},{64,128},{128,192},{1,65},{65,129},{129,193},{2,66},{66,130... | collective-permute-start | bytes 12296 | tf_op jit(solution)/shard_map/ppermute | solution.py:17
  59.5 10.7 %collective-permute-start.2 = (f32[16,64]{1,0:T(8,128)S(1)}, f32[16,64]{1,0:T(8,128)S(1)}, u32[]{:S(2)}, u32[]{:S(2)}) collective-permute-start(f32[16,64]{1,0:T(8,128)S(1)} %slice_add_fusion), channel_id=1, source_target_pairs={{0,128},{64,192},{1,129},{65,193},{2,130},{66,194},{3,131},{67,195... | collective-permute-start | bytes 12296 | tf_op jit(solution)/shard_map/ppermute | solution.py:17
  64.0 6.2 %collective-permute-start.3 = (f32[16,64]{1,0:T(8,128)S(1)}, f32[16,64]{1,0:T(8,128)S(1)}, u32[]{:S(2)}, u32[]{:S(2)}) collective-permute-start(f32[16,64]{1,0:T(8,128)S(1)} %slice_add_fusion), channel_id=1, source_target_pairs={{0,192},{1,193},{2,194},{3,195},{4,196},{5,197},{6,198},{7,199},{8... | collective-permute-start | bytes 12296 | tf_op jit(solution)/shard_map/ppermute | solution.py:17
  65.7 4.5 %copy-start.3 = (f32[16,128]{1,0:T(8,128)S(1)}, f32[16,128]{1,0:T(8,128)}, u32[]{:S(2)}) copy-start(f32[16,128]{1,0:T(8,128)} %get-tuple-element.8) | copy-start | bytes 24580
  66.6 10.5 %all-to-all-start.1 = ((bf16[4,32,16,128]{3,2,1,0:T(8,128)(2,1)}), bf16[4,32,16,128]{3,2,1,0:T(8,128)(2,1)S(1)}, u32[]{:S(2)}, u32[]{:S(2)}) async-start(bf16[4,32,16,128]{3,2,1,0:T(8,128)(2,1)} %broadcast_in_dim.2), calls=%async_computation.1 | async-start | bytes 1048576 | tf_op jit(solution)/shard_map/all_to_all | solution.py:125
  70.4 1.4 %copy-start = (f32[1024,128]{1,0:T(8,128)S(1)}, f32[1024,128]{1,0:T(8,128)}, u32[]{:S(2)}) copy-start(f32[1024,128]{1,0:T(8,128)} %get-tuple-element.7) | copy-start | bytes 1572868
  72.7 4.4 %collective-permute-start.4 = (bf16[16,64]{1,0:T(8,128)(2,1)S(1)}, bf16[16,64]{1,0:T(8,128)(2,1)S(1)}, u32[]{:S(2)}, u32[]{:S(2)}) collective-permute-start(bf16[16,64]{1,0:T(8,128)(2,1)S(1)} %slice.208), channel_id=1, source_target_pairs={{64,0},{128,64},{192,128},{65,1},{129,65},{193,129},{66,2},{130,66... | collective-permute-start | bytes 6152 | tf_op jit(solution)/shard_map/ppermute | solution.py:17
  77.6 9.4 %copy-start.7 = (u32[256]{0:T(256)S(1)}, u32[256]{0:T(256)}, u32[]{:S(2)}) copy-start(u32[256]{0:T(256)} %constant.37) | copy-start | bytes 3076
  80.3 18.1 %all-to-all-start.2 = ((bf16[16,2,4608]{2,1,0:T(2,128)(2,1)}), bf16[16,2,4608]{2,1,0:T(2,128)(2,1)S(1)}, u32[]{:S(2)}, u32[]{:S(2)}) async-start(bf16[16,2,4608]{2,1,0:T(2,128)(2,1)} %reshape.172), calls=%async_computation.2 | async-start | bytes 589824 | tf_op jit(solution)/shard_map/all_to_all | solution.py:162

commit v7 on v6

--- a/solution.py
+++ b/solution.py
@@ -112,14 +112,18 @@
     key_short = short_pass(key_input, before[1], short_filter[:, 1])
     value_short = short_pass(value_input, before[2], short_filter[:, 2])
     gated_rows = (key_short * value_short).astype(jnp.bfloat16)
-    payload = jnp.concatenate([before[0], query_input, gated_rows], axis=0)
-    depth = payload.shape[0]
-    payload = payload.reshape(1, depth, width_u, width_v, piece)
-    columns = lax.all_to_all(payload, "v", split_axis=3, concat_axis=0, tiled=True)
-    columns = columns.reshape(width_v, depth, narrow)
+    def columns_of(values):
+        depth = values.shape[0]
+        parted = values.reshape(1, depth, width_u, width_v, piece)
+        moved = lax.all_to_all(parted, "v", split_axis=3, concat_axis=0, tiled=True)
+        return moved.reshape(width_v, depth, narrow)
+
+    gated = columns_of(gated_rows).reshape(span, narrow)
+    query_rows = jnp.concatenate([before[0], query_input], axis=0)
+    query_rows, gated = lax.optimization_barrier((query_rows, gated))
+    columns = columns_of(query_rows)
     query_before = columns[0, :2]
-    query_cols = columns[:, 2 : 2 + tokens].reshape(span, narrow)
-    gated = columns[:, 2 + tokens :].reshape(span, narrow)
+    query_cols = columns[:, 2:].reshape(span, narrow)
     head_weight, gated = lax.optimization_barrier((head_weight, gated))
     weight_rep = jnp.broadcast_to(head_weight[None], (width_u,) + head_weight.shape)
     weight_cols = lax.all_to_all(weight_rep, "u", split_axis=0, concat_axis=0, tiled=True)

time: 113 us -> 127 us (1.12)
  waiting for transfers between devices: 32.2 us -> 40.4 us
  blocking collectives: 8.97 us -> 12.1 us
  starting transfers between devices: 34.7 us -> 37 us
    all_to_all x1, waiting for transfers between devices: 0.01 us -> 5.26 us  [shards(): lax.all_to_all(weight_rep, 'u', split_axis=0, concat_axis=0, tiled=True)]
    all_to_all x1 -> x2, starting transfers between devices: 8.82 us -> 12.7 us  [columns_of(): moved = lax.all_to_all(parted, 'v', split_axis=3, concat_axis=0, tiled=True)]
    unnamed x1, blocking collectives: 8.97 us -> 12.1 us
    all_to_all x1 -> x2, waiting for transfers between devices: 19.4 us -> 22.5 us  [columns_of(): moved = lax.all_to_all(parted, 'v', split_axis=3, concat_axis=0, tiled=True)]
    reshape x2, local copies, waits for them, and re-layouts: 0.4 us -> 2.09 us  [pick(): shaped = values.reshape(values.shape[0], width_u, width_v, piece)]
    all_to_all x1, starting transfers between devices: 6.67 us -> 5.01 us  [shards(): lax.all_to_all(outgoing, 'v', split_axis=0, concat_axis=0, tiled=True)]
    unnamed x26 -> x28, local copies, waits for them, and re-layouts: 6.52 us -> 4.88 us
    reshape x0 -> x2, local copies, waits for them, and re-layouts: none -> 1.6 us  [columns_of(): parted = values.reshape(1, depth, width_u, width_v, piece)]
  transfers between devices with their start and end apart: 8 -> 9, of which waited for: 3 -> 5; matrix products, arithmetic and copies ran while one was open for 10% -> 9% of each run, Pallas kernels for 0% -> 0%
where the time goes in v7:
time: 127 us; the launch traced here: 126 us
  waiting for transfers between devices  40.4 us (32%)
  starting transfers between devices  37 us (29%)
  local copies, waits for them, and re-layouts  18.3 us (14%)
  blocking collectives  12.1 us (10%)
  other arithmetic  8.74 us (7%)
  Pallas kernels  7.02 us (6%)
  between operations  1.82 us (1%)
    all_to_all x2, waiting for transfers between devices, columns_of(): moved = lax.all_to_all(parted, 'v', split_axis=3, concat_axis=0, tiled=True)  22.5 us
    ppermute x5, starting transfers between devices, from_behind(): return lax.ppermute(block, axis, route)  15.8 us
    all_to_all x2, starting transfers between devices, columns_of(): moved = lax.all_to_all(parted, 'v', split_axis=3, concat_axis=0, tiled=True)  12.7 us
    unnamed x1, blocking collectives  12.1 us
    all_to_all x1, waiting for transfers between devices, shards(): lax.all_to_all(outgoing, 'v', split_axis=0, concat_axis=0, tiled=True)  10.1 us
    pallas_call x1, Pallas kernels, modal_conv(): pl.pallas_call(conv_kernel, out_shape=(jax.ShapeDtypeStruct((half, 2 * wi...  7.02 us
    all_to_all x1, waiting for transfers between devices, shards(): lax.all_to_all(weight_rep, 'u', split_axis=0, concat_axis=0, tiled=True)  5.26 us
    all_to_all x1, starting transfers between devices, shards(): lax.all_to_all(outgoing, 'v', split_axis=0, concat_axis=0, tiled=True)  5.01 us
  transfers between devices with their start and end apart: 9, of which 5 were waited for; matrix products, arithmetic and copies ran while one was open for 9% of the time, Pallas kernels for 0%

profile of v7, /device:TPU:1, one launch (start us, length us, event | category | flops | bytes accessed | tf_op | source)
XLA Modules:
  0.0 126.1 jit_solution(11027344173418117613)
XLA Ops:
  0.6 0.8 slice_bitcast_fusion.2
  1.4 0.7 slice_bitcast_fusion
  2.2 5.5 %collective-permute-start = (bf16[3,2,1024]{2,1,0:T(2,128)(2,1)S(1)}, bf16[3,2,1024]{2,1,0:T(2,128)(2,1)S(1)}, u32[]{:S(2)}, u32[]{:S(2)}) collective-permute-start(bf16[3,2,1024]{2,1,0:T(2,128)(2,1)S(1)} %pad_maximum_fusion.3), channel_id=1, source_target_pairs={{0,4},{4,8},{8,12},{12,16},{16,20},{20,24},{24,28},{28,32},{32,36}... | collective-permute-start | bytes 36872 | tf_op jit(solution)/shard_map/ppermute | solution.py:17
  7.7 0.8 fusion.19
  8.5 1.0 reshape.147
  9.6 1.0 reshape.149
  10.9 1.1 copy.79
  12.6 0.2 maximum_convert_fusion.1
  12.9 0.2 maximum_convert_fusion.2
  13.1 1.5 %fusion.9 = bf16[128,1024]{0,1:T(8,128)(2,1)S(1)} fusion(f32[130,1024]{0,1:T(8,128)S(1)} %maximum_convert_fusion.2, f32[130,1024]{0,1:T(8,128)S(1)} %maximum_convert_fusion.1, f32[1024]{0:T(1024)S(1)} %bitcast.96, f32[1024]{0:T(1024)S(1)} %bitcast.97, f32[1024]{0:T(1024)S(1)} %bitcast.93, f32[1024]{0:T(1024)S(1)} %bitcast.94, f32[1024]{0:T(1024)S(1)} %bitcast.95, ...), kind=kLoop, calls=%fused_computation.19 | loop fusion | flops 1572864 | bytes 3432448 | tf_op jit(solution)/shard_map/convert_element_type | solution.py:114
  14.7 0.7 copy.82
  15.4 8.7 %all-to-all-start = ((bf16[1,128,4,16,16]{1,4,2,0,3:T(8,128)(2,1)}), bf16[1,128,4,16,16]{1,4,2,0,3:T(8,128)(2,1)S(1)}, u32[]{:S(2)}, u32[]{:S(2)}) async-start(bf16[1,128,4,16,16]{1,4,2,0,3:T(8,128)(2,1)} %copy.82), calls=%async_computation | async-start | bytes 524288 | tf_op jit(solution)/shard_map/all_to_all | solution.py:118
  24.1 0.7 pad_maximum_fusion.5.w_ref
  25.3 0.7 fusion.15
  26.4 9.4 %all-to-all-done = bf16[1,128,4,16,16]{1,4,2,0,3:T(8,128)(2,1)S(1)} async-done(((bf16[1,128,4,16,16]{1,4,2,0,3:T(8,128)(2,1)}), bf16[1,128,4,16,16]{1,4,2,0,3:T(8,128)(2,1)S(1)}, u32[]{:S(2)}, u32[]{:S(2)}) %all-to-all-start) | async-done | bytes 262176 | tf_op jit(solution)/shard_map/all_to_all | solution.py:118
  36.0 0.3 copy.87
  36.4 1.0 pad_maximum_fusion.2.g_ref
  37.4 7.0 %shard_map.95 = (f32[1024,128]{1,0:T(8,128)}, f32[16,128]{1,0:T(8,128)}) custom-call(f32[1024,128]{1,0:T(8,128)} %pad_maximum_fusion.2.g_ref, f32[16,128]{1,0:T(8,128)} %get-tuple-element.40.d_ref, f32[16,128]{1,0:T(8,128)} %pad_maximum_fusion.5.w_ref), custom_call_target="tpu_custom_call" | custom-call | tf_op jit(solution)/shard_map/pallas_call | solution.py:73
  44.4 0.9 slice_add_fusion
  45.3 3.2 %collective-permute-start.1 = (f32[16,64]{1,0:T(8,128)S(1)}, f32[16,64]{1,0:T(8,128)S(1)}, u32[]{:S(2)}, u32[]{:S(2)}) collective-permute-start(f32[16,64]{1,0:T(8,128)S(1)} %slice_add_fusion), channel_id=1, source_target_pairs={{0,64},{64,128},{128,192},{1,65},{65,129},{129,193},{2,66},{66,130... | collective-permute-start | bytes 12296 | tf_op jit(solution)/shard_map/ppermute | solution.py:17
  48.5 4.5 %collective-permute-start.2 = (f32[16,64]{1,0:T(8,128)S(1)}, f32[16,64]{1,0:T(8,128)S(1)}, u32[]{:S(2)}, u32[]{:S(2)}) collective-permute-start(f32[16,64]{1,0:T(8,128)S(1)} %slice_add_fusion), channel_id=1, source_target_pairs={{0,128},{64,192},{1,129},{65,193},{2,130},{66,194},{3,131},{67,195... | collective-permute-start | bytes 12296 | tf_op jit(solution)/shard_map/ppermute | solution.py:17
  53.1 1.3 %collective-permute-start.3 = (f32[16,64]{1,0:T(8,128)S(1)}, f32[16,64]{1,0:T(8,128)S(1)}, u32[]{:S(2)}, u32[]{:S(2)}) collective-permute-start(f32[16,64]{1,0:T(8,128)S(1)} %slice_add_fusion), channel_id=1, source_target_pairs={{0,192},{1,193},{2,194},{3,195},{4,196},{5,197},{6,198},{7,199},{8... | collective-permute-start | bytes 12296 | tf_op jit(solution)/shard_map/ppermute | solution.py:17
  54.6 0.9 copy.84
  55.4 0.9 broadcast_in_dim.2
  56.3 3.5 %all-to-all-start.2 = ((bf16[4,32,16,128]{3,2,1,0:T(8,128)(2,1)}), bf16[4,32,16,128]{3,2,1,0:T(8,128)(2,1)S(1)}, u32[]{:S(2)}, u32[]{:S(2)}) async-start(bf16[4,32,16,128]{3,2,1,0:T(8,128)(2,1)} %broadcast_in_dim.2), calls=%async_computation.2 | async-start | bytes 1048576 | tf_op jit(solution)/shard_map/all_to_all | solution.py:129
  60.0 1.4 %multiply_reduce_fusion = f32[1024,128]{1,0:T(8,128)S(1)} fusion(f32[1024]{0:T(1024)S(1)} %iota_add_fusion, f32[16,128]{1,0:T(8,128)S(1)} %get-tuple-element.39, f32[16,128]{1,0:T(8,128)S(1)} %maximum_multiply_fusion), kind=kLoop, calls=%fused_computation | loop fusion | flops 6160384 | bytes 544768 | tf_op jit(solution)/shard_map/reduce_sum | solution.py:96
  61.4 5.3 %all-to-all-done.2 = bf16[4,32,16,128]{3,2,1,0:T(8,128)(2,1)S(1)} async-done(((bf16[4,32,16,128]{3,2,1,0:T(8,128)(2,1)}), bf16[4,32,16,128]{3,2,1,0:T(8,128)(2,1)S(1)}, u32[]{:S(2)}, u32[]{:S(2)}) %all-to-all-start.2) | async-done | bytes 524320 | tf_op jit(solution)/shard_map/all_to_all | solution.py:129
  66.7 4.0 %all-to-all-start.1 = ((bf16[1,130,4,16,16]{1,4,2,0,3:T(8,128)(2,1)}), bf16[1,130,4,16,16]{1,4,2,0,3:T(8,128)(2,1)S(1)}, u32[]{:S(2)}, u32[]{:S(2)}) async-start(bf16[1,130,4,16,16]{1,4,2,0,3:T(8,128)(2,1)} %copy.84), calls=%async_computation.1 | async-start | bytes 1048576 | tf_op jit(solution)/shard_map/all_to_all | solution.py:118
  71.0 13.1 %all-to-all-done.1 = bf16[1,130,4,16,16]{1,4,2,0,3:T(8,128)(2,1)S(1)} async-done(((bf16[1,130,4,16,16]{1,4,2,0,3:T(8,128)(2,1)}), bf16[1,130,4,16,16]{1,4,2,0,3:T(8,128)(2,1)S(1)}, u32[]{:S(2)}, u32[]{:S(2)}) %all-to-all-start.1) | async-done | bytes 266272 | tf_op jit(solution)/shard_map/all_to_all | solution.py:118
  84.3 0.3 copy.86
  84.8 0.5 fusion.4
  85.4 1.3 %collective-permute-start.4 = (bf16[16,64]{1,0:T(8,128)(2,1)S(1)}, bf16[16,64]{1,0:T(8,128)(2,1)S(1)}, u32[]{:S(2)}, u32[]{:S(2)}) collective-permute-start(bf16[16,64]{1,0:T(8,128)(2,1)S(1)} %slice.203), channel_id=1, source_target_pairs={{64,0},{128,64},{192,128},{65,1},{129,65},{193,129},{66,2},{130,66... | collective-permute-start | bytes 6152 | tf_op jit(solution)/shard_map/ppermute | solution.py:17
  86.7 0.3 convolution_bitcast_fusion.1
  87.0 0.5 reshape.151
  87.5 2.5 %collective-permute-done.4 = bf16[16,64]{1,0:T(8,128)(2,1)S(1)} collective-permute-done((bf16[16,64]{1,0:T(8,128)(2,1)S(1)}, bf16[16,64]{1,0:T(8,128)(2,1)S(1)}, u32[]{:S(2)}, u32[]{:S(2)}) %collective-permute-start.4) | collective-permute-done | bytes 2080 | tf_op jit(solution)/shard_map/ppermute | solution.py:17
  90.1 0.3 fusion.1
  90.5 0.5 broadcast.15
  91.1 0.8 reduce.9
  91.9 0.9 reshape.172
  92.8 5.0 %all-to-all-start.3 = ((bf16[16,2,4608]{2,1,0:T(2,128)(2,1)}), bf16[16,2,4608]{2,1,0:T(2,128)(2,1)S(1)}, u32[]{:S(2)}, u32[]{:S(2)}) async-start(bf16[16,2,4608]{2,1,0:T(2,128)(2,1)} %reshape.172), calls=%async_computation.3 | async-start | bytes 589824 | tf_op jit(solution)/shard_map/all_to_all | solution.py:166
  97.9 0.6 dynamic-slice.4
  99.1 10.1 %all-to-all-done.3 = bf16[16,2,4608]{2,1,0:T(2,128)(2,1)S(1)} async-done(((bf16[16,2,4608]{2,1,0:T(2,128)(2,1)}), bf16[16,2,4608]{2,1,0:T(2,128)(2,1)S(1)}, u32[]{:S(2)}, u32[]{:S(2)}) %all-to-all-start.3) | async-done | bytes 294944 | tf_op jit(solution)/shard_map/all_to_all | solution.py:166
  109.2 0.2 reshape.173
  109.6 1.7 %reshape.155 = bf16[16,128,4,16]{3,2,1,0:T(4,128)(2,1)S(1)} reshape(bf16[16,8192]{1,0:T(8,128)(2,1)S(1)} %slice.205) | data formatting | bytes 524288 | tf_op jit(solution)/shard_map/reshape | solution.py:167
  111.4 1.2 copy.95
  112.6 0.9 copy.96
  113.4 12.1 %all-reduce = bf16[8,128]{1,0:T(8,128)(2,1)S(1)} all-reduce(f32[8,128]{1,0:T(8,128)S(1)} %bitcast.98), channel_id=2, replica_groups=mesh['u'=4,'v'=16,'tp'=4] {'tp'}, use_global_device_ids=true, to_apply=%region_2.3.clone | all-reduce | flops 1024 | bytes 6144
  125.5 0.5 dynamic-slice_convert_fusion
  (61 shorter events, 3.4 us)
Async XLA Ops:
  0.6 11.4 %copy-start.1 = (bf16[128,1024]{1,0:T(8,128)(2,1)S(1)}, bf16[128,1024]{1,0:T(8,128)(2,1)}, u32[]{:S(2)}) copy-start(bf16[128,1024]{1,0:T(8,128)(2,1)} %param.10) | copy-start | bytes 786436
  2.2 10.0 %collective-permute-start = (bf16[3,2,1024]{2,1,0:T(2,128)(2,1)S(1)}, bf16[3,2,1024]{2,1,0:T(2,128)(2,1)S(1)}, u32[]{:S(2)}, u32[]{:S(2)}) collective-permute-start(bf16[3,2,1024]{2,1,0:T(2,128)(2,1)S(1)} %pad_maximum_fusion.3), channel_id=1, source_target_pairs={{0,4},{4,8},{8,12},{12,16},{16,20},{20,24},{24,28},{28,32},{32,36}... | collective-permute-start | bytes 36872 | tf_op jit(solution)/shard_map/ppermute | solution.py:17
  13.1 11.7 %copy-start.2 = (bf16[128,1024]{1,0:T(8,128)(2,1)S(1)}, bf16[128,1024]{1,0:T(8,128)(2,1)}, u32[]{:S(2)}) copy-start(bf16[128,1024]{1,0:T(8,128)(2,1)} %param.8) | copy-start | bytes 786436
  13.1 11.8 %copy-start.4 = (f32[3,3,1024]{2,1,0:T(4,128)S(1)}, f32[3,3,1024]{2,1,0:T(4,128)}, u32[]{:S(2)}) copy-start(f32[3,3,1024]{2,1,0:T(4,128)} %param.11) | copy-start | bytes 110596
  15.4 20.4 %all-to-all-start = ((bf16[1,128,4,16,16]{1,4,2,0,3:T(8,128)(2,1)}), bf16[1,128,4,16,16]{1,4,2,0,3:T(8,128)(2,1)S(1)}, u32[]{:S(2)}, u32[]{:S(2)}) async-start(bf16[1,128,4,16,16]{1,4,2,0,3:T(8,128)(2,1)} %copy.82), calls=%async_computation | async-start | bytes 524288 | tf_op jit(solution)/shard_map/all_to_all | solution.py:118
  36.3 18.1 %copy-start.6 = (f32[1024]{0:T(1024)S(1)}, f32[1024]{0:T(1024)}, u32[]{:S(2)}) copy-start(f32[1024]{0:T(1024)} %param.14) | copy-start | bytes 12292
  36.4 19.0 %copy-start.3 = (bf16[32,16,128]{2,1,0:T(8,128)(2,1)S(1)}, bf16[32,16,128]{2,1,0:T(8,128)(2,1)}, u32[]{:S(2)}) copy-start(bf16[32,16,128]{2,1,0:T(8,128)(2,1)} %param.15) | copy-start | bytes 393220
  44.4 15.4 %copy-start.5 = (f32[16,128]{1,0:T(8,128)S(1)}, f32[16,128]{1,0:T(8,128)}, u32[]{:S(2)}) copy-start(f32[16,128]{1,0:T(8,128)} %get-tuple-element.12) | copy-start | bytes 24580
  45.3 14.5 %collective-permute-start.1 = (f32[16,64]{1,0:T(8,128)S(1)}, f32[16,64]{1,0:T(8,128)S(1)}, u32[]{:S(2)}, u32[]{:S(2)}) collective-permute-start(f32[16,64]{1,0:T(8,128)S(1)} %slice_add_fusion), channel_id=1, source_target_pairs={{0,64},{64,128},{128,192},{1,65},{65,129},{129,193},{2,66},{66,130... | collective-permute-start | bytes 12296 | tf_op jit(solution)/shard_map/ppermute | solution.py:17
  48.5 11.3 %collective-permute-start.2 = (f32[16,64]{1,0:T(8,128)S(1)}, f32[16,64]{1,0:T(8,128)S(1)}, u32[]{:S(2)}, u32[]{:S(2)}) collective-permute-start(f32[16,64]{1,0:T(8,128)S(1)} %slice_add_fusion), channel_id=1, source_target_pairs={{0,128},{64,192},{1,129},{65,193},{2,130},{66,194},{3,131},{67,195... | collective-permute-start | bytes 12296 | tf_op jit(solution)/shard_map/ppermute | solution.py:17
  53.1 6.8 %collective-permute-start.3 = (f32[16,64]{1,0:T(8,128)S(1)}, f32[16,64]{1,0:T(8,128)S(1)}, u32[]{:S(2)}, u32[]{:S(2)}) collective-permute-start(f32[16,64]{1,0:T(8,128)S(1)} %slice_add_fusion), channel_id=1, source_target_pairs={{0,192},{1,193},{2,194},{3,195},{4,196},{5,197},{6,198},{7,199},{8... | collective-permute-start | bytes 12296 | tf_op jit(solution)/shard_map/ppermute | solution.py:17
  56.3 10.4 %all-to-all-start.2 = ((bf16[4,32,16,128]{3,2,1,0:T(8,128)(2,1)}), bf16[4,32,16,128]{3,2,1,0:T(8,128)(2,1)S(1)}, u32[]{:S(2)}, u32[]{:S(2)}) async-start(bf16[4,32,16,128]{3,2,1,0:T(8,128)(2,1)} %broadcast_in_dim.2), calls=%async_computation.2 | async-start | bytes 1048576 | tf_op jit(solution)/shard_map/all_to_all | solution.py:129
  59.8 1.6 %copy-start = (f32[1024,128]{1,0:T(8,128)S(1)}, f32[1024,128]{1,0:T(8,128)}, u32[]{:S(2)}) copy-start(f32[1024,128]{1,0:T(8,128)} %get-tuple-element.11) | copy-start | bytes 1572868
  66.7 17.4 %all-to-all-start.1 = ((bf16[1,130,4,16,16]{1,4,2,0,3:T(8,128)(2,1)}), bf16[1,130,4,16,16]{1,4,2,0,3:T(8,128)(2,1)S(1)}, u32[]{:S(2)}, u32[]{:S(2)}) async-start(bf16[1,130,4,16,16]{1,4,2,0,3:T(8,128)(2,1)} %copy.84), calls=%async_computation.1 | async-start | bytes 1048576 | tf_op jit(solution)/shard_map/all_to_all | solution.py:118
  85.4 4.6 %collective-permute-start.4 = (bf16[16,64]{1,0:T(8,128)(2,1)S(1)}, bf16[16,64]{1,0:T(8,128)(2,1)S(1)}, u32[]{:S(2)}, u32[]{:S(2)}) collective-permute-start(bf16[16,64]{1,0:T(8,128)(2,1)S(1)} %slice.203), channel_id=1, source_target_pairs={{64,0},{128,64},{192,128},{65,1},{129,65},{193,129},{66,2},{130,66... | collective-permute-start | bytes 6152 | tf_op jit(solution)/shard_map/ppermute | solution.py:17
  87.5 10.4 %copy-start.7 = (u32[256]{0:T(256)S(1)}, u32[256]{0:T(256)}, u32[]{:S(2)}) copy-start(u32[256]{0:T(256)} %constant.37) | copy-start | bytes 3076
  92.8 16.4 %all-to-all-start.3 = ((bf16[16,2,4608]{2,1,0:T(2,128)(2,1)}), bf16[16,2,4608]{2,1,0:T(2,128)(2,1)S(1)}, u32[]{:S(2)}, u32[]{:S(2)}) async-start(bf16[16,2,4608]{2,1,0:T(2,128)(2,1)} %reshape.172), calls=%async_computation.3 | async-start | bytes 589824 | tf_op jit(solution)/shard_map/all_to_all | solution.py:166

commit v8 on v7

--- a/solution.py
+++ b/solution.py
@@ -124,7 +124,7 @@
     columns = columns_of(query_rows)
     query_before = columns[0, :2]
     query_cols = columns[:, 2:].reshape(span, narrow)
-    head_weight, gated = lax.optimization_barrier((head_weight, gated))
+    head_weight, query_cols = lax.optimization_barrier((head_weight, query_cols))
     weight_rep = jnp.broadcast_to(head_weight[None], (width_u,) + head_weight.shape)
     weight_cols = lax.all_to_all(weight_rep, "u", split_axis=0, concat_axis=0, tiled=True)
     weight_cols = jnp.transpose(weight_cols, (1, 0, 2, 3)).reshape(

time: 127 us -> 122 us (0.961)
  waiting for transfers between devices: 40.4 us -> 36.8 us
    all_to_all x1, waiting for transfers between devices: 5.26 us -> 1.35 us  [shards(): lax.all_to_all(weight_rep, 'u', split_axis=0, concat_axis=0, tiled=True)]
where the time goes in v8:
time: 122 us; the launch traced here: 121 us
  waiting for transfers between devices  36.8 us (30%)
  starting transfers between devices  36 us (30%)
  local copies, waits for them, and re-layouts  18.2 us (15%)
  blocking collectives  11.6 us (10%)
  other arithmetic  8.73 us (7%)
  Pallas kernels  7.02 us (6%)
  between operations  1.82 us (1%)
    all_to_all x2, waiting for transfers between devices, columns_of(): moved = lax.all_to_all(parted, 'v', split_axis=3, concat_axis=0, tiled=True)  22.3 us
    ppermute x5, starting transfers between devices, from_behind(): return lax.ppermute(block, axis, route)  15.8 us
    all_to_all x2, starting transfers between devices, columns_of(): moved = lax.all_to_all(parted, 'v', split_axis=3, concat_axis=0, tiled=True)  12.3 us
    unnamed x1, blocking collectives  11.6 us
    all_to_all x1, waiting for transfers between devices, shards(): lax.all_to_all(outgoing, 'v', split_axis=0, concat_axis=0, tiled=True)  10.1 us
    pallas_call x1, Pallas kernels, modal_conv(): pl.pallas_call(conv_kernel, out_shape=(jax.ShapeDtypeStruct((half, 2 * wi...  7.02 us
    unnamed x28, local copies, waits for them, and re-layouts  4.88 us
    all_to_all x1, starting transfers between devices, shards(): lax.all_to_all(outgoing, 'v', split_axis=0, concat_axis=0, tiled=True)  4.46 us
  transfers between devices with their start and end apart: 9, of which 5 were waited for; matrix products, arithmetic and copies ran while one was open for 9% of the time, Pallas kernels for 0%

profile of v8, /device:TPU:1, one launch (start us, length us, event | category | flops | bytes accessed | tf_op | source)
XLA Modules:
  0.0 120.9 jit_solution(7051128696952001651)
XLA Ops:
  0.6 0.8 slice_bitcast_fusion.2
  1.4 0.7 slice_bitcast_fusion
  2.2 5.5 %collective-permute-start = (bf16[3,2,1024]{2,1,0:T(2,128)(2,1)S(1)}, bf16[3,2,1024]{2,1,0:T(2,128)(2,1)S(1)}, u32[]{:S(2)}, u32[]{:S(2)}) collective-permute-start(bf16[3,2,1024]{2,1,0:T(2,128)(2,1)S(1)} %pad_maximum_fusion.3), channel_id=1, source_target_pairs={{0,4},{4,8},{8,12},{12,16},{16,20},{20,24},{24,28},{28,32},{32,36}... | collective-permute-start | bytes 36872 | tf_op jit(solution)/shard_map/ppermute | solution.py:17
  7.7 0.8 fusion.19
  8.5 1.0 reshape.147
  9.6 1.0 reshape.149
  10.9 1.1 copy.79
  12.6 0.2 maximum_convert_fusion.1
  12.9 0.2 maximum_convert_fusion.2
  13.1 1.5 %fusion.9 = bf16[128,1024]{0,1:T(8,128)(2,1)S(1)} fusion(f32[130,1024]{0,1:T(8,128)S(1)} %maximum_convert_fusion.2, f32[130,1024]{0,1:T(8,128)S(1)} %maximum_convert_fusion.1, f32[1024]{0:T(1024)S(1)} %bitcast.96, f32[1024]{0:T(1024)S(1)} %bitcast.97, f32[1024]{0:T(1024)S(1)} %bitcast.93, f32[1024]{0:T(1024)S(1)} %bitcast.94, f32[1024]{0:T(1024)S(1)} %bitcast.95, ...), kind=kLoop, calls=%fused_computation.19 | loop fusion | flops 1572864 | bytes 3432448 | tf_op jit(solution)/shard_map/convert_element_type | solution.py:114
  14.7 0.7 copy.82
  15.4 8.7 %all-to-all-start = ((bf16[1,128,4,16,16]{1,4,2,0,3:T(8,128)(2,1)}), bf16[1,128,4,16,16]{1,4,2,0,3:T(8,128)(2,1)S(1)}, u32[]{:S(2)}, u32[]{:S(2)}) async-start(bf16[1,128,4,16,16]{1,4,2,0,3:T(8,128)(2,1)} %copy.82), calls=%async_computation | async-start | bytes 524288 | tf_op jit(solution)/shard_map/all_to_all | solution.py:118
  24.1 0.7 pad_maximum_fusion.5.w_ref
  25.3 0.7 fusion.15
  26.4 9.4 %all-to-all-done = bf16[1,128,4,16,16]{1,4,2,0,3:T(8,128)(2,1)S(1)} async-done(((bf16[1,128,4,16,16]{1,4,2,0,3:T(8,128)(2,1)}), bf16[1,128,4,16,16]{1,4,2,0,3:T(8,128)(2,1)S(1)}, u32[]{:S(2)}, u32[]{:S(2)}) %all-to-all-start) | async-done | bytes 262176 | tf_op jit(solution)/shard_map/all_to_all | solution.py:118
  36.0 0.3 copy.87
  36.4 1.0 pad_maximum_fusion.2.g_ref
  37.4 7.0 %shard_map.95 = (f32[1024,128]{1,0:T(8,128)}, f32[16,128]{1,0:T(8,128)}) custom-call(f32[1024,128]{1,0:T(8,128)} %pad_maximum_fusion.2.g_ref, f32[16,128]{1,0:T(8,128)} %get-tuple-element.40.d_ref, f32[16,128]{1,0:T(8,128)} %pad_maximum_fusion.5.w_ref), custom_call_target="tpu_custom_call" | custom-call | tf_op jit(solution)/shard_map/pallas_call | solution.py:73
  44.4 0.9 slice_add_fusion
  45.3 3.2 %collective-permute-start.1 = (f32[16,64]{1,0:T(8,128)S(1)}, f32[16,64]{1,0:T(8,128)S(1)}, u32[]{:S(2)}, u32[]{:S(2)}) collective-permute-start(f32[16,64]{1,0:T(8,128)S(1)} %slice_add_fusion), channel_id=1, source_target_pairs={{0,64},{64,128},{128,192},{1,65},{65,129},{129,193},{2,66},{66,130... | collective-permute-start | bytes 12296 | tf_op jit(solution)/shard_map/ppermute | solution.py:17
  48.5 4.5 %collective-permute-start.2 = (f32[16,64]{1,0:T(8,128)S(1)}, f32[16,64]{1,0:T(8,128)S(1)}, u32[]{:S(2)}, u32[]{:S(2)}) collective-permute-start(f32[16,64]{1,0:T(8,128)S(1)} %slice_add_fusion), channel_id=1, source_target_pairs={{0,128},{64,192},{1,129},{65,193},{2,130},{66,194},{3,131},{67,195... | collective-permute-start | bytes 12296 | tf_op jit(solution)/shard_map/ppermute | solution.py:17
  53.0 1.3 %collective-permute-start.3 = (f32[16,64]{1,0:T(8,128)S(1)}, f32[16,64]{1,0:T(8,128)S(1)}, u32[]{:S(2)}, u32[]{:S(2)}) collective-permute-start(f32[16,64]{1,0:T(8,128)S(1)} %slice_add_fusion), channel_id=1, source_target_pairs={{0,192},{1,193},{2,194},{3,195},{4,196},{5,197},{6,198},{7,199},{8... | collective-permute-start | bytes 12296 | tf_op jit(solution)/shard_map/ppermute | solution.py:17
  54.5 0.9 copy.84
  55.4 3.6 %all-to-all-start.1 = ((bf16[1,130,4,16,16]{1,4,2,0,3:T(8,128)(2,1)}), bf16[1,130,4,16,16]{1,4,2,0,3:T(8,128)(2,1)S(1)}, u32[]{:S(2)}, u32[]{:S(2)}) async-start(bf16[1,130,4,16,16]{1,4,2,0,3:T(8,128)(2,1)} %copy.84), calls=%async_computation.1 | async-start | bytes 1048576 | tf_op jit(solution)/shard_map/all_to_all | solution.py:118
  59.2 1.4 %multiply_reduce_fusion = f32[1024,128]{1,0:T(8,128)S(1)} fusion(f32[1024]{0:T(1024)S(1)} %iota_add_fusion, f32[16,128]{1,0:T(8,128)S(1)} %get-tuple-element.39, f32[16,128]{1,0:T(8,128)S(1)} %maximum_multiply_fusion), kind=kLoop, calls=%fused_computation | loop fusion | flops 6160384 | bytes 544768 | tf_op jit(solution)/shard_map/reduce_sum | solution.py:96
  60.9 12.9 %all-to-all-done.1 = bf16[1,130,4,16,16]{1,4,2,0,3:T(8,128)(2,1)S(1)} async-done(((bf16[1,130,4,16,16]{1,4,2,0,3:T(8,128)(2,1)}), bf16[1,130,4,16,16]{1,4,2,0,3:T(8,128)(2,1)S(1)}, u32[]{:S(2)}, u32[]{:S(2)}) %all-to-all-start.1) | async-done | bytes 266272 | tf_op jit(solution)/shard_map/all_to_all | solution.py:118
  73.9 0.3 copy.86
  74.3 0.9 broadcast_in_dim.2
  75.2 3.5 %all-to-all-start.2 = ((bf16[4,32,16,128]{3,2,1,0:T(8,128)(2,1)}), bf16[4,32,16,128]{3,2,1,0:T(8,128)(2,1)S(1)}, u32[]{:S(2)}, u32[]{:S(2)}) async-start(bf16[4,32,16,128]{3,2,1,0:T(8,128)(2,1)} %broadcast_in_dim.2), calls=%async_computation.2 | async-start | bytes 1048576 | tf_op jit(solution)/shard_map/all_to_all | solution.py:129
  78.8 0.5 fusion.4
  79.4 1.3 %collective-permute-start.4 = (bf16[16,64]{1,0:T(8,128)(2,1)S(1)}, bf16[16,64]{1,0:T(8,128)(2,1)S(1)}, u32[]{:S(2)}, u32[]{:S(2)}) collective-permute-start(bf16[16,64]{1,0:T(8,128)(2,1)S(1)} %slice.203), channel_id=1, source_target_pairs={{64,0},{128,64},{192,128},{65,1},{129,65},{193,129},{66,2},{130,66... | collective-permute-start | bytes 6152 | tf_op jit(solution)/shard_map/ppermute | solution.py:17
  80.7 0.5 reshape.151
  81.1 3.0 %collective-permute-done.4 = bf16[16,64]{1,0:T(8,128)(2,1)S(1)} collective-permute-done((bf16[16,64]{1,0:T(8,128)(2,1)S(1)}, bf16[16,64]{1,0:T(8,128)(2,1)S(1)}, u32[]{:S(2)}, u32[]{:S(2)}) %collective-permute-start.4) | collective-permute-done | bytes 2080 | tf_op jit(solution)/shard_map/ppermute | solution.py:17
  84.2 1.4 %all-to-all-done.2 = bf16[4,32,16,128]{3,2,1,0:T(8,128)(2,1)S(1)} async-done(((bf16[4,32,16,128]{3,2,1,0:T(8,128)(2,1)}), bf16[4,32,16,128]{3,2,1,0:T(8,128)(2,1)S(1)}, u32[]{:S(2)}, u32[]{:S(2)}) %all-to-all-start.2) | async-done | bytes 524320 | tf_op jit(solution)/shard_map/all_to_all | solution.py:129
  85.7 0.3 convolution_bitcast_fusion.1
  86.0 0.3 fusion.1
  86.4 0.5 broadcast.15
  86.9 0.8 reduce.9
  87.8 0.9 reshape.172
  88.7 4.5 %all-to-all-start.3 = ((bf16[16,2,4608]{2,1,0:T(2,128)(2,1)}), bf16[16,2,4608]{2,1,0:T(2,128)(2,1)S(1)}, u32[]{:S(2)}, u32[]{:S(2)}) async-start(bf16[16,2,4608]{2,1,0:T(2,128)(2,1)} %reshape.172), calls=%async_computation.3 | async-start | bytes 589824 | tf_op jit(solution)/shard_map/all_to_all | solution.py:166
  93.2 0.6 dynamic-slice.4
  94.4 10.1 %all-to-all-done.3 = bf16[16,2,4608]{2,1,0:T(2,128)(2,1)S(1)} async-done(((bf16[16,2,4608]{2,1,0:T(2,128)(2,1)}), bf16[16,2,4608]{2,1,0:T(2,128)(2,1)S(1)}, u32[]{:S(2)}, u32[]{:S(2)}) %all-to-all-start.3) | async-done | bytes 294944 | tf_op jit(solution)/shard_map/all_to_all | solution.py:166
  104.5 0.2 reshape.173
  104.9 1.7 %reshape.155 = bf16[16,128,4,16]{3,2,1,0:T(4,128)(2,1)S(1)} reshape(bf16[16,8192]{1,0:T(8,128)(2,1)S(1)} %slice.205) | data formatting | bytes 524288 | tf_op jit(solution)/shard_map/reshape | solution.py:167
  106.7 1.2 copy.95
  107.9 0.9 copy.96
  108.7 11.6 %all-reduce = bf16[8,128]{1,0:T(8,128)(2,1)S(1)} all-reduce(f32[8,128]{1,0:T(8,128)S(1)} %bitcast.98), channel_id=2, replica_groups=mesh['u'=4,'v'=16,'tp'=4] {'tp'}, use_global_device_ids=true, to_apply=%region_2.3.clone | all-reduce | flops 1024 | bytes 6144
  120.3 0.5 dynamic-slice_convert_fusion
  (61 shorter events, 3.4 us)
Async XLA Ops:
  0.6 11.4 %copy-start.1 = (bf16[128,1024]{1,0:T(8,128)(2,1)S(1)}, bf16[128,1024]{1,0:T(8,128)(2,1)}, u32[]{:S(2)}) copy-start(bf16[128,1024]{1,0:T(8,128)(2,1)} %param.10) | copy-start | bytes 786436
  2.2 10.0 %collective-permute-start = (bf16[3,2,1024]{2,1,0:T(2,128)(2,1)S(1)}, bf16[3,2,1024]{2,1,0:T(2,128)(2,1)S(1)}, u32[]{:S(2)}, u32[]{:S(2)}) collective-permute-start(bf16[3,2,1024]{2,1,0:T(2,128)(2,1)S(1)} %pad_maximum_fusion.3), channel_id=1, source_target_pairs={{0,4},{4,8},{8,12},{12,16},{16,20},{20,24},{24,28},{28,32},{32,36}... | collective-permute-start | bytes 36872 | tf_op jit(solution)/shard_map/ppermute | solution.py:17
  13.1 11.7 %copy-start.2 = (bf16[128,1024]{1,0:T(8,128)(2,1)S(1)}, bf16[128,1024]{1,0:T(8,128)(2,1)}, u32[]{:S(2)}) copy-start(bf16[128,1024]{1,0:T(8,128)(2,1)} %param.8) | copy-start | bytes 786436
  13.1 11.8 %copy-start.4 = (f32[3,3,1024]{2,1,0:T(4,128)S(1)}, f32[3,3,1024]{2,1,0:T(4,128)}, u32[]{:S(2)}) copy-start(f32[3,3,1024]{2,1,0:T(4,128)} %param.11) | copy-start | bytes 110596
  15.4 20.4 %all-to-all-start = ((bf16[1,128,4,16,16]{1,4,2,0,3:T(8,128)(2,1)}), bf16[1,128,4,16,16]{1,4,2,0,3:T(8,128)(2,1)S(1)}, u32[]{:S(2)}, u32[]{:S(2)}) async-start(bf16[1,128,4,16,16]{1,4,2,0,3:T(8,128)(2,1)} %copy.82), calls=%async_computation | async-start | bytes 524288 | tf_op jit(solution)/shard_map/all_to_all | solution.py:118
  36.3 18.0 %copy-start.6 = (f32[1024]{0:T(1024)S(1)}, f32[1024]{0:T(1024)}, u32[]{:S(2)}) copy-start(f32[1024]{0:T(1024)} %param.14) | copy-start | bytes 12292
  44.4 14.6 %copy-start.5 = (f32[16,128]{1,0:T(8,128)S(1)}, f32[16,128]{1,0:T(8,128)}, u32[]{:S(2)}) copy-start(f32[16,128]{1,0:T(8,128)} %get-tuple-element.12) | copy-start | bytes 24580
  45.3 13.7 %collective-permute-start.1 = (f32[16,64]{1,0:T(8,128)S(1)}, f32[16,64]{1,0:T(8,128)S(1)}, u32[]{:S(2)}, u32[]{:S(2)}) collective-permute-start(f32[16,64]{1,0:T(8,128)S(1)} %slice_add_fusion), channel_id=1, source_target_pairs={{0,64},{64,128},{128,192},{1,65},{65,129},{129,193},{2,66},{66,130... | collective-permute-start | bytes 12296 | tf_op jit(solution)/shard_map/ppermute | solution.py:17
  48.5 10.5 %collective-permute-start.2 = (f32[16,64]{1,0:T(8,128)S(1)}, f32[16,64]{1,0:T(8,128)S(1)}, u32[]{:S(2)}, u32[]{:S(2)}) collective-permute-start(f32[16,64]{1,0:T(8,128)S(1)} %slice_add_fusion), channel_id=1, source_target_pairs={{0,128},{64,192},{1,129},{65,193},{2,130},{66,194},{3,131},{67,195... | collective-permute-start | bytes 12296 | tf_op jit(solution)/shard_map/ppermute | solution.py:17
  53.0 6.0 %collective-permute-start.3 = (f32[16,64]{1,0:T(8,128)S(1)}, f32[16,64]{1,0:T(8,128)S(1)}, u32[]{:S(2)}, u32[]{:S(2)}) collective-permute-start(f32[16,64]{1,0:T(8,128)S(1)} %slice_add_fusion), channel_id=1, source_target_pairs={{0,192},{1,193},{2,194},{3,195},{4,196},{5,197},{6,198},{7,199},{8... | collective-permute-start | bytes 12296 | tf_op jit(solution)/shard_map/ppermute | solution.py:17
  55.4 18.4 %all-to-all-start.1 = ((bf16[1,130,4,16,16]{1,4,2,0,3:T(8,128)(2,1)}), bf16[1,130,4,16,16]{1,4,2,0,3:T(8,128)(2,1)S(1)}, u32[]{:S(2)}, u32[]{:S(2)}) async-start(bf16[1,130,4,16,16]{1,4,2,0,3:T(8,128)(2,1)} %copy.84), calls=%async_computation.1 | async-start | bytes 1048576 | tf_op jit(solution)/shard_map/all_to_all | solution.py:118
  59.0 1.6 %copy-start = (f32[1024,128]{1,0:T(8,128)S(1)}, f32[1024,128]{1,0:T(8,128)}, u32[]{:S(2)}) copy-start(f32[1024,128]{1,0:T(8,128)} %get-tuple-element.11) | copy-start | bytes 1572868
  60.7 13.6 %copy-start.3 = (bf16[32,16,128]{2,1,0:T(8,128)(2,1)S(1)}, bf16[32,16,128]{2,1,0:T(8,128)(2,1)}, u32[]{:S(2)}) copy-start(bf16[32,16,128]{2,1,0:T(8,128)(2,1)} %param.15) | copy-start | bytes 393220
  75.2 10.4 %all-to-all-start.2 = ((bf16[4,32,16,128]{3,2,1,0:T(8,128)(2,1)}), bf16[4,32,16,128]{3,2,1,0:T(8,128)(2,1)S(1)}, u32[]{:S(2)}, u32[]{:S(2)}) async-start(bf16[4,32,16,128]{3,2,1,0:T(8,128)(2,1)} %broadcast_in_dim.2), calls=%async_computation.2 | async-start | bytes 1048576 | tf_op jit(solution)/shard_map/all_to_all | solution.py:129
  79.4 4.7 %collective-permute-start.4 = (bf16[16,64]{1,0:T(8,128)(2,1)S(1)}, bf16[16,64]{1,0:T(8,128)(2,1)S(1)}, u32[]{:S(2)}, u32[]{:S(2)}) collective-permute-start(bf16[16,64]{1,0:T(8,128)(2,1)S(1)} %slice.203), channel_id=1, source_target_pairs={{64,0},{128,64},{192,128},{65,1},{129,65},{193,129},{66,2},{130,66... | collective-permute-start | bytes 6152 | tf_op jit(solution)/shard_map/ppermute | solution.py:17
  85.7 7.5 %copy-start.7 = (u32[256]{0:T(256)S(1)}, u32[256]{0:T(256)}, u32[]{:S(2)}) copy-start(u32[256]{0:T(256)} %constant.37) | copy-start | bytes 3076
  88.7 15.9 %all-to-all-start.3 = ((bf16[16,2,4608]{2,1,0:T(2,128)(2,1)}), bf16[16,2,4608]{2,1,0:T(2,128)(2,1)S(1)}, u32[]{:S(2)}, u32[]{:S(2)}) async-start(bf16[16,2,4608]{2,1,0:T(2,128)(2,1)} %reshape.172), calls=%async_computation.3 | async-start | bytes 589824 | tf_op jit(solution)/shard_map/all_to_all | solution.py:166

commit v9 on v6

--- a/solution.py
+++ b/solution.py
@@ -112,11 +112,16 @@
     key_short = short_pass(key_input, before[1], short_filter[:, 1])
     value_short = short_pass(value_input, before[2], short_filter[:, 2])
     gated_rows = (key_short * value_short).astype(jnp.bfloat16)
-    payload = jnp.concatenate([before[0], query_input, gated_rows], axis=0)
-    depth = payload.shape[0]
-    payload = payload.reshape(1, depth, width_u, width_v, piece)
-    columns = lax.all_to_all(payload, "v", split_axis=3, concat_axis=0, tiled=True)
-    columns = columns.reshape(width_v, depth, narrow)
+    def by_target(values):
+        depth = values.shape[0]
+        shaped = values.reshape(depth, width_u, width_v, piece)
+        return jnp.transpose(shaped, (2, 0, 1, 3)).reshape(width_v, depth, narrow)
+
+    payload = jnp.concatenate(
+        [by_target(before[0]), by_target(query_input), by_target(gated_rows)], axis=1
+    )
+    depth = payload.shape[1]
+    columns = lax.all_to_all(payload, "v", split_axis=0, concat_axis=0, tiled=True)
     query_before = columns[0, :2]
     query_cols = columns[:, 2 : 2 + tokens].reshape(span, narrow)
     gated = columns[:, 2 + tokens :].reshape(span, narrow)
@@ -152,20 +157,15 @@
     partial_sum = running + jnp.einsum(
         "jic,ico->jo", late_rows, weight_cols[STRIDE:], preferred_element_type=jnp.float32
     )
+    sums = partial_sum.astype(jnp.bfloat16).reshape(width_v, -1, width_u, 1, piece)
+    extra = sums.shape[1]
     outgoing = jnp.concatenate(
-        [
-            op_cols.reshape(width_v, tokens * narrow),
-            partial_sum.astype(jnp.bfloat16).reshape(width_v, -1),
-        ],
-        axis=1,
+        [op_cols.reshape(width_v, tokens, width_u, 1, piece), sums], axis=1
     )
-    incoming = lax.all_to_all(outgoing, "v", split_axis=0, concat_axis=0, tiled=True)
-    back = incoming[:, : tokens * narrow].reshape(width_v, tokens, width_u, piece)
-    operator_out = jnp.transpose(back, (1, 2, 0, 3)).reshape(tokens, chan_width)
-    block_sum = jnp.sum(
-        incoming[:, tokens * narrow :].astype(jnp.float32).reshape(width_v, rows // width_v, -1),
-        axis=0,
-    )
+    incoming = lax.all_to_all(outgoing, "v", split_axis=0, concat_axis=3, tiled=True)[0]
+    operator_out = incoming[:tokens].reshape(tokens, chan_width)
+    sums = jnp.transpose(incoming[tokens:], (2, 0, 1, 3)).astype(jnp.float32)
+    block_sum = jnp.sum(sums.reshape(width_v, rows // width_v, -1), axis=0)
     probe_out = lax.psum_scatter(block_sum, "tp", scatter_dimension=0, tiled=True).astype(
         jnp.bfloat16
     )

time: 113 us -> 112 us (level)
  local copies, waits for them, and re-layouts: 17.7 us -> 13.5 us
  waiting for transfers between devices: 32.2 us -> 34.8 us
    all_to_all x2, waiting for transfers between devices: 29.6 us -> 32 us  [the longest x1 18.1 us: shards(): lax.all_to_all(payload, 'v', split_axis=0, concat_axis=0, tiled=True)]
    unnamed x26, local copies, waits for them, and re-layouts: 6.52 us -> 4.84 us
    reshape x3 -> x2, local copies, waits for them, and re-layouts: 2.18 us -> 0.5 us  [shards(): partial_sum.astype(jnp.bfloat16).reshape(width_v, -1, width_u, 1, piece)]
    transpose x1 -> x2, local copies, waits for them, and re-layouts: 1.19 us -> 0.04 us  [by_target(): return jnp.transpose(shaped, (2, 0, 1, 3)).reshape(width_v, depth, narrow)]
  transfers between devices with their start and end apart: 8 -> 8, of which waited for: 3 -> 3; matrix products, arithmetic and copies ran while one was open for 10% -> 9% of each run, Pallas kernels for 0% -> 0%
where the time goes in v9:
time: 112 us; the launch traced here: 111 us
  starting transfers between devices  34.8 us (31%)
  waiting for transfers between devices  34.8 us (31%)
  local copies, waits for them, and re-layouts  13.5 us (12%)
  blocking collectives  9.56 us (9%)
  other arithmetic  9.16 us (8%)
  Pallas kernels  7.05 us (6%)
  between operations  1.79 us (2%)
    all_to_all x1, waiting for transfers between devices, shards(): lax.all_to_all(payload, 'v', split_axis=0, concat_axis=0, tiled=True)  18.1 us
    ppermute x5, starting transfers between devices, from_behind(): return lax.ppermute(block, axis, route)  15.8 us
    all_to_all x1, waiting for transfers between devices, shards(): lax.all_to_all(outgoing, 'v', split_axis=0, concat_axis=3, tiled=True)[0]  13.9 us
    unnamed x1, blocking collectives  9.56 us
    all_to_all x1, starting transfers between devices, shards(): lax.all_to_all(payload, 'v', split_axis=0, concat_axis=0, tiled=True)  8.85 us
    pallas_call x1, Pallas kernels, modal_conv(): pl.pallas_call(conv_kernel, out_shape=(jax.ShapeDtypeStruct((half, 2 * wi...  7.05 us
    all_to_all x1, starting transfers between devices, shards(): lax.all_to_all(outgoing, 'v', split_axis=0, concat_axis=3, tiled=True)[0]  6.73 us
    unnamed x26, local copies, waits for them, and re-layouts  4.84 us
  transfers between devices with their start and end apart: 8, of which 3 were waited for; matrix products, arithmetic and copies ran while one was open for 9% of the time, Pallas kernels for 0%

profile of v9, /device:TPU:1, one launch (start us, length us, event | category | flops | bytes accessed | tf_op | source)
XLA Modules:
  0.0 111.4 jit_solution(11016031817195889746)
XLA Ops:
  0.6 0.8 slice_bitcast_fusion.2
  1.4 0.7 slice_bitcast_fusion
  2.2 5.5 %collective-permute-start = (bf16[3,2,1024]{2,1,0:T(2,128)(2,1)S(1)}, bf16[3,2,1024]{2,1,0:T(2,128)(2,1)S(1)}, u32[]{:S(2)}, u32[]{:S(2)}) collective-permute-start(bf16[3,2,1024]{2,1,0:T(2,128)(2,1)S(1)} %pad_maximum_fusion.4), channel_id=1, source_target_pairs={{0,4},{4,8},{8,12},{12,16},{16,20},{20,24},{24,28},{28,32},{32,36}... | collective-permute-start | bytes 36872 | tf_op jit(solution)/shard_map/ppermute | solution.py:17
  7.7 0.8 fusion.20
  8.5 1.1 %copy.89 = bf16[128,1024]{0,1:T(8,128)(2,1)S(1)} copy(bf16[128,1024]{1,0:T(8,128)(2,1)} %param.9) | data formatting | bytes 524288 | tf_op args[1]
  9.6 1.1 %copy.91 = bf16[128,1024]{0,1:T(8,128)(2,1)S(1)} copy(bf16[128,1024]{1,0:T(8,128)(2,1)} %param.10) | data formatting | bytes 524288 | tf_op args[2]
  11.0 0.2 copy.110
  11.2 0.2 copy.111
  11.4 0.2 maximum_convert_fusion.1
  11.7 0.2 maximum_convert_fusion.2
  11.9 1.5 %fusion.9 = bf16[128,1024]{0,1:T(8,128)(2,1)S(1)} fusion(f32[130,1024]{0,1:T(8,128)S(1)} %maximum_convert_fusion.2, f32[130,1024]{0,1:T(8,128)S(1)} %maximum_convert_fusion.1, f32[1024]{0:T(1024)S(1)} %bitcast.93, f32[1024]{0:T(1024)S(1)} %bitcast.94, f32[1024]{0:T(1024)S(1)} %bitcast.90, f32[1024]{0:T(1024)S(1)} %bitcast.91, f32[1024]{0:T(1024)S(1)} %bitcast.92, ...), kind=kLoop, calls=%fused_computation.20 | loop fusion | flops 1572864 | bytes 3432448 | tf_op jit(solution)/shard_map/convert_element_type | solution.py:114
  13.6 0.5 copy.85
  14.1 1.3 %pad_maximum_fusion = bf16[16,258,64]{1,2,0:T(8,128)(2,1)} fusion(bf16[16,128,64]{1,2,0:T(8,128)(2,1)S(1)} %bitcast.79, bf16[16,128,64]{1,2,0:T(8,128)(2,1)S(1)} %bitcast.77, bf16[16,2,64]{1,2,0:T(8,128)(2,1)S(1)} %bitcast.82), kind=kLoop, calls=%fused_computation.14 | loop fusion | flops 1585152 | bytes 1056768 | tf_op jit(solution)/shard_map/concatenate | solution.py:120
  15.4 8.8 %all-to-all-start = ((bf16[16,258,64]{1,2,0:T(8,128)(2,1)}), bf16[16,258,64]{1,2,0:T(8,128)(2,1)S(1)}, u32[]{:S(2)}, u32[]{:S(2)}) async-start(bf16[16,258,64]{1,2,0:T(8,128)(2,1)} %pad_maximum_fusion), calls=%async_computation | async-start | bytes 1572864 | tf_op jit(solution)/shard_map/all_to_all | solution.py:124
  24.4 0.2 reshape.157
  24.6 0.2 reshape.159
  25.5 0.7 pad_maximum_fusion.6.w_ref
  26.1 0.7 fusion.15
  26.8 18.1 %all-to-all-done = bf16[16,258,64]{1,2,0:T(8,128)(2,1)S(1)} async-done(((bf16[16,258,64]{1,2,0:T(8,128)(2,1)}), bf16[16,258,64]{1,2,0:T(8,128)(2,1)S(1)}, u32[]{:S(2)}, u32[]{:S(2)}) %all-to-all-start) | async-done | bytes 528416 | tf_op jit(solution)/shard_map/all_to_all | solution.py:124
  44.9 0.2 fusion.16
  45.1 0.3 copy.95
  45.5 1.0 pad_maximum_fusion.2.g_ref
  46.5 7.1 %shard_map.95 = (f32[1024,128]{1,0:T(8,128)}, f32[16,128]{1,0:T(8,128)}) custom-call(f32[1024,128]{1,0:T(8,128)} %pad_maximum_fusion.2.g_ref, f32[16,128]{1,0:T(8,128)} %get-tuple-element.38.d_ref, f32[16,128]{1,0:T(8,128)} %pad_maximum_fusion.6.w_ref), custom_call_target="tpu_custom_call" | custom-call | tf_op jit(solution)/shard_map/pallas_call | solution.py:73
  53.6 0.8 slice_add_fusion
  54.4 3.2 %collective-permute-start.1 = (f32[16,64]{1,0:T(8,128)S(1)}, f32[16,64]{1,0:T(8,128)S(1)}, u32[]{:S(2)}, u32[]{:S(2)}) collective-permute-start(f32[16,64]{1,0:T(8,128)S(1)} %slice_add_fusion), channel_id=1, source_target_pairs={{0,64},{64,128},{128,192},{1,65},{65,129},{129,193},{2,66},{66,130... | collective-permute-start | bytes 12296 | tf_op jit(solution)/shard_map/ppermute | solution.py:17
  57.6 4.5 %collective-permute-start.2 = (f32[16,64]{1,0:T(8,128)S(1)}, f32[16,64]{1,0:T(8,128)S(1)}, u32[]{:S(2)}, u32[]{:S(2)}) collective-permute-start(f32[16,64]{1,0:T(8,128)S(1)} %slice_add_fusion), channel_id=1, source_target_pairs={{0,128},{64,192},{1,129},{65,193},{2,130},{66,194},{3,131},{67,195... | collective-permute-start | bytes 12296 | tf_op jit(solution)/shard_map/ppermute | solution.py:17
  62.1 1.3 %collective-permute-start.3 = (f32[16,64]{1,0:T(8,128)S(1)}, f32[16,64]{1,0:T(8,128)S(1)}, u32[]{:S(2)}, u32[]{:S(2)}) collective-permute-start(f32[16,64]{1,0:T(8,128)S(1)} %slice_add_fusion), channel_id=1, source_target_pairs={{0,192},{1,193},{2,194},{3,195},{4,196},{5,197},{6,198},{7,199},{8... | collective-permute-start | bytes 12296 | tf_op jit(solution)/shard_map/ppermute | solution.py:17
  63.4 0.3 copy.94
  63.8 0.9 broadcast_in_dim.2
  64.7 3.5 %all-to-all-start.1 = ((bf16[4,32,16,128]{3,2,1,0:T(8,128)(2,1)}), bf16[4,32,16,128]{3,2,1,0:T(8,128)(2,1)S(1)}, u32[]{:S(2)}, u32[]{:S(2)}) async-start(bf16[4,32,16,128]{3,2,1,0:T(8,128)(2,1)} %broadcast_in_dim.2), calls=%async_computation.1 | async-start | bytes 1048576 | tf_op jit(solution)/shard_map/all_to_all | solution.py:130
  68.4 0.5 copy-done.4
  69.0 1.4 %multiply_reduce_fusion = f32[1024,128]{1,0:T(8,128)S(1)} fusion(f32[1024]{0:T(1024)S(1)} %iota_add_fusion, f32[16,128]{1,0:T(8,128)S(1)} %get-tuple-element.37, f32[16,128]{1,0:T(8,128)S(1)} %maximum_multiply_fusion), kind=kLoop, calls=%fused_computation | loop fusion | flops 6160384 | bytes 544768 | tf_op jit(solution)/shard_map/reduce_sum | solution.py:96
  70.5 0.2 fusion.18
  70.7 0.6 fusion.4
  71.3 1.3 %collective-permute-start.4 = (bf16[16,64]{1,0:T(8,128)(2,1)S(1)}, bf16[16,64]{1,0:T(8,128)(2,1)S(1)}, u32[]{:S(2)}, u32[]{:S(2)}) collective-permute-start(bf16[16,64]{1,0:T(8,128)(2,1)S(1)} %slice.210), channel_id=1, source_target_pairs={{64,0},{128,64},{192,128},{65,1},{129,65},{193,129},{66,2},{130,66... | collective-permute-start | bytes 6152 | tf_op jit(solution)/shard_map/ppermute | solution.py:17
  72.6 0.2 copy.98
  72.8 2.8 %collective-permute-done.4 = bf16[16,64]{1,0:T(8,128)(2,1)S(1)} collective-permute-done((bf16[16,64]{1,0:T(8,128)(2,1)S(1)}, bf16[16,64]{1,0:T(8,128)(2,1)S(1)}, u32[]{:S(2)}, u32[]{:S(2)}) %collective-permute-start.4) | collective-permute-done | bytes 2080 | tf_op jit(solution)/shard_map/ppermute | solution.py:17
  75.9 0.3 convolution_bitcast_fusion.1
  76.2 0.3 fusion.1
  76.5 0.2 reshape.164
  76.7 0.3 copy.103
  77.2 1.0 copy.104
  78.2 6.7 %all-to-all-start.2 = ((bf16[16,144,4,1,16]{1,4,2,3,0:T(8,128)(2,1)}), bf16[16,144,4,1,16]{1,4,2,3,0:T(8,128)(2,1)S(1)}, u32[]{:S(2)}, u32[]{:S(2)}) async-start(bf16[16,144,4,1,16]{1,4,2,3,0:T(8,128)(2,1)} %copy.104), calls=%async_computation.2 | async-start | bytes 1048576 | tf_op jit(solution)/shard_map/all_to_all | solution.py:165
  84.9 0.6 dynamic-slice.4
  86.2 13.9 %all-to-all-done.2 = bf16[16,144,4,1,16]{1,4,2,3,0:T(8,128)(2,1)S(1)} async-done(((bf16[16,144,4,1,16]{1,4,2,3,0:T(8,128)(2,1)}), bf16[16,144,4,1,16]{1,4,2,3,0:T(8,128)(2,1)S(1)}, u32[]{:S(2)}, u32[]{:S(2)}) %all-to-all-start.2) | async-done | bytes 294944 | tf_op jit(solution)/shard_map/all_to_all | solution.py:165
  100.3 0.9 copy.108
  101.3 9.6 %all-reduce = bf16[8,128]{1,0:T(8,128)(2,1)S(1)} all-reduce(f32[8,128]{1,0:T(8,128)S(1)} %reduce_sum.22), channel_id=2, replica_groups=mesh['u'=4,'v'=16,'tp'=4] {'tp'}, use_global_device_ids=true, to_apply=%region_2.3.clone | all-reduce | flops 1024 | bytes 6144
  110.8 0.5 dynamic-slice_convert_fusion
  (59 shorter events, 2.3 us)
Async XLA Ops:
  0.6 10.1 %copy-start.1 = (bf16[128,1024]{1,0:T(8,128)(2,1)S(1)}, bf16[128,1024]{1,0:T(8,128)(2,1)}, u32[]{:S(2)}) copy-start(bf16[128,1024]{1,0:T(8,128)(2,1)} %param.8) | copy-start | bytes 786436
  2.2 8.8 %collective-permute-start = (bf16[3,2,1024]{2,1,0:T(2,128)(2,1)S(1)}, bf16[3,2,1024]{2,1,0:T(2,128)(2,1)S(1)}, u32[]{:S(2)}, u32[]{:S(2)}) collective-permute-start(bf16[3,2,1024]{2,1,0:T(2,128)(2,1)S(1)} %pad_maximum_fusion.4), channel_id=1, source_target_pairs={{0,4},{4,8},{8,12},{12,16},{16,20},{20,24},{24,28},{28,32},{32,36}... | collective-permute-start | bytes 36872 | tf_op jit(solution)/shard_map/ppermute | solution.py:17
  15.4 8.9 %copy-start.3 = (f32[3,3,1024]{2,1,0:T(4,128)S(1)}, f32[3,3,1024]{2,1,0:T(4,128)}, u32[]{:S(2)}) copy-start(f32[3,3,1024]{2,1,0:T(4,128)} %param.11) | copy-start | bytes 110596
  15.4 9.0 %copy-start.5 = (f32[16,1024]{1,0:T(8,128)S(1)}, f32[16,1024]{1,0:T(8,128)}, u32[]{:S(2)}) copy-start(f32[16,1024]{1,0:T(8,128)} %param.13) | copy-start | bytes 196612
  15.4 9.3 %copy-start.6 = (f32[16,1024]{1,0:T(8,128)S(1)}, f32[16,1024]{1,0:T(8,128)}, u32[]{:S(2)}) copy-start(f32[16,1024]{1,0:T(8,128)} %param.12) | copy-start | bytes 196612
  15.4 29.5 %all-to-all-start = ((bf16[16,258,64]{1,2,0:T(8,128)(2,1)}), bf16[16,258,64]{1,2,0:T(8,128)(2,1)S(1)}, u32[]{:S(2)}, u32[]{:S(2)}) async-start(bf16[16,258,64]{1,2,0:T(8,128)(2,1)} %pad_maximum_fusion), calls=%async_computation | async-start | bytes 1572864 | tf_op jit(solution)/shard_map/all_to_all | solution.py:124
  24.2 1.0 copy-start.7
  46.5 17.3 %copy-start.2 = (bf16[32,16,128]{2,1,0:T(8,128)(2,1)S(1)}, bf16[32,16,128]{2,1,0:T(8,128)(2,1)}, u32[]{:S(2)}) copy-start(bf16[32,16,128]{2,1,0:T(8,128)(2,1)} %param.15) | copy-start | bytes 393220
  54.4 14.0 %collective-permute-start.1 = (f32[16,64]{1,0:T(8,128)S(1)}, f32[16,64]{1,0:T(8,128)S(1)}, u32[]{:S(2)}, u32[]{:S(2)}) collective-permute-start(f32[16,64]{1,0:T(8,128)S(1)} %slice_add_fusion), channel_id=1, source_target_pairs={{0,64},{64,128},{128,192},{1,65},{65,129},{129,193},{2,66},{66,130... | collective-permute-start | bytes 12296 | tf_op jit(solution)/shard_map/ppermute | solution.py:17
  57.6 10.8 %collective-permute-start.2 = (f32[16,64]{1,0:T(8,128)S(1)}, f32[16,64]{1,0:T(8,128)S(1)}, u32[]{:S(2)}, u32[]{:S(2)}) collective-permute-start(f32[16,64]{1,0:T(8,128)S(1)} %slice_add_fusion), channel_id=1, source_target_pairs={{0,128},{64,192},{1,129},{65,193},{2,130},{66,194},{3,131},{67,195... | collective-permute-start | bytes 12296 | tf_op jit(solution)/shard_map/ppermute | solution.py:17
  62.1 6.2 %collective-permute-start.3 = (f32[16,64]{1,0:T(8,128)S(1)}, f32[16,64]{1,0:T(8,128)S(1)}, u32[]{:S(2)}, u32[]{:S(2)}) collective-permute-start(f32[16,64]{1,0:T(8,128)S(1)} %slice_add_fusion), channel_id=1, source_target_pairs={{0,192},{1,193},{2,194},{3,195},{4,196},{5,197},{6,198},{7,199},{8... | collective-permute-start | bytes 12296 | tf_op jit(solution)/shard_map/ppermute | solution.py:17
  64.7 11.0 %all-to-all-start.1 = ((bf16[4,32,16,128]{3,2,1,0:T(8,128)(2,1)}), bf16[4,32,16,128]{3,2,1,0:T(8,128)(2,1)S(1)}, u32[]{:S(2)}, u32[]{:S(2)}) async-start(bf16[4,32,16,128]{3,2,1,0:T(8,128)(2,1)} %broadcast_in_dim.2), calls=%async_computation.1 | async-start | bytes 1048576 | tf_op jit(solution)/shard_map/all_to_all | solution.py:130
  68.2 0.7 copy-start.4
  69.0 1.4 %copy-start = (f32[1024,128]{1,0:T(8,128)S(1)}, f32[1024,128]{1,0:T(8,128)}, u32[]{:S(2)}) copy-start(f32[1024,128]{1,0:T(8,128)} %get-tuple-element.7) | copy-start | bytes 1572868
  71.3 4.4 %collective-permute-start.4 = (bf16[16,64]{1,0:T(8,128)(2,1)S(1)}, bf16[16,64]{1,0:T(8,128)(2,1)S(1)}, u32[]{:S(2)}, u32[]{:S(2)}) collective-permute-start(bf16[16,64]{1,0:T(8,128)(2,1)S(1)} %slice.210), channel_id=1, source_target_pairs={{64,0},{128,64},{192,128},{65,1},{129,65},{193,129},{66,2},{130,66... | collective-permute-start | bytes 6152 | tf_op jit(solution)/shard_map/ppermute | solution.py:17
  77.2 7.7 %copy-start.8 = (u32[256]{0:T(256)S(1)}, u32[256]{0:T(256)}, u32[]{:S(2)}) copy-start(u32[256]{0:T(256)} %constant.37) | copy-start | bytes 3076
  78.2 21.9 %all-to-all-start.2 = ((bf16[16,144,4,1,16]{1,4,2,3,0:T(8,128)(2,1)}), bf16[16,144,4,1,16]{1,4,2,3,0:T(8,128)(2,1)S(1)}, u32[]{:S(2)}, u32[]{:S(2)}) async-start(bf16[16,144,4,1,16]{1,4,2,3,0:T(8,128)(2,1)} %copy.104), calls=%async_computation.2 | async-start | bytes 1048576 | tf_op jit(solution)/shard_map/all_to_all | solution.py:165

commit v10 on v9

--- a/solution.py
+++ b/solution.py
@@ -82,11 +82,14 @@
     first_end, second_end = ends[:, :width], ends[:, width:]
     total = hop_half * first_end + second_end
     outer = None
-    for m in range(1, groups):
-        term = from_behind(total, "u", m)
-        if m > 1:
-            term = jnp.exp(-decays * float(span * (m - 1))) * term
-        outer = term if outer is None else outer + term
+    if groups > 1:
+        shared = jnp.broadcast_to(total[None], (groups,) + total.shape)
+        shared = lax.all_to_all(shared, "u", split_axis=0, concat_axis=0, tiled=True)
+        source = jnp.arange(groups, dtype=jnp.int32)
+        lag = lax.axis_index("u") - 1 - source
+        gap = (float(span) * jnp.maximum(lag, 0).astype(jnp.float32))[:, None, None]
+        factor = jnp.where((lag >= 0)[:, None, None], jnp.exp(-decays[None] * gap), 0.0)
+        outer = jnp.sum(factor * shared, axis=0)
     if outer is None:
         entry = jnp.concatenate([jnp.zeros_like(first_end), first_end], axis=1)
     else:

time: 112 us -> 114 us (1.018)
  starting transfers between devices: 34.8 us -> 28.6 us
  waiting for transfers between devices: 34.8 us -> 40.3 us
    ppermute x5 -> x2, starting transfers between devices: 15.8 us -> 6.76 us  [from_behind(): return lax.ppermute(block, axis, route)]
    all_to_all x0 -> x1, starting transfers between devices: none -> 4.18 us  [modal_conv(): lax.all_to_all(shared, 'u', split_axis=0, concat_axis=0, tiled=True)]
    all_to_all x0 -> x1, waiting for transfers between devices: none -> 3.64 us  [modal_conv(): lax.all_to_all(shared, 'u', split_axis=0, concat_axis=0, tiled=True)]
    all_to_all x1, waiting for transfers between devices: 18.1 us -> 20.6 us  [shards(): lax.all_to_all(payload, 'v', split_axis=0, concat_axis=0, tiled=True)]
    reshape x2, local copies, waits for them, and re-layouts: 0.4 us -> 2.14 us  [pick(): shaped = values.reshape(values.shape[0], width_u, width_v, piece)]
    unnamed x26 -> x28, local copies, waits for them, and re-layouts: 4.84 us -> 3.22 us
    all_to_all x1, starting transfers between devices: 6.73 us -> 5.53 us  [shards(): lax.all_to_all(outgoing, 'v', split_axis=0, concat_axis=3, tiled=True)[0]]
    ppermute x5 -> x2, waiting for transfers between devices: 2.81 us -> 3.14 us  [from_behind(): return lax.ppermute(block, axis, route)]
  transfers between devices with their start and end apart: 8 -> 6, of which waited for: 3 -> 4; matrix products, arithmetic and copies ran while one was open for 9% -> 10% of each run, Pallas kernels for 0% -> 0%
where the time goes in v10:
time: 114 us; the launch traced here: 113 us
  waiting for transfers between devices  40.3 us (35%)
  starting transfers between devices  28.6 us (25%)
  local copies, waits for them, and re-layouts  14.1 us (12%)
  blocking collectives  10.5 us (9%)
  other arithmetic  9.87 us (9%)
  Pallas kernels  7.02 us (6%)
  between operations  1.79 us (2%)
    all_to_all x1, waiting for transfers between devices, shards(): lax.all_to_all(payload, 'v', split_axis=0, concat_axis=0, tiled=True)  20.6 us
    all_to_all x1, waiting for transfers between devices, shards(): lax.all_to_all(outgoing, 'v', split_axis=0, concat_axis=3, tiled=True)[0]  12.9 us
    unnamed x1, blocking collectives  10.5 us
    all_to_all x1, starting transfers between devices, shards(): lax.all_to_all(payload, 'v', split_axis=0, concat_axis=0, tiled=True)  8.69 us
    pallas_call x1, Pallas kernels, modal_conv(): pl.pallas_call(conv_kernel, out_shape=(jax.ShapeDtypeStruct((half, 2 * wi...  7.02 us
    ppermute x2, starting transfers between devices, from_behind(): return lax.ppermute(block, axis, route)  6.76 us
    all_to_all x1, starting transfers between devices, shards(): lax.all_to_all(outgoing, 'v', split_axis=0, concat_axis=3, tiled=True)[0]  5.53 us
    all_to_all x1, starting transfers between devices, modal_conv(): lax.all_to_all(shared, 'u', split_axis=0, concat_axis=0, tiled=True)  4.18 us
  transfers between devices with their start and end apart: 6, of which 4 were waited for; matrix products, arithmetic and copies ran while one was open for 10% of the time, Pallas kernels for 0%

profile of v10, /device:TPU:1, one launch (start us, length us, event | category | flops | bytes accessed | tf_op | source)
XLA Modules:
  0.0 112.9 jit_solution(11294607585271224234)
XLA Ops:
  0.7 0.8 slice_bitcast_fusion.2
  1.4 0.7 slice_bitcast_fusion
  2.2 5.5 %collective-permute-start = (bf16[3,2,1024]{2,1,0:T(2,128)(2,1)S(1)}, bf16[3,2,1024]{2,1,0:T(2,128)(2,1)S(1)}, u32[]{:S(2)}, u32[]{:S(2)}) collective-permute-start(bf16[3,2,1024]{2,1,0:T(2,128)(2,1)S(1)} %pad_maximum_fusion.4), channel_id=1, source_target_pairs={{0,4},{4,8},{8,12},{12,16},{16,20},{20,24},{24,28},{28,32},{32,36}... | collective-permute-start | bytes 36872 | tf_op jit(solution)/shard_map/ppermute | solution.py:17
  7.7 0.8 fusion.21
  8.5 1.1 reshape.176
  9.7 1.1 reshape.178
  10.8 0.2 copy.89
  12.1 0.2 copy.110
  12.3 0.2 copy.111
  12.5 0.2 maximum_convert_fusion.1
  12.7 0.2 maximum_convert_fusion.2
  13.0 1.5 %fusion.9 = bf16[128,1024]{0,1:T(8,128)(2,1)S(1)} fusion(f32[130,1024]{0,1:T(8,128)S(1)} %maximum_convert_fusion.2, f32[130,1024]{0,1:T(8,128)S(1)} %maximum_convert_fusion.1, f32[1024]{0:T(1024)S(1)} %bitcast.93, f32[1024]{0:T(1024)S(1)} %bitcast.94, f32[1024]{0:T(1024)S(1)} %bitcast.90, f32[1024]{0:T(1024)S(1)} %bitcast.91, f32[1024]{0:T(1024)S(1)} %bitcast.92, ...), kind=kLoop, calls=%fused_computation.20 | loop fusion | flops 1572864 | bytes 3432448 | tf_op jit(solution)/shard_map/convert_element_type | solution.py:117
  14.6 0.5 copy.85
  15.1 1.3 %pad_maximum_fusion = bf16[16,258,64]{1,2,0:T(8,128)(2,1)} fusion(bf16[16,128,64]{1,2,0:T(8,128)(2,1)S(1)} %bitcast.79, bf16[16,128,64]{1,2,0:T(8,128)(2,1)S(1)} %bitcast.77, bf16[16,2,64]{1,2,0:T(8,128)(2,1)S(1)} %bitcast.82), kind=kLoop, calls=%fused_computation.14 | loop fusion | flops 1585152 | bytes 1056768 | tf_op jit(solution)/shard_map/concatenate | solution.py:123
  16.4 8.7 %all-to-all-start = ((bf16[16,258,64]{1,2,0:T(8,128)(2,1)}), bf16[16,258,64]{1,2,0:T(8,128)(2,1)S(1)}, u32[]{:S(2)}, u32[]{:S(2)}) async-start(bf16[16,258,64]{1,2,0:T(8,128)(2,1)} %pad_maximum_fusion), calls=%async_computation | async-start | bytes 1572864 | tf_op jit(solution)/shard_map/all_to_all | solution.py:127
  25.2 0.7 pad_maximum_fusion.6.w_ref
  25.8 0.7 fusion.16
  26.5 20.6 %all-to-all-done = bf16[16,258,64]{1,2,0:T(8,128)(2,1)S(1)} async-done(((bf16[16,258,64]{1,2,0:T(8,128)(2,1)}), bf16[16,258,64]{1,2,0:T(8,128)(2,1)S(1)}, u32[]{:S(2)}, u32[]{:S(2)}) %all-to-all-start) | async-done | bytes 528416 | tf_op jit(solution)/shard_map/all_to_all | solution.py:127
  47.1 0.2 fusion.17
  47.3 0.3 copy.95
  47.7 1.0 pad_maximum_fusion.2.g_ref
  48.7 7.0 %shard_map.95 = (f32[1024,128]{1,0:T(8,128)}, f32[16,128]{1,0:T(8,128)}) custom-call(f32[1024,128]{1,0:T(8,128)} %pad_maximum_fusion.2.g_ref, f32[16,128]{1,0:T(8,128)} %get-tuple-element.38.d_ref, f32[16,128]{1,0:T(8,128)} %pad_maximum_fusion.6.w_ref), custom_call_target="tpu_custom_call" | custom-call | tf_op jit(solution)/shard_map/pallas_call | solution.py:73
  55.7 0.8 fusion.23
  56.6 0.7 reshape.200
  57.3 4.2 %all-to-all-start.1 = ((f32[4,1,1024]{2,1,0:T(1,128)}), f32[4,1,1024]{2,1,0:T(1,128)S(1)}, u32[]{:S(2)}, u32[]{:S(2)}) async-start(f32[4,1,1024]{2,1,0:T(1,128)} %reshape.200), calls=%async_computation.1 | async-start | bytes 32768 | tf_op jit(solution)/shard_map/all_to_all | solution.py:87
  61.5 0.3 copy.94
  62.0 3.6 %all-to-all-done.1 = f32[4,1,1024]{2,1,0:T(1,128)S(1)} async-done(((f32[4,1,1024]{2,1,0:T(1,128)}), f32[4,1,1024]{2,1,0:T(1,128)S(1)}, u32[]{:S(2)}, u32[]{:S(2)}) %all-to-all-start.1) | async-done | bytes 16416 | tf_op jit(solution)/shard_map/all_to_all | solution.py:87
  65.7 0.8 broadcast_in_dim.19
  66.5 3.5 %all-to-all-start.2 = ((bf16[4,32,16,128]{3,2,1,0:T(8,128)(2,1)}), bf16[4,32,16,128]{3,2,1,0:T(8,128)(2,1)S(1)}, u32[]{:S(2)}, u32[]{:S(2)}) async-start(bf16[4,32,16,128]{3,2,1,0:T(8,128)(2,1)} %broadcast_in_dim.19), calls=%async_computation.2 | async-start | bytes 1048576 | tf_op jit(solution)/shard_map/all_to_all | solution.py:133
  70.0 0.5 broadcast.46
  70.5 0.7 reduce.11
  71.5 1.4 %multiply_reduce_fusion = f32[1024,128]{1,0:T(8,128)S(1)} fusion(f32[1024]{0:T(1024)S(1)} %iota_add_fusion, f32[16,128]{1,0:T(8,128)S(1)} %get-tuple-element.37, f32[16,128]{1,0:T(8,128)S(1)} %maximum_multiply_fusion), kind=kLoop, calls=%fused_computation | loop fusion | flops 6160384 | bytes 544768 | tf_op jit(solution)/shard_map/reduce_sum | solution.py:99
  73.0 0.2 fusion.19
  73.2 0.5 fusion.4
  73.7 1.3 %collective-permute-start.1 = (bf16[16,64]{1,0:T(8,128)(2,1)S(1)}, bf16[16,64]{1,0:T(8,128)(2,1)S(1)}, u32[]{:S(2)}, u32[]{:S(2)}) collective-permute-start(bf16[16,64]{1,0:T(8,128)(2,1)S(1)} %slice.210), channel_id=1, source_target_pairs={{64,0},{128,64},{192,128},{65,1},{129,65},{193,129},{66,2},{130,66... | collective-permute-start | bytes 6152 | tf_op jit(solution)/shard_map/ppermute | solution.py:17
  75.0 0.2 copy.98
  75.3 3.1 %collective-permute-done.1 = bf16[16,64]{1,0:T(8,128)(2,1)S(1)} collective-permute-done((bf16[16,64]{1,0:T(8,128)(2,1)S(1)}, bf16[16,64]{1,0:T(8,128)(2,1)S(1)}, u32[]{:S(2)}, u32[]{:S(2)}) %collective-permute-start.1) | collective-permute-done | bytes 2080 | tf_op jit(solution)/shard_map/ppermute | solution.py:17
  78.7 0.3 convolution_bitcast_fusion.1
  79.0 0.3 fusion.1
  79.3 0.2 reshape.183
  79.6 0.3 copy.103
  80.0 1.0 copy.104
  81.0 5.5 %all-to-all-start.3 = ((bf16[16,144,4,1,16]{1,4,2,3,0:T(8,128)(2,1)}), bf16[16,144,4,1,16]{1,4,2,3,0:T(8,128)(2,1)S(1)}, u32[]{:S(2)}, u32[]{:S(2)}) async-start(bf16[16,144,4,1,16]{1,4,2,3,0:T(8,128)(2,1)} %copy.104), calls=%async_computation.3 | async-start | bytes 1048576 | tf_op jit(solution)/shard_map/all_to_all | solution.py:168
  86.5 0.6 dynamic-slice.4
  87.8 12.9 %all-to-all-done.3 = bf16[16,144,4,1,16]{1,4,2,3,0:T(8,128)(2,1)S(1)} async-done(((bf16[16,144,4,1,16]{1,4,2,3,0:T(8,128)(2,1)}), bf16[16,144,4,1,16]{1,4,2,3,0:T(8,128)(2,1)S(1)}, u32[]{:S(2)}, u32[]{:S(2)}) %all-to-all-start.3) | async-done | bytes 294944 | tf_op jit(solution)/shard_map/all_to_all | solution.py:168
  100.9 0.9 copy.108
  101.9 10.5 %all-reduce = bf16[8,128]{1,0:T(8,128)(2,1)S(1)} all-reduce(f32[8,128]{1,0:T(8,128)S(1)} %reduce_sum.32), channel_id=2, replica_groups=mesh['u'=4,'v'=16,'tp'=4] {'tp'}, use_global_device_ids=true, to_apply=%region_3.4.clone | all-reduce | flops 1024 | bytes 6144
  112.4 0.5 dynamic-slice_convert_fusion
  (63 shorter events, 2.6 us)
Async XLA Ops:
  0.6 10.3 %copy-start.2 = (bf16[128,1024]{1,0:T(8,128)(2,1)S(1)}, bf16[128,1024]{1,0:T(8,128)(2,1)}, u32[]{:S(2)}) copy-start(bf16[128,1024]{1,0:T(8,128)(2,1)} %param.10) | copy-start | bytes 786436
  0.6 10.1 %copy-start.1 = (bf16[128,1024]{1,0:T(8,128)(2,1)S(1)}, bf16[128,1024]{1,0:T(8,128)(2,1)}, u32[]{:S(2)}) copy-start(bf16[128,1024]{1,0:T(8,128)(2,1)} %param.9) | copy-start | bytes 786436
  2.2 9.8 %collective-permute-start = (bf16[3,2,1024]{2,1,0:T(2,128)(2,1)S(1)}, bf16[3,2,1024]{2,1,0:T(2,128)(2,1)S(1)}, u32[]{:S(2)}, u32[]{:S(2)}) collective-permute-start(bf16[3,2,1024]{2,1,0:T(2,128)(2,1)S(1)} %pad_maximum_fusion.4), channel_id=1, source_target_pairs={{0,4},{4,8},{8,12},{12,16},{16,20},{20,24},{24,28},{28,32},{32,36}... | collective-permute-start | bytes 36872 | tf_op jit(solution)/shard_map/ppermute | solution.py:17
  8.5 2.6 %copy-start.3 = (bf16[128,1024]{1,0:T(8,128)(2,1)S(1)}, bf16[128,1024]{1,0:T(8,128)(2,1)}, u32[]{:S(2)}) copy-start(bf16[128,1024]{1,0:T(8,128)(2,1)} %param.8) | copy-start | bytes 786436
  9.6 1.7 %copy-start.5 = (f32[3,3,1024]{2,1,0:T(4,128)S(1)}, f32[3,3,1024]{2,1,0:T(4,128)}, u32[]{:S(2)}) copy-start(f32[3,3,1024]{2,1,0:T(4,128)} %param.11) | copy-start | bytes 110596
  11.0 0.9 copy-start.7
  16.4 30.7 %all-to-all-start = ((bf16[16,258,64]{1,2,0:T(8,128)(2,1)}), bf16[16,258,64]{1,2,0:T(8,128)(2,1)S(1)}, u32[]{:S(2)}, u32[]{:S(2)}) async-start(bf16[16,258,64]{1,2,0:T(8,128)(2,1)} %pad_maximum_fusion), calls=%async_computation | async-start | bytes 1572864 | tf_op jit(solution)/shard_map/all_to_all | solution.py:127
  57.3 8.4 %all-to-all-start.1 = ((f32[4,1,1024]{2,1,0:T(1,128)}), f32[4,1,1024]{2,1,0:T(1,128)S(1)}, u32[]{:S(2)}, u32[]{:S(2)}) async-start(f32[4,1,1024]{2,1,0:T(1,128)} %reshape.200), calls=%async_computation.1 | async-start | bytes 32768 | tf_op jit(solution)/shard_map/all_to_all | solution.py:87
  61.5 4.2 %copy-start.4 = (bf16[32,16,128]{2,1,0:T(8,128)(2,1)S(1)}, bf16[32,16,128]{2,1,0:T(8,128)(2,1)}, u32[]{:S(2)}) copy-start(bf16[32,16,128]{2,1,0:T(8,128)(2,1)} %param.15) | copy-start | bytes 393220
  62.0 9.4 %copy-start.6 = (f32[16,128]{1,0:T(8,128)S(1)}, f32[16,128]{1,0:T(8,128)}, u32[]{:S(2)}) copy-start(f32[16,128]{1,0:T(8,128)} %get-tuple-element.8) | copy-start | bytes 24580
  66.5 12.0 %all-to-all-start.2 = ((bf16[4,32,16,128]{3,2,1,0:T(8,128)(2,1)}), bf16[4,32,16,128]{3,2,1,0:T(8,128)(2,1)S(1)}, u32[]{:S(2)}, u32[]{:S(2)}) async-start(bf16[4,32,16,128]{3,2,1,0:T(8,128)(2,1)} %broadcast_in_dim.19), calls=%async_computation.2 | async-start | bytes 1048576 | tf_op jit(solution)/shard_map/all_to_all | solution.py:133
  71.5 1.4 %copy-start = (f32[1024,128]{1,0:T(8,128)S(1)}, f32[1024,128]{1,0:T(8,128)}, u32[]{:S(2)}) copy-start(f32[1024,128]{1,0:T(8,128)} %get-tuple-element.7) | copy-start | bytes 1572868
  73.7 4.7 %collective-permute-start.1 = (bf16[16,64]{1,0:T(8,128)(2,1)S(1)}, bf16[16,64]{1,0:T(8,128)(2,1)S(1)}, u32[]{:S(2)}, u32[]{:S(2)}) collective-permute-start(bf16[16,64]{1,0:T(8,128)(2,1)S(1)} %slice.210), channel_id=1, source_target_pairs={{64,0},{128,64},{192,128},{65,1},{129,65},{193,129},{66,2},{130,66... | collective-permute-start | bytes 6152 | tf_op jit(solution)/shard_map/ppermute | solution.py:17
  80.0 6.5 %copy-start.8 = (u32[256]{0:T(256)S(1)}, u32[256]{0:T(256)}, u32[]{:S(2)}) copy-start(u32[256]{0:T(256)} %constant.44) | copy-start | bytes 3076
  81.0 19.7 %all-to-all-start.3 = ((bf16[16,144,4,1,16]{1,4,2,3,0:T(8,128)(2,1)}), bf16[16,144,4,1,16]{1,4,2,3,0:T(8,128)(2,1)S(1)}, u32[]{:S(2)}, u32[]{:S(2)}) async-start(bf16[16,144,4,1,16]{1,4,2,3,0:T(8,128)(2,1)} %copy.104), calls=%async_computation.3 | async-start | bytes 1048576 | tf_op jit(solution)/shard_map/all_to_all | solution.py:168

commit v11 on v10

--- a/solution.py
+++ b/solution.py
@@ -177,7 +177,7 @@
 
 def solution(mesh):
     seq_size, tp_size = mesh.devices.shape
-    width_u = 4 if seq_size % 4 == 0 else 1
+    width_u = 8 if seq_size % 8 == 0 else 1
     split = jax.sharding.Mesh(
         mesh.devices.reshape(width_u, seq_size // width_u, tp_size), ("u", "v", "tp")
     )

time: 114 us -> 136 us (1.19)
  starting transfers between devices: 28.6 us -> 42.9 us
  local copies, waits for them, and re-layouts: 14.1 us -> 21.7 us
  waiting for transfers between devices: 40.3 us -> 45.4 us
  blocking collectives: 10.5 us -> 7 us
  other arithmetic: 9.87 us -> 8.05 us
    all_to_all x1, starting transfers between devices: 5.53 us -> 18 us  [shards(): lax.all_to_all(outgoing, 'v', split_axis=0, concat_axis=3, tiled=True)[0]]
    all_to_all x1, waiting for transfers between devices: 20.6 us -> 12 us  [shards(): lax.all_to_all(payload, 'v', split_axis=0, concat_axis=0, tiled=True)]
    ppermute x2, waiting for transfers between devices: 3.14 us -> 10.7 us  [from_behind(): return lax.ppermute(block, axis, route)]
    slice x1 -> x2, local copies, waits for them, and re-layouts: 0.05 us -> 4.69 us  [shards(): operator_out = incoming[:tokens].reshape(tokens, chan_width)]
    all_to_all x1, waiting for transfers between devices: 3.64 us -> 8.18 us  [modal_conv(): lax.all_to_all(shared, 'u', split_axis=0, concat_axis=0, tiled=True)]
    unnamed x1, blocking collectives: 10.5 us -> 7 us
    all_to_all x1, local copies, waits for them, and re-layouts: 0.03 us -> 3.23 us  [shards(): lax.all_to_all(outgoing, 'v', split_axis=0, concat_axis=3, tiled=True)[0]]
    all_to_all x1, waiting for transfers between devices: 0.01 us -> 2.33 us  [shards(): lax.all_to_all(weight_rep, 'u', split_axis=0, concat_axis=0, tiled=True)]
  transfers between devices with their start and end apart: 6 -> 6, of which waited for: 4 -> 5; matrix products, arithmetic and copies ran while one was open for 10% -> 7% of each run, Pallas kernels for 0% -> 0%
where the time goes in v11:
time: 136 us; the launch traced here: 135 us
  waiting for transfers between devices  45.4 us (33%)
  starting transfers between devices  42.9 us (32%)
  local copies, waits for them, and re-layouts  21.7 us (16%)
  other arithmetic  8.05 us (6%)
  Pallas kernels  7.64 us (6%)
  blocking collectives  7 us (5%)
  between operations  1.8 us (1%)
    all_to_all x1, starting transfers between devices, shards(): lax.all_to_all(outgoing, 'v', split_axis=0, concat_axis=3, tiled=True)[0]  18 us
    all_to_all x1, waiting for transfers between devices, shards(): lax.all_to_all(outgoing, 'v', split_axis=0, concat_axis=3, tiled=True)[0]  12.2 us
    all_to_all x1, waiting for transfers between devices, shards(): lax.all_to_all(payload, 'v', split_axis=0, concat_axis=0, tiled=True)  12 us
    ppermute x2, waiting for transfers between devices, from_behind(): return lax.ppermute(block, axis, route)  10.7 us
    all_to_all x1, waiting for transfers between devices, modal_conv(): lax.all_to_all(shared, 'u', split_axis=0, concat_axis=0, tiled=True)  8.18 us
    all_to_all x1, starting transfers between devices, shards(): lax.all_to_all(payload, 'v', split_axis=0, concat_axis=0, tiled=True)  8.13 us
    pallas_call x1, Pallas kernels, modal_conv(): pl.pallas_call(conv_kernel, out_shape=(jax.ShapeDtypeStruct((half, 2 * wi...  7.64 us
    unnamed x1, blocking collectives  7 us
  transfers between devices with their start and end apart: 6, of which 5 were waited for; matrix products, arithmetic and copies ran while one was open for 7% of the time, Pallas kernels for 0%

profile of v11, /device:TPU:1, one launch (start us, length us, event | category | flops | bytes accessed | tf_op | source)
XLA Modules:
  0.0 134.9 jit_solution(18100693879507725093)
XLA Ops:
  0.6 0.7 slice_bitcast_fusion.2
  1.4 0.7 slice_bitcast_fusion
  2.1 5.5 %collective-permute-start = (bf16[3,2,1024]{2,1,0:T(2,128)(2,1)S(1)}, bf16[3,2,1024]{2,1,0:T(2,128)(2,1)S(1)}, u32[]{:S(2)}, u32[]{:S(2)}) collective-permute-start(bf16[3,2,1024]{2,1,0:T(2,128)(2,1)S(1)} %pad_maximum_fusion.5), channel_id=1, source_target_pairs={{0,4},{4,8},{8,12},{12,16},{16,20},{20,24},{24,28},{28,32},{32,36}... | collective-permute-start | bytes 36872 | tf_op jit(solution)/shard_map/ppermute | solution.py:17
  7.6 0.8 fusion.20
  8.4 1.1 copy.84
  9.6 1.1 copy.87
  10.7 1.1 copy.89
  11.9 0.2 copy.91
  12.3 0.2 copy.108
  12.5 0.2 copy.109
  12.7 0.2 maximum_convert_fusion.1
  12.9 0.2 maximum_convert_fusion
  13.2 1.5 %fusion.8 = bf16[128,1024]{0,1:T(8,128)(2,1)S(1)} fusion(f32[130,1024]{0,1:T(8,128)S(1)} %maximum_convert_fusion.1, f32[130,1024]{0,1:T(8,128)S(1)} %maximum_convert_fusion, f32[1024]{0:T(1024)S(1)} %bitcast.102, f32[1024]{0:T(1024)S(1)} %bitcast.103, f32[1024]{0:T(1024)S(1)} %bitcast.99, f32[1024]{0:T(1024)S(1)} %bitcast.100, f32[1024]{0:T(1024)S(1)} %bitcast.101, ...), kind=kLoop, calls=%fused_computation.16 | loop fusion | flops 1572864 | bytes 3432448 | tf_op jit(solution)/shard_map/convert_element_type | solution.py:117
  14.8 0.2 copy.92
  15.0 0.9 pad_maximum_fusion
  15.9 8.1 %all-to-all-start = ((bf16[8,258,128]{2,1,0:T(8,128)(2,1)}), bf16[8,258,128]{2,1,0:T(8,128)(2,1)S(1)}, u32[]{:S(2)}, u32[]{:S(2)}) async-start(bf16[8,258,128]{2,1,0:T(8,128)(2,1)} %pad_maximum_fusion), calls=%async_computation | async-start | bytes 1081344 | tf_op jit(solution)/shard_map/all_to_all | solution.py:127
  24.4 0.2 reshape.178
  24.6 0.2 reshape.176
  25.2 0.6 pad_maximum_fusion.4.w_ref
  25.8 12.0 %all-to-all-done = bf16[8,258,128]{2,1,0:T(8,128)(2,1)S(1)} async-done(((bf16[8,258,128]{2,1,0:T(8,128)(2,1)}), bf16[8,258,128]{2,1,0:T(8,128)(2,1)S(1)}, u32[]{:S(2)}, u32[]{:S(2)}) %all-to-all-start) | async-done | bytes 528416 | tf_op jit(solution)/shard_map/all_to_all | solution.py:127
  38.0 0.8 pad_maximum_fusion.1.g_ref
  38.8 7.6 %shard_map.95 = (f32[512,256]{1,0:T(8,128)}, f32[16,256]{1,0:T(8,128)}) custom-call(f32[512,256]{1,0:T(8,128)} %pad_maximum_fusion.1.g_ref, f32[16,256]{1,0:T(8,128)} %copy-done.3, f32[16,256]{1,0:T(8,128)} %pad_maximum_fusion.4.w_ref), custom_call_target="tpu_custom_call" | custom-call | tf_op jit(solution)/shard_map/pallas_call | solution.py:73
  46.5 0.7 fusion.22
  47.2 0.6 broadcast_in_dim.18
  47.8 6.4 %all-to-all-start.1 = ((f32[8,16,128]{2,1,0:T(8,128)}), f32[8,16,128]{2,1,0:T(8,128)S(1)}, u32[]{:S(2)}, u32[]{:S(2)}) async-start(f32[8,16,128]{2,1,0:T(8,128)} %broadcast_in_dim.18), calls=%async_computation.1 | async-start | bytes 131072 | tf_op jit(solution)/shard_map/all_to_all | solution.py:87
  54.2 0.7 neg.25
  55.1 8.2 %all-to-all-done.1 = f32[8,16,128]{2,1,0:T(8,128)S(1)} async-done(((f32[8,16,128]{2,1,0:T(8,128)}), f32[8,16,128]{2,1,0:T(8,128)S(1)}, u32[]{:S(2)}, u32[]{:S(2)}) %all-to-all-start.1) | async-done | bytes 65568 | tf_op jit(solution)/shard_map/all_to_all | solution.py:87
  63.3 1.1 broadcast_in_dim.19
  64.4 3.6 %all-to-all-start.2 = ((bf16[8,32,16,128]{3,2,1,0:T(8,128)(2,1)}), bf16[8,32,16,128]{3,2,1,0:T(8,128)(2,1)S(1)}, u32[]{:S(2)}, u32[]{:S(2)}) async-start(bf16[8,32,16,128]{3,2,1,0:T(8,128)(2,1)} %broadcast_in_dim.19), calls=%async_computation.2 | async-start | bytes 2097152 | tf_op jit(solution)/shard_map/all_to_all | solution.py:133
  68.2 1.4 %multiply_reduce_fusion = f32[512,256]{1,0:T(8,128)S(1)} fusion(f32[512]{0:T(512)S(1)} %iota_add_fusion, f32[16,256]{1,0:T(8,128)S(1)} %neg.25, f32[16,256]{1,0:T(8,128)S(1)} %maximum_multiply_fusion), kind=kLoop, calls=%fused_computation | loop fusion | flops 6160384 | bytes 559104 | tf_op jit(solution)/shard_map/reduce_sum | solution.py:99
  69.8 0.3 fusion.4
  70.1 1.3 collective-permute-start.1
  71.6 10.7 %collective-permute-done.1 = bf16[16,128]{1,0:T(8,128)(2,1)S(1)} collective-permute-done((bf16[16,128]{1,0:T(8,128)(2,1)S(1)}, bf16[16,128]{1,0:T(8,128)(2,1)S(1)}, u32[]{:S(2)}, u32[]{:S(2)}) %collective-permute-start.1) | collective-permute-done | bytes 4128 | tf_op jit(solution)/shard_map/ppermute | solution.py:17
  82.3 2.3 %all-to-all-done.2 = bf16[8,32,16,128]{3,2,1,0:T(8,128)(2,1)S(1)} async-done(((bf16[8,32,16,128]{3,2,1,0:T(8,128)(2,1)}), bf16[8,32,16,128]{3,2,1,0:T(8,128)(2,1)S(1)}, u32[]{:S(2)}, u32[]{:S(2)}) %all-to-all-start.2) | async-done | bytes 1048608 | tf_op jit(solution)/shard_map/all_to_all | solution.py:133
  84.6 0.2 fusion.16
  85.0 0.2 convolution_bitcast_fusion.1
  85.2 0.2 fusion.1
  85.6 0.2 copy.100
  86.0 0.9 copy.101
  86.9 18.0 %all-to-all-start.3 = ((bf16[8,136,8,1,16]{1,4,2,3,0:T(8,128)(2,1)}), bf16[8,136,8,1,16]{1,4,2,3,0:T(8,128)(2,1)S(1)}, u32[]{:S(2)}, u32[]{:S(2)}) async-start(bf16[8,136,8,1,16]{1,4,2,3,0:T(8,128)(2,1)} %copy.101), calls=%async_computation.3 | async-start | bytes 1048576 | tf_op jit(solution)/shard_map/all_to_all | solution.py:168
  104.9 0.6 dynamic-slice.4
  106.1 12.2 %all-to-all-done.3 = bf16[8,136,8,1,16]{1,4,2,3,0:T(8,128)(2,1)S(1)} async-done(((bf16[8,136,8,1,16]{1,4,2,3,0:T(8,128)(2,1)}), bf16[8,136,8,1,16]{1,4,2,3,0:T(8,128)(2,1)S(1)}, u32[]{:S(2)}, u32[]{:S(2)}) %all-to-all-start.3) | async-done | bytes 278560 | tf_op jit(solution)/shard_map/all_to_all | solution.py:168
  118.4 3.2 %copy.102 = bf16[8,136,8,1,16]{4,0,2,1,3:T(8,128)(2,1)S(1)} copy(bf16[8,136,8,1,16]{1,4,2,3,0:T(8,128)(2,1)S(1)} %all-to-all-done.3) | data formatting | bytes 557056 | tf_op jit(solution)/shard_map/all_to_all | solution.py:168
  121.7 1.5 %slice.212 = bf16[1,128,8,8,1,16]{5,3,4,2,1,0:T(8,128)(2,1)} slice(bf16[1,136,8,8,1,16]{5,3,4,2,1,0:T(8,128)(2,1)S(1)} %bitcast.76), slice={[0:1], [0:128], [0:8], [0:8], [0:1], [0:16]} | slice | bytes 524288 | tf_op jit(solution)/shard_map/slice | solution.py:169
  123.2 3.2 %copy.103 = bf16[1,128,8,8,1,16]{1,5,3,2,4,0:T(8,128)(2,1)S(1)} copy(bf16[1,128,8,8,1,16]{5,3,4,2,1,0:T(8,128)(2,1)} %slice.212) | data formatting | bytes 524288 | tf_op jit(solution)/shard_map/slice | solution.py:169
  126.4 0.9 copy.106
  127.4 7.0 %all-reduce = bf16[8,128]{1,0:T(8,128)(2,1)S(1)} all-reduce(f32[8,128]{1,0:T(8,128)S(1)} %copy.105), channel_id=2, replica_groups=mesh['u'=8,'v'=8,'tp'=4] {'tp'}, use_global_device_ids=true, to_apply=%region_3.4.clone | all-reduce | flops 1024 | bytes 6144
  134.4 0.5 dynamic-slice_convert_fusion
  (61 shorter events, 2.3 us)
Async XLA Ops:
  2.1 9.9 %collective-permute-start = (bf16[3,2,1024]{2,1,0:T(2,128)(2,1)S(1)}, bf16[3,2,1024]{2,1,0:T(2,128)(2,1)S(1)}, u32[]{:S(2)}, u32[]{:S(2)}) collective-permute-start(bf16[3,2,1024]{2,1,0:T(2,128)(2,1)S(1)} %pad_maximum_fusion.5), channel_id=1, source_target_pairs={{0,4},{4,8},{8,12},{12,16},{16,20},{20,24},{24,28},{28,32},{32,36}... | collective-permute-start | bytes 36872 | tf_op jit(solution)/shard_map/ppermute | solution.py:17
  14.7 9.3 %copy-start.2 = (f32[3,3,1024]{2,1,0:T(4,128)S(1)}, f32[3,3,1024]{2,1,0:T(4,128)}, u32[]{:S(2)}) copy-start(f32[3,3,1024]{2,1,0:T(4,128)} %param.11) | copy-start | bytes 110596
  14.7 9.7 %copy-start.4 = (f32[16,1024]{1,0:T(8,128)S(1)}, f32[16,1024]{1,0:T(8,128)}, u32[]{:S(2)}) copy-start(f32[16,1024]{1,0:T(8,128)} %param.12) | copy-start | bytes 196612
  14.7 9.9 %copy-start.5 = (f32[16,1024]{1,0:T(8,128)S(1)}, f32[16,1024]{1,0:T(8,128)}, u32[]{:S(2)}) copy-start(f32[16,1024]{1,0:T(8,128)} %param.13) | copy-start | bytes 196612
  15.9 21.9 %all-to-all-start = ((bf16[8,258,128]{2,1,0:T(8,128)(2,1)}), bf16[8,258,128]{2,1,0:T(8,128)(2,1)S(1)}, u32[]{:S(2)}, u32[]{:S(2)}) async-start(bf16[8,258,128]{2,1,0:T(8,128)(2,1)} %pad_maximum_fusion), calls=%async_computation | async-start | bytes 1081344 | tf_op jit(solution)/shard_map/all_to_all | solution.py:127
  24.9 30.1 %copy-start.7 = (f32[1024]{0:T(1024)S(1)}, f32[1024]{0:T(1024)}, u32[]{:S(2)}) copy-start(f32[1024]{0:T(1024)} %param.14) | copy-start | bytes 12292
  24.9 38.5 %copy-start.1 = (bf16[32,16,128]{2,1,0:T(8,128)(2,1)S(1)}, bf16[32,16,128]{2,1,0:T(8,128)(2,1)}, u32[]{:S(2)}) copy-start(bf16[32,16,128]{2,1,0:T(8,128)(2,1)} %param.15) | copy-start | bytes 393220
  25.2 13.6 %copy-start.3 = (f32[16,256]{1,0:T(8,128)}, f32[16,256]{1,0:T(8,128)S(1)}, u32[]{:S(2)}) copy-start(f32[16,256]{1,0:T(8,128)S(1)} %constant_dynamic-update-slice_fusion.d_ref) | copy-start | bytes 49156
  47.2 21.0 %copy-start.6 = (f32[16,256]{1,0:T(8,128)S(1)}, f32[16,256]{1,0:T(8,128)}, u32[]{:S(2)}) copy-start(f32[16,256]{1,0:T(8,128)} %get-tuple-element.8) | copy-start | bytes 49156
  47.8 15.5 %all-to-all-start.1 = ((f32[8,16,128]{2,1,0:T(8,128)}), f32[8,16,128]{2,1,0:T(8,128)S(1)}, u32[]{:S(2)}, u32[]{:S(2)}) async-start(f32[8,16,128]{2,1,0:T(8,128)} %broadcast_in_dim.18), calls=%async_computation.1 | async-start | bytes 131072 | tf_op jit(solution)/shard_map/all_to_all | solution.py:87
  64.4 20.2 %all-to-all-start.2 = ((bf16[8,32,16,128]{3,2,1,0:T(8,128)(2,1)}), bf16[8,32,16,128]{3,2,1,0:T(8,128)(2,1)S(1)}, u32[]{:S(2)}, u32[]{:S(2)}) async-start(bf16[8,32,16,128]{3,2,1,0:T(8,128)(2,1)} %broadcast_in_dim.19), calls=%async_computation.2 | async-start | bytes 2097152 | tf_op jit(solution)/shard_map/all_to_all | solution.py:133
  68.1 1.6 %copy-start = (f32[512,256]{1,0:T(8,128)S(1)}, f32[512,256]{1,0:T(8,128)}, u32[]{:S(2)}) copy-start(f32[512,256]{1,0:T(8,128)} %get-tuple-element.7) | copy-start | bytes 1572868
  70.1 12.2 %collective-permute-start.1 = (bf16[16,128]{1,0:T(8,128)(2,1)S(1)}, bf16[16,128]{1,0:T(8,128)(2,1)S(1)}, u32[]{:S(2)}, u32[]{:S(2)}) collective-permute-start(bf16[16,128]{1,0:T(8,128)(2,1)S(1)} %slice.210), channel_id=1, source_target_pairs={{32,0},{64,32},{96,64},{128,96},{160,128},{192,160},{224,192},{33,... | collective-permute-start | bytes 12296 | tf_op jit(solution)/shard_map/ppermute | solution.py:17
  85.2 19.7 %copy-start.8 = (u32[256]{0:T(256)S(1)}, u32[256]{0:T(256)}, u32[]{:S(2)}) copy-start(u32[256]{0:T(256)} %constant.43) | copy-start | bytes 3076
  86.9 31.5 %all-to-all-start.3 = ((bf16[8,136,8,1,16]{1,4,2,3,0:T(8,128)(2,1)}), bf16[8,136,8,1,16]{1,4,2,3,0:T(8,128)(2,1)S(1)}, u32[]{:S(2)}, u32[]{:S(2)}) async-start(bf16[8,136,8,1,16]{1,4,2,3,0:T(8,128)(2,1)} %copy.101), calls=%async_computation.3 | async-start | bytes 1048576 | tf_op jit(solution)/shard_map/all_to_all | solution.py:168

commit v12 on v11

--- a/solution.py
+++ b/solution.py
@@ -129,11 +129,7 @@
     query_cols = columns[:, 2 : 2 + tokens].reshape(span, narrow)
     gated = columns[:, 2 + tokens :].reshape(span, narrow)
     head_weight, gated = lax.optimization_barrier((head_weight, gated))
-    weight_rep = jnp.broadcast_to(head_weight[None], (width_u,) + head_weight.shape)
-    weight_cols = lax.all_to_all(weight_rep, "u", split_axis=0, concat_axis=0, tiled=True)
-    weight_cols = jnp.transpose(weight_cols, (1, 0, 2, 3)).reshape(
-        head_weight.shape[0], narrow, head_weight.shape[2]
-    )
+    weight_cols = lax.all_gather(head_weight, "u", axis=1, tiled=True)
     sf = short_filter.reshape(3, 3, width_u, width_v, piece)
     sf = jnp.transpose(sf, (0, 1, 3, 2, 4))
     sf = lax.dynamic_index_in_dim(sf, lax.axis_index("v"), axis=2, keepdims=False)

time: 136 us -> 151 us (1.11)
  starting transfers between devices: 42.9 us -> 27 us
  waiting for transfers between devices: 45.4 us -> 60.5 us
  between operations: 1.8 us -> 15.2 us
  blocking collectives: 7 us -> 9.41 us
  matrix products: 0.44 us -> 2.53 us
  local copies, waits for them, and re-layouts: 21.7 us -> 20.1 us
    all_gather x0 -> x1, waiting for transfers between devices: none -> 21.9 us  [shards(): weight_cols = lax.all_gather(head_weight, 'u', axis=1, tiled=True)]
    all_to_all x1, starting transfers between devices: 18 us -> 5.72 us  [shards(): lax.all_to_all(outgoing, 'v', split_axis=0, concat_axis=3, tiled=True)[0]]
    ppermute x2, waiting for transfers between devices: 10.7 us -> 6.76 us  [from_behind(): return lax.ppermute(block, axis, route)]
    all_to_all x1 -> x0, starting transfers between devices: 3.56 us -> none  [shards(): lax.all_to_all(weight_rep, 'u', split_axis=0, concat_axis=0, tiled=True)]
    all_to_all x1, waiting for transfers between devices: 12.2 us -> 9.81 us  [shards(): lax.all_to_all(outgoing, 'v', split_axis=0, concat_axis=3, tiled=True)[0]]
    unnamed x1, blocking collectives: 7 us -> 9.41 us
    all_to_all x1 -> x0, waiting for transfers between devices: 2.33 us -> none  [shards(): lax.all_to_all(weight_rep, 'u', split_axis=0, concat_axis=0, tiled=True)]
    unnamed x27 -> x23, local copies, waits for them, and re-layouts: 5.39 us -> 3.47 us
  transfers between devices with their start and end apart: 6 -> 6, of which waited for: 5 -> 5; matrix products, arithmetic and copies ran while one was open for 7% -> 8% of each run, Pallas kernels for 0% -> 5%
where the time goes in v12:
time: 151 us; the launch traced here: 150 us
  waiting for transfers between devices  60.5 us (40%)
  starting transfers between devices  27 us (18%)
  local copies, waits for them, and re-layouts  20.1 us (13%)
  between operations  15.2 us (10%)
  blocking collectives  9.41 us (6%)
  other arithmetic  8.04 us (5%)
  Pallas kernels  7.59 us (5%)
  matrix products  2.53 us (2%)
    all_gather x1, waiting for transfers between devices, shards(): weight_cols = lax.all_gather(head_weight, 'u', axis=1, tiled=True)  21.9 us
    all_to_all x1, waiting for transfers between devices, shards(): lax.all_to_all(payload, 'v', split_axis=0, concat_axis=0, tiled=True)  13 us
    all_to_all x1, waiting for transfers between devices, shards(): lax.all_to_all(outgoing, 'v', split_axis=0, concat_axis=3, tiled=True)[0]  9.81 us
    unnamed x1, blocking collectives  9.41 us
    all_to_all x1, waiting for transfers between devices, modal_conv(): lax.all_to_all(shared, 'u', split_axis=0, concat_axis=0, tiled=True)  9.03 us
    all_to_all x1, starting transfers between devices, shards(): lax.all_to_all(payload, 'v', split_axis=0, concat_axis=0, tiled=True)  8.13 us
    pallas_call x1, Pallas kernels, modal_conv(): pl.pallas_call(conv_kernel, out_shape=(jax.ShapeDtypeStruct((half, 2 * wi...  7.59 us
    ppermute x2, starting transfers between devices, from_behind(): return lax.ppermute(block, axis, route)  6.76 us
  transfers between devices with their start and end apart: 6, of which 5 were waited for; matrix products, arithmetic and copies ran while one was open for 8% of the time, Pallas kernels for 5%

profile of v12, /device:TPU:1, one launch (start us, length us, event | category | flops | bytes accessed | tf_op | source)
XLA Modules:
  0.0 150.4 jit_solution(17228279267384539044)
XLA Ops:
  7.2 0.8 slice_bitcast_fusion.2
  8.0 0.7 slice_bitcast_fusion
  8.8 5.5 %collective-permute-start = (bf16[3,2,1024]{2,1,0:T(2,128)(2,1)S(1)}, bf16[3,2,1024]{2,1,0:T(2,128)(2,1)S(1)}, u32[]{:S(2)}, u32[]{:S(2)}) collective-permute-start(bf16[3,2,1024]{2,1,0:T(2,128)(2,1)S(1)} %pad_maximum_fusion.5), channel_id=1, source_target_pairs={{0,4},{4,8},{8,12},{12,16},{16,20},{20,24},{24,28},{28,32},{32,36}... | collective-permute-start | bytes 36872 | tf_op jit(solution)/shard_map/ppermute | solution.py:17
  14.3 0.8 fusion.21
  15.1 1.0 reshape.174
  16.2 1.0 reshape.172
  17.3 1.1 copy.80
  18.4 0.2 copy.83
  18.6 0.2 copy.85
  18.8 0.1 reshape.163
  19.2 0.2 copy.87
  20.0 0.2 copy.102
  20.2 0.2 copy.103
  20.4 0.2 maximum_convert_fusion.1
  20.6 0.2 maximum_convert_fusion
  20.9 1.5 %fusion.10 = bf16[128,1024]{0,1:T(8,128)(2,1)S(1)} fusion(f32[130,1024]{0,1:T(8,128)S(1)} %maximum_convert_fusion.1, f32[130,1024]{0,1:T(8,128)S(1)} %maximum_convert_fusion, f32[1024]{0:T(1024)S(1)} %bitcast.94, f32[1024]{0:T(1024)S(1)} %bitcast.95, f32[1024]{0:T(1024)S(1)} %bitcast.91, f32[1024]{0:T(1024)S(1)} %bitcast.92, f32[1024]{0:T(1024)S(1)} %bitcast.93, ...), kind=kLoop, calls=%fused_computation.18 | loop fusion | flops 1572864 | bytes 3432448 | tf_op jit(solution)/shard_map/convert_element_type | solution.py:117
  22.4 0.2 copy.88
  22.6 1.0 pad_maximum_fusion
  23.6 8.1 %all-to-all-start = ((bf16[8,258,128]{2,1,0:T(8,128)(2,1)}), bf16[8,258,128]{2,1,0:T(8,128)(2,1)S(1)}, u32[]{:S(2)}, u32[]{:S(2)}) async-start(bf16[8,258,128]{2,1,0:T(8,128)(2,1)} %pad_maximum_fusion), calls=%async_computation | async-start | bytes 1081344 | tf_op jit(solution)/shard_map/all_to_all | solution.py:127
  31.9 0.6 pad_maximum_fusion.4.w_ref
  32.5 13.0 %all-to-all-done = bf16[8,258,128]{2,1,0:T(8,128)(2,1)S(1)} async-done(((bf16[8,258,128]{2,1,0:T(8,128)(2,1)}), bf16[8,258,128]{2,1,0:T(8,128)(2,1)S(1)}, u32[]{:S(2)}, u32[]{:S(2)}) %all-to-all-start) | async-done | bytes 528416 | tf_op jit(solution)/shard_map/all_to_all | solution.py:127
  45.5 0.2 fusion.18
  45.7 0.9 pad_maximum_fusion.1.g_ref
  46.6 7.6 %shard_map.95 = (f32[512,256]{1,0:T(8,128)}, f32[16,256]{1,0:T(8,128)}) custom-call(f32[512,256]{1,0:T(8,128)} %pad_maximum_fusion.1.g_ref, f32[16,256]{1,0:T(8,128)} %copy-done.4, f32[16,256]{1,0:T(8,128)} %pad_maximum_fusion.4.w_ref), custom_call_target="tpu_custom_call" | custom-call | tf_op jit(solution)/shard_map/pallas_call | solution.py:73
  54.1 0.7 fusion.23
  54.9 0.6 broadcast_in_dim.16
  55.5 6.4 %all-to-all-start.1 = ((f32[8,16,128]{2,1,0:T(8,128)}), f32[8,16,128]{2,1,0:T(8,128)S(1)}, u32[]{:S(2)}, u32[]{:S(2)}) async-start(f32[8,16,128]{2,1,0:T(8,128)} %broadcast_in_dim.16), calls=%async_computation.1 | async-start | bytes 131072 | tf_op jit(solution)/shard_map/all_to_all | solution.py:87
  62.0 9.0 %all-to-all-done.1 = f32[8,16,128]{2,1,0:T(8,128)S(1)} async-done(((f32[8,16,128]{2,1,0:T(8,128)}), f32[8,16,128]{2,1,0:T(8,128)S(1)}, u32[]{:S(2)}, u32[]{:S(2)}) %all-to-all-start.1) | async-done | bytes 65568 | tf_op jit(solution)/shard_map/all_to_all | solution.py:87
  71.1 0.7 multiply_add_fusion
  71.8 1.4 multiply_reduce_fusion
  73.4 0.3 fusion.6
  73.7 1.3 collective-permute-start.1
  75.0 0.1 copy.91
  75.2 6.8 %collective-permute-done.1 = bf16[16,128]{1,0:T(8,128)(2,1)S(1)} collective-permute-done((bf16[16,128]{1,0:T(8,128)(2,1)S(1)}, bf16[16,128]{1,0:T(8,128)(2,1)S(1)}, u32[]{:S(2)}, u32[]{:S(2)}) %collective-permute-start.1) | collective-permute-done | bytes 4128 | tf_op jit(solution)/shard_map/ppermute | solution.py:17
  81.9 21.9 %all-gather.2.cloned.1.call-done = bf16[32,128,128]{2,1,0:T(8,128)(2,1)} async-done(((bf16[32,16,128]{2,1,0:T(8,128)(2,1)}), bf16[32,128,128]{2,1,0:T(8,128)(2,1)}) %all-gather.2.cloned.1.call-update) | async-done | bytes 1048592 | tf_op jit(solution)/shard_map/all_gather | solution.py:132
  103.9 1.3 convolution_bitcast_fusion.1
  105.2 1.3 fusion.1
  106.6 0.2 copy.94
  106.9 0.9 copy.95
  107.8 5.7 %all-to-all-start.2 = ((bf16[8,136,8,1,16]{1,4,2,3,0:T(8,128)(2,1)}), bf16[8,136,8,1,16]{1,4,2,3,0:T(8,128)(2,1)S(1)}, u32[]{:S(2)}, u32[]{:S(2)}) async-start(bf16[8,136,8,1,16]{1,4,2,3,0:T(8,128)(2,1)} %copy.95), calls=%async_computation.2 | async-start | bytes 1048576 | tf_op jit(solution)/shard_map/all_to_all | solution.py:164
  113.5 0.6 dynamic-slice.4
  114.8 9.8 %all-to-all-done.2 = bf16[8,136,8,1,16]{1,4,2,3,0:T(8,128)(2,1)S(1)} async-done(((bf16[8,136,8,1,16]{1,4,2,3,0:T(8,128)(2,1)}), bf16[8,136,8,1,16]{1,4,2,3,0:T(8,128)(2,1)S(1)}, u32[]{:S(2)}, u32[]{:S(2)}) %all-to-all-start.2) | async-done | bytes 278560 | tf_op jit(solution)/shard_map/all_to_all | solution.py:164
  124.6 3.2 %copy.96 = bf16[8,136,8,1,16]{4,0,2,1,3:T(8,128)(2,1)S(1)} copy(bf16[8,136,8,1,16]{1,4,2,3,0:T(8,128)(2,1)S(1)} %all-to-all-done.2) | data formatting | bytes 557056 | tf_op jit(solution)/shard_map/all_to_all | solution.py:164
  127.9 1.5 slice.204
  129.4 3.2 %copy.97 = bf16[1,128,8,8,1,16]{1,5,3,2,4,0:T(8,128)(2,1)S(1)} copy(bf16[1,128,8,8,1,16]{5,3,4,2,1,0:T(8,128)(2,1)} %slice.204) | data formatting | bytes 524288 | tf_op jit(solution)/shard_map/slice | solution.py:165
  132.6 0.9 copy.100
  133.6 9.4 %all-reduce = bf16[8,128]{1,0:T(8,128)(2,1)S(1)} all-reduce(f32[8,128]{1,0:T(8,128)S(1)} %copy.99), channel_id=2, replica_groups=mesh['u'=8,'v'=8,'tp'=4] {'tp'}, use_global_device_ids=true, to_apply=%region_3.4.clone | all-reduce | flops 1024 | bytes 6144
  143.0 0.5 dynamic-slice_convert_fusion
  (54 shorter events, 1.9 us)
Async XLA Ops:
  7.2 11.5 %copy-start.2 = (bf16[128,1024]{1,0:T(8,128)(2,1)S(1)}, bf16[128,1024]{1,0:T(8,128)(2,1)}, u32[]{:S(2)}) copy-start(bf16[128,1024]{1,0:T(8,128)(2,1)} %param.10) | copy-start | bytes 786436
  7.2 11.3 %copy-start.1 = (bf16[128,1024]{1,0:T(8,128)(2,1)S(1)}, bf16[128,1024]{1,0:T(8,128)(2,1)}, u32[]{:S(2)}) copy-start(bf16[128,1024]{1,0:T(8,128)(2,1)} %param.9) | copy-start | bytes 786436
  7.2 11.6 %copy-start.3 = (f32[3,3,1024]{2,1,0:T(4,128)S(1)}, f32[3,3,1024]{2,1,0:T(4,128)}, u32[]{:S(2)}) copy-start(f32[3,3,1024]{2,1,0:T(4,128)} %param.11) | copy-start | bytes 110596
  7.2 11.8 %copy-start.5 = (f32[1024]{0:T(1024)S(1)}, f32[1024]{0:T(1024)}, u32[]{:S(2)}) copy-start(f32[1024]{0:T(1024)} %param.14) | copy-start | bytes 12292
  8.8 11.0 %collective-permute-start = (bf16[3,2,1024]{2,1,0:T(2,128)(2,1)S(1)}, bf16[3,2,1024]{2,1,0:T(2,128)(2,1)S(1)}, u32[]{:S(2)}, u32[]{:S(2)}) collective-permute-start(bf16[3,2,1024]{2,1,0:T(2,128)(2,1)S(1)} %pad_maximum_fusion.5), channel_id=1, source_target_pairs={{0,4},{4,8},{8,12},{12,16},{16,20},{20,24},{24,28},{28,32},{32,36}... | collective-permute-start | bytes 36872 | tf_op jit(solution)/shard_map/ppermute | solution.py:17
  23.6 21.9 %all-to-all-start = ((bf16[8,258,128]{2,1,0:T(8,128)(2,1)}), bf16[8,258,128]{2,1,0:T(8,128)(2,1)S(1)}, u32[]{:S(2)}, u32[]{:S(2)}) async-start(bf16[8,258,128]{2,1,0:T(8,128)(2,1)} %pad_maximum_fusion), calls=%async_computation | async-start | bytes 1081344 | tf_op jit(solution)/shard_map/all_to_all | solution.py:127
  31.7 72.1 %all-gather.2.cloned.1.call-start = ((), (), s32[]{:S(2)}) async-start(), calls=%async_computation.3 | async-start | bytes 1179648 | tf_op jit(solution)/shard_map/all_gather | solution.py:132
  31.8 14.7 %copy-start.4 = (f32[16,256]{1,0:T(8,128)}, f32[16,256]{1,0:T(8,128)S(1)}, u32[]{:S(2)}) copy-start(f32[16,256]{1,0:T(8,128)S(1)} %constant_dynamic-update-slice_fusion.d_ref) | copy-start | bytes 49156
  55.5 15.5 %all-to-all-start.1 = ((f32[8,16,128]{2,1,0:T(8,128)}), f32[8,16,128]{2,1,0:T(8,128)S(1)}, u32[]{:S(2)}, u32[]{:S(2)}) async-start(f32[8,16,128]{2,1,0:T(8,128)} %broadcast_in_dim.16), calls=%async_computation.1 | async-start | bytes 131072 | tf_op jit(solution)/shard_map/all_to_all | solution.py:87
  62.0 11.3 %copy-start = (f32[512,256]{1,0:T(8,128)S(1)}, f32[512,256]{1,0:T(8,128)}, u32[]{:S(2)}) copy-start(f32[512,256]{1,0:T(8,128)} %get-tuple-element.7) | copy-start | bytes 1572868
  73.7 8.3 %collective-permute-start.1 = (bf16[16,128]{1,0:T(8,128)(2,1)S(1)}, bf16[16,128]{1,0:T(8,128)(2,1)S(1)}, u32[]{:S(2)}, u32[]{:S(2)}) collective-permute-start(bf16[16,128]{1,0:T(8,128)(2,1)S(1)} %slice.202), channel_id=1, source_target_pairs={{32,0},{64,32},{96,64},{128,96},{160,128},{192,160},{224,192},{33,... | collective-permute-start | bytes 12296 | tf_op jit(solution)/shard_map/ppermute | solution.py:17
  105.1 8.4 %copy-start.6 = (u32[256]{0:T(256)S(1)}, u32[256]{0:T(256)}, u32[]{:S(2)}) copy-start(u32[256]{0:T(256)} %constant.43) | copy-start | bytes 3076
  107.8 16.8 %all-to-all-start.2 = ((bf16[8,136,8,1,16]{1,4,2,3,0:T(8,128)(2,1)}), bf16[8,136,8,1,16]{1,4,2,3,0:T(8,128)(2,1)S(1)}, u32[]{:S(2)}, u32[]{:S(2)}) async-start(bf16[8,136,8,1,16]{1,4,2,3,0:T(8,128)(2,1)} %copy.95), calls=%async_computation.2 | async-start | bytes 1048576 | tf_op jit(solution)/shard_map/all_to_all | solution.py:164
Sparse Core Ops, SparseCore 0:
  45.8 58.0 all-gather.1

commit v13 on v9

--- a/solution.py
+++ b/solution.py
@@ -63,38 +63,44 @@
 
 def modal_conv(gated, residues, decays):
     span, width = gated.shape
-    half = span // 2
+    parts = max(1, min(128 // width, span // CHUNK))
+    seg = span // parts
     groups = lax.axis_size("u")
     weight = residues * jnp.sqrt(-jnp.expm1(-2.0 * decays))
     g = gated.astype(jnp.float32)
-    packed = jnp.concatenate([g[:half], g[half:]], axis=1)
-    decays2 = jnp.concatenate([decays, decays], axis=1)
-    weight2 = jnp.concatenate([weight, weight], axis=1)
+    packed = jnp.concatenate([g[s * seg : (s + 1) * seg] for s in range(parts)], axis=1)
+    decays_p = jnp.concatenate([decays] * parts, axis=1)
+    weight_p = jnp.concatenate([weight] * parts, axis=1)
     local, ends = pl.pallas_call(
         conv_kernel,
         out_shape=(
-            jax.ShapeDtypeStruct((half, 2 * width), jnp.float32),
-            jax.ShapeDtypeStruct(decays2.shape, jnp.float32),
+            jax.ShapeDtypeStruct((seg, parts * width), jnp.float32),
+            jax.ShapeDtypeStruct(decays_p.shape, jnp.float32),
         ),
         interpret=INTERPRET,
-    )(packed, decays2, weight2)
-    hop_half = jnp.exp(-decays * float(half))
-    first_end, second_end = ends[:, :width], ends[:, width:]
-    total = hop_half * first_end + second_end
+    )(packed, decays_p, weight_p)
+    ends = ends.reshape(decays.shape[0], parts, width)
+    index = jnp.arange(parts)
+    lag = index[:, None] - 1 - index[None, :]
+    gap = (float(seg) * jnp.maximum(lag, 0).astype(jnp.float32))[None, :, :, None]
+    table = jnp.where((lag >= 0)[None, :, :, None], jnp.exp(-decays[:, None, None, :] * gap), 0.0)
+    inner = jnp.sum(table * ends[:, None, :, :], axis=2)
+    last = (float(seg) * (parts - 1 - index).astype(jnp.float32))[None, :, None]
+    total = jnp.sum(jnp.exp(-decays[:, None, :] * last) * ends, axis=1)
     outer = None
     for m in range(1, groups):
         term = from_behind(total, "u", m)
         if m > 1:
             term = jnp.exp(-decays * float(span * (m - 1))) * term
         outer = term if outer is None else outer + term
-    if outer is None:
-        entry = jnp.concatenate([jnp.zeros_like(first_end), first_end], axis=1)
-    else:
-        entry = jnp.concatenate([outer, hop_half * outer + first_end], axis=1)
-    steps = jnp.arange(half, dtype=jnp.float32)
-    after = jnp.exp(-decays2[:, None, :] * (steps[None, :, None] + 1.0))
-    joined = local + jnp.sum((weight2 * entry)[:, None, :] * after, axis=0)
-    return jnp.concatenate([joined[:, :width], joined[:, width:]], axis=0)
+    if outer is not None:
+        lead = (float(seg) * index.astype(jnp.float32))[None, :, None]
+        inner = inner + jnp.exp(-decays[:, None, :] * lead) * outer[:, None, :]
+    entry = inner.reshape(decays.shape[0], parts * width)
+    steps = jnp.arange(seg, dtype=jnp.float32)
+    after = jnp.exp(-decays_p[:, None, :] * (steps[None, :, None] + 1.0))
+    joined = local + jnp.sum((weight_p * entry)[:, None, :] * after, axis=0)
+    return jnp.concatenate([joined[:, s * width : (s + 1) * width] for s in range(parts)], axis=0)
 
 
 def shards(
@@ -146,7 +152,10 @@
     gain = pick(skip_gain[None])[0]
     carried = (convolved + gain * gated.astype(jnp.float32)).astype(jnp.bfloat16)
     op_cols = (query_short * carried.astype(jnp.float32)).astype(jnp.bfloat16)
-    rim_rows = from_behind(op_cols[:STRIDE], "u", -1)
+    if width_u > 1:
+        rim_rows = from_behind(op_cols[:STRIDE], "u", -1)
+    else:
+        rim_rows = jnp.zeros_like(op_cols[:STRIDE])
     extended = jnp.concatenate([op_cols, rim_rows], axis=0)
     rows = span // STRIDE
     early_rows = extended[:span].reshape(rows, STRIDE, narrow)
@@ -174,7 +183,7 @@
 
 def solution(mesh):
     seq_size, tp_size = mesh.devices.shape
-    width_u = 4 if seq_size % 4 == 0 else 1
+    width_u = 1
     split = jax.sharding.Mesh(
         mesh.devices.reshape(width_u, seq_size // width_u, tp_size), ("u", "v", "tp")
     )

time: 112 us -> 129 us (1.15)
  local copies, waits for them, and re-layouts: 13.5 us -> 37.3 us
  starting transfers between devices: 34.8 us -> 25.2 us
  other arithmetic: 9.16 us -> 14.1 us
    ppermute x5 -> x1, starting transfers between devices: 15.8 us -> 5.47 us  [from_behind(): return lax.ppermute(block, axis, route)]
    reshape x4 -> x6, local copies, waits for them, and re-layouts: 0.39 us -> 8.01 us  [the longest x1 2.99 us: shards(): early_rows = extended[:span].reshape(rows, STRIDE, narrow)]
    unnamed x26 -> x45, local copies, waits for them, and re-layouts: 4.84 us -> 10.6 us
    concatenate x1 -> x4, local copies, waits for them, and re-layouts: 0.95 us -> 5.19 us  [the longest x1 4.21 us: modal_conv(): jnp.concatenate([g[s * seg:(s + 1) * seg] for s in range(parts)], axis=1)]
    all_to_all x1, starting transfers between devices: 8.85 us -> 12.4 us  [shards(): lax.all_to_all(payload, 'v', split_axis=0, concat_axis=0, tiled=True)]
    all_to_all x1 -> x0, starting transfers between devices: 3.47 us -> none  [shards(): lax.all_to_all(weight_rep, 'u', split_axis=0, concat_axis=0, tiled=True)]
    ppermute x5 -> x1, waiting for transfers between devices: 2.81 us -> 0.01 us  [from_behind(): return lax.ppermute(block, axis, route)]
    convert_element_type x3, other arithmetic: 0.61 us -> 2.46 us  [short_pass(): joined = jnp.concatenate([before, rows], axis=0).astype(jnp.float32)]
  transfers between devices with their start and end apart: 8 -> 3, of which waited for: 3 -> 2; matrix products, arithmetic and copies ran while one was open for 9% -> 10% of each run, Pallas kernels for 0% -> 0%
where the time goes in v13:
time: 129 us; the launch traced here: 128 us
  local copies, waits for them, and re-layouts  37.3 us (29%)
  waiting for transfers between devices  33.8 us (26%)
  starting transfers between devices  25.2 us (20%)
  other arithmetic  14.1 us (11%)
  blocking collectives  8.32 us (6%)
  Pallas kernels  7.03 us (5%)
  between operations  1.72 us (1%)
    all_to_all x1, waiting for transfers between devices, shards(): lax.all_to_all(payload, 'v', split_axis=0, concat_axis=0, tiled=True)  18.2 us
    all_to_all x1, waiting for transfers between devices, shards(): lax.all_to_all(outgoing, 'v', split_axis=0, concat_axis=3, tiled=True)[0]  15.6 us
    all_to_all x1, starting transfers between devices, shards(): lax.all_to_all(payload, 'v', split_axis=0, concat_axis=0, tiled=True)  12.4 us
    unnamed x45, local copies, waits for them, and re-layouts  10.6 us
    unnamed x1, blocking collectives  8.32 us
    all_to_all x1, starting transfers between devices, shards(): lax.all_to_all(outgoing, 'v', split_axis=0, concat_axis=3, tiled=True)[0]  7.32 us
    pallas_call x1, Pallas kernels, modal_conv(): pl.pallas_call(conv_kernel, out_shape=(jax.ShapeDtypeStruct((seg, parts *...  7.03 us
    ppermute x1, starting transfers between devices, from_behind(): return lax.ppermute(block, axis, route)  5.47 us
  transfers between devices with their start and end apart: 3, of which 2 were waited for; matrix products, arithmetic and copies ran while one was open for 10% of the time, Pallas kernels for 0%

profile of v13, /device:TPU:1, one launch (start us, length us, event | category | flops | bytes accessed | tf_op | source)
XLA Modules:
  0.0 128.0 jit_solution(17297626613758636292)
XLA Ops:
  0.6 0.7 slice_bitcast_fusion.2
  1.4 0.7 slice_bitcast_fusion
  2.1 5.5 %collective-permute-start = (bf16[3,2,1024]{2,1,0:T(2,128)(2,1)S(1)}, bf16[3,2,1024]{2,1,0:T(2,128)(2,1)S(1)}, u32[]{:S(2)}, u32[]{:S(2)}) collective-permute-start(bf16[3,2,1024]{2,1,0:T(2,128)(2,1)S(1)} %pad_maximum_fusion.2), channel_id=1, source_target_pairs={{0,4},{4,8},{8,12},{12,16},{16,20},{20,24},{24,28},{28,32},{32,36}... | collective-permute-start | bytes 36872 | tf_op jit(solution)/shard_map/ppermute | solution.py:17
  7.6 0.8 fusion.19
  8.5 1.0 reshape.284
  9.5 1.0 reshape.286
  10.6 1.1 copy.95
  11.7 1.1 copy.97
  12.9 1.1 copy.93
  14.0 0.9 transpose_reshape.3
  15.5 0.5 copy.98
  16.5 1.5 %fusion.8 = bf16[128,1024]{0,1:T(8,128)(2,1)S(1)} fusion(f32[130,1024]{0,1:T(8,128)S(1)} %maximum_convert_fusion.2, f32[130,1024]{0,1:T(8,128)S(1)} %maximum_convert_fusion.1, f32[1024]{0:T(1024)S(1)} %bitcast.91, f32[1024]{0:T(1024)S(1)} %bitcast.92, f32[1024]{0:T(1024)S(1)} %bitcast.88, f32[1024]{0:T(1024)S(1)} %bitcast.89, f32[1024]{0:T(1024)S(1)} %bitcast.90, ...), kind=kLoop, calls=%fused_computation.27 | loop fusion | flops 1572864 | bytes 3432448 | tf_op jit(solution)/shard_map/convert_element_type | solution.py:120
  18.0 1.3 %pad_maximum_fusion = bf16[64,258,16]{1,2,0:T(8,128)(2,1)} fusion(bf16[64,128,16]{1,2,0:T(8,128)(2,1)S(1)} %bitcast.74, bf16[64,128,16]{1,2,0:T(8,128)(2,1)S(1)} %bitcast.71, bf16[64,2,16]{1,2,0:T(8,128)(2,1)S(1)} %copy.98), kind=kLoop, calls=%fused_computation.15 | loop fusion | flops 1585152 | bytes 1056768 | tf_op jit(solution)/shard_map/concatenate | solution.py:126
  19.3 12.4 %all-to-all-start = ((bf16[64,258,16]{1,2,0:T(8,128)(2,1)}), bf16[64,258,16]{1,2,0:T(8,128)(2,1)S(1)}, u32[]{:S(2)}, u32[]{:S(2)}) async-start(bf16[64,258,16]{1,2,0:T(8,128)(2,1)} %pad_maximum_fusion), calls=%async_computation | async-start | bytes 1572864 | tf_op jit(solution)/shard_map/all_to_all | solution.py:130
  31.9 0.7 concatenate.44.w_ref
  32.5 0.6 neg.25
  33.2 0.5 fusion.15
  33.7 0.6 iota_add_fusion
  34.3 0.6 fusion.14
  35.0 0.6 slice_bitcast_fusion.5
  35.6 0.7 convert_multiply_fusion
  36.2 18.2 %all-to-all-done = bf16[64,258,16]{1,2,0:T(8,128)(2,1)S(1)} async-done(((bf16[64,258,16]{1,2,0:T(8,128)(2,1)}), bf16[64,258,16]{1,2,0:T(8,128)(2,1)S(1)}, u32[]{:S(2)}, u32[]{:S(2)}) %all-to-all-start) | async-done | bytes 528416 | tf_op jit(solution)/shard_map/all_to_all | solution.py:130
  54.5 0.9 fusion.18
  55.4 1.0 copy.102
  56.4 1.8 %fusion.17 = (f32[1024,16]{1,0:T(8,128)S(1)}, f32[1024,16]{1,0:T(8,128)}, f32[1024,16]{1,0:T(8,128)}, f32[1024,16]{1,0:T(8,128)}, f32[1024,16]{1,0:T(8,128)}, /*...) fusion(bf16[8192,16]{1,0:T(8,128)(2,1)S(1)} %bitcast.62), kind=kLoop, calls=%fused_computation.64 | loop fusion | bytes 1048576 | tf_op jit(solution)/shard_map/slice | solution.py:71
  58.2 4.2 %concatenate.42.g_ref = f32[1024,128]{1,0:T(8,128)} concatenate(f32[1024,16]{1,0:T(8,128)} %get-tuple-element.27, f32[1024,16]{1,0:T(8,128)} %get-tuple-element.26, f32[1024,16]{1,0:T(8,128)} %get-tuple-element.25, f32[1024,16]{1,0:T(8,128)} %get-tuple-element.24, f32[1024,16]{1,0:T(8,128)} %get-tuple-element.23, f32[1024,16]{1,0:T(8,128)} %get-tuple-element.22, ...), dimensions={1} | concatenate | bytes 1048576 | tf_op jit(solution)/shard_map/concatenate | solution.py:71
  62.4 7.0 %shard_map.95 = (f32[1024,128]{1,0:T(8,128)}, f32[16,128]{1,0:T(8,128)}) custom-call(f32[1024,128]{1,0:T(8,128)} %concatenate.42.g_ref, f32[16,128]{1,0:T(8,128)} %copy-done.8, f32[16,128]{1,0:T(8,128)} %concatenate.44.w_ref), custom_call_target="tpu_custom_call" | custom-call | tf_op jit(solution)/shard_map/pallas_call | solution.py:74
  69.5 0.8 mul.233
  70.3 1.0 multiply_reduce_fusion.1
  71.4 2.2 %multiply_reduce_fusion = f32[1024,128]{1,0:T(8,128)S(1)} fusion(f32[1024]{0:T(1024)} %iota_add_fusion, f32[16,128]{1,0:T(8,128)} %neg.25, f32[16,128]{1,0:T(8,128)S(1)} %mul.236), kind=kLoop, calls=%fused_computation | loop fusion | flops 6160384 | bytes 544768 | tf_op jit(solution)/shard_map/reduce_sum | solution.py:102
  75.1 2.0 %copy-done.2 = f32[8192,16]{1,0:T(8,128)} copy-done((f32[8192,16]{1,0:T(8,128)}, f32[8192,16]{1,0:T(8,128)S(1)}, u32[]{:S(2)}) %copy-start.2) | copy-done | bytes 524312
  77.1 1.8 %copy.111 = bf16[64,128,16]{2,1,0:T(8,128)(2,1)} copy(bf16[64,128,16]{1,2,0:T(8,128)(2,1)S(1)} %copy-done.4) | data formatting | bytes 524288 | tf_op jit(solution)/shard_map/reshape | solution.py:132
  79.0 2.0 %maximum_convert_fusion = f32[8194,16]{1,0:T(8,128)S(1)} fusion(bf16[8192,16]{1,0:T(8,128)(2,1)} %bitcast.67, bf16[2,16]{1,0:T(2,128)(2,1)S(1)} %bitcast.94), kind=kLoop, calls=%fused_computation.10 | loop fusion | flops 524416 | bytes 786624 | tf_op jit(solution)/shard_map/convert_element_type | solution.py:21
  81.0 0.8 copy-done.3
  81.8 1.9 %fusion.2 = bf16[8192,16]{1,0:T(8,128)(2,1)S(1)} fusion(f32[8194,16]{1,0:T(8,128)S(1)} %maximum_convert_fusion, f32[8192,16]{1,0:T(8,128)S(1)} %copy-done.3, f32[16]{0:T(128)S(1)} %copy-done.13, f32[16]{0:T(128)S(1)} %copy-done.11, f32[16]{0:T(128)S(1)} %copy-done.12, f32[16]{0:T(128)S(1)} %copy-done.10, bf16[8192,16]{1,0:T(8,128)(2,1)S(1)} %bitcast.63), kind=kLoop, calls=%fused_computation.4 | loop fusion | flops 1572864 | bytes 2621696 | tf_op jit(solution)/shard_map/convert_element_type | solution.py:154
  83.8 1.3 %copy-done = bf16[8192,16]{1,0:T(8,128)(2,1)} copy-done((bf16[8192,16]{1,0:T(8,128)(2,1)}, bf16[8192,16]{1,0:T(8,128)(2,1)S(1)}, u32[]{:S(2)}) %copy-start) | copy-done | bytes 262168
  85.1 0.4 pad_slice_fusion
  85.5 1.9 %copy.106 = bf16[512,16,16]{0,1,2:T(8,128)(2,1)S(1)} copy(bf16[512,16,16]{2,1,0:T(8,128)(2,1)S(1)} %bitcast.66) | data formatting | bytes 524288 | tf_op jit(solution)/shard_map/reshape | solution.py:162
  87.5 3.0 %copy.104 = bf16[512,16,16]{0,1,2:T(8,128)(2,1)S(1)} copy(bf16[512,16,16]{2,1,0:T(8,128)(2,1)} %bitcast.64) | data formatting | bytes 524288 | tf_op jit(solution)/shard_map/reshape | solution.py:161
  91.0 0.7 reshape.292
  92.1 0.8 copy.107
  92.9 0.9 pad_maximum_fusion.1
  93.8 7.3 %all-to-all-start.1 = ((bf16[64,192,1,1,16]{1,4,3,2,0:T(8,128)(2,1)}), bf16[64,192,1,1,16]{1,4,3,2,0:T(8,128)(2,1)S(1)}, u32[]{:S(2)}, u32[]{:S(2)}) async-start(bf16[64,192,1,1,16]{1,4,3,2,0:T(8,128)(2,1)} %pad_maximum_fusion.1), calls=%async_computation.1 | async-start | bytes 1048576 | tf_op jit(solution)/shard_map/all_to_all | solution.py:174
  101.2 0.6 dynamic-slice
  102.4 15.6 %all-to-all-done.1 = bf16[64,192,1,1,16]{1,4,3,2,0:T(8,128)(2,1)S(1)} async-done(((bf16[64,192,1,1,16]{1,4,3,2,0:T(8,128)(2,1)}), bf16[64,192,1,1,16]{1,4,3,2,0:T(8,128)(2,1)S(1)}, u32[]{:S(2)}, u32[]{:S(2)}) %all-to-all-start.1) | async-done | bytes 393248 | tf_op jit(solution)/shard_map/all_to_all | solution.py:174
  118.1 0.8 copy.110
  119.1 8.3 %all-reduce.1 = bf16[8,128]{1,0:T(8,128)(2,1)S(1)} all-reduce(f32[8,128]{1,0:T(8,128)S(1)} %reduce_sum.32), channel_id=2, replica_groups=mesh['seq'=64,'tp'=4] {'tp'}, use_global_device_ids=true, to_apply=%region_3.4.clone | all-reduce | flops 1024 | bytes 6144
  127.4 0.5 dynamic-slice_convert_fusion
  (63 shorter events, 4.2 us)
Async XLA Ops:
  2.1 12.8 %collective-permute-start = (bf16[3,2,1024]{2,1,0:T(2,128)(2,1)S(1)}, bf16[3,2,1024]{2,1,0:T(2,128)(2,1)S(1)}, u32[]{:S(2)}, u32[]{:S(2)}) collective-permute-start(bf16[3,2,1024]{2,1,0:T(2,128)(2,1)S(1)} %pad_maximum_fusion.2), channel_id=1, source_target_pairs={{0,4},{4,8},{8,12},{12,16},{16,20},{20,24},{24,28},{28,32},{32,36}... | collective-permute-start | bytes 36872 | tf_op jit(solution)/shard_map/ppermute | solution.py:17
  16.2 16.9 %copy-start.9 = (f32[1024]{0:T(1024)S(1)}, f32[1024]{0:T(1024)}, u32[]{:S(2)}) copy-start(f32[1024]{0:T(1024)} %param.14) | copy-start | bytes 12292
  19.3 35.1 %all-to-all-start = ((bf16[64,258,16]{1,2,0:T(8,128)(2,1)}), bf16[64,258,16]{1,2,0:T(8,128)(2,1)S(1)}, u32[]{:S(2)}, u32[]{:S(2)}) async-start(bf16[64,258,16]{1,2,0:T(8,128)(2,1)} %pad_maximum_fusion), calls=%async_computation | async-start | bytes 1572864 | tf_op jit(solution)/shard_map/all_to_all | solution.py:130
  31.8 26.4 %copy-start.8 = (f32[16,128]{1,0:T(8,128)}, f32[16,128]{1,0:T(8,128)S(1)}, u32[]{:S(2)}) copy-start(f32[16,128]{1,0:T(8,128)S(1)} %concatenate.43.d_ref) | copy-start | bytes 24580
  58.2 13.2 %copy-start.7 = (f32[16,128]{1,0:T(8,128)S(1)}, f32[16,128]{1,0:T(8,128)}, u32[]{:S(2)}) copy-start(f32[16,128]{1,0:T(8,128)} %concatenate.44.w_ref) | copy-start | bytes 24580
  69.5 4.1 %copy-start.5 = (f32[1024,128]{1,0:T(8,128)S(1)}, f32[1024,128]{1,0:T(8,128)}, u32[]{:S(2)}) copy-start(f32[1024,128]{1,0:T(8,128)} %get-tuple-element.7) | copy-start | bytes 1572868
  73.6 3.5 %copy-start.4 = (bf16[64,128,16]{1,2,0:T(8,128)(2,1)S(1)}, bf16[64,128,16]{1,2,0:T(8,128)(2,1)}, u32[]{:S(2)}) copy-start(bf16[64,128,16]{1,2,0:T(8,128)(2,1)} %get-tuple-element.29) | copy-start | bytes 786436
  75.1 2.0 %copy-start.2 = (f32[8192,16]{1,0:T(8,128)}, f32[8192,16]{1,0:T(8,128)S(1)}, u32[]{:S(2)}) copy-start(f32[8192,16]{1,0:T(8,128)S(1)} %slice_dynamic-update-slice_fusion) | copy-start | bytes 1572868
  77.1 3.9 %copy-start.10 = (f32[16]{0:T(128)S(1)}, f32[16]{0:T(128)}, u32[]{:S(2)}) copy-start(f32[16]{0:T(128)} %get-tuple-element.39) | copy-start | bytes 196
  77.1 3.9 %copy-start.11 = (f32[16]{0:T(128)S(1)}, f32[16]{0:T(128)}, u32[]{:S(2)}) copy-start(f32[16]{0:T(128)} %get-tuple-element.40) | copy-start | bytes 196
  77.1 3.9 %copy-start.12 = (f32[16]{0:T(128)S(1)}, f32[16]{0:T(128)}, u32[]{:S(2)}) copy-start(f32[16]{0:T(128)} %get-tuple-element.41) | copy-start | bytes 196
  77.1 3.9 %copy-start.13 = (f32[16]{0:T(128)S(1)}, f32[16]{0:T(128)}, u32[]{:S(2)}) copy-start(f32[16]{0:T(128)} %fusion.15) | copy-start | bytes 196
  79.0 2.8 %copy-start.3 = (f32[8192,16]{1,0:T(8,128)S(1)}, f32[8192,16]{1,0:T(8,128)}, u32[]{:S(2)}) copy-start(f32[8192,16]{1,0:T(8,128)} %copy-done.2) | copy-start | bytes 1572868
  83.8 1.3 %copy-start = (bf16[8192,16]{1,0:T(8,128)(2,1)}, bf16[8192,16]{1,0:T(8,128)(2,1)S(1)}, u32[]{:S(2)}) copy-start(bf16[8192,16]{1,0:T(8,128)(2,1)S(1)} %fusion.2) | copy-start | bytes 786436
  85.1 2.3 %copy-start.6 = (bf16[32,16,128]{2,1,0:T(8,128)(2,1)S(1)}, bf16[32,16,128]{2,1,0:T(8,128)(2,1)}, u32[]{:S(2)}) copy-start(bf16[32,16,128]{2,1,0:T(8,128)(2,1)} %param.15) | copy-start | bytes 393220
  87.5 4.6 %copy-start.1 = (bf16[8192,16]{1,0:T(8,128)(2,1)S(1)}, bf16[8192,16]{1,0:T(8,128)(2,1)}, u32[]{:S(2)}) copy-start(bf16[8192,16]{1,0:T(8,128)(2,1)} %copy-done) | copy-start | bytes 786436
  90.7 10.4 %copy-start.14 = (u32[256]{0:T(256)S(1)}, u32[256]{0:T(256)}, u32[]{:S(2)}) copy-start(u32[256]{0:T(256)} %constant.41) | copy-start | bytes 3076
  93.8 24.2 %all-to-all-start.1 = ((bf16[64,192,1,1,16]{1,4,3,2,0:T(8,128)(2,1)}), bf16[64,192,1,1,16]{1,4,3,2,0:T(8,128)(2,1)S(1)}, u32[]{:S(2)}, u32[]{:S(2)}) async-start(bf16[64,192,1,1,16]{1,4,3,2,0:T(8,128)(2,1)} %pad_maximum_fusion.1), calls=%async_computation.1 | async-start | bytes 1048576 | tf_op jit(solution)/shard_map/all_to_all | solution.py:174

commit v14 on v13

v14 whole, which is shorter than its diff:
```python
import jax
import jax.numpy as jnp
from jax import lax
from jax.experimental import pallas as pl
from jax.sharding import PartitionSpec as P

STRIDE = 16
CHUNK = 128
INTERPRET = False

highest = lax.Precision.HIGHEST


def from_behind(block, axis, distance):
    devices = range(lax.axis_size(axis))
    route = [(i - distance, i) for i in devices if i - distance in devices]
    return lax.ppermute(block, axis, route)


def short_pass(rows, before, tap_weights):
    joined = jnp.concatenate([before, rows], axis=0).astype(jnp.float32)
    row_count = rows.shape[0]
    return (
        tap_weights[0] * joined[2 : 2 + row_count]
        + tap_weights[1] * joined[1 : 1 + row_count]
        + tap_weights[2] * joined[0:row_count]
    )


def conv_kernel(g_ref, d_ref, w_ref, out_ref, total_ref):
    span, width = g_ref.shape
    chunks = span // CHUNK
    row = lax.broadcasted_iota(jnp.int32, (CHUNK, CHUNK), 0)
    col = lax.broadcasted_iota(jnp.int32, (CHUNK, CHUNK), 1)
    lower = (row >= col).astype(jnp.bfloat16)
    steps = lax.broadcasted_iota(jnp.int32, (CHUNK, width), 0).astype(jnp.float32)
    out_ref[...] = jnp.zeros(out_ref.shape, jnp.float32)

    def mode(r, carry):
        d = d_ref[pl.ds(r, 1), :]
        w = w_ref[pl.ds(r, 1), :]
        grow = jnp.exp(d * steps)
        shrink = w * jnp.exp(-d * steps)
        after = w * jnp.exp(-d * (steps + 1.0))
        tail = jnp.exp(-d * float(CHUNK - 1))
        hop = jnp.exp(-d * float(CHUNK))
        state = jnp.zeros((1, width), jnp.float32)
        for k in range(chunks):
            rows = slice(k * CHUNK, (k + 1) * CHUNK)
            scaled = grow * g_ref[rows, :]
            high = scaled.astype(jnp.bfloat16)
            low = (scaled - high.astype(jnp.float32)).astype(jnp.bfloat16)
            y = jnp.dot(lower, high, preferred_element_type=jnp.float32) + jnp.dot(
                lower, low, preferred_element_type=jnp.float32
            )
            out_ref[rows, :] += shrink * y + after * state
            state = hop * state + tail * y[CHUNK - 1 : CHUNK, :]
        total_ref[pl.ds(r, 1), :] = state
        return carry

    lax.fori_loop(0, d_ref.shape[0], mode, 0)


def packed_conv(packed, residues, decays, parts):
    seg, lanes = packed.shape
    width = lanes // parts
    modes = decays.shape[0]
    weight = residues * jnp.sqrt(-jnp.expm1(-2.0 * decays))
    decays_p = jnp.concatenate([decays] * parts, axis=1)
    weight_p = jnp.concatenate([weight] * parts, axis=1)
    local, ends = pl.pallas_call(
        conv_kernel,
        out_shape=(
            jax.ShapeDtypeStruct((seg, lanes), jnp.float32),
            jax.ShapeDtypeStruct(decays_p.shape, jnp.float32),
        ),
        interpret=INTERPRET,
    )(packed, decays_p, weight_p)
    ends = ends.reshape(modes, parts, width)
    index = jnp.arange(parts)
    lag = index[:, None] - 1 - index[None, :]
    gap = (float(seg) * jnp.maximum(lag, 0).astype(jnp.float32))[None, :, :, None]
    table = jnp.where((lag >= 0)[None, :, :, None], jnp.exp(-decays[:, None, None, :] * gap), 0.0)
    entry = jnp.sum(table * ends[:, None, :, :], axis=2).reshape(modes, lanes)
    steps = jnp.arange(seg, dtype=jnp.float32)
    after = jnp.exp(-decays_p[:, None, :] * (steps[None, :, None] + 1.0))
    return local + jnp.sum((weight_p * entry)[:, None, :] * after, axis=0)


def shards(
    query_input, key_input, value_input, short_filter, residues, decays, skip_gain, head_weight
):
    tokens, chan_width = query_input.shape
    width_v = lax.axis_size("v")
    piece = head_weight.shape[1]
    span = tokens * width_v
    parts = max(1, 128 // piece)
    seg = span // parts
    blocks = width_v // parts
    lanes = parts * piece
    before = from_behind(
        jnp.stack([query_input[-2:], key_input[-2:], value_input[-2:]], axis=0), "v", 1
    )
    key_short = short_pass(key_input, before[1], short_filter[:, 1])
    value_short = short_pass(value_input, before[2], short_filter[:, 2])
    gated_rows = (key_short * value_short).astype(jnp.bfloat16)

    def by_target(values):
        depth = values.shape[0]
        return jnp.transpose(values.reshape(depth, width_v, piece), (1, 0, 2))

    payload = jnp.concatenate(
        [by_target(before[0]), by_target(query_input), by_target(gated_rows)], axis=1
    )
    depth = payload.shape[1]
    columns = lax.all_to_all(payload, "v", split_axis=0, concat_axis=0, tiled=True)
    columns = jnp.transpose(columns.reshape(parts, blocks, depth, piece), (1, 2, 0, 3))
    query_before = columns[0, :2].reshape(2, lanes)
    query_p = columns[:, 2 : 2 + tokens].reshape(seg, lanes)
    gated_p = columns[:, 2 + tokens :].reshape(seg, lanes)
    head = lax.axis_index("v") * piece

    def own(values):
        return lax.dynamic_slice_in_dim(values, head, piece, axis=values.ndim - 1)

    sf = jnp.concatenate([own(short_filter)] * parts, axis=2)
    gain = jnp.concatenate([own(skip_gain)] * parts, axis=0)
    query_short = short_pass(query_p, query_before, sf[:, 0])
    convolved = packed_conv(gated_p, own(residues), own(decays), parts)
    carried = (convolved + gain * gated_p.astype(jnp.float32)).astype(jnp.bfloat16)
    op_p = (query_short * carried.astype(jnp.float32)).astype(jnp.bfloat16)
    following = jnp.concatenate(
        [op_p[:STRIDE, piece:], jnp.zeros((STRIDE, piece), op_p.dtype)], axis=1
    )
    extended = jnp.concatenate([op_p, following], axis=0)
    rows_seg = seg // STRIDE
    early_rows = extended[:seg].reshape(rows_seg, STRIDE, parts, piece)
    late_rows = extended[STRIDE:].reshape(rows_seg, STRIDE, parts, piece)
    partial_sum = jnp.einsum(
        "jisc,ico->sjo", early_rows, head_weight[:STRIDE], preferred_element_type=jnp.float32
    ) + jnp.einsum(
        "jisc,ico->sjo", late_rows, head_weight[STRIDE:], preferred_element_type=jnp.float32
    )
    op_t = jnp.transpose(op_p.reshape(blocks, tokens, parts, piece), (2, 0, 1, 3))
    op_t = op_t.reshape(width_v, tokens, 1, 1, piece)
    sums = partial_sum.astype(jnp.bfloat16).reshape(width_v, -1, 1, 1, piece)
    outgoing = jnp.concatenate([op_t, sums], axis=1)
    incoming = lax.all_to_all(outgoing, "v", split_axis=0, concat_axis=3, tiled=True)[0]
    operator_out = incoming[:tokens].reshape(tokens, chan_width)
    sums = jnp.transpose(incoming[tokens:], (2, 0, 1, 3)).astype(jnp.float32)
    block_sum = jnp.sum(sums.reshape(width_v, tokens // STRIDE, -1), axis=0)
    probe_out = lax.psum_scatter(block_sum, "tp", scatter_dimension=0, tiled=True).astype(
        jnp.bfloat16
    )
    return (operator_out, probe_out)


def solution(mesh):
    seq_size, tp_size = mesh.devices.shape
    width_u = 1
    split = jax.sharding.Mesh(
        mesh.devices.reshape(width_u, seq_size // width_u, tp_size), ("u", "v", "tp")
    )
    seq = ("u", "v")
    placed = (
        P(seq, "tp"),
        P(seq, "tp"),
        P(seq, "tp"),
        P(None, None, "tp"),
        P(None, "tp"),
        P(None, "tp"),
        P("tp"),
        P(None, ("tp", "u", "v"), None),
    )
    return jax.shard_map(
        shards,
        mesh=split,
        in_specs=placed,
        out_specs=(P(seq, "tp"), P(("u", "v", "tp"), None)),
        check_vma=False,
    )
```

time: 129 us -> 108 us (0.84)
  local copies, waits for them, and re-layouts: 37.3 us -> 18.8 us
  other arithmetic: 14.1 us -> 8.16 us
  matrix products: 0.52 us -> 2.81 us
    reshape x10 -> x7, local copies, waits for them, and re-layouts: 11.1 us -> 5.85 us  [the longest x1 2.39 us: shards(): late_rows = extended[STRIDE:].reshape(rows_seg, STRIDE, parts, piece)]
    unnamed x45 -> x22, local copies, waits for them, and re-layouts: 10.6 us -> 5.38 us
    concatenate x4, local copies, waits for them, and re-layouts: 5.19 us -> 0.96 us  [the longest x1 0.68 us: packed_conv(): weight_p = jnp.concatenate([weight] * parts, axis=1)]
    slice x6 -> x5, local copies, waits for them, and re-layouts: 4.26 us -> 0.44 us  [the longest x2 0.29 us: shards(): gated_p = columns[:, 2 + tokens:].reshape(seg, lanes)]
    dot_general x2, matrix products: 0.52 us -> 2.81 us  [the longest x1 2.19 us: shards(): jnp.einsum('jisc,ico->sjo', late_rows, head_weight[STRIDE:], preferred_el...]
    convert_element_type x3, other arithmetic: 2.46 us -> 0.55 us  [short_pass(): joined = jnp.concatenate([before, rows], axis=0).astype(jnp.float32)]
    convert_element_type x1, other arithmetic: 1.95 us -> 0.28 us  [shards(): op_p = (query_short * carried.astype(jnp.float32)).astype(jnp.bfloat16)]
    dynamic_slice x1 -> x2, local copies, waits for them, and re-layouts: 0.02 us -> 1.54 us  [own(): return lax.dynamic_slice_in_dim(values, head, piece, axis=values.ndim - 1)]
  transfers between devices with their start and end apart: 3 -> 3, of which waited for: 2 -> 2; matrix products, arithmetic and copies ran while one was open for 10% -> 8% of each run, Pallas kernels for 0% -> 0%
where the time goes in v14:
time: 108 us; the launch traced here: 107 us
  waiting for transfers between devices  35 us (32%)
  starting transfers between devices  25 us (23%)
  local copies, waits for them, and re-layouts  18.8 us (17%)
  blocking collectives  8.33 us (8%)
  other arithmetic  8.16 us (8%)
  Pallas kernels  6.95 us (6%)
  matrix products  2.81 us (3%)
  between operations  1.64 us (2%)
    all_to_all x1, waiting for transfers between devices, shards(): lax.all_to_all(payload, 'v', split_axis=0, concat_axis=0, tiled=True)  19.4 us
    all_to_all x1, waiting for transfers between devices, shards(): lax.all_to_all(outgoing, 'v', split_axis=0, concat_axis=3, tiled=True)[0]  15.6 us
    all_to_all x1, starting transfers between devices, shards(): lax.all_to_all(payload, 'v', split_axis=0, concat_axis=0, tiled=True)  12.2 us
    unnamed x1, blocking collectives  8.33 us
    all_to_all x1, starting transfers between devices, shards(): lax.all_to_all(outgoing, 'v', split_axis=0, concat_axis=3, tiled=True)[0]  7.31 us
    pallas_call x1, Pallas kernels, packed_conv(): pl.pallas_call(conv_kernel, out_shape=(jax.ShapeDtypeStruct((seg, lanes),...  6.95 us
    ppermute x1, starting transfers between devices, from_behind(): return lax.ppermute(block, axis, route)  5.47 us
    unnamed x22, local copies, waits for them, and re-layouts  5.38 us
  transfers between devices with their start and end apart: 3, of which 2 were waited for; matrix products, arithmetic and copies ran while one was open for 8% of the time, Pallas kernels for 0%

profile of v14, /device:TPU:1, one launch (start us, length us, event | category | flops | bytes accessed | tf_op | source)
XLA Modules:
  0.0 106.7 jit_solution(5416708110496544190)
XLA Ops:
  0.6 0.7 slice_bitcast_fusion.2
  1.4 0.7 slice_bitcast_fusion
  2.1 5.5 %collective-permute-start = (bf16[3,2,1024]{2,1,0:T(2,128)(2,1)S(1)}, bf16[3,2,1024]{2,1,0:T(2,128)(2,1)S(1)}, u32[]{:S(2)}, u32[]{:S(2)}) collective-permute-start(bf16[3,2,1024]{2,1,0:T(2,128)(2,1)S(1)} %pad_maximum_fusion.2), channel_id=1, source_target_pairs={{0,4},{4,8},{8,12},{12,16},{16,20},{20,24},{24,28},{28,32},{32,36}... | collective-permute-start | bytes 36872 | tf_op jit(solution)/shard_map/ppermute | solution.py:17
  7.6 0.8 fusion.22
  8.5 0.8 fusion.20
  9.2 1.1 %copy.57 = bf16[128,1024]{0,1:T(8,128)(2,1)S(1)} copy(bf16[128,1024]{1,0:T(8,128)(2,1)} %param.9) | data formatting | bytes 524288 | tf_op args[1]
  10.4 1.1 %copy.59 = bf16[128,1024]{0,1:T(8,128)(2,1)S(1)} copy(bf16[128,1024]{1,0:T(8,128)(2,1)} %param.10) | data formatting | bytes 524288 | tf_op args[2]
  11.5 1.1 %copy.55 = bf16[128,1024]{0,1:T(8,128)(2,1)S(1)} copy(bf16[128,1024]{1,0:T(8,128)(2,1)} %param.8) | data formatting | bytes 524288 | tf_op args[0]
  12.6 0.2 copy.76
  12.8 0.2 copy.77
  13.1 0.1 reshape_squeeze.6
  13.2 0.5 copy.60
  13.6 0.2 maximum_convert_fusion
  13.9 0.2 maximum_convert_fusion.1
  14.1 1.5 %fusion.9 = bf16[128,1024]{0,1:T(8,128)(2,1)S(1)} fusion(f32[130,1024]{0,1:T(8,128)S(1)} %maximum_convert_fusion.1, f32[130,1024]{0,1:T(8,128)S(1)} %maximum_convert_fusion, f32[1024]{0:T(1024)S(1)} %bitcast.102, f32[1024]{0:T(1024)S(1)} %bitcast.103, f32[1024]{0:T(1024)S(1)} %bitcast.99, f32[1024]{0:T(1024)S(1)} %bitcast.100, f32[1024]{0:T(1024)S(1)} %bitcast.101, ...), kind=kLoop, calls=%fused_computation.18 | loop fusion | flops 1572864 | bytes 3432448 | tf_op jit(solution)/shard_map/convert_element_type | solution.py:106
  15.7 1.3 %pad_maximum_fusion = bf16[64,258,16]{1,2,0:T(8,128)(2,1)} fusion(bf16[64,128,16]{1,2,0:T(8,128)(2,1)S(1)} %bitcast.95, bf16[64,128,16]{1,2,0:T(8,128)(2,1)S(1)} %bitcast.91, bf16[64,2,16]{1,2,0:T(8,128)(2,1)S(1)} %copy.60), kind=kLoop, calls=%fused_computation.6 | loop fusion | flops 1585152 | bytes 1056768 | tf_op jit(solution)/shard_map/concatenate | solution.py:112
  17.0 12.2 %all-to-all-start = ((bf16[64,258,16]{1,2,0:T(8,128)(2,1)}), bf16[64,258,16]{1,2,0:T(8,128)(2,1)S(1)}, u32[]{:S(2)}, u32[]{:S(2)}) async-start(bf16[64,258,16]{1,2,0:T(8,128)(2,1)} %pad_maximum_fusion), calls=%async_computation | async-start | bytes 1572864 | tf_op jit(solution)/shard_map/all_to_all | solution.py:116
  29.2 0.8 sqrt_multiply_fusion
  30.0 0.1 concatenate.46.d_ref
  30.1 0.7 concatenate.47.w_ref
  30.8 0.8 constant_dynamic-slice_fusion.1
  31.5 0.1 concatenate.41
  31.6 0.8 dynamic_slice.15
  32.4 0.1 concatenate.48
  32.7 19.4 %all-to-all-done = bf16[64,258,16]{1,2,0:T(8,128)(2,1)S(1)} async-done(((bf16[64,258,16]{1,2,0:T(8,128)(2,1)}), bf16[64,258,16]{1,2,0:T(8,128)(2,1)S(1)}, u32[]{:S(2)}, u32[]{:S(2)}) %all-to-all-start) | async-done | bytes 528416 | tf_op jit(solution)/shard_map/all_to_all | solution.py:116
  52.1 0.2 fusion.21
  52.5 0.8 copy.65.g_ref
  53.3 6.9 %shard_map.95 = (f32[1024,128]{1,0:T(8,128)}, f32[16,128]{1,0:T(8,128)}) custom-call(bf16[1024,128]{1,0:T(8,128)(2,1)} %copy.65.g_ref, f32[16,128]{1,0:T(8,128)} %copy-done.4, f32[16,128]{1,0:T(8,128)} %concatenate.47.w_ref), custom_call_target="tpu_custom_call" | custom-call | tf_op jit(solution)/shard_map/pallas_call | solution.py:71
  60.3 0.8 mul.214
  61.0 0.3 multiply_reduce_fusion.1
  61.6 0.2 copy.63
  61.9 1.4 %multiply_reduce_fusion = f32[1024,128]{1,0:T(8,128)S(1)} fusion(f32[1024]{0:T(1024)S(1)} %iota_add_fusion, f32[16,128]{1,0:T(8,128)S(1)} %neg.17, f32[16,128]{1,0:T(8,128)S(1)} %mul.217), kind=kLoop, calls=%fused_computation | loop fusion | flops 6160384 | bytes 544768 | tf_op jit(solution)/shard_map/reduce_sum | solution.py:87
  63.4 0.3 fusion.5
  63.7 1.3 %reshape.254 = bf16[64,16,8,16]{3,2,1,0:T(8,128)(2,1)S(1)} reshape(bf16[1024,128]{1,0:T(8,128)(2,1)S(1)} %fusion.5) | data formatting | bytes 524288 | tf_op jit(solution)/shard_map/reshape | solution.py:137
  65.1 0.1 copy.67
  65.3 2.4 %reshape.255 = bf16[64,16,8,16]{3,2,1,0:T(8,128)(2,1)} reshape(bf16[1024,128]{1,0:T(8,128)(2,1)S(1)} %fusion.14) | data formatting | bytes 524288 | tf_op jit(solution)/shard_map/reshape | solution.py:138
  67.7 2.2 %convolution_bitcast_fusion = f32[64,8,128]{2,1,0:T(8,128)S(1)} fusion(bf16[64,16,8,16]{3,2,1,0:T(8,128)(2,1)} %reshape.255, bf16[32,16,128]{2,1,0:T(8,128)(2,1)S(1)} %copy-done.2), kind=kOutput, calls=%fused_computation.1 | convolution fusion | flops 33554432 | bytes 589824 | tf_op jit(solution)/shard_map/jisc,ico->sjo/dot_general | solution.py:141
  69.9 0.6 fusion.2
  70.5 0.7 reshape.256
  71.2 0.4 copy.70
  71.7 0.9 pad_maximum_fusion.1
  72.6 7.3 %all-to-all-start.1 = ((bf16[64,192,1,1,16]{1,4,3,2,0:T(8,128)(2,1)}), bf16[64,192,1,1,16]{1,4,3,2,0:T(8,128)(2,1)S(1)}, u32[]{:S(2)}, u32[]{:S(2)}) async-start(bf16[64,192,1,1,16]{1,4,3,2,0:T(8,128)(2,1)} %pad_maximum_fusion.1), calls=%async_computation.1 | async-start | bytes 1048576 | tf_op jit(solution)/shard_map/all_to_all | solution.py:148
  79.9 0.6 dynamic-slice
  81.2 15.6 %all-to-all-done.1 = bf16[64,192,1,1,16]{1,4,3,2,0:T(8,128)(2,1)S(1)} async-done(((bf16[64,192,1,1,16]{1,4,3,2,0:T(8,128)(2,1)}), bf16[64,192,1,1,16]{1,4,3,2,0:T(8,128)(2,1)S(1)}, u32[]{:S(2)}, u32[]{:S(2)}) %all-to-all-start.1) | async-done | bytes 393248 | tf_op jit(solution)/shard_map/all_to_all | solution.py:148
  96.9 0.8 copy.72
  97.7 0.1 copy.71
  97.9 8.3 %all-reduce.1 = bf16[8,128]{1,0:T(8,128)(2,1)S(1)} all-reduce(f32[8,128]{1,0:T(8,128)S(1)} %reduce_sum.32), channel_id=2, replica_groups=mesh['seq'=64,'tp'=4] {'tp'}, use_global_device_ids=true, to_apply=%region_3.4.clone | all-reduce | flops 1024 | bytes 6144
  106.2 0.5 dynamic-slice_convert_fusion
  (38 shorter events, 1.1 us)
Async XLA Ops:
  2.1 10.5 %collective-permute-start = (bf16[3,2,1024]{2,1,0:T(2,128)(2,1)S(1)}, bf16[3,2,1024]{2,1,0:T(2,128)(2,1)S(1)}, u32[]{:S(2)}, u32[]{:S(2)}) collective-permute-start(bf16[3,2,1024]{2,1,0:T(2,128)(2,1)S(1)} %pad_maximum_fusion.2), channel_id=1, source_target_pairs={{0,4},{4,8},{8,12},{12,16},{16,20},{20,24},{24,28},{28,32},{32,36}... | collective-permute-start | bytes 36872 | tf_op jit(solution)/shard_map/ppermute | solution.py:17
  17.0 35.1 %all-to-all-start = ((bf16[64,258,16]{1,2,0:T(8,128)(2,1)}), bf16[64,258,16]{1,2,0:T(8,128)(2,1)S(1)}, u32[]{:S(2)}, u32[]{:S(2)}) async-start(bf16[64,258,16]{1,2,0:T(8,128)(2,1)} %pad_maximum_fusion), calls=%async_computation | async-start | bytes 1572864 | tf_op jit(solution)/shard_map/all_to_all | solution.py:116
  30.1 23.3 %copy-start.4 = (f32[16,128]{1,0:T(8,128)}, f32[16,128]{1,0:T(8,128)S(1)}, u32[]{:S(2)}) copy-start(f32[16,128]{1,0:T(8,128)S(1)} %concatenate.46.d_ref) | copy-start | bytes 24580
  30.8 30.7 %copy-start.3 = (f32[16,128]{1,0:T(8,128)S(1)}, f32[16,128]{1,0:T(8,128)}, u32[]{:S(2)}) copy-start(f32[16,128]{1,0:T(8,128)} %concatenate.47.w_ref) | copy-start | bytes 24580
  61.9 1.4 %copy-start = (bf16[1024,128]{1,0:T(8,128)(2,1)S(1)}, bf16[1024,128]{1,0:T(8,128)(2,1)}, u32[]{:S(2)}) copy-start(bf16[1024,128]{1,0:T(8,128)(2,1)} %copy.65.g_ref) | copy-start | bytes 786436
  61.9 1.4 %copy-start.1 = (f32[1024,128]{1,0:T(8,128)S(1)}, f32[1024,128]{1,0:T(8,128)}, u32[]{:S(2)}) copy-start(f32[1024,128]{1,0:T(8,128)} %get-tuple-element.4) | copy-start | bytes 1572868
  65.1 2.6 %copy-start.2 = (bf16[32,16,128]{2,1,0:T(8,128)(2,1)S(1)}, bf16[32,16,128]{2,1,0:T(8,128)(2,1)}, u32[]{:S(2)}) copy-start(bf16[32,16,128]{2,1,0:T(8,128)(2,1)} %param.15) | copy-start | bytes 393220
  71.2 8.7 %copy-start.5 = (u32[256]{0:T(256)S(1)}, u32[256]{0:T(256)}, u32[]{:S(2)}) copy-start(u32[256]{0:T(256)} %constant.31) | copy-start | bytes 3076
  72.6 24.1 %all-to-all-start.1 = ((bf16[64,192,1,1,16]{1,4,3,2,0:T(8,128)(2,1)}), bf16[64,192,1,1,16]{1,4,3,2,0:T(8,128)(2,1)S(1)}, u32[]{:S(2)}, u32[]{:S(2)}) async-start(bf16[64,192,1,1,16]{1,4,3,2,0:T(8,128)(2,1)} %pad_maximum_fusion.1), calls=%async_computation.1 | async-start | bytes 1048576 | tf_op jit(solution)/shard_map/all_to_all | solution.py:148

commit v15 on v14

--- a/solution.py
+++ b/solution.py
@@ -134,13 +134,20 @@
     )
     extended = jnp.concatenate([op_p, following], axis=0)
     rows_seg = seg // STRIDE
-    early_rows = extended[:seg].reshape(rows_seg, STRIDE, parts, piece)
-    late_rows = extended[STRIDE:].reshape(rows_seg, STRIDE, parts, piece)
-    partial_sum = jnp.einsum(
-        "jisc,ico->sjo", early_rows, head_weight[:STRIDE], preferred_element_type=jnp.float32
-    ) + jnp.einsum(
-        "jisc,ico->sjo", late_rows, head_weight[STRIDE:], preferred_element_type=jnp.float32
-    )
+    eye = jnp.eye(parts, dtype=head_weight.dtype)
+
+    def spread(taps):
+        return jnp.einsum("ico,ts->itcso", taps, eye).reshape(STRIDE * lanes, parts * taps.shape[2])
+
+    early_rows = extended[:seg].reshape(rows_seg, STRIDE * lanes)
+    late_rows = extended[STRIDE:].reshape(rows_seg, STRIDE * lanes)
+    by_lane = jnp.dot(
+        early_rows, spread(head_weight[:STRIDE]), preferred_element_type=jnp.float32
+    ) + jnp.dot(late_rows, spread(head_weight[STRIDE:]), preferred_element_type=jnp.float32)
+    per_block = tokens // STRIDE
+    partial_sum = jnp.transpose(
+        by_lane.reshape(blocks, per_block, parts, -1), (2, 0, 1, 3)
+    ).reshape(width_v, per_block, -1)
     op_t = jnp.transpose(op_p.reshape(blocks, tokens, parts, piece), (2, 0, 1, 3))
     op_t = op_t.reshape(width_v, tokens, 1, 1, piece)
     sums = partial_sum.astype(jnp.bfloat16).reshape(width_v, -1, 1, 1, piece)

time: 108 us -> 108 us (level)
  other arithmetic: 8.16 us -> 12.1 us
  local copies, waits for them, and re-layouts: 18.8 us -> 15.7 us
  waiting for transfers between devices: 35 us -> 32.9 us
  matrix products: 2.81 us -> 4.03 us
    reshape x4 -> x2, local copies, waits for them, and re-layouts: 4.76 us -> 0.23 us  [the longest x1 0.12 us: shards(): late_rows = extended[STRIDE:].reshape(rows_seg, STRIDE * lanes)]
    dot_general x0 -> x1, other arithmetic: none -> 3.84 us  [spread(): jnp.einsum('ico,ts->itcso', taps, eye)]
    all_to_all x1, waiting for transfers between devices: 19.4 us -> 17.3 us  [shards(): lax.all_to_all(payload, 'v', split_axis=0, concat_axis=0, tiled=True)]
    dot_general x2, matrix products: 2.81 us -> 4.03 us  [the longest x1 3.18 us: shards(): jnp.dot(late_rows, spread(head_weight[STRIDE:]), preferred_element_type=j...]
    unnamed x22 -> x24, local copies, waits for them, and re-layouts: 5.38 us -> 5.64 us
  transfers between devices with their start and end apart: 3 -> 3, of which waited for: 2 -> 2; matrix products, arithmetic and copies ran while one was open for 8% -> 12% of each run, Pallas kernels for 0% -> 0%
where the time goes in v15:
time: 108 us; the launch traced here: 107 us
  waiting for transfers between devices  32.9 us (30%)
  starting transfers between devices  25 us (23%)
  local copies, waits for them, and re-layouts  15.7 us (15%)
  other arithmetic  12.1 us (11%)
  blocking collectives  8.33 us (8%)
  Pallas kernels  7.04 us (7%)
  matrix products  4.03 us (4%)
  between operations  1.68 us (2%)
    all_to_all x1, waiting for transfers between devices, shards(): lax.all_to_all(payload, 'v', split_axis=0, concat_axis=0, tiled=True)  17.3 us
    all_to_all x1, waiting for transfers between devices, shards(): lax.all_to_all(outgoing, 'v', split_axis=0, concat_axis=3, tiled=True)[0]  15.6 us
    all_to_all x1, starting transfers between devices, shards(): lax.all_to_all(payload, 'v', split_axis=0, concat_axis=0, tiled=True)  12.2 us
    unnamed x1, blocking collectives  8.33 us
    all_to_all x1, starting transfers between devices, shards(): lax.all_to_all(outgoing, 'v', split_axis=0, concat_axis=3, tiled=True)[0]  7.31 us
    pallas_call x1, Pallas kernels, packed_conv(): pl.pallas_call(conv_kernel, out_shape=(jax.ShapeDtypeStruct((seg, lanes),...  7.04 us
    unnamed x24, local copies, waits for them, and re-layouts  5.64 us
    ppermute x1, starting transfers between devices, from_behind(): return lax.ppermute(block, axis, route)  5.47 us
  transfers between devices with their start and end apart: 3, of which 2 were waited for; matrix products, arithmetic and copies ran while one was open for 12% of the time, Pallas kernels for 0%

profile of v15, /device:TPU:1, one launch (start us, length us, event | category | flops | bytes accessed | tf_op | source)
XLA Modules:
  0.0 106.7 jit_solution(8984696106072037018)
XLA Ops:
  0.6 0.7 slice_bitcast_fusion.2
  1.4 0.7 slice_bitcast_fusion
  2.1 5.5 %collective-permute-start = (bf16[3,2,1024]{2,1,0:T(2,128)(2,1)S(1)}, bf16[3,2,1024]{2,1,0:T(2,128)(2,1)S(1)}, u32[]{:S(2)}, u32[]{:S(2)}) collective-permute-start(bf16[3,2,1024]{2,1,0:T(2,128)(2,1)S(1)} %pad_maximum_fusion.2), channel_id=1, source_target_pairs={{0,4},{4,8},{8,12},{12,16},{16,20},{20,24},{24,28},{28,32},{32,36}... | collective-permute-start | bytes 36872 | tf_op jit(solution)/shard_map/ppermute | solution.py:17
  7.6 0.8 fusion.32
  8.5 0.8 constant_dynamic-slice_fusion.1
  9.2 0.8 fusion.29
  10.0 0.1 concatenate.41
  10.1 0.8 sqrt_multiply_fusion
  11.0 1.1 %copy.49 = bf16[128,1024]{0,1:T(8,128)(2,1)S(1)} copy(bf16[128,1024]{1,0:T(8,128)(2,1)} %param.9) | data formatting | bytes 524288 | tf_op args[1]
  12.1 1.1 %copy.51 = bf16[128,1024]{0,1:T(8,128)(2,1)S(1)} copy(bf16[128,1024]{1,0:T(8,128)(2,1)} %param.10) | data formatting | bytes 524288 | tf_op args[2]
  13.2 1.1 %copy.47 = bf16[128,1024]{0,1:T(8,128)(2,1)S(1)} copy(bf16[128,1024]{1,0:T(8,128)(2,1)} %param.8) | data formatting | bytes 524288 | tf_op args[0]
  14.4 0.2 copy.66
  14.6 0.2 copy.67
  14.8 0.1 reshape_squeeze.6
  14.9 0.5 copy.52
  15.4 0.2 maximum_convert_fusion
  15.6 0.2 maximum_convert_fusion.1
  15.9 1.5 %fusion.21 = bf16[128,1024]{0,1:T(8,128)(2,1)S(1)} fusion(f32[130,1024]{0,1:T(8,128)S(1)} %maximum_convert_fusion.1, f32[130,1024]{0,1:T(8,128)S(1)} %maximum_convert_fusion, f32[1024]{0:T(1024)S(1)} %bitcast.110, f32[1024]{0:T(1024)S(1)} %bitcast.111, f32[1024]{0:T(1024)S(1)} %bitcast.107, f32[1024]{0:T(1024)S(1)} %bitcast.108, f32[1024]{0:T(1024)S(1)} %bitcast.109, ...), kind=kLoop, calls=%fused_computation.24 | loop fusion | flops 1572864 | bytes 3432448 | tf_op jit(solution)/shard_map/convert_element_type | solution.py:106
  17.4 1.4 %pad_maximum_fusion = bf16[64,258,16]{1,2,0:T(8,128)(2,1)} fusion(bf16[64,128,16]{1,2,0:T(8,128)(2,1)S(1)} %bitcast.102, bf16[64,128,16]{1,2,0:T(8,128)(2,1)S(1)} %bitcast.98, bf16[64,2,16]{1,2,0:T(8,128)(2,1)S(1)} %copy.52), kind=kLoop, calls=%fused_computation.12 | loop fusion | flops 1585152 | bytes 1056768 | tf_op jit(solution)/shard_map/concatenate | solution.py:112
  18.8 12.2 %all-to-all-start = ((bf16[64,258,16]{1,2,0:T(8,128)(2,1)}), bf16[64,258,16]{1,2,0:T(8,128)(2,1)S(1)}, u32[]{:S(2)}, u32[]{:S(2)}) async-start(bf16[64,258,16]{1,2,0:T(8,128)(2,1)} %pad_maximum_fusion), calls=%async_computation | async-start | bytes 1572864 | tf_op jit(solution)/shard_map/all_to_all | solution.py:116
  31.0 0.1 concatenate.46.d_ref
  31.1 0.7 concatenate.47.w_ref
  31.8 0.8 dynamic_slice.15
  32.8 3.8 %broadcast_multiply_fusion.1 = (bf16[8,8,16,16,128]{4,1,3,0,2:T(8,128)(2,1)}, bf16[8,8,16,16,128]{4,1,3,0,2:T(8,128)(2,1)}) fusion(bf16[16,16,128]{2,1,0:T(8,128)(2,1)S(1)} %get-tuple-element.16, bf16[8,8]{1,0:T(8,128)(2,1)S(1)} %fusion.28, bf16[16,16,128]{2,1,0:T(8,128)(2,1)S(1)} %get-tuple-element.17), kind=kLoop, calls=%fused_computation.8 | loop fusion | flops 4194304 | bytes 8519808 | tf_op jit(solution)/shard_map/ico,ts->itcso/dot_general | solution.py:140
  36.6 17.3 %all-to-all-done = bf16[64,258,16]{1,2,0:T(8,128)(2,1)S(1)} async-done(((bf16[64,258,16]{1,2,0:T(8,128)(2,1)}), bf16[64,258,16]{1,2,0:T(8,128)(2,1)S(1)}, u32[]{:S(2)}, u32[]{:S(2)}) %all-to-all-start) | async-done | bytes 528416 | tf_op jit(solution)/shard_map/all_to_all | solution.py:116
  53.9 0.2 fusion.30
  54.3 0.8 copy.57.g_ref
  55.1 7.0 %shard_map.95 = (f32[1024,128]{1,0:T(8,128)}, f32[16,128]{1,0:T(8,128)}) custom-call(bf16[1024,128]{1,0:T(8,128)(2,1)} %copy.57.g_ref, f32[16,128]{1,0:T(8,128)} %copy-done.5, f32[16,128]{1,0:T(8,128)} %concatenate.47.w_ref), custom_call_target="tpu_custom_call" | custom-call | tf_op jit(solution)/shard_map/pallas_call | solution.py:71
  62.2 0.8 mul.214
  63.0 0.3 multiply_reduce_fusion.1
  63.6 0.2 copy.55
  63.9 1.4 %multiply_reduce_fusion = f32[1024,128]{1,0:T(8,128)S(1)} fusion(f32[1024]{0:T(1024)S(1)} %iota_add_fusion, f32[16,128]{1,0:T(8,128)S(1)} %neg.17, f32[16,128]{1,0:T(8,128)S(1)} %mul.217), kind=kLoop, calls=%fused_computation | loop fusion | flops 6160384 | bytes 544768 | tf_op jit(solution)/shard_map/reduce_sum | solution.py:87
  65.3 0.3 fusion.17
  65.7 0.1 reshape.272
  65.8 0.1 copy.59
  66.0 0.1 reshape.274
  66.1 3.2 %fusion = f32[64,1024]{1,0:T(8,128)S(1)} fusion(bf16[64,2048]{1,0:T(8,128)(2,1)S(1)} %reshape.274, bf16[256,8,8,128]{3,2,1,0:T(8,128)(2,1)} %bitcast.86), kind=kOutput, calls=%fused_computation.1 | convolution fusion | flops 268435456 | bytes 4718592 | tf_op jit(solution)/shard_map/dot_general | solution.py:146
  69.3 0.3 copy-done
  69.6 0.8 fusion.12
  70.5 0.7 convert_element_type.71
  71.1 0.4 copy.62
  71.6 0.9 pad_maximum_fusion.1
  72.6 7.3 %all-to-all-start.1 = ((bf16[64,192,1,1,16]{1,4,3,2,0:T(8,128)(2,1)}), bf16[64,192,1,1,16]{1,4,3,2,0:T(8,128)(2,1)S(1)}, u32[]{:S(2)}, u32[]{:S(2)}) async-start(bf16[64,192,1,1,16]{1,4,3,2,0:T(8,128)(2,1)} %pad_maximum_fusion.1), calls=%async_computation.1 | async-start | bytes 1048576 | tf_op jit(solution)/shard_map/all_to_all | solution.py:155
  79.9 0.6 dynamic-slice
  81.1 15.6 %all-to-all-done.1 = bf16[64,192,1,1,16]{1,4,3,2,0:T(8,128)(2,1)S(1)} async-done(((bf16[64,192,1,1,16]{1,4,3,2,0:T(8,128)(2,1)}), bf16[64,192,1,1,16]{1,4,3,2,0:T(8,128)(2,1)S(1)}, u32[]{:S(2)}, u32[]{:S(2)}) %all-to-all-start.1) | async-done | bytes 393248 | tf_op jit(solution)/shard_map/all_to_all | solution.py:155
  96.8 0.8 copy.64
  97.8 8.3 %all-reduce.1 = bf16[8,128]{1,0:T(8,128)(2,1)S(1)} all-reduce(f32[8,128]{1,0:T(8,128)S(1)} %reduce_sum.32), channel_id=2, replica_groups=mesh['seq'=64,'tp'=4] {'tp'}, use_global_device_ids=true, to_apply=%region_3.4.clone | all-reduce | flops 1024 | bytes 6144
  106.2 0.5 dynamic-slice_convert_fusion
  (43 shorter events, 1.3 us)
Async XLA Ops:
  2.1 12.2 %collective-permute-start = (bf16[3,2,1024]{2,1,0:T(2,128)(2,1)S(1)}, bf16[3,2,1024]{2,1,0:T(2,128)(2,1)S(1)}, u32[]{:S(2)}, u32[]{:S(2)}) collective-permute-start(bf16[3,2,1024]{2,1,0:T(2,128)(2,1)S(1)} %pad_maximum_fusion.2), channel_id=1, source_target_pairs={{0,4},{4,8},{8,12},{12,16},{16,20},{20,24},{24,28},{28,32},{32,36}... | collective-permute-start | bytes 36872 | tf_op jit(solution)/shard_map/ppermute | solution.py:17
  15.6 17.1 %copy-start.3 = (bf16[32,16,128]{2,1,0:T(8,128)(2,1)S(1)}, bf16[32,16,128]{2,1,0:T(8,128)(2,1)}, u32[]{:S(2)}) copy-start(bf16[32,16,128]{2,1,0:T(8,128)(2,1)} %param.15) | copy-start | bytes 393220
  18.8 35.1 %all-to-all-start = ((bf16[64,258,16]{1,2,0:T(8,128)(2,1)}), bf16[64,258,16]{1,2,0:T(8,128)(2,1)S(1)}, u32[]{:S(2)}, u32[]{:S(2)}) async-start(bf16[64,258,16]{1,2,0:T(8,128)(2,1)} %pad_maximum_fusion), calls=%async_computation | async-start | bytes 1572864 | tf_op jit(solution)/shard_map/all_to_all | solution.py:116
  31.1 5.5 %copy-start.5 = (f32[16,128]{1,0:T(8,128)}, f32[16,128]{1,0:T(8,128)S(1)}, u32[]{:S(2)}) copy-start(f32[16,128]{1,0:T(8,128)S(1)} %concatenate.46.d_ref) | copy-start | bytes 24580
  32.8 30.7 %copy-start.4 = (f32[16,128]{1,0:T(8,128)S(1)}, f32[16,128]{1,0:T(8,128)}, u32[]{:S(2)}) copy-start(f32[16,128]{1,0:T(8,128)} %concatenate.47.w_ref) | copy-start | bytes 24580
  55.1 10.2 %copy-start.1 = (bf16[1024,128]{1,0:T(8,128)(2,1)S(1)}, bf16[1024,128]{1,0:T(8,128)(2,1)}, u32[]{:S(2)}) copy-start(bf16[1024,128]{1,0:T(8,128)(2,1)} %copy.57.g_ref) | copy-start | bytes 786436
  62.2 3.1 %copy-start.2 = (f32[1024,128]{1,0:T(8,128)S(1)}, f32[1024,128]{1,0:T(8,128)}, u32[]{:S(2)}) copy-start(f32[1024,128]{1,0:T(8,128)} %get-tuple-element.4) | copy-start | bytes 1572868
  66.1 3.5 %copy-start = (bf16[8,8,16,16,128]{4,1,3,0,2:T(8,128)(2,1)S(1)}, bf16[8,8,16,16,128]{4,1,3,0,2:T(8,128)(2,1)}, u32[]{:S(2)}) copy-start(bf16[8,8,16,16,128]{4,1,3,0,2:T(8,128)(2,1)} %get-tuple-element.30) | copy-start | bytes 12582916
  70.4 9.5 %copy-start.6 = (u32[256]{0:T(256)S(1)}, u32[256]{0:T(256)}, u32[]{:S(2)}) copy-start(u32[256]{0:T(256)} %constant.31) | copy-start | bytes 3076
  72.6 24.1 %all-to-all-start.1 = ((bf16[64,192,1,1,16]{1,4,3,2,0:T(8,128)(2,1)}), bf16[64,192,1,1,16]{1,4,3,2,0:T(8,128)(2,1)S(1)}, u32[]{:S(2)}, u32[]{:S(2)}) async-start(bf16[64,192,1,1,16]{1,4,3,2,0:T(8,128)(2,1)} %pad_maximum_fusion.1), calls=%async_computation.1 | async-start | bytes 1048576 | tf_op jit(solution)/shard_map/all_to_all | solution.py:155

commit v16 on v14

--- a/solution.py
+++ b/solution.py
@@ -98,26 +98,24 @@
     seg = span // parts
     blocks = width_v // parts
     lanes = parts * piece
-    before = from_behind(
-        jnp.stack([query_input[-2:], key_input[-2:], value_input[-2:]], axis=0), "v", 1
-    )
-    key_short = short_pass(key_input, before[1], short_filter[:, 1])
-    value_short = short_pass(value_input, before[2], short_filter[:, 2])
-    gated_rows = (key_short * value_short).astype(jnp.bfloat16)
-
     def by_target(values):
         depth = values.shape[0]
         return jnp.transpose(values.reshape(depth, width_v, piece), (1, 0, 2))
 
     payload = jnp.concatenate(
-        [by_target(before[0]), by_target(query_input), by_target(gated_rows)], axis=1
+        [by_target(key_input), by_target(value_input), by_target(query_input)], axis=1
     )
     depth = payload.shape[1]
     columns = lax.all_to_all(payload, "v", split_axis=0, concat_axis=0, tiled=True)
     columns = jnp.transpose(columns.reshape(parts, blocks, depth, piece), (1, 2, 0, 3))
-    query_before = columns[0, :2].reshape(2, lanes)
-    query_p = columns[:, 2 : 2 + tokens].reshape(seg, lanes)
-    gated_p = columns[:, 2 + tokens :].reshape(seg, lanes)
+    key_p, value_p, query_p = (
+        columns[:, i * tokens : (i + 1) * tokens].reshape(seg, lanes) for i in range(3)
+    )
+
+    def behind(values):
+        lead = jnp.zeros((2, piece), values.dtype)
+        return jnp.concatenate([lead, values[-2:, : lanes - piece]], axis=1)
+
     head = lax.axis_index("v") * piece
 
     def own(values):
@@ -125,7 +123,10 @@
 
     sf = jnp.concatenate([own(short_filter)] * parts, axis=2)
     gain = jnp.concatenate([own(skip_gain)] * parts, axis=0)
-    query_short = short_pass(query_p, query_before, sf[:, 0])
+    key_short = short_pass(key_p, behind(key_p), sf[:, 1])
+    value_short = short_pass(value_p, behind(value_p), sf[:, 2])
+    gated_p = (key_short * value_short).astype(jnp.bfloat16)
+    query_short = short_pass(query_p, behind(query_p), sf[:, 0])
     convolved = packed_conv(gated_p, own(residues), own(decays), parts)
     carried = (convolved + gain * gated_p.astype(jnp.float32)).astype(jnp.bfloat16)
     op_p = (query_short * carried.astype(jnp.float32)).astype(jnp.bfloat16)

time: 108 us -> 99.1 us (0.918)
  local copies, waits for them, and re-layouts: 18.8 us -> 14.4 us
  starting transfers between devices: 25 us -> 22.5 us
  other arithmetic: 8.16 us -> 6.99 us
    ppermute x1 -> x0, starting transfers between devices: 5.47 us -> none  [from_behind(): return lax.ppermute(block, axis, route)]
    all_to_all x1, starting transfers between devices: 12.2 us -> 15.1 us  [shards(): lax.all_to_all(payload, 'v', split_axis=0, concat_axis=0, tiled=True)]
    another operation x4 -> x0, local copies, waits for them, and re-layouts: 1.64 us -> none  [the longest x2 1.47 us: shards(): jnp.stack([query_input[-2:], key_input[-2:], value_input[-2:]], axis=0)]
    unnamed x22 -> x23, local copies, waits for them, and re-layouts: 5.38 us -> 5.03 us
  transfers between devices with their start and end apart: 3 -> 2, of which waited for: 2 -> 2; matrix products, arithmetic and copies ran while one was open for 8% -> 4% of each run, Pallas kernels for 0% -> 0%
where the time goes in v16:
time: 99.1 us; the launch traced here: 98.5 us
  waiting for transfers between devices  35 us (35%)
  starting transfers between devices  22.5 us (23%)
  local copies, waits for them, and re-layouts  14.4 us (15%)
  blocking collectives  8.26 us (8%)
  other arithmetic  6.99 us (7%)
  Pallas kernels  6.93 us (7%)
  matrix products  2.81 us (3%)
  between operations  1.63 us (2%)
    all_to_all x1, waiting for transfers between devices, shards(): lax.all_to_all(payload, 'v', split_axis=0, concat_axis=0, tiled=True)  19.4 us
    all_to_all x1, waiting for transfers between devices, shards(): lax.all_to_all(outgoing, 'v', split_axis=0, concat_axis=3, tiled=True)[0]  15.6 us
    all_to_all x1, starting transfers between devices, shards(): lax.all_to_all(payload, 'v', split_axis=0, concat_axis=0, tiled=True)  15.1 us
    unnamed x1, blocking collectives  8.26 us
    all_to_all x1, starting transfers between devices, shards(): lax.all_to_all(outgoing, 'v', split_axis=0, concat_axis=3, tiled=True)[0]  7.41 us
    pallas_call x1, Pallas kernels, packed_conv(): pl.pallas_call(conv_kernel, out_shape=(jax.ShapeDtypeStruct((seg, lanes),...  6.93 us
    unnamed x23, local copies, waits for them, and re-layouts  5.03 us
    reshape x1, local copies, waits for them, and re-layouts, shards(): late_rows = extended[STRIDE:].reshape(rows_seg, STRIDE, parts, piece)  2.37 us
  transfers between devices with their start and end apart: 2, of which 2 were waited for; matrix products, arithmetic and copies ran while one was open for 4% of the time, Pallas kernels for 0%

profile of v16, /device:TPU:1, one launch (start us, length us, event | category | flops | bytes accessed | tf_op | source)
XLA Modules:
  0.0 98.5 jit_solution(15159314956419444245)
XLA Ops:
  0.6 1.1 %copy.53 = bf16[128,1024]{0,1:T(8,128)(2,1)S(1)} copy(bf16[128,1024]{1,0:T(8,128)(2,1)} %param.9) | data formatting | bytes 524288 | tf_op args[1]
  1.8 1.1 %copy.54 = bf16[128,1024]{0,1:T(8,128)(2,1)S(1)} copy(bf16[128,1024]{1,0:T(8,128)(2,1)} %param.10) | data formatting | bytes 524288 | tf_op args[2]
  2.9 1.1 %copy.55 = bf16[128,1024]{0,1:T(8,128)(2,1)S(1)} copy(bf16[128,1024]{1,0:T(8,128)(2,1)} %param.8) | data formatting | bytes 524288 | tf_op args[0]
  4.0 1.0 %pad_maximum_fusion = bf16[64,384,16]{1,2,0:T(8,128)(2,1)} fusion(bf16[64,128,16]{1,2,0:T(8,128)(2,1)S(1)} %bitcast.100, bf16[64,128,16]{1,2,0:T(8,128)(2,1)S(1)} %bitcast.99, bf16[64,128,16]{1,2,0:T(8,128)(2,1)S(1)} %bitcast.98), kind=kLoop, calls=%fused_computation.6 | loop fusion | flops 2359296 | bytes 1572864 | tf_op jit(solution)/shard_map/concatenate | solution.py:105
  5.0 15.1 %all-to-all-start = ((bf16[64,384,16]{1,2,0:T(8,128)(2,1)}), bf16[64,384,16]{1,2,0:T(8,128)(2,1)S(1)}, u32[]{:S(2)}, u32[]{:S(2)}) async-start(bf16[64,384,16]{1,2,0:T(8,128)(2,1)} %pad_maximum_fusion), calls=%async_computation | async-start | bytes 1572864 | tf_op jit(solution)/shard_map/all_to_all | solution.py:109
  20.2 0.1 constant_dynamic-slice_fusion.1
  20.2 0.1 concatenate.50
  20.4 0.8 fusion.29
  21.1 0.1 concatenate.58.d_ref
  21.2 0.8 sqrt_multiply_fusion
  22.0 0.7 concatenate.59.w_ref
  22.7 0.8 dynamic_slice.15
  23.5 0.1 concatenate.60
  23.6 0.1 fusion.28
  23.6 0.1 convert_multiply_fusion
  23.7 19.4 %all-to-all-done = bf16[64,384,16]{1,2,0:T(8,128)(2,1)S(1)} async-done(((bf16[64,384,16]{1,2,0:T(8,128)(2,1)}), bf16[64,384,16]{1,2,0:T(8,128)(2,1)S(1)}, u32[]{:S(2)}, u32[]{:S(2)}) %all-to-all-start) | async-done | bytes 786464 | tf_op jit(solution)/shard_map/all_to_all | solution.py:109
  43.1 0.2 fusion.30
  43.3 0.1 copy.59
  43.4 0.2 copy.60
  43.8 0.2 copy.63
  44.0 0.1 fusion.20
  44.1 1.0 %fusion.8.g_ref = bf16[1024,128]{1,0:T(8,128)(2,1)} fusion(f32[1026,128]{1,0:T(8,128)S(1)} %get-tuple-element.27, f32[1026,128]{1,0:T(8,128)S(1)} %get-tuple-element.26, f32[128]{0:T(128)S(1)} %get-tuple-element.18, f32[128]{0:T(128)S(1)} %get-tuple-element.19, f32[128]{0:T(128)S(1)} %get-tuple-element.20, f32[128]{0:T(128)S(1)} %get-tuple-element.21, ...), kind=kLoop, calls=%fused_computation.15 | loop fusion | flops 1572864 | bytes 3410944 | tf_op jit(solution)/shard_map/convert_element_type | solution.py:128
  45.1 6.9 %shard_map.95 = (f32[1024,128]{1,0:T(8,128)}, f32[16,128]{1,0:T(8,128)}) custom-call(bf16[1024,128]{1,0:T(8,128)(2,1)} %fusion.8.g_ref, f32[16,128]{1,0:T(8,128)} %copy-done.5, f32[16,128]{1,0:T(8,128)} %concatenate.59.w_ref), custom_call_target="tpu_custom_call" | custom-call | tf_op jit(solution)/shard_map/pallas_call | solution.py:71
  52.1 0.8 mul.214
  52.9 0.3 multiply_reduce_fusion.1
  53.2 0.1 reshape.259
  53.4 0.2 copy.57
  53.6 0.1 fusion.18
  53.7 1.4 %multiply_reduce_fusion = f32[1024,128]{1,0:T(8,128)S(1)} fusion(f32[1024]{0:T(1024)S(1)} %iota_add_fusion, f32[16,128]{1,0:T(8,128)S(1)} %neg.17, f32[16,128]{1,0:T(8,128)S(1)} %mul.217), kind=kLoop, calls=%fused_computation | loop fusion | flops 6160384 | bytes 544768 | tf_op jit(solution)/shard_map/reduce_sum | solution.py:87
  55.1 0.3 fusion.14
  55.4 0.1 slice.167
  55.5 1.3 %reshape.262 = bf16[64,16,8,16]{3,2,1,0:T(8,128)(2,1)S(1)} reshape(bf16[1024,128]{1,0:T(8,128)(2,1)S(1)} %fusion.14) | data formatting | bytes 524288 | tf_op jit(solution)/shard_map/reshape | solution.py:138
  56.8 0.1 copy.65
  57.0 2.4 %reshape.263 = bf16[64,16,8,16]{3,2,1,0:T(8,128)(2,1)} reshape(bf16[1024,128]{1,0:T(8,128)(2,1)S(1)} %fusion.23) | data formatting | bytes 524288 | tf_op jit(solution)/shard_map/reshape | solution.py:139
  59.4 2.2 %convolution_bitcast_fusion = f32[64,8,128]{2,1,0:T(8,128)S(1)} fusion(bf16[64,16,8,16]{3,2,1,0:T(8,128)(2,1)} %reshape.263, bf16[32,16,128]{2,1,0:T(8,128)(2,1)S(1)} %copy-done.3), kind=kOutput, calls=%fused_computation.1 | convolution fusion | flops 33554432 | bytes 589824 | tf_op jit(solution)/shard_map/jisc,ico->sjo/dot_general | solution.py:142
  61.6 0.6 fusion.2
  62.2 0.7 reshape.264
  62.9 0.4 copy.68
  63.4 0.9 pad_maximum_fusion.1
  64.3 7.4 %all-to-all-start.1 = ((bf16[64,192,1,1,16]{1,4,3,2,0:T(8,128)(2,1)}), bf16[64,192,1,1,16]{1,4,3,2,0:T(8,128)(2,1)S(1)}, u32[]{:S(2)}, u32[]{:S(2)}) async-start(bf16[64,192,1,1,16]{1,4,3,2,0:T(8,128)(2,1)} %pad_maximum_fusion.1), calls=%async_computation.1 | async-start | bytes 1048576 | tf_op jit(solution)/shard_map/all_to_all | solution.py:149
  71.7 0.6 dynamic-slice
  73.0 15.6 %all-to-all-done.1 = bf16[64,192,1,1,16]{1,4,3,2,0:T(8,128)(2,1)S(1)} async-done(((bf16[64,192,1,1,16]{1,4,3,2,0:T(8,128)(2,1)}), bf16[64,192,1,1,16]{1,4,3,2,0:T(8,128)(2,1)S(1)}, u32[]{:S(2)}, u32[]{:S(2)}) %all-to-all-start.1) | async-done | bytes 393248 | tf_op jit(solution)/shard_map/all_to_all | solution.py:149
  88.7 0.1 convert_reduce_fusion
  88.8 0.8 copy.70
  89.6 0.1 copy.69
  89.7 0.1 reduce_sum.32
  89.8 8.3 %all-reduce.4 = bf16[8,128]{1,0:T(8,128)(2,1)S(1)} all-reduce(f32[8,128]{1,0:T(8,128)S(1)} %reduce_sum.32), channel_id=2, replica_groups=mesh['seq'=64,'tp'=4] {'tp'}, use_global_device_ids=true, to_apply=%region_3.4.clone | all-reduce | flops 1024 | bytes 6144
  98.0 0.5 dynamic-slice_convert_fusion
  (32 shorter events, 0.5 us)
Async XLA Ops:
  0.6 19.5 %copy-start = (f32[3,3,1024]{2,1,0:T(4,128)S(1)}, f32[3,3,1024]{2,1,0:T(4,128)}, u32[]{:S(2)}) copy-start(f32[3,3,1024]{2,1,0:T(4,128)} %param.11) | copy-start | bytes 110596
  5.0 38.1 %all-to-all-start = ((bf16[64,384,16]{1,2,0:T(8,128)(2,1)}), bf16[64,384,16]{1,2,0:T(8,128)(2,1)S(1)}, u32[]{:S(2)}, u32[]{:S(2)}) async-start(bf16[64,384,16]{1,2,0:T(8,128)(2,1)} %pad_maximum_fusion), calls=%async_computation | async-start | bytes 1572864 | tf_op jit(solution)/shard_map/all_to_all | solution.py:109
  21.2 22.5 %copy-start.5 = (f32[16,128]{1,0:T(8,128)}, f32[16,128]{1,0:T(8,128)S(1)}, u32[]{:S(2)}) copy-start(f32[16,128]{1,0:T(8,128)S(1)} %concatenate.58.d_ref) | copy-start | bytes 24580
  44.1 9.2 %copy-start.4 = (f32[16,128]{1,0:T(8,128)S(1)}, f32[16,128]{1,0:T(8,128)}, u32[]{:S(2)}) copy-start(f32[16,128]{1,0:T(8,128)} %concatenate.59.w_ref) | copy-start | bytes 24580
  53.7 1.4 %copy-start.1 = (bf16[1024,128]{1,0:T(8,128)(2,1)S(1)}, bf16[1024,128]{1,0:T(8,128)(2,1)}, u32[]{:S(2)}) copy-start(bf16[1024,128]{1,0:T(8,128)(2,1)} %fusion.8.g_ref) | copy-start | bytes 786436
  53.7 1.4 %copy-start.2 = (f32[1024,128]{1,0:T(8,128)S(1)}, f32[1024,128]{1,0:T(8,128)}, u32[]{:S(2)}) copy-start(f32[1024,128]{1,0:T(8,128)} %get-tuple-element.4) | copy-start | bytes 1572868
  56.8 2.6 %copy-start.3 = (bf16[32,16,128]{2,1,0:T(8,128)(2,1)S(1)}, bf16[32,16,128]{2,1,0:T(8,128)(2,1)}, u32[]{:S(2)}) copy-start(bf16[32,16,128]{2,1,0:T(8,128)(2,1)} %param.15) | copy-start | bytes 393220
  62.9 8.8 %copy-start.6 = (u32[256]{0:T(256)S(1)}, u32[256]{0:T(256)}, u32[]{:S(2)}) copy-start(u32[256]{0:T(256)} %constant.38) | copy-start | bytes 3076
  64.3 24.3 %all-to-all-start.1 = ((bf16[64,192,1,1,16]{1,4,3,2,0:T(8,128)(2,1)}), bf16[64,192,1,1,16]{1,4,3,2,0:T(8,128)(2,1)S(1)}, u32[]{:S(2)}, u32[]{:S(2)}) async-start(bf16[64,192,1,1,16]{1,4,3,2,0:T(8,128)(2,1)} %pad_maximum_fusion.1), calls=%async_computation.1 | async-start | bytes 1048576 | tf_op jit(solution)/shard_map/all_to_all | solution.py:149

commit v17 on v16

--- a/solution.py
+++ b/solution.py
@@ -143,13 +143,12 @@
         "jisc,ico->sjo", late_rows, head_weight[STRIDE:], preferred_element_type=jnp.float32
     )
     op_t = jnp.transpose(op_p.reshape(blocks, tokens, parts, piece), (2, 0, 1, 3))
-    op_t = op_t.reshape(width_v, tokens, 1, 1, piece)
-    sums = partial_sum.astype(jnp.bfloat16).reshape(width_v, -1, 1, 1, piece)
-    outgoing = jnp.concatenate([op_t, sums], axis=1)
-    incoming = lax.all_to_all(outgoing, "v", split_axis=0, concat_axis=3, tiled=True)[0]
-    operator_out = incoming[:tokens].reshape(tokens, chan_width)
-    sums = jnp.transpose(incoming[tokens:], (2, 0, 1, 3)).astype(jnp.float32)
-    block_sum = jnp.sum(sums.reshape(width_v, tokens // STRIDE, -1), axis=0)
+    op_t = op_t.reshape(width_v, tokens, 1, piece)
+    incoming = lax.all_to_all(op_t, "v", split_axis=0, concat_axis=2, tiled=True)[0]
+    operator_out = incoming.reshape(tokens, chan_width)
+    block_sum = lax.psum_scatter(
+        partial_sum.reshape(span // STRIDE, -1), "v", scatter_dimension=0, tiled=True
+    )
     probe_out = lax.psum_scatter(block_sum, "tp", scatter_dimension=0, tiled=True).astype(
         jnp.bfloat16
     )

time: 99.1 us -> 741 us (7.48)
  waiting for transfers between devices: 35 us -> 636 us
  blocking collectives: 8.26 us -> 35.3 us
  between operations: 1.63 us -> 15.6 us
    unnamed x0 -> x2, waiting for transfers between devices: none -> 617 us
    unnamed x1, blocking collectives: 8.26 us -> 35.3 us
    all_to_all x1, waiting for transfers between devices: 15.6 us -> 0.01 us  [shards(): lax.all_to_all(op_t, 'v', split_axis=0, concat_axis=2, tiled=True)[0]]
  transfers between devices with their start and end apart: 2 -> 3, of which waited for: 2 -> 2; matrix products, arithmetic and copies ran while one was open for 4% -> 1% of each run, Pallas kernels for 0% -> 0%
where the time goes in v17:
time: 741 us
  waiting for transfers between devices  636 us (86%)
  blocking collectives  35.3 us (5%)
  starting transfers between devices  22.5 us (3%)
  local copies, waits for them, and re-layouts  16.8 us (2%)
  between operations  15.6 us (2%)
    unnamed x2, waiting for transfers between devices  617 us
    unnamed x1, blocking collectives  35.3 us
    all_to_all x1, waiting for transfers between devices, shards(): lax.all_to_all(payload, 'v', split_axis=0, concat_axis=0, tiled=True)  19.4 us
    all_to_all x1, starting transfers between devices, shards(): lax.all_to_all(payload, 'v', split_axis=0, concat_axis=0, tiled=True)  15.1 us
  transfers between devices with their start and end apart: 3, of which 2 were waited for; matrix products, arithmetic and copies ran while one was open for 1% of the time, Pallas kernels for 0%

profile of v17, /device:TPU:1, one launch (start us, length us, event | category | flops | bytes accessed | tf_op | source)
XLA Modules:
  0.0 740.6 jit_solution(16868211134418277385)
XLA Ops:
  7.2 1.1 copy.50
  8.3 1.1 copy.51
  9.4 1.1 copy.52
  10.6 1.0 pad_maximum_fusion
  11.6 15.1 %all-to-all-start = ((bf16[64,384,16]{1,2,0:T(8,128)(2,1)}), bf16[64,384,16]{1,2,0:T(8,128)(2,1)S(1)}, u32[]{:S(2)}, u32[]{:S(2)}) async-start(bf16[64,384,16]{1,2,0:T(8,128)(2,1)} %pad_maximum_fusion), calls=%async_computation | async-start | bytes 1572864 | tf_op jit(solution)/shard_map/all_to_all | solution.py:109
  26.7 0.1 constant_dynamic-slice_fusion.2
  26.8 0.1 concatenate.47
  26.9 0.8 fusion.28
  27.7 0.1 concatenate.55.d_ref
  27.8 0.8 sqrt_multiply_fusion
  28.5 0.7 concatenate.56.w_ref
  29.2 0.8 dynamic_slice.15
  30.0 0.1 concatenate.57
  30.1 0.1 fusion.27
  30.2 0.1 convert_multiply_fusion
  30.2 19.4 %all-to-all-done = bf16[64,384,16]{1,2,0:T(8,128)(2,1)S(1)} async-done(((bf16[64,384,16]{1,2,0:T(8,128)(2,1)}), bf16[64,384,16]{1,2,0:T(8,128)(2,1)S(1)}, u32[]{:S(2)}, u32[]{:S(2)}) %all-to-all-start) | async-done | bytes 786464 | tf_op jit(solution)/shard_map/all_to_all | solution.py:109
  49.6 0.1 fusion.29
  49.8 0.1 copy.56
  49.9 0.2 copy.57
  50.1 0.1 copy.59
  50.2 0.2 copy.60
  50.4 0.1 fusion.19
  50.5 1.0 fusion.7.g_ref
  51.6 6.9 shard_map.95
  58.5 0.8 mul.214
  59.3 0.3 multiply_reduce_fusion.1
  59.6 0.1 reshape.248
  59.9 0.2 copy.54
  60.1 0.1 fusion.17
  60.1 1.4 multiply_reduce_fusion
  61.6 0.3 fusion.13
  61.9 0.1 slice.157
  61.9 2.4 reshape.251
  64.3 0.1 copy.62
  64.5 1.4 reshape.252
  65.9 0.8 copy.63
  66.7 7.4 all-to-all-start.1
  74.1 0.6 convolution_bitcast_fusion
  74.7 1.0 copy-done.1
  75.7 0.6 fusion.1
  76.3 0.8 copy.64
  77.1 0.6 dynamic-slice
  77.7 0.6 dynamic-slice.2
  79.6 616.8 %all-reduce.8.cloned.1.call-done = f32[512,128]{1,0:T(8,128)} async-done(((f32[512,128]{1,0:T(8,128)}), f32[512,128]{1,0:T(8,128)}) %all-reduce.8.cloned.1.call-update) | async-done | bytes 262160
  696.4 0.7 constant_dynamic-slice_fusion
  697.1 35.3 %all-reduce.5 = bf16[8,128]{1,0:T(8,128)(2,1)S(1)} all-reduce(f32[8,128]{1,0:T(8,128)S(1)} %constant_dynamic-slice_fusion), channel_id=3, replica_groups=mesh['seq'=64,'tp'=4] {'tp'}, use_global_device_ids=true, to_apply=%region_3.4.clone | all-reduce | flops 1024 | bytes 6144
  732.4 0.5 dynamic-slice_convert_fusion
  732.9 0.8 copy.65
  (34 shorter events, 0.4 us)
Async XLA Ops:
  7.2 19.5 %copy-start = (f32[3,3,1024]{2,1,0:T(4,128)S(1)}, f32[3,3,1024]{2,1,0:T(4,128)}, u32[]{:S(2)}) copy-start(f32[3,3,1024]{2,1,0:T(4,128)} %param.11) | copy-start | bytes 110596
  11.6 38.1 %all-to-all-start = ((bf16[64,384,16]{1,2,0:T(8,128)(2,1)}), bf16[64,384,16]{1,2,0:T(8,128)(2,1)S(1)}, u32[]{:S(2)}, u32[]{:S(2)}) async-start(bf16[64,384,16]{1,2,0:T(8,128)(2,1)} %pad_maximum_fusion), calls=%async_computation | async-start | bytes 1572864 | tf_op jit(solution)/shard_map/all_to_all | solution.py:109
  27.8 22.5 %copy-start.6 = (f32[16,128]{1,0:T(8,128)}, f32[16,128]{1,0:T(8,128)S(1)}, u32[]{:S(2)}) copy-start(f32[16,128]{1,0:T(8,128)S(1)} %concatenate.55.d_ref) | copy-start | bytes 24580
  50.5 9.2 %copy-start.5 = (f32[16,128]{1,0:T(8,128)S(1)}, f32[16,128]{1,0:T(8,128)}, u32[]{:S(2)}) copy-start(f32[16,128]{1,0:T(8,128)} %concatenate.56.w_ref) | copy-start | bytes 24580
  60.1 1.4 copy-start.2
  60.1 1.4 copy-start.3
  64.5 9.7 %copy-start.4 = (bf16[32,16,128]{2,1,0:T(8,128)(2,1)S(1)}, bf16[32,16,128]{2,1,0:T(8,128)(2,1)}, u32[]{:S(2)}) copy-start(bf16[32,16,128]{2,1,0:T(8,128)(2,1)} %param.15) | copy-start | bytes 393220
  66.7 666.2 %all-to-all-start.1 = ((bf16[64,128,1,16]{1,3,2,0:T(8,128)(2,1)}), bf16[64,128,1,16]{1,3,2,0:T(8,128)(2,1)S(1)}, u32[]{:S(2)}, u32[]{:S(2)}) async-start(bf16[64,128,1,16]{1,3,2,0:T(8,128)(2,1)} %bitcast.19), calls=%async_computation.1 | async-start | bytes 524288 | tf_op jit(solution)/shard_map/all_to_all | solution.py:147
  74.1 622.4 %all-reduce.8.cloned.1.call-start = ((), (), s32[]{:S(2)}) async-start(), calls=%async_computation.2 | async-start | bytes 524288
  74.1 1.6 copy-start.1
  75.7 1.4 copy-start.8
  75.7 2.0 copy-start.7
Sparse Core Ops, SparseCore 0:
  77.5 618.8 all-reduce.7

commit v18 on v16

--- a/solution.py
+++ b/solution.py
@@ -135,13 +135,20 @@
     )
     extended = jnp.concatenate([op_p, following], axis=0)
     rows_seg = seg // STRIDE
-    early_rows = extended[:seg].reshape(rows_seg, STRIDE, parts, piece)
-    late_rows = extended[STRIDE:].reshape(rows_seg, STRIDE, parts, piece)
-    partial_sum = jnp.einsum(
-        "jisc,ico->sjo", early_rows, head_weight[:STRIDE], preferred_element_type=jnp.float32
-    ) + jnp.einsum(
-        "jisc,ico->sjo", late_rows, head_weight[STRIDE:], preferred_element_type=jnp.float32
-    )
+    eye = jnp.eye(parts, dtype=head_weight.dtype)
+
+    def spread(taps):
+        return jnp.einsum("ico,ts->itcso", taps, eye).reshape(STRIDE * lanes, parts * taps.shape[2])
+
+    early_rows = extended[:seg].reshape(rows_seg, STRIDE * lanes)
+    late_rows = extended[STRIDE:].reshape(rows_seg, STRIDE * lanes)
+    by_lane = jnp.dot(
+        early_rows, spread(head_weight[:STRIDE]), preferred_element_type=jnp.float32
+    ) + jnp.dot(late_rows, spread(head_weight[STRIDE:]), preferred_element_type=jnp.float32)
+    per_block = tokens // STRIDE
+    partial_sum = jnp.transpose(
+        by_lane.reshape(blocks, per_block, parts, -1), (2, 0, 1, 3)
+    ).reshape(width_v, per_block, -1)
     op_t = jnp.transpose(op_p.reshape(blocks, tokens, parts, piece), (2, 0, 1, 3))
     op_t = op_t.reshape(width_v, tokens, 1, 1, piece)
     sums = partial_sum.astype(jnp.bfloat16).reshape(width_v, -1, 1, 1, piece)

time: 99.1 us -> 97.3 us (0.982)
  other arithmetic: 6.99 us -> 10.9 us
  waiting for transfers between devices: 35 us -> 31.1 us
  local copies, waits for them, and re-layouts: 14.4 us -> 11.2 us
  matrix products: 2.81 us -> 4.02 us
    reshape x4 -> x2, local copies, waits for them, and re-layouts: 4.73 us -> 0.23 us  [the longest x1 0.12 us: shards(): late_rows = extended[STRIDE:].reshape(rows_seg, STRIDE * lanes)]
    all_to_all x1, waiting for transfers between devices: 19.4 us -> 15.5 us  [shards(): lax.all_to_all(payload, 'v', split_axis=0, concat_axis=0, tiled=True)]
    dot_general x0 -> x1, other arithmetic: none -> 3.85 us  [spread(): jnp.einsum('ico,ts->itcso', taps, eye)]
    dot_general x2, matrix products: 2.81 us -> 4.02 us  [the longest x1 3.18 us: shards(): jnp.dot(late_rows, spread(head_weight[STRIDE:]), preferred_element_type=j...]
    convert_element_type x1 -> x3, local copies, waits for them, and re-layouts: 0.02 us -> 1.04 us  [shards(): sums = partial_sum.astype(jnp.bfloat16).reshape(width_v, -1, 1, 1, piece)]
    unnamed x23 -> x25, local copies, waits for them, and re-layouts: 5.03 us -> 5.31 us
  transfers between devices with their start and end apart: 2 -> 2, of which waited for: 2 -> 2; matrix products, arithmetic and copies ran while one was open for 4% -> 8% of each run, Pallas kernels for 0% -> 0%
where the time goes in v18:
time: 97.3 us; the launch traced here: 96.8 us
  waiting for transfers between devices  31.1 us (32%)
  starting transfers between devices  22.5 us (23%)
  local copies, waits for them, and re-layouts  11.2 us (12%)
  other arithmetic  10.9 us (11%)
  blocking collectives  8.26 us (8%)
  Pallas kernels  7.03 us (7%)
  matrix products  4.02 us (4%)
  between operations  1.66 us (2%)
    all_to_all x1, waiting for transfers between devices, shards(): lax.all_to_all(outgoing, 'v', split_axis=0, concat_axis=3, tiled=True)[0]  15.6 us
    all_to_all x1, waiting for transfers between devices, shards(): lax.all_to_all(payload, 'v', split_axis=0, concat_axis=0, tiled=True)  15.5 us
    all_to_all x1, starting transfers between devices, shards(): lax.all_to_all(payload, 'v', split_axis=0, concat_axis=0, tiled=True)  15.1 us
    unnamed x1, blocking collectives  8.26 us
    all_to_all x1, starting transfers between devices, shards(): lax.all_to_all(outgoing, 'v', split_axis=0, concat_axis=3, tiled=True)[0]  7.4 us
    pallas_call x1, Pallas kernels, packed_conv(): pl.pallas_call(conv_kernel, out_shape=(jax.ShapeDtypeStruct((seg, lanes),...  7.03 us
    unnamed x25, local copies, waits for them, and re-layouts  5.31 us
    dot_general x1, other arithmetic, spread(): jnp.einsum('ico,ts->itcso', taps, eye)  3.85 us
  transfers between devices with their start and end apart: 2, of which 2 were waited for; matrix products, arithmetic and copies ran while one was open for 8% of the time, Pallas kernels for 0%

profile of v18, /device:TPU:1, one launch (start us, length us, event | category | flops | bytes accessed | tf_op | source)
XLA Modules:
  0.0 96.8 jit_solution(17917788256491628482)
XLA Ops:
  0.7 1.2 %copy.45 = bf16[128,1024]{0,1:T(8,128)(2,1)S(1)} copy(bf16[128,1024]{1,0:T(8,128)(2,1)} %param.9) | data formatting | bytes 524288 | tf_op args[1]
  1.8 1.1 %copy.46 = bf16[128,1024]{0,1:T(8,128)(2,1)S(1)} copy(bf16[128,1024]{1,0:T(8,128)(2,1)} %param.10) | data formatting | bytes 524288 | tf_op args[2]
  2.9 1.1 %copy.47 = bf16[128,1024]{0,1:T(8,128)(2,1)S(1)} copy(bf16[128,1024]{1,0:T(8,128)(2,1)} %param.8) | data formatting | bytes 524288 | tf_op args[0]
  4.1 1.0 %pad_maximum_fusion = bf16[64,384,16]{1,2,0:T(8,128)(2,1)} fusion(bf16[64,128,16]{1,2,0:T(8,128)(2,1)S(1)} %bitcast.107, bf16[64,128,16]{1,2,0:T(8,128)(2,1)S(1)} %bitcast.106, bf16[64,128,16]{1,2,0:T(8,128)(2,1)S(1)} %bitcast.105), kind=kLoop, calls=%fused_computation.12 | loop fusion | flops 2359296 | bytes 1572864 | tf_op jit(solution)/shard_map/concatenate | solution.py:105
  5.1 15.1 %all-to-all-start = ((bf16[64,384,16]{1,2,0:T(8,128)(2,1)}), bf16[64,384,16]{1,2,0:T(8,128)(2,1)S(1)}, u32[]{:S(2)}, u32[]{:S(2)}) async-start(bf16[64,384,16]{1,2,0:T(8,128)(2,1)} %pad_maximum_fusion), calls=%async_computation | async-start | bytes 1572864 | tf_op jit(solution)/shard_map/all_to_all | solution.py:109
  20.3 0.1 constant_dynamic-slice_fusion.1
  20.3 0.1 concatenate.50
  20.5 0.8 fusion.38
  21.2 0.1 concatenate.58.d_ref
  21.3 0.8 sqrt_multiply_fusion
  22.1 0.7 concatenate.59.w_ref
  22.8 0.8 dynamic_slice.15
  23.6 0.1 concatenate.60
  23.6 0.1 fusion.36
  23.8 3.8 %broadcast_multiply_fusion.1 = (bf16[8,8,16,16,128]{4,1,3,0,2:T(8,128)(2,1)}, bf16[8,8,16,16,128]{4,1,3,0,2:T(8,128)(2,1)}) fusion(bf16[16,16,128]{2,1,0:T(8,128)(2,1)S(1)} %get-tuple-element.17, bf16[8,8]{1,0:T(8,128)(2,1)S(1)} %fusion.37, bf16[16,16,128]{2,1,0:T(8,128)(2,1)S(1)} %get-tuple-element.18), kind=kLoop, calls=%fused_computation.8 | loop fusion | flops 4194304 | bytes 8519808 | tf_op jit(solution)/shard_map/ico,ts->itcso/dot_general | solution.py:141
  27.7 15.5 %all-to-all-done = bf16[64,384,16]{1,2,0:T(8,128)(2,1)S(1)} async-done(((bf16[64,384,16]{1,2,0:T(8,128)(2,1)}), bf16[64,384,16]{1,2,0:T(8,128)(2,1)S(1)}, u32[]{:S(2)}, u32[]{:S(2)}) %all-to-all-start) | async-done | bytes 786464 | tf_op jit(solution)/shard_map/all_to_all | solution.py:109
  43.2 0.2 fusion.39
  43.5 0.2 copy.52
  43.9 0.2 copy.55
  44.0 0.1 fusion.32
  44.2 1.0 %fusion.20.g_ref = bf16[1024,128]{1,0:T(8,128)(2,1)} fusion(f32[1026,128]{1,0:T(8,128)S(1)} %get-tuple-element.31, f32[1026,128]{1,0:T(8,128)S(1)} %get-tuple-element.30, f32[128]{0:T(128)S(1)} %get-tuple-element.20, f32[128]{0:T(128)S(1)} %get-tuple-element.21, f32[128]{0:T(128)S(1)} %get-tuple-element.22, f32[128]{0:T(128)S(1)} %get-tuple-element.23, ...), kind=kLoop, calls=%fused_computation.21 | loop fusion | flops 1572864 | bytes 3410944 | tf_op jit(solution)/shard_map/convert_element_type | solution.py:128
  45.2 7.0 %shard_map.95 = (f32[1024,128]{1,0:T(8,128)}, f32[16,128]{1,0:T(8,128)}) custom-call(bf16[1024,128]{1,0:T(8,128)(2,1)} %fusion.20.g_ref, f32[16,128]{1,0:T(8,128)} %copy-done.6, f32[16,128]{1,0:T(8,128)} %concatenate.59.w_ref), custom_call_target="tpu_custom_call" | custom-call | tf_op jit(solution)/shard_map/pallas_call | solution.py:71
  52.2 0.8 mul.214
  53.1 0.3 multiply_reduce_fusion.1
  53.4 0.1 reshape.277
  53.6 0.2 copy.49
  53.8 0.1 fusion.30
  53.9 1.4 %multiply_reduce_fusion = f32[1024,128]{1,0:T(8,128)S(1)} fusion(f32[1024]{0:T(1024)S(1)} %iota_add_fusion, f32[16,128]{1,0:T(8,128)S(1)} %neg.17, f32[16,128]{1,0:T(8,128)S(1)} %mul.217), kind=kLoop, calls=%fused_computation | loop fusion | flops 6160384 | bytes 544768 | tf_op jit(solution)/shard_map/reduce_sum | solution.py:87
  55.3 0.3 fusion.26
  55.6 0.1 slice.167
  55.7 0.1 reshape.280
  55.8 0.1 copy.57
  56.0 0.1 reshape.282
  56.1 3.2 %fusion = f32[64,1024]{1,0:T(8,128)S(1)} fusion(bf16[64,2048]{1,0:T(8,128)(2,1)S(1)} %reshape.282, bf16[256,8,8,128]{3,2,1,0:T(8,128)(2,1)} %bitcast.92), kind=kOutput, calls=%fused_computation.1 | convolution fusion | flops 268435456 | bytes 4718592 | tf_op jit(solution)/shard_map/dot_general | solution.py:147
  59.3 0.3 copy-done.1
  59.6 0.8 fusion.12
  60.5 0.7 convert_element_type.71
  61.1 0.4 copy.60
  61.6 0.9 pad_maximum_fusion.1
  62.5 7.4 %all-to-all-start.1 = ((bf16[64,192,1,1,16]{1,4,3,2,0:T(8,128)(2,1)}), bf16[64,192,1,1,16]{1,4,3,2,0:T(8,128)(2,1)S(1)}, u32[]{:S(2)}, u32[]{:S(2)}) async-start(bf16[64,192,1,1,16]{1,4,3,2,0:T(8,128)(2,1)} %pad_maximum_fusion.1), calls=%async_computation.1 | async-start | bytes 1048576 | tf_op jit(solution)/shard_map/all_to_all | solution.py:156
  70.0 0.6 dynamic-slice
  71.2 15.6 %all-to-all-done.1 = bf16[64,192,1,1,16]{1,4,3,2,0:T(8,128)(2,1)S(1)} async-done(((bf16[64,192,1,1,16]{1,4,3,2,0:T(8,128)(2,1)}), bf16[64,192,1,1,16]{1,4,3,2,0:T(8,128)(2,1)S(1)}, u32[]{:S(2)}, u32[]{:S(2)}) %all-to-all-start.1) | async-done | bytes 393248 | tf_op jit(solution)/shard_map/all_to_all | solution.py:156
  86.9 0.1 convert_reduce_fusion
  87.0 0.8 copy.62
  87.8 0.1 copy.61
  87.9 0.1 reduce_sum.32
  88.0 8.3 %all-reduce.4 = bf16[8,128]{1,0:T(8,128)(2,1)S(1)} all-reduce(f32[8,128]{1,0:T(8,128)S(1)} %reduce_sum.32), channel_id=2, replica_groups=mesh['seq'=64,'tp'=4] {'tp'}, use_global_device_ids=true, to_apply=%region_3.4.clone | all-reduce | flops 1024 | bytes 6144
  96.2 0.5 dynamic-slice_convert_fusion
  (37 shorter events, 0.7 us)
Async XLA Ops:
  0.6 19.6 %copy-start = (f32[3,3,1024]{2,1,0:T(4,128)S(1)}, f32[3,3,1024]{2,1,0:T(4,128)}, u32[]{:S(2)}) copy-start(f32[3,3,1024]{2,1,0:T(4,128)} %param.11) | copy-start | bytes 110596
  0.6 23.2 %copy-start.4 = (bf16[32,16,128]{2,1,0:T(8,128)(2,1)S(1)}, bf16[32,16,128]{2,1,0:T(8,128)(2,1)}, u32[]{:S(2)}) copy-start(bf16[32,16,128]{2,1,0:T(8,128)(2,1)} %param.15) | copy-start | bytes 393220
  5.1 38.1 %all-to-all-start = ((bf16[64,384,16]{1,2,0:T(8,128)(2,1)}), bf16[64,384,16]{1,2,0:T(8,128)(2,1)S(1)}, u32[]{:S(2)}, u32[]{:S(2)}) async-start(bf16[64,384,16]{1,2,0:T(8,128)(2,1)} %pad_maximum_fusion), calls=%async_computation | async-start | bytes 1572864 | tf_op jit(solution)/shard_map/all_to_all | solution.py:109
  21.3 6.4 %copy-start.6 = (f32[16,128]{1,0:T(8,128)}, f32[16,128]{1,0:T(8,128)S(1)}, u32[]{:S(2)}) copy-start(f32[16,128]{1,0:T(8,128)S(1)} %concatenate.58.d_ref) | copy-start | bytes 24580
  43.5 10.0 %copy-start.5 = (f32[16,128]{1,0:T(8,128)S(1)}, f32[16,128]{1,0:T(8,128)}, u32[]{:S(2)}) copy-start(f32[16,128]{1,0:T(8,128)} %concatenate.59.w_ref) | copy-start | bytes 24580
  45.2 10.1 %copy-start.2 = (bf16[1024,128]{1,0:T(8,128)(2,1)S(1)}, bf16[1024,128]{1,0:T(8,128)(2,1)}, u32[]{:S(2)}) copy-start(bf16[1024,128]{1,0:T(8,128)(2,1)} %fusion.20.g_ref) | copy-start | bytes 786436
  52.2 3.1 %copy-start.3 = (f32[1024,128]{1,0:T(8,128)S(1)}, f32[1024,128]{1,0:T(8,128)}, u32[]{:S(2)}) copy-start(f32[1024,128]{1,0:T(8,128)} %get-tuple-element.4) | copy-start | bytes 1572868
  56.1 3.5 %copy-start.1 = (bf16[8,8,16,16,128]{4,1,3,0,2:T(8,128)(2,1)S(1)}, bf16[8,8,16,16,128]{4,1,3,0,2:T(8,128)(2,1)}, u32[]{:S(2)}) copy-start(bf16[8,8,16,16,128]{4,1,3,0,2:T(8,128)(2,1)} %get-tuple-element.28) | copy-start | bytes 12582916
  60.4 9.5 %copy-start.7 = (u32[256]{0:T(256)S(1)}, u32[256]{0:T(256)}, u32[]{:S(2)}) copy-start(u32[256]{0:T(256)} %constant.38) | copy-start | bytes 3076
  62.5 24.3 %all-to-all-start.1 = ((bf16[64,192,1,1,16]{1,4,3,2,0:T(8,128)(2,1)}), bf16[64,192,1,1,16]{1,4,3,2,0:T(8,128)(2,1)S(1)}, u32[]{:S(2)}, u32[]{:S(2)}) async-start(bf16[64,192,1,1,16]{1,4,3,2,0:T(8,128)(2,1)} %pad_maximum_fusion.1), calls=%async_computation.1 | async-start | bytes 1048576 | tf_op jit(solution)/shard_map/all_to_all | solution.py:156

commit v19 on v18

--- a/solution.py
+++ b/solution.py
@@ -41,7 +41,7 @@
         w = w_ref[pl.ds(r, 1), :]
         grow = jnp.exp(d * steps)
         shrink = w * jnp.exp(-d * steps)
-        after = w * jnp.exp(-d * (steps + 1.0))
+        step = jnp.exp(-d)
         tail = jnp.exp(-d * float(CHUNK - 1))
         hop = jnp.exp(-d * float(CHUNK))
         state = jnp.zeros((1, width), jnp.float32)
@@ -53,7 +53,7 @@
             y = jnp.dot(lower, high, preferred_element_type=jnp.float32) + jnp.dot(
                 lower, low, preferred_element_type=jnp.float32
             )
-            out_ref[rows, :] += shrink * y + after * state
+            out_ref[rows, :] += shrink * (y + step * state)
             state = hop * state + tail * y[CHUNK - 1 : CHUNK, :]
         total_ref[pl.ds(r, 1), :] = state
         return carry
@@ -102,9 +102,9 @@
         depth = values.shape[0]
         return jnp.transpose(values.reshape(depth, width_v, piece), (1, 0, 2))
 
-    payload = jnp.concatenate(
-        [by_target(key_input), by_target(value_input), by_target(query_input)], axis=1
-    )
+    payload = jnp.stack([key_input, value_input, query_input], axis=0)
+    payload = jnp.transpose(payload.reshape(3, tokens, width_v, piece), (2, 0, 1, 3))
+    payload = payload.reshape(width_v, 3 * tokens, piece)
     depth = payload.shape[1]
     columns = lax.all_to_all(payload, "v", split_axis=0, concat_axis=0, tiled=True)
     columns = jnp.transpose(columns.reshape(parts, blocks, depth, piece), (1, 2, 0, 3))

time: 97.3 us -> 97.3 us (level)
    reshape x0 -> x1, other arithmetic: none -> 1.04 us  [shards(): payload = payload.reshape(width_v, 3 * tokens, piece)]
    concatenate x1 -> x0, other arithmetic: 1.04 us -> none  [shards(): jnp.concatenate([by_target(key_input), by_target(value_input), by_target(...]
where the time goes in v19:
time: 97.3 us; the launch traced here: 96.8 us
  waiting for transfers between devices  31.1 us (32%)
  starting transfers between devices  22.5 us (23%)
  local copies, waits for them, and re-layouts  11.2 us (12%)
  other arithmetic  10.9 us (11%)
  blocking collectives  8.26 us (8%)
  Pallas kernels  7.02 us (7%)
  matrix products  4.03 us (4%)
  between operations  1.66 us (2%)
    all_to_all x1, waiting for transfers between devices, shards(): lax.all_to_all(outgoing, 'v', split_axis=0, concat_axis=3, tiled=True)[0]  15.6 us
    all_to_all x1, waiting for transfers between devices, shards(): lax.all_to_all(payload, 'v', split_axis=0, concat_axis=0, tiled=True)  15.5 us
    all_to_all x1, starting transfers between devices, shards(): lax.all_to_all(payload, 'v', split_axis=0, concat_axis=0, tiled=True)  15.1 us
    unnamed x1, blocking collectives  8.26 us
    all_to_all x1, starting transfers between devices, shards(): lax.all_to_all(outgoing, 'v', split_axis=0, concat_axis=3, tiled=True)[0]  7.4 us
    pallas_call x1, Pallas kernels, packed_conv(): pl.pallas_call(conv_kernel, out_shape=(jax.ShapeDtypeStruct((seg, lanes),...  7.02 us
    unnamed x25, local copies, waits for them, and re-layouts  5.31 us
    dot_general x1, other arithmetic, spread(): jnp.einsum('ico,ts->itcso', taps, eye)  3.85 us
  transfers between devices with their start and end apart: 2, of which 2 were waited for; matrix products, arithmetic and copies ran while one was open for 8% of the time, Pallas kernels for 0%

profile of v19, /device:TPU:1, one launch (start us, length us, event | category | flops | bytes accessed | tf_op | source)
XLA Modules:
  0.0 96.8 jit_solution(13902279162409681340)
XLA Ops:
  0.7 1.2 %copy.64 = bf16[128,1024]{0,1:T(8,128)(2,1)S(1)} copy(bf16[128,1024]{1,0:T(8,128)(2,1)} %param.9) | data formatting | bytes 524288 | tf_op args[1]
  1.8 1.1 %copy.65 = bf16[128,1024]{0,1:T(8,128)(2,1)S(1)} copy(bf16[128,1024]{1,0:T(8,128)(2,1)} %param.10) | data formatting | bytes 524288 | tf_op args[2]
  2.9 1.1 %copy.66 = bf16[128,1024]{0,1:T(8,128)(2,1)S(1)} copy(bf16[128,1024]{1,0:T(8,128)(2,1)} %param.8) | data formatting | bytes 524288 | tf_op args[0]
  4.1 1.0 %copy_bitcast_fusion = bf16[64,384,16]{1,2,0:T(8,128)(2,1)} fusion(bf16[1,128,64,16]{1,3,2,0:T(8,128)(2,1)S(1)} %bitcast.107, bf16[1,128,64,16]{1,3,2,0:T(8,128)(2,1)S(1)} %bitcast.106, bf16[1,128,64,16]{1,3,2,0:T(8,128)(2,1)S(1)} %bitcast.105), kind=kLoop, calls=%fused_computation.12 | loop fusion | flops 786432 | bytes 1572864 | tf_op jit(solution)/shard_map/reshape | solution.py:107
  5.1 15.1 %all-to-all-start = ((bf16[64,384,16]{1,2,0:T(8,128)(2,1)}), bf16[64,384,16]{1,2,0:T(8,128)(2,1)S(1)}, u32[]{:S(2)}, u32[]{:S(2)}) async-start(bf16[64,384,16]{1,2,0:T(8,128)(2,1)} %copy_bitcast_fusion), calls=%async_computation | async-start | bytes 1572864 | tf_op jit(solution)/shard_map/all_to_all | solution.py:109
  20.3 0.1 constant_dynamic-slice_fusion.1
  20.3 0.1 concatenate.48
  20.5 0.8 fusion.38
  21.2 0.1 concatenate.55.d_ref
  21.3 0.8 sqrt_multiply_fusion
  22.1 0.7 concatenate.56.w_ref
  22.8 0.8 dynamic_slice.15
  23.6 0.1 concatenate.57
  23.6 0.1 fusion.36
  23.8 3.8 %broadcast_multiply_fusion.1 = (bf16[8,8,16,16,128]{4,1,3,0,2:T(8,128)(2,1)}, bf16[8,8,16,16,128]{4,1,3,0,2:T(8,128)(2,1)}) fusion(bf16[16,16,128]{2,1,0:T(8,128)(2,1)S(1)} %get-tuple-element.19, bf16[8,8]{1,0:T(8,128)(2,1)S(1)} %fusion.37, bf16[16,16,128]{2,1,0:T(8,128)(2,1)S(1)} %get-tuple-element.20), kind=kLoop, calls=%fused_computation.8 | loop fusion | flops 4194304 | bytes 8519808 | tf_op jit(solution)/shard_map/ico,ts->itcso/dot_general | solution.py:141
  27.7 15.5 %all-to-all-done = bf16[64,384,16]{1,2,0:T(8,128)(2,1)S(1)} async-done(((bf16[64,384,16]{1,2,0:T(8,128)(2,1)}), bf16[64,384,16]{1,2,0:T(8,128)(2,1)S(1)}, u32[]{:S(2)}, u32[]{:S(2)}) %all-to-all-start) | async-done | bytes 786464 | tf_op jit(solution)/shard_map/all_to_all | solution.py:109
  43.2 0.2 fusion.39
  43.5 0.2 copy.72
  43.9 0.2 copy.75
  44.0 0.1 fusion.32
  44.2 1.0 %fusion.20.g_ref = bf16[1024,128]{1,0:T(8,128)(2,1)} fusion(f32[1026,128]{1,0:T(8,128)S(1)} %get-tuple-element.33, f32[1026,128]{1,0:T(8,128)S(1)} %get-tuple-element.32, f32[128]{0:T(128)S(1)} %get-tuple-element.22, f32[128]{0:T(128)S(1)} %get-tuple-element.23, f32[128]{0:T(128)S(1)} %get-tuple-element.24, f32[128]{0:T(128)S(1)} %get-tuple-element.25, ...), kind=kLoop, calls=%fused_computation.22 | loop fusion | flops 1572864 | bytes 3410944 | tf_op jit(solution)/shard_map/convert_element_type | solution.py:128
  45.2 7.0 %shard_map.95 = (f32[1024,128]{1,0:T(8,128)}, f32[16,128]{1,0:T(8,128)}) custom-call(bf16[1024,128]{1,0:T(8,128)(2,1)} %fusion.20.g_ref, f32[16,128]{1,0:T(8,128)} %copy-done.6, f32[16,128]{1,0:T(8,128)} %concatenate.56.w_ref), custom_call_target="tpu_custom_call" | custom-call | tf_op jit(solution)/shard_map/pallas_call | solution.py:71
  52.2 0.8 mul.214
  53.1 0.3 multiply_reduce_fusion.1
  53.4 0.1 reshape.276
  53.6 0.2 copy.69
  53.8 0.1 fusion.30
  53.9 1.4 %multiply_reduce_fusion = f32[1024,128]{1,0:T(8,128)S(1)} fusion(f32[1024]{0:T(1024)S(1)} %iota_add_fusion, f32[16,128]{1,0:T(8,128)S(1)} %neg.17, f32[16,128]{1,0:T(8,128)S(1)} %mul.217), kind=kLoop, calls=%fused_computation | loop fusion | flops 6160384 | bytes 544768 | tf_op jit(solution)/shard_map/reduce_sum | solution.py:87
  55.3 0.3 fusion.26
  55.6 0.1 slice.167
  55.7 0.1 reshape.279
  55.8 0.1 copy.77
  56.0 0.1 reshape.281
  56.1 3.2 %fusion = f32[64,1024]{1,0:T(8,128)S(1)} fusion(bf16[64,2048]{1,0:T(8,128)(2,1)S(1)} %reshape.281, bf16[256,8,8,128]{3,2,1,0:T(8,128)(2,1)} %bitcast.92), kind=kOutput, calls=%fused_computation.1 | convolution fusion | flops 268435456 | bytes 4718592 | tf_op jit(solution)/shard_map/dot_general | solution.py:147
  59.3 0.3 copy-done.1
  59.6 0.8 fusion.12
  60.5 0.7 convert_element_type.71
  61.1 0.4 copy.80
  61.6 0.9 pad_maximum_fusion
  62.5 7.4 %all-to-all-start.1 = ((bf16[64,192,1,1,16]{1,4,3,2,0:T(8,128)(2,1)}), bf16[64,192,1,1,16]{1,4,3,2,0:T(8,128)(2,1)S(1)}, u32[]{:S(2)}, u32[]{:S(2)}) async-start(bf16[64,192,1,1,16]{1,4,3,2,0:T(8,128)(2,1)} %pad_maximum_fusion), calls=%async_computation.1 | async-start | bytes 1048576 | tf_op jit(solution)/shard_map/all_to_all | solution.py:156
  70.0 0.6 dynamic-slice
  71.2 15.6 %all-to-all-done.1 = bf16[64,192,1,1,16]{1,4,3,2,0:T(8,128)(2,1)S(1)} async-done(((bf16[64,192,1,1,16]{1,4,3,2,0:T(8,128)(2,1)}), bf16[64,192,1,1,16]{1,4,3,2,0:T(8,128)(2,1)S(1)}, u32[]{:S(2)}, u32[]{:S(2)}) %all-to-all-start.1) | async-done | bytes 393248 | tf_op jit(solution)/shard_map/all_to_all | solution.py:156
  86.9 0.1 convert_reduce_fusion
  87.0 0.8 copy.82
  87.8 0.1 copy.81
  87.9 0.1 reduce_sum.32
  88.0 8.3 %all-reduce.4 = bf16[8,128]{1,0:T(8,128)(2,1)S(1)} all-reduce(f32[8,128]{1,0:T(8,128)S(1)} %reduce_sum.32), channel_id=2, replica_groups=mesh['seq'=64,'tp'=4] {'tp'}, use_global_device_ids=true, to_apply=%region_3.4.clone | all-reduce | flops 1024 | bytes 6144
  96.2 0.5 dynamic-slice_convert_fusion
  (37 shorter events, 0.7 us)
Async XLA Ops:
  0.6 19.6 %copy-start = (f32[3,3,1024]{2,1,0:T(4,128)S(1)}, f32[3,3,1024]{2,1,0:T(4,128)}, u32[]{:S(2)}) copy-start(f32[3,3,1024]{2,1,0:T(4,128)} %param.11) | copy-start | bytes 110596
  0.6 23.2 %copy-start.4 = (bf16[32,16,128]{2,1,0:T(8,128)(2,1)S(1)}, bf16[32,16,128]{2,1,0:T(8,128)(2,1)}, u32[]{:S(2)}) copy-start(bf16[32,16,128]{2,1,0:T(8,128)(2,1)} %param.15) | copy-start | bytes 393220
  5.1 38.1 %all-to-all-start = ((bf16[64,384,16]{1,2,0:T(8,128)(2,1)}), bf16[64,384,16]{1,2,0:T(8,128)(2,1)S(1)}, u32[]{:S(2)}, u32[]{:S(2)}) async-start(bf16[64,384,16]{1,2,0:T(8,128)(2,1)} %copy_bitcast_fusion), calls=%async_computation | async-start | bytes 1572864 | tf_op jit(solution)/shard_map/all_to_all | solution.py:109
  21.3 6.4 %copy-start.6 = (f32[16,128]{1,0:T(8,128)}, f32[16,128]{1,0:T(8,128)S(1)}, u32[]{:S(2)}) copy-start(f32[16,128]{1,0:T(8,128)S(1)} %concatenate.55.d_ref) | copy-start | bytes 24580
  43.5 10.0 %copy-start.5 = (f32[16,128]{1,0:T(8,128)S(1)}, f32[16,128]{1,0:T(8,128)}, u32[]{:S(2)}) copy-start(f32[16,128]{1,0:T(8,128)} %concatenate.56.w_ref) | copy-start | bytes 24580
  45.2 10.1 %copy-start.2 = (bf16[1024,128]{1,0:T(8,128)(2,1)S(1)}, bf16[1024,128]{1,0:T(8,128)(2,1)}, u32[]{:S(2)}) copy-start(bf16[1024,128]{1,0:T(8,128)(2,1)} %fusion.20.g_ref) | copy-start | bytes 786436
  52.2 3.1 %copy-start.3 = (f32[1024,128]{1,0:T(8,128)S(1)}, f32[1024,128]{1,0:T(8,128)}, u32[]{:S(2)}) copy-start(f32[1024,128]{1,0:T(8,128)} %get-tuple-element.4) | copy-start | bytes 1572868
  56.1 3.5 %copy-start.1 = (bf16[8,8,16,16,128]{4,1,3,0,2:T(8,128)(2,1)S(1)}, bf16[8,8,16,16,128]{4,1,3,0,2:T(8,128)(2,1)}, u32[]{:S(2)}) copy-start(bf16[8,8,16,16,128]{4,1,3,0,2:T(8,128)(2,1)} %get-tuple-element.30) | copy-start | bytes 12582916
  60.4 9.5 %copy-start.7 = (u32[256]{0:T(256)S(1)}, u32[256]{0:T(256)}, u32[]{:S(2)}) copy-start(u32[256]{0:T(256)} %constant.38) | copy-start | bytes 3076
  62.5 24.3 %all-to-all-start.1 = ((bf16[64,192,1,1,16]{1,4,3,2,0:T(8,128)(2,1)}), bf16[64,192,1,1,16]{1,4,3,2,0:T(8,128)(2,1)S(1)}, u32[]{:S(2)}, u32[]{:S(2)}) async-start(bf16[64,192,1,1,16]{1,4,3,2,0:T(8,128)(2,1)} %pad_maximum_fusion), calls=%async_computation.1 | async-start | bytes 1048576 | tf_op jit(solution)/shard_map/all_to_all | solution.py:156

commit v20 on v18

--- a/solution.py
+++ b/solution.py
@@ -58,7 +58,8 @@
         total_ref[pl.ds(r, 1), :] = state
         return carry
 
-    lax.fori_loop(0, d_ref.shape[0], mode, 0)
+    for r in range(d_ref.shape[0]):
+        mode(r, 0)
 
 
 def packed_conv(packed, residues, decays, parts):

time: 97.3 us -> 96 us (0.987)
  Pallas kernels: 7.03 us -> 5.78 us
    pallas_call x1, Pallas kernels: 7.03 us -> 5.78 us  [packed_conv(): pl.pallas_call(conv_kernel, out_shape=(jax.ShapeDtypeStruct((seg, lanes),...]
where the time goes in v20:
time: 96 us; the launch traced here: 95.5 us
  waiting for transfers between devices  31.1 us (32%)
  starting transfers between devices  22.5 us (23%)
  local copies, waits for them, and re-layouts  11.2 us (12%)
  other arithmetic  10.9 us (11%)
  blocking collectives  8.26 us (9%)
  Pallas kernels  5.78 us (6%)
  matrix products  4.03 us (4%)
  between operations  1.66 us (2%)
    all_to_all x1, waiting for transfers between devices, shards(): lax.all_to_all(outgoing, 'v', split_axis=0, concat_axis=3, tiled=True)[0]  15.6 us
    all_to_all x1, waiting for transfers between devices, shards(): lax.all_to_all(payload, 'v', split_axis=0, concat_axis=0, tiled=True)  15.5 us
    all_to_all x1, starting transfers between devices, shards(): lax.all_to_all(payload, 'v', split_axis=0, concat_axis=0, tiled=True)  15.1 us
    unnamed x1, blocking collectives  8.26 us
    all_to_all x1, starting transfers between devices, shards(): lax.all_to_all(outgoing, 'v', split_axis=0, concat_axis=3, tiled=True)[0]  7.4 us
    pallas_call x1, Pallas kernels, packed_conv(): pl.pallas_call(conv_kernel, out_shape=(jax.ShapeDtypeStruct((seg, lanes),...  5.78 us
    unnamed x25, local copies, waits for them, and re-layouts  5.31 us
    dot_general x1, other arithmetic, spread(): jnp.einsum('ico,ts->itcso', taps, eye)  3.85 us
  transfers between devices with their start and end apart: 2, of which 2 were waited for; matrix products, arithmetic and copies ran while one was open for 8% of the time, Pallas kernels for 0%

profile of v20, /device:TPU:1, one launch (start us, length us, event | category | flops | bytes accessed | tf_op | source)
XLA Modules:
  0.0 95.5 jit_solution(3447744290193998987)
XLA Ops:
  0.7 1.2 %copy.45 = bf16[128,1024]{0,1:T(8,128)(2,1)S(1)} copy(bf16[128,1024]{1,0:T(8,128)(2,1)} %param.9) | data formatting | bytes 524288 | tf_op args[1]
  1.8 1.1 %copy.46 = bf16[128,1024]{0,1:T(8,128)(2,1)S(1)} copy(bf16[128,1024]{1,0:T(8,128)(2,1)} %param.10) | data formatting | bytes 524288 | tf_op args[2]
  2.9 1.1 %copy.47 = bf16[128,1024]{0,1:T(8,128)(2,1)S(1)} copy(bf16[128,1024]{1,0:T(8,128)(2,1)} %param.8) | data formatting | bytes 524288 | tf_op args[0]
  4.1 1.0 %pad_maximum_fusion = bf16[64,384,16]{1,2,0:T(8,128)(2,1)} fusion(bf16[64,128,16]{1,2,0:T(8,128)(2,1)S(1)} %bitcast.107, bf16[64,128,16]{1,2,0:T(8,128)(2,1)S(1)} %bitcast.106, bf16[64,128,16]{1,2,0:T(8,128)(2,1)S(1)} %bitcast.105), kind=kLoop, calls=%fused_computation.12 | loop fusion | flops 2359296 | bytes 1572864 | tf_op jit(solution)/shard_map/concatenate | solution.py:106
  5.1 15.1 %all-to-all-start = ((bf16[64,384,16]{1,2,0:T(8,128)(2,1)}), bf16[64,384,16]{1,2,0:T(8,128)(2,1)S(1)}, u32[]{:S(2)}, u32[]{:S(2)}) async-start(bf16[64,384,16]{1,2,0:T(8,128)(2,1)} %pad_maximum_fusion), calls=%async_computation | async-start | bytes 1572864 | tf_op jit(solution)/shard_map/all_to_all | solution.py:110
  20.3 0.1 constant_dynamic-slice_fusion.1
  20.3 0.1 concatenate.50
  20.5 0.8 fusion.38
  21.2 0.1 concatenate.58.d_ref
  21.3 0.8 sqrt_multiply_fusion
  22.1 0.7 concatenate.59.w_ref
  22.8 0.8 dynamic_slice.15
  23.6 0.1 concatenate.60
  23.6 0.1 fusion.36
  23.8 3.8 %broadcast_multiply_fusion.1 = (bf16[8,8,16,16,128]{4,1,3,0,2:T(8,128)(2,1)}, bf16[8,8,16,16,128]{4,1,3,0,2:T(8,128)(2,1)}) fusion(bf16[16,16,128]{2,1,0:T(8,128)(2,1)S(1)} %get-tuple-element.17, bf16[8,8]{1,0:T(8,128)(2,1)S(1)} %fusion.37, bf16[16,16,128]{2,1,0:T(8,128)(2,1)S(1)} %get-tuple-element.18), kind=kLoop, calls=%fused_computation.8 | loop fusion | flops 4194304 | bytes 8519808 | tf_op jit(solution)/shard_map/ico,ts->itcso/dot_general | solution.py:142
  27.7 15.5 %all-to-all-done = bf16[64,384,16]{1,2,0:T(8,128)(2,1)S(1)} async-done(((bf16[64,384,16]{1,2,0:T(8,128)(2,1)}), bf16[64,384,16]{1,2,0:T(8,128)(2,1)S(1)}, u32[]{:S(2)}, u32[]{:S(2)}) %all-to-all-start) | async-done | bytes 786464 | tf_op jit(solution)/shard_map/all_to_all | solution.py:110
  43.2 0.2 fusion.39
  43.5 0.2 copy.52
  43.9 0.2 copy.55
  44.0 0.1 fusion.32
  44.2 1.0 %fusion.20.g_ref = bf16[1024,128]{1,0:T(8,128)(2,1)} fusion(f32[1026,128]{1,0:T(8,128)S(1)} %get-tuple-element.31, f32[1026,128]{1,0:T(8,128)S(1)} %get-tuple-element.30, f32[128]{0:T(128)S(1)} %get-tuple-element.20, f32[128]{0:T(128)S(1)} %get-tuple-element.21, f32[128]{0:T(128)S(1)} %get-tuple-element.22, f32[128]{0:T(128)S(1)} %get-tuple-element.23, ...), kind=kLoop, calls=%fused_computation.21 | loop fusion | flops 1572864 | bytes 3410944 | tf_op jit(solution)/shard_map/convert_element_type | solution.py:129
  45.2 5.8 %shard_map.95 = (f32[1024,128]{1,0:T(8,128)}, f32[16,128]{1,0:T(8,128)}) custom-call(bf16[1024,128]{1,0:T(8,128)(2,1)} %fusion.20.g_ref, f32[16,128]{1,0:T(8,128)} %copy-done.6, f32[16,128]{1,0:T(8,128)} %concatenate.59.w_ref), custom_call_target="tpu_custom_call" | custom-call | tf_op jit(solution)/shard_map/pallas_call | solution.py:72
  51.0 0.8 mul.214
  51.8 0.3 multiply_reduce_fusion.1
  52.1 0.1 reshape.277
  52.4 0.2 copy.49
  52.6 0.1 fusion.30
  52.6 1.4 %multiply_reduce_fusion = f32[1024,128]{1,0:T(8,128)S(1)} fusion(f32[1024]{0:T(1024)S(1)} %iota_add_fusion, f32[16,128]{1,0:T(8,128)S(1)} %neg.17, f32[16,128]{1,0:T(8,128)S(1)} %mul.217), kind=kLoop, calls=%fused_computation | loop fusion | flops 6160384 | bytes 544768 | tf_op jit(solution)/shard_map/reduce_sum | solution.py:88
  54.1 0.3 fusion.26
  54.4 0.1 slice.167
  54.4 0.1 reshape.280
  54.6 0.1 copy.57
  54.7 0.1 reshape.282
  54.9 3.2 %fusion = f32[64,1024]{1,0:T(8,128)S(1)} fusion(bf16[64,2048]{1,0:T(8,128)(2,1)S(1)} %reshape.282, bf16[256,8,8,128]{3,2,1,0:T(8,128)(2,1)} %bitcast.92), kind=kOutput, calls=%fused_computation.1 | convolution fusion | flops 268435456 | bytes 4718592 | tf_op jit(solution)/shard_map/dot_general | solution.py:148
  58.1 0.3 copy-done.1
  58.3 0.8 fusion.12
  59.2 0.7 convert_element_type.71
  59.9 0.4 copy.60
  60.3 0.9 pad_maximum_fusion.1
  61.3 7.4 %all-to-all-start.1 = ((bf16[64,192,1,1,16]{1,4,3,2,0:T(8,128)(2,1)}), bf16[64,192,1,1,16]{1,4,3,2,0:T(8,128)(2,1)S(1)}, u32[]{:S(2)}, u32[]{:S(2)}) async-start(bf16[64,192,1,1,16]{1,4,3,2,0:T(8,128)(2,1)} %pad_maximum_fusion.1), calls=%async_computation.1 | async-start | bytes 1048576 | tf_op jit(solution)/shard_map/all_to_all | solution.py:157
  68.7 0.6 dynamic-slice
  69.9 15.6 %all-to-all-done.1 = bf16[64,192,1,1,16]{1,4,3,2,0:T(8,128)(2,1)S(1)} async-done(((bf16[64,192,1,1,16]{1,4,3,2,0:T(8,128)(2,1)}), bf16[64,192,1,1,16]{1,4,3,2,0:T(8,128)(2,1)S(1)}, u32[]{:S(2)}, u32[]{:S(2)}) %all-to-all-start.1) | async-done | bytes 393248 | tf_op jit(solution)/shard_map/all_to_all | solution.py:157
  85.6 0.1 convert_reduce_fusion
  85.7 0.8 copy.62
  86.6 0.1 copy.61
  86.6 0.1 reduce_sum.32
  86.7 8.3 %all-reduce.4 = bf16[8,128]{1,0:T(8,128)(2,1)S(1)} all-reduce(f32[8,128]{1,0:T(8,128)S(1)} %reduce_sum.32), channel_id=2, replica_groups=mesh['seq'=64,'tp'=4] {'tp'}, use_global_device_ids=true, to_apply=%region_3.4.clone | all-reduce | flops 1024 | bytes 6144
  95.0 0.5 dynamic-slice_convert_fusion
  (37 shorter events, 0.7 us)
Async XLA Ops:
  0.6 19.6 %copy-start = (f32[3,3,1024]{2,1,0:T(4,128)S(1)}, f32[3,3,1024]{2,1,0:T(4,128)}, u32[]{:S(2)}) copy-start(f32[3,3,1024]{2,1,0:T(4,128)} %param.11) | copy-start | bytes 110596
  0.6 23.2 %copy-start.4 = (bf16[32,16,128]{2,1,0:T(8,128)(2,1)S(1)}, bf16[32,16,128]{2,1,0:T(8,128)(2,1)}, u32[]{:S(2)}) copy-start(bf16[32,16,128]{2,1,0:T(8,128)(2,1)} %param.15) | copy-start | bytes 393220
  5.1 38.1 %all-to-all-start = ((bf16[64,384,16]{1,2,0:T(8,128)(2,1)}), bf16[64,384,16]{1,2,0:T(8,128)(2,1)S(1)}, u32[]{:S(2)}, u32[]{:S(2)}) async-start(bf16[64,384,16]{1,2,0:T(8,128)(2,1)} %pad_maximum_fusion), calls=%async_computation | async-start | bytes 1572864 | tf_op jit(solution)/shard_map/all_to_all | solution.py:110
  21.3 6.4 %copy-start.6 = (f32[16,128]{1,0:T(8,128)}, f32[16,128]{1,0:T(8,128)S(1)}, u32[]{:S(2)}) copy-start(f32[16,128]{1,0:T(8,128)S(1)} %concatenate.58.d_ref) | copy-start | bytes 24580
  43.5 8.8 %copy-start.5 = (f32[16,128]{1,0:T(8,128)S(1)}, f32[16,128]{1,0:T(8,128)}, u32[]{:S(2)}) copy-start(f32[16,128]{1,0:T(8,128)} %concatenate.59.w_ref) | copy-start | bytes 24580
  45.2 8.8 %copy-start.2 = (bf16[1024,128]{1,0:T(8,128)(2,1)S(1)}, bf16[1024,128]{1,0:T(8,128)(2,1)}, u32[]{:S(2)}) copy-start(bf16[1024,128]{1,0:T(8,128)(2,1)} %fusion.20.g_ref) | copy-start | bytes 786436
  51.0 3.1 %copy-start.3 = (f32[1024,128]{1,0:T(8,128)S(1)}, f32[1024,128]{1,0:T(8,128)}, u32[]{:S(2)}) copy-start(f32[1024,128]{1,0:T(8,128)} %get-tuple-element.4) | copy-start | bytes 1572868
  54.9 3.5 %copy-start.1 = (bf16[8,8,16,16,128]{4,1,3,0,2:T(8,128)(2,1)S(1)}, bf16[8,8,16,16,128]{4,1,3,0,2:T(8,128)(2,1)}, u32[]{:S(2)}) copy-start(bf16[8,8,16,16,128]{4,1,3,0,2:T(8,128)(2,1)} %get-tuple-element.28) | copy-start | bytes 12582916
  59.2 9.5 %copy-start.7 = (u32[256]{0:T(256)S(1)}, u32[256]{0:T(256)}, u32[]{:S(2)}) copy-start(u32[256]{0:T(256)} %constant.38) | copy-start | bytes 3076
  61.3 24.3 %all-to-all-start.1 = ((bf16[64,192,1,1,16]{1,4,3,2,0:T(8,128)(2,1)}), bf16[64,192,1,1,16]{1,4,3,2,0:T(8,128)(2,1)S(1)}, u32[]{:S(2)}, u32[]{:S(2)}) async-start(bf16[64,192,1,1,16]{1,4,3,2,0:T(8,128)(2,1)} %pad_maximum_fusion.1), calls=%async_computation.1 | async-start | bytes 1048576 | tf_op jit(solution)/shard_map/all_to_all | solution.py:157

commit v21 on v20

--- a/solution.py
+++ b/solution.py
@@ -34,14 +34,13 @@
     col = lax.broadcasted_iota(jnp.int32, (CHUNK, CHUNK), 1)
     lower = (row >= col).astype(jnp.bfloat16)
     steps = lax.broadcasted_iota(jnp.int32, (CHUNK, width), 0).astype(jnp.float32)
-    out_ref[...] = jnp.zeros(out_ref.shape, jnp.float32)
 
     def mode(r, carry):
         d = d_ref[pl.ds(r, 1), :]
         w = w_ref[pl.ds(r, 1), :]
         grow = jnp.exp(d * steps)
         shrink = w * jnp.exp(-d * steps)
-        after = w * jnp.exp(-d * (steps + 1.0))
+        step = jnp.exp(-d)
         tail = jnp.exp(-d * float(CHUNK - 1))
         hop = jnp.exp(-d * float(CHUNK))
         state = jnp.zeros((1, width), jnp.float32)
@@ -53,7 +52,11 @@
             y = jnp.dot(lower, high, preferred_element_type=jnp.float32) + jnp.dot(
                 lower, low, preferred_element_type=jnp.float32
             )
-            out_ref[rows, :] += shrink * y + after * state
+            part = shrink * (y + step * state)
+            if r == 0:
+                out_ref[rows, :] = part
+            else:
+                out_ref[rows, :] += part
             state = hop * state + tail * y[CHUNK - 1 : CHUNK, :]
         total_ref[pl.ds(r, 1), :] = state
         return carry

time: 96 us -> 95.3 us (level)
  no operation moved by 1% of the time
where the time goes in v21:
time: 95.3 us; the launch traced here: 94.8 us
  waiting for transfers between devices  31.1 us (33%)
  starting transfers between devices  22.5 us (24%)
  local copies, waits for them, and re-layouts  11.2 us (12%)
  other arithmetic  10.9 us (11%)
  blocking collectives  8.26 us (9%)
  Pallas kernels  5.02 us (5%)
  matrix products  4.03 us (4%)
  between operations  1.66 us (2%)
    all_to_all x1, waiting for transfers between devices, shards(): lax.all_to_all(outgoing, 'v', split_axis=0, concat_axis=3, tiled=True)[0]  15.6 us
    all_to_all x1, waiting for transfers between devices, shards(): lax.all_to_all(payload, 'v', split_axis=0, concat_axis=0, tiled=True)  15.5 us
    all_to_all x1, starting transfers between devices, shards(): lax.all_to_all(payload, 'v', split_axis=0, concat_axis=0, tiled=True)  15.1 us
    unnamed x1, blocking collectives  8.26 us
    all_to_all x1, starting transfers between devices, shards(): lax.all_to_all(outgoing, 'v', split_axis=0, concat_axis=3, tiled=True)[0]  7.4 us
    unnamed x25, local copies, waits for them, and re-layouts  5.31 us
    pallas_call x1, Pallas kernels, packed_conv(): pl.pallas_call(conv_kernel, out_shape=(jax.ShapeDtypeStruct((seg, lanes),...  5.02 us
    dot_general x1, other arithmetic, spread(): jnp.einsum('ico,ts->itcso', taps, eye)  3.85 us
  transfers between devices with their start and end apart: 2, of which 2 were waited for; matrix products, arithmetic and copies ran while one was open for 8% of the time, Pallas kernels for 0%

profile of v21, /device:TPU:1, one launch (start us, length us, event | category | flops | bytes accessed | tf_op | source)
XLA Modules:
  0.0 94.8 jit_solution(5619664007599443588)
XLA Ops:
  0.7 1.2 %copy.45 = bf16[128,1024]{0,1:T(8,128)(2,1)S(1)} copy(bf16[128,1024]{1,0:T(8,128)(2,1)} %param.9) | data formatting | bytes 524288 | tf_op args[1]
  1.8 1.1 %copy.46 = bf16[128,1024]{0,1:T(8,128)(2,1)S(1)} copy(bf16[128,1024]{1,0:T(8,128)(2,1)} %param.10) | data formatting | bytes 524288 | tf_op args[2]
  2.9 1.1 %copy.47 = bf16[128,1024]{0,1:T(8,128)(2,1)S(1)} copy(bf16[128,1024]{1,0:T(8,128)(2,1)} %param.8) | data formatting | bytes 524288 | tf_op args[0]
  4.1 1.0 %pad_maximum_fusion = bf16[64,384,16]{1,2,0:T(8,128)(2,1)} fusion(bf16[64,128,16]{1,2,0:T(8,128)(2,1)S(1)} %bitcast.107, bf16[64,128,16]{1,2,0:T(8,128)(2,1)S(1)} %bitcast.106, bf16[64,128,16]{1,2,0:T(8,128)(2,1)S(1)} %bitcast.105), kind=kLoop, calls=%fused_computation.12 | loop fusion | flops 2359296 | bytes 1572864 | tf_op jit(solution)/shard_map/concatenate | solution.py:109
  5.1 15.1 %all-to-all-start = ((bf16[64,384,16]{1,2,0:T(8,128)(2,1)}), bf16[64,384,16]{1,2,0:T(8,128)(2,1)S(1)}, u32[]{:S(2)}, u32[]{:S(2)}) async-start(bf16[64,384,16]{1,2,0:T(8,128)(2,1)} %pad_maximum_fusion), calls=%async_computation | async-start | bytes 1572864 | tf_op jit(solution)/shard_map/all_to_all | solution.py:113
  20.3 0.1 constant_dynamic-slice_fusion.1
  20.3 0.1 concatenate.50
  20.5 0.8 fusion.38
  21.2 0.1 concatenate.58.d_ref
  21.3 0.8 sqrt_multiply_fusion
  22.1 0.7 concatenate.59.w_ref
  22.8 0.8 dynamic_slice.15
  23.6 0.1 concatenate.60
  23.6 0.1 fusion.36
  23.8 3.8 %broadcast_multiply_fusion.1 = (bf16[8,8,16,16,128]{4,1,3,0,2:T(8,128)(2,1)}, bf16[8,8,16,16,128]{4,1,3,0,2:T(8,128)(2,1)}) fusion(bf16[16,16,128]{2,1,0:T(8,128)(2,1)S(1)} %get-tuple-element.17, bf16[8,8]{1,0:T(8,128)(2,1)S(1)} %fusion.37, bf16[16,16,128]{2,1,0:T(8,128)(2,1)S(1)} %get-tuple-element.18), kind=kLoop, calls=%fused_computation.8 | loop fusion | flops 4194304 | bytes 8519808 | tf_op jit(solution)/shard_map/ico,ts->itcso/dot_general | solution.py:145
  27.7 15.5 %all-to-all-done = bf16[64,384,16]{1,2,0:T(8,128)(2,1)S(1)} async-done(((bf16[64,384,16]{1,2,0:T(8,128)(2,1)}), bf16[64,384,16]{1,2,0:T(8,128)(2,1)S(1)}, u32[]{:S(2)}, u32[]{:S(2)}) %all-to-all-start) | async-done | bytes 786464 | tf_op jit(solution)/shard_map/all_to_all | solution.py:113
  43.2 0.2 fusion.39
  43.5 0.2 copy.52
  43.9 0.2 copy.55
  44.0 0.1 fusion.32
  44.2 1.0 %fusion.20.g_ref = bf16[1024,128]{1,0:T(8,128)(2,1)} fusion(f32[1026,128]{1,0:T(8,128)S(1)} %get-tuple-element.31, f32[1026,128]{1,0:T(8,128)S(1)} %get-tuple-element.30, f32[128]{0:T(128)S(1)} %get-tuple-element.20, f32[128]{0:T(128)S(1)} %get-tuple-element.21, f32[128]{0:T(128)S(1)} %get-tuple-element.22, f32[128]{0:T(128)S(1)} %get-tuple-element.23, ...), kind=kLoop, calls=%fused_computation.21 | loop fusion | flops 1572864 | bytes 3410944 | tf_op jit(solution)/shard_map/convert_element_type | solution.py:132
  45.2 5.0 %shard_map.95 = (f32[1024,128]{1,0:T(8,128)}, f32[16,128]{1,0:T(8,128)}) custom-call(bf16[1024,128]{1,0:T(8,128)(2,1)} %fusion.20.g_ref, f32[16,128]{1,0:T(8,128)} %copy-done.6, f32[16,128]{1,0:T(8,128)} %concatenate.59.w_ref), custom_call_target="tpu_custom_call" | custom-call | tf_op jit(solution)/shard_map/pallas_call | solution.py:75
  50.2 0.8 mul.214
  51.1 0.3 multiply_reduce_fusion.1
  51.4 0.1 reshape.277
  51.6 0.2 copy.49
  51.8 0.1 fusion.30
  51.9 1.4 %multiply_reduce_fusion = f32[1024,128]{1,0:T(8,128)S(1)} fusion(f32[1024]{0:T(1024)S(1)} %iota_add_fusion, f32[16,128]{1,0:T(8,128)S(1)} %neg.17, f32[16,128]{1,0:T(8,128)S(1)} %mul.217), kind=kLoop, calls=%fused_computation | loop fusion | flops 6160384 | bytes 544768 | tf_op jit(solution)/shard_map/reduce_sum | solution.py:91
  53.3 0.3 fusion.26
  53.6 0.1 slice.167
  53.7 0.1 reshape.280
  53.8 0.1 copy.57
  54.0 0.1 reshape.282
  54.1 3.2 %fusion = f32[64,1024]{1,0:T(8,128)S(1)} fusion(bf16[64,2048]{1,0:T(8,128)(2,1)S(1)} %reshape.282, bf16[256,8,8,128]{3,2,1,0:T(8,128)(2,1)} %bitcast.92), kind=kOutput, calls=%fused_computation.1 | convolution fusion | flops 268435456 | bytes 4718592 | tf_op jit(solution)/shard_map/dot_general | solution.py:151
  57.3 0.3 copy-done.1
  57.6 0.8 fusion.12
  58.5 0.7 convert_element_type.71
  59.1 0.4 copy.60
  59.6 0.9 pad_maximum_fusion.1
  60.5 7.4 %all-to-all-start.1 = ((bf16[64,192,1,1,16]{1,4,3,2,0:T(8,128)(2,1)}), bf16[64,192,1,1,16]{1,4,3,2,0:T(8,128)(2,1)S(1)}, u32[]{:S(2)}, u32[]{:S(2)}) async-start(bf16[64,192,1,1,16]{1,4,3,2,0:T(8,128)(2,1)} %pad_maximum_fusion.1), calls=%async_computation.1 | async-start | bytes 1048576 | tf_op jit(solution)/shard_map/all_to_all | solution.py:160
  67.9 0.6 dynamic-slice
  69.2 15.6 %all-to-all-done.1 = bf16[64,192,1,1,16]{1,4,3,2,0:T(8,128)(2,1)S(1)} async-done(((bf16[64,192,1,1,16]{1,4,3,2,0:T(8,128)(2,1)}), bf16[64,192,1,1,16]{1,4,3,2,0:T(8,128)(2,1)S(1)}, u32[]{:S(2)}, u32[]{:S(2)}) %all-to-all-start.1) | async-done | bytes 393248 | tf_op jit(solution)/shard_map/all_to_all | solution.py:160
  84.9 0.1 convert_reduce_fusion
  85.0 0.8 copy.62
  85.8 0.1 copy.61
  85.9 0.1 reduce_sum.32
  86.0 8.3 %all-reduce.4 = bf16[8,128]{1,0:T(8,128)(2,1)S(1)} all-reduce(f32[8,128]{1,0:T(8,128)S(1)} %reduce_sum.32), channel_id=2, replica_groups=mesh['seq'=64,'tp'=4] {'tp'}, use_global_device_ids=true, to_apply=%region_3.4.clone | all-reduce | flops 1024 | bytes 6144
  94.2 0.5 dynamic-slice_convert_fusion
  (37 shorter events, 0.7 us)
Async XLA Ops:
  0.6 19.6 %copy-start = (f32[3,3,1024]{2,1,0:T(4,128)S(1)}, f32[3,3,1024]{2,1,0:T(4,128)}, u32[]{:S(2)}) copy-start(f32[3,3,1024]{2,1,0:T(4,128)} %param.11) | copy-start | bytes 110596
  0.6 23.2 %copy-start.4 = (bf16[32,16,128]{2,1,0:T(8,128)(2,1)S(1)}, bf16[32,16,128]{2,1,0:T(8,128)(2,1)}, u32[]{:S(2)}) copy-start(bf16[32,16,128]{2,1,0:T(8,128)(2,1)} %param.15) | copy-start | bytes 393220
  5.1 38.1 %all-to-all-start = ((bf16[64,384,16]{1,2,0:T(8,128)(2,1)}), bf16[64,384,16]{1,2,0:T(8,128)(2,1)S(1)}, u32[]{:S(2)}, u32[]{:S(2)}) async-start(bf16[64,384,16]{1,2,0:T(8,128)(2,1)} %pad_maximum_fusion), calls=%async_computation | async-start | bytes 1572864 | tf_op jit(solution)/shard_map/all_to_all | solution.py:113
  21.3 6.4 %copy-start.6 = (f32[16,128]{1,0:T(8,128)}, f32[16,128]{1,0:T(8,128)S(1)}, u32[]{:S(2)}) copy-start(f32[16,128]{1,0:T(8,128)S(1)} %concatenate.58.d_ref) | copy-start | bytes 24580
  43.5 8.0 %copy-start.5 = (f32[16,128]{1,0:T(8,128)S(1)}, f32[16,128]{1,0:T(8,128)}, u32[]{:S(2)}) copy-start(f32[16,128]{1,0:T(8,128)} %concatenate.59.w_ref) | copy-start | bytes 24580
  45.2 8.1 %copy-start.2 = (bf16[1024,128]{1,0:T(8,128)(2,1)S(1)}, bf16[1024,128]{1,0:T(8,128)(2,1)}, u32[]{:S(2)}) copy-start(bf16[1024,128]{1,0:T(8,128)(2,1)} %fusion.20.g_ref) | copy-start | bytes 786436
  50.2 3.1 %copy-start.3 = (f32[1024,128]{1,0:T(8,128)S(1)}, f32[1024,128]{1,0:T(8,128)}, u32[]{:S(2)}) copy-start(f32[1024,128]{1,0:T(8,128)} %get-tuple-element.4) | copy-start | bytes 1572868
  54.1 3.5 %copy-start.1 = (bf16[8,8,16,16,128]{4,1,3,0,2:T(8,128)(2,1)S(1)}, bf16[8,8,16,16,128]{4,1,3,0,2:T(8,128)(2,1)}, u32[]{:S(2)}) copy-start(bf16[8,8,16,16,128]{4,1,3,0,2:T(8,128)(2,1)} %get-tuple-element.28) | copy-start | bytes 12582916
  58.4 9.5 %copy-start.7 = (u32[256]{0:T(256)S(1)}, u32[256]{0:T(256)}, u32[]{:S(2)}) copy-start(u32[256]{0:T(256)} %constant.38) | copy-start | bytes 3076
  60.5 24.3 %all-to-all-start.1 = ((bf16[64,192,1,1,16]{1,4,3,2,0:T(8,128)(2,1)}), bf16[64,192,1,1,16]{1,4,3,2,0:T(8,128)(2,1)S(1)}, u32[]{:S(2)}, u32[]{:S(2)}) async-start(bf16[64,192,1,1,16]{1,4,3,2,0:T(8,128)(2,1)} %pad_maximum_fusion.1), calls=%async_computation.1 | async-start | bytes 1048576 | tf_op jit(solution)/shard_map/all_to_all | solution.py:160
